TPU v7x, 32 devices: a whole 2x2x4 slice. The times are simulated.
32 devices in a mesh: groups: 1, tok: 32 (over z, y, x, core).
Axes of the slice: x: 2, y: 2, z: 4, core: 2. Of those that a mesh axis runs over, the one named last changes fastest.
Arguments:
- queries: bfloat16 [4096, 2560], P(('groups', 'tok')), may hold values from -5 to 5
- key_rows: bfloat16 [4096, 2560], P(('groups', 'tok')), may hold values from -5 to 5
- value_rows: bfloat16 [4096, 2560], P(('groups', 'tok')), may hold values from -6 to 6
- learn_rates: float32 [4096, 8], P(('groups', 'tok')), may hold values from 0.0002 to 0.002
- frame_order: int32 [4096], P('groups'), may hold values from 0 to 4095, as said below
- window_ids: int32 [4096], P('groups'), may hold values from 0 to 7, never falling along the last dimension, each value on 1 to 2048 neighbouring positions
- fast_init: bfloat16 [640, 3, 2560], replicated, may hold values from -0.3125 to 0.3125
- norm_gain: float32 [2560], replicated, may hold values from 0.5 to 1.5
Outputs:
- layer_out: bfloat16 [4096, 2560], P(('groups', 'tok'))
Inputs may be any that keep to these rules, and one draw needn't show every extreme that they name: frame_order[i] is the sequence position of the token stored at row i; every position appears once, and every aligned block of 128 stored rows holds exactly 4 positions of every aligned block of 128 positions.
All inputs are finite; a program needn't handle non-finite values.
Results may differ from a plain program's by a relative error of at most 0.025.
Values may be sent and summed in bfloat16 or wider, within the bound.
No kernel may reach another device: no remote copies, remote signals or barrier semaphores. Data moves between devices by JAX's collectives and lax.ppermute only.
A program may use at most 192 MiB of HBM per device.

v0:
```python
import functools
import math

import jax
import jax.numpy as jnp
from jax import lax
from jax.experimental import pallas as pl
from jax.experimental.pallas import tpu as pltpu
from jax.sharding import PartitionSpec as P


HEADS = 8
HEAD_DIM = 320
ATT_DIM = 128
WINDOW = 1024
WIDTH = 2560
ATT_HEADS = 20
LANES = 128
EPS = 1e-06

PARTS = math.gcd(HEADS, ATT_HEADS)
PART_WIDTH = WIDTH // PARTS
PART_FAST = HEADS // PARTS
PART_ATT = ATT_HEADS // PARTS
SPAN = -(-HEAD_DIM // LANES) * LANES


F32 = jnp.float32
BF16 = jnp.bfloat16
VMEM = pltpu.VMEM


def iota(shape, dim):
    return lax.broadcasted_iota(jnp.int32, shape, dim)


def dot(a, b, dims=((1,), (0,))):
    return lax.dot_general(a, b, (dims, ((), ())), preferred_element_type=F32)


def column_of(row):
    n = row.shape[1]
    square = jnp.broadcast_to(row.astype(F32), (n, n))
    diagonal = iota((n, n), 0) == iota((n, n), 1)
    return jnp.sum(jnp.where(diagonal, square, 0.0), axis=1, keepdims=True)


def call(kernel, outs, ins, scratch=(), smem=0, flops=0, grid=None, in_specs=None, out_specs=None):
    specs = [pl.BlockSpec(memory_space=pltpu.SMEM)] * smem
    specs += in_specs or [pl.BlockSpec(memory_space=VMEM)] * (len(ins) - smem)
    moved = sum(x.size * x.dtype.itemsize for x in list(ins) + list(outs))
    extra = {} if grid is None else {"grid": grid}
    return pl.pallas_call(
        kernel,
        out_shape=list(outs),
        in_specs=specs,
        out_specs=out_specs or [pl.BlockSpec(memory_space=VMEM)] * len(outs),
        scratch_shapes=list(scratch),
        compiler_params=pltpu.CompilerParams(vmem_limit_bytes=48 << 20),
        cost_estimate=pl.CostEstimate(flops=flops, bytes_accessed=moved, transcendentals=0),
        **extra,
    )(*ins)


def pack_kernel(group_shift, low_shift, slots, place_ref, order_ref, rate_ref, query_ref, key_ref, value_ref, kv_ref, q_ref, choose_buf, extra_buf):
    n = query_ref.shape[0]
    planes, _, cores = kv_ref.shape[:3]

    @pl.when(pl.program_id(0) == 0)
    def _():
        pos = order_ref[pl.ds(place_ref[0], 1), :]
        pos_col = column_of(pos).astype(jnp.int32)
        group = lax.shift_right_logical(pos, group_shift)
        group_col = lax.shift_right_logical(pos_col, group_shift)
        earlier = (group_col == group) & (iota((n, n), 0) < iota((n, n), 1))
        rank = jnp.sum(jnp.where(earlier, 1.0, 0.0), axis=0, keepdims=True)
        slot = group * slots + rank.astype(jnp.int32)
        choose = jnp.where(iota((n, n), 0) == slot, 1.0, 0.0).astype(BF16)
        choose_buf[...] = choose
        rates = rate_ref[...]
        heads = rates.shape[1]
        extra = jnp.zeros((n, LANES), F32)
        for part in range(3):
            piece = rates.astype(BF16)
            rates = rates - piece.astype(F32)
            put = iota((heads, LANES), 1) == iota((heads, LANES), 0) + part * heads
            extra += dot(piece, jnp.where(put, 1.0, 0.0).astype(BF16))
        within = pos_col & ((1 << group_shift) - 1)
        high = lax.shift_right_logical(within, low_shift).astype(F32)
        low = (within & ((1 << low_shift) - 1)).astype(F32)
        lane = iota((n, LANES), 1)
        extra += jnp.where(lane == 3 * heads, high, 0.0) + jnp.where(lane == 3 * heads + 1, low, 0.0)
        extra_buf[...] = dot(choose, extra.astype(BF16)).astype(BF16)

    def put_rows(ref, rows, begin):
        width = rows.shape[1]
        for plane in range(planes):
            for core in range(cores):
                at = (plane * cores + core) * slots
                ref[plane, 0, core, :, begin : begin + width] = rows[at : at + slots]

    choose = choose_buf[...]
    put_rows(kv_ref, dot(choose, key_ref[...]).astype(BF16), 0)
    put_rows(kv_ref, dot(choose, value_ref[...]).astype(BF16), PART_WIDTH)
    put_rows(kv_ref, extra_buf[...], 2 * PART_WIDTH)
    put_rows(q_ref, dot(choose, query_ref[...]).astype(BF16), 0)


def arrival_choice(extra, low_shift):
    n = extra.shape[0]
    pick = iota((8, LANES), 1) == iota((8, LANES), 0) + 3 * HEADS
    rows = dot(jnp.where(pick, 1.0, 0.0).astype(BF16), extra, ((1,), (1,)))
    pos = rows[0:1] * float(1 << low_shift) + rows[1:2]
    return jnp.where(iota((n, n), 0) == pos.astype(jnp.int32), 1.0, 0.0).astype(BF16)


def place_kernel(low_shift, kv_in_ref, kv_ref, choose_ref):
    choose = arrival_choice(kv_in_ref[:, 2 * PART_WIDTH :], low_shift)
    choose_ref[...] = choose
    for part in range(2):
        lanes = slice(part * PART_WIDTH, (part + 1) * PART_WIDTH)
        kv_ref[:, lanes] = dot(choose, kv_in_ref[:, lanes]).astype(BF16)


def window_of(head):
    begin = head * HEAD_DIM // LANES * LANES
    begin = min(begin, PART_WIDTH - SPAN)
    return begin, head * HEAD_DIM - begin


def head_mask(head):
    _, offset = window_of(head)
    lane = iota((1, SPAN), 1)
    return (lane >= offset) & (lane < offset + HEAD_DIM)


def grads_kernel(chunk, place_ref, kv_ref, weight_ref, mine_ref, other_ref, key_buf, target_buf, dg_buf, du_buf, pr_buf, sums):
    n = kv_ref.shape[0]
    hidden = weight_ref.shape[2]
    part, core = place_ref[1], place_ref[2]
    for head in range(PART_FAST):
        begin, offset = window_of(head)
        valid = head_mask(head)
        rows = pl.ds(begin, SPAN)
        for at in range(0, n, chunk):
            here = pl.ds(at, chunk)
            extra = kv_ref[here, 2 * PART_WIDTH :].astype(F32)
            lane = iota((1, LANES), 1)
            own = part * PART_FAST + head
            wanted = (lane == own) | (lane == HEADS + own) | (lane == 2 * HEADS + own)
            rate = jnp.sum(jnp.where(wanted, extra, 0.0), axis=1, keepdims=True)
            key = jnp.where(valid, kv_ref[here, begin : begin + SPAN], jnp.zeros((), BF16))
            value = kv_ref[here, PART_WIDTH + begin : PART_WIDTH + begin + SPAN].astype(F32)
            target = jnp.where(valid, value * rate, 0.0).astype(BF16)
            key_buf[here, :] = key
            target_buf[here, :] = target
            gate = dot(key, weight_ref[0, rows, :])
            upward = dot(key, weight_ref[1, rows, :])
            backward = dot(target, weight_ref[2, rows, :])
            sigmoid = jax.nn.sigmoid(gate)
            active = gate * sigmoid
            pr_buf[here, :] = (active * upward).astype(BF16)
            du_buf[here, :] = (backward * active).astype(BF16)
            dg_buf[here, :] = (backward * upward * sigmoid * (1.0 + gate * (1.0 - sigmoid))).astype(BF16)
        for index, (left, right) in enumerate(((key_buf, dg_buf), (key_buf, du_buf), (target_buf, pr_buf))):
            total = dot(left[...], right[...], ((0,), (0,)))
            sums[head, :, index * hidden : (index + 1) * hidden] = total[offset : offset + HEAD_DIM].astype(BF16)
    mine_ref[...] = sums[core]
    other_ref[...] = sums[1 - core]


def attention_kernel(block, place_ref, choose_ref, query_in_ref, ids_ref, key_ref, key_low_ref, key_high_ref, value_ref, value_low_ref, value_high_ref, out_ref, query_ref, bias):
    n = choose_ref.shape[0]
    half = WINDOW // 2
    group = place_ref[3]
    last = ids_ref.shape[0] - 1

    @pl.when(pl.program_id(0) == 0)
    def _():
        mid = ids_ref[pl.ds(group, 1), :]
        low = ids_ref[pl.ds(jnp.maximum(group - 1, 0), 1), :]
        high = ids_ref[pl.ds(jnp.minimum(group + 1, last), 1), :]
        low = jnp.where(group > 0, low, -1)
        high = jnp.where(group < last, high, -1)
        for at in range(0, n, block):
            own = column_of(mid[:, at : at + block]).astype(jnp.int32)
            ids = jnp.concatenate([low[:, at:], mid, high[:, : at + block]], axis=1)
            span = ids.shape[1]
            gap = iota((block, span), 1) - iota((block, span), 0) - half
            allowed = (gap < half) & (gap > -half) & (own == ids)
            bias[at // block, :, :] = jnp.where(allowed, 0.0, -1e30)

    query = dot(choose_ref[...], query_in_ref[...]).astype(BF16)
    query_ref[...] = query
    factor = ATT_DIM ** (-0.5) * math.log2(math.e)
    for at in range(0, n, block):
        part = query[at : at + block]
        stops = (0, half - at, half - at + n, half + n + block - half)
        keys = (key_low_ref[at:, :], key_ref[...], key_high_ref[: at + block, :])
        values = (value_low_ref[at:, :], value_ref[...], value_high_ref[: at + block, :])
        scores = []
        for index in range(3):
            lanes = slice(stops[index], stops[index] + keys[index].shape[0])
            scores.append(dot(part, keys[index], ((1,), (1,))) + bias[at // block, :, lanes])
        peak = functools.reduce(jnp.maximum, [jnp.max(s, axis=1, keepdims=True) for s in scores])
        total = jnp.zeros_like(peak)
        mixed = jnp.zeros((block, ATT_DIM), F32)
        for score, value in zip(scores, values):
            weight = jnp.exp2((score - peak) * factor)
            total += jnp.sum(weight, axis=1, keepdims=True)
            mixed += dot(weight.astype(BF16), value)
        out_ref[pl.ds(at, block), :] = mixed / total


def apply_kernel(chunk, place_ref, weight_ref, query_ref, attended_ref, *refs):
    n = query_ref.shape[0]
    hidden = weight_ref.shape[2]
    planes = (len(refs) - 2) // 2
    mine_refs, other_refs, (out_ref, fresh) = refs[:planes], refs[planes : 2 * planes], refs[2 * planes :]
    piece = mine_refs[0].shape[0]
    core, plane = place_ref[2], place_ref[4 + PARTS]
    for head in range(PART_FAST):
        _, offset = window_of(head)
        for index in range(3):
            lanes = slice(index * hidden, (index + 1) * hidden)
            anchor = jnp.full((1, hidden), EPS, F32)
            length = jnp.full((1, hidden), EPS, F32)
            for step in range(planes):
                at = pl.multiple_of((plane + (planes - step)) % planes * piece, 16)
                base = weight_ref[index, pl.ds(at + head * HEAD_DIM, piece), :].astype(F32)
                grad = jnp.where(core == head, mine_refs[step][:, lanes], other_refs[step][:, lanes]).astype(F32)
                update = base + grad
                anchor += jnp.sum(base * base, axis=0, keepdims=True)
                length += jnp.sum(update * update, axis=0, keepdims=True)
            scale = jnp.sqrt(anchor) / jnp.sqrt(length)
            if offset:
                fresh[head, index, :offset, :] = jnp.zeros((offset, hidden), BF16)
            if offset + HEAD_DIM < SPAN:
                fresh[head, index, offset + HEAD_DIM :, :] = jnp.zeros((SPAN - offset - HEAD_DIM, hidden), BF16)
            for step in range(planes):
                at = pl.multiple_of((plane + (planes - step)) % planes * piece, 16)
                base = weight_ref[index, pl.ds(at + head * HEAD_DIM, piece), :].astype(F32)
                grad = jnp.where(core == head, mine_refs[step][:, lanes], other_refs[step][:, lanes]).astype(F32)
                fresh[head, index, pl.ds(at + offset, piece), :] = ((base + grad) * scale).astype(BF16)
    for at in range(0, n, chunk):
        here = pl.ds(at, chunk)
        parts = []
        for head in range(PART_FAST):
            begin, offset = window_of(head)
            query = query_ref[here, begin : begin + SPAN]
            gate = dot(query, fresh[head, 0])
            upward = dot(query, fresh[head, 1])
            product = (gate * jax.nn.sigmoid(gate) * upward).astype(BF16)
            parts.append((begin, dot(product, fresh[head, 2], ((1,), (1,)))))
        for lane in range(0, PART_WIDTH, LANES):
            total = attended_ref[here, lane : lane + LANES]
            for begin, value in parts:
                if begin <= lane < begin + SPAN:
                    total += value[:, lane - begin : lane - begin + LANES]
            out_ref[here, lane : lane + LANES] = total.astype(BF16)


def norm_kernel(place_ref, *refs):
    part_refs, gain_ref, out_ref, buf = refs[:PARTS], refs[PARTS], refs[PARTS + 1], refs[PARTS + 2]
    square = jnp.zeros((out_ref.shape[0], 1), F32)
    for index, ref in enumerate(part_refs):
        rows = ref[...]
        buf[place_ref[4 + index]] = rows
        wide = rows.astype(F32)
        square += jnp.sum(wide * wide, axis=1, keepdims=True)
    factor = lax.rsqrt(square / WIDTH + EPS)
    for part in range(PARTS):
        lanes = slice(part * PART_WIDTH, (part + 1) * PART_WIDTH)
        out_ref[:, lanes] = (buf[part].astype(F32) * factor * gain_ref[:, lanes]).astype(BF16)


def shards(queries, key_rows, value_rows, learn_rates, frame_order, window_ids, fast_init, norm_gain):
    tok_dev = queries.shape[0]
    hidden = fast_init.shape[0]
    sections = lax.axis_size("tok")
    plane_size = PARTS * PART_FAST
    planes = sections // plane_size
    group_rows = tok_dev * PARTS
    groups = planes * PART_FAST
    slots = tok_dev // groups
    half = WINDOW // 2
    assert PART_FAST == 2 and half == group_rows and group_rows & (group_rows - 1) == 0
    group_shift = group_rows.bit_length() - 1
    low_shift = group_shift // 2

    rank = lax.axis_index("tok")
    plane = rank // plane_size
    part = rank // PART_FAST % PARTS
    core = rank % PART_FAST
    row, column = part // 2, part % 2
    group = plane * PART_FAST + core

    def at(plane, row, column, core):
        return plane * plane_size + (row * 2 + column) * PART_FAST + core

    everyone = [(z, y, x, c) for z in range(planes) for y in range(2) for x in range(2) for c in range(2)]

    def permute(array, target):
        route = []
        for source in everyone:
            goal = target(*source)
            if goal is not None:
                route.append((at(*source), at(*goal)))
        return lax.ppermute(array, "tok", route)

    sources = [2 * (core ^ j // 2) + (column ^ j % 2) for j in range(PARTS)]
    place = jnp.stack([rank, part, core, group] + sources + [plane]).astype(jnp.int32)

    def weight_part():
        own = lax.dynamic_slice_in_dim(fast_init, part * PART_WIDTH, PART_WIDTH, 2)
        return jnp.transpose(own, (1, 2, 0))

    weights = weight_part()

    full = lambda a: pl.BlockSpec(a.shape, lambda h: (0,) * a.ndim)
    kv_width = 2 * PART_WIDTH + LANES
    shape = (planes, PARTS, PART_FAST, slots)
    orders = frame_order.reshape(sections, tok_dev)
    cut = pl.BlockSpec((tok_dev, PART_WIDTH), lambda h: (0, h))
    kv_out, q_out = call(
        functools.partial(pack_kernel, group_shift, low_shift, slots),
        [jax.ShapeDtypeStruct(shape + (kv_width,), BF16), jax.ShapeDtypeStruct(shape + (PART_WIDTH,), BF16)],
        [place, orders, learn_rates, queries, key_rows, value_rows],
        in_specs=[full(orders), full(learn_rates), cut, cut, cut],
        out_specs=[
            pl.BlockSpec((planes, 1, PART_FAST, slots, width), lambda h: (0, h, 0, 0, 0))
            for width in (kv_width, PART_WIDTH)
        ],
        grid=(PARTS,),
        scratch=[VMEM((tok_dev, tok_dev), BF16), VMEM((tok_dev, LANES), BF16)],
        smem=1, flops=2 * tok_dev * tok_dev * 3 * WIDTH,
    )

    def exchange(array):
        flat = array.reshape(sections, slots, array.shape[-1])
        return lax.all_to_all(flat, "tok", split_axis=0, concat_axis=0, tiled=True).reshape(group_rows, array.shape[-1])

    kv_in = exchange(kv_out)
    q_in = exchange(q_out)

    kv_seq, choose = call(
        functools.partial(place_kernel, low_shift),
        [jax.ShapeDtypeStruct((group_rows, 2 * PART_WIDTH), BF16), jax.ShapeDtypeStruct((group_rows, group_rows), BF16)],
        [kv_in], flops=2 * group_rows * group_rows * 2 * PART_WIDTH,
    )

    def neighbour(step):
        def target(z, y, x, c):
            goal = z * PART_FAST + c + step
            return (goal // PART_FAST, y, x, goal % PART_FAST) if 0 <= goal < groups else None

        return target

    kv_low = permute(kv_seq, neighbour(1))
    kv_high = permute(kv_seq, neighbour(-1))

    grad_shape = jax.ShapeDtypeStruct((HEAD_DIM, 3 * hidden), BF16)
    mine, other = call(
        functools.partial(grads_kernel, group_rows),
        [grad_shape, grad_shape], [place, kv_in, weights],
        scratch=[VMEM((group_rows, SPAN), BF16)] * 2 + [VMEM((group_rows, hidden), BF16)] * 3
        + [VMEM((PART_FAST, HEAD_DIM, 3 * hidden), BF16)],
        smem=1, flops=12 * group_rows * PART_WIDTH * hidden,
    )
    swap = lambda z, y, x, c: (z, y, x, 1 - c)
    pair = (mine.astype(F32) + permute(other, swap).astype(F32)).astype(BF16)

    piece = HEAD_DIM // planes
    assert piece * planes == HEAD_DIM and piece % 16 == 0

    def turned(step):
        return lambda z, y, x, c: ((z + step) % planes, y, x, c)

    def piece_of(which):
        return lax.dynamic_slice_in_dim(pair, which * piece, piece, 0)

    total = piece_of(plane).astype(F32)
    for step in range(1, planes):
        total += permute(piece_of((plane + step) % planes), turned(step)).astype(F32)
    total = total.astype(BF16)
    pieces = [total]
    for step in range(1, planes):
        pieces.append(permute(total, turned(step)))
    pieces_other = []
    for step in range(planes):
        pieces_other.append(permute(pieces[step], swap))

    block = min(LANES, group_rows)
    lane_block = lambda rows, shift: pl.BlockSpec((rows, ATT_DIM), lambda h: (0, h + shift))
    ids = window_ids.reshape(groups, group_rows)
    attended, query_seq = call(
        functools.partial(attention_kernel, block),
        [jax.ShapeDtypeStruct((group_rows, PART_WIDTH), F32), jax.ShapeDtypeStruct((group_rows, PART_WIDTH), BF16)],
        [place, choose, q_in, ids, kv_seq, kv_low, kv_high, kv_seq, kv_low, kv_high],
        in_specs=[full(choose), lane_block(group_rows, 0), full(ids)]
        + [lane_block(group_rows, 0)] * 3 + [lane_block(group_rows, PART_ATT)] * 3,
        out_specs=[lane_block(group_rows, 0)] * 2,
        grid=(PART_ATT,),
        scratch=[VMEM((group_rows // block, block, WINDOW + block), F32)],
        smem=1, flops=4 * group_rows * (WINDOW + block) * PART_WIDTH,
    )

    (combined,) = call(
        functools.partial(apply_kernel, group_rows),
        [jax.ShapeDtypeStruct((group_rows, PART_WIDTH), BF16)],
        [place, weights, query_seq, attended] + pieces + pieces_other,
        scratch=[VMEM((PART_FAST, 3, SPAN, hidden), BF16)],
        smem=1, flops=6 * group_rows * PART_WIDTH * hidden,
    )

    blocks = combined.reshape(PARTS, tok_dev, PART_WIDTH)
    parts = []
    for j in range(PARTS):
        goal = 2 * (column ^ j % 2) + (row ^ j // 2)
        send = lax.dynamic_index_in_dim(blocks, goal, 0, keepdims=False)
        parts.append(permute(send, lambda z, y, x, c, j=j: (z, c, x ^ j % 2, y ^ j // 2)))

    (out,) = call(
        norm_kernel,
        [jax.ShapeDtypeStruct((tok_dev, WIDTH), BF16)],
        [place] + parts + [norm_gain.reshape(1, WIDTH)],
        scratch=[VMEM((PARTS, tok_dev, PART_WIDTH), BF16)],
        smem=1, flops=6 * tok_dev * WIDTH,
    )
    return out


def solution(mesh):
    rows = P(("groups", "tok"), None)
    return jax.shard_map(
        shards,
        mesh=mesh,
        in_specs=(rows, rows, rows, rows, P("groups"), P("groups"), P(), P()),
        out_specs=rows,
        check_vma=False,
    )
```

profile of v0, /device:TPU:0, one launch (start us, length us, event | category | flops | bytes accessed | tf_op | source)
XLA Modules:
  0.0 184.4 jit_solution(9824789739492614094)
XLA Ops:
  4.9 3.4 %shard_map.82 = (bf16[4,4,2,16,1408]{4,3,2,1,0:T(8,128)(2,1)}, bf16[4,4,2,16,640]{4,3,2,1,0:T(8,128)(2,1)}) custom-call(s32[9]{0:T(128)S(1)} %stack.39.place_ref, s32[32,128]{1,0:T(8,128)S(1)} %bitcast.28, f32[128,8]{1,0:T(8,128)S(1)} %copy.10.rate_ref, bf16[128,2560]{1,0:T(8,128)(2,1)S(1)} %copy-done.3, bf16[128,2560]{1,0:T(8,128)(2,1)S(1)} %copy-done.4, ...), custom_call_target="tpu_custom_call" | custom-call | flops 251658240 | bytes 4083748 | tf_op jit(solution)/shard_map/pallas_call | solution.py:53
  8.3 7.3 %all-to-all-start = ((bf16[32,16,1408]{2,1,0:T(8,128)(2,1)}), bf16[32,16,1408]{2,1,0:T(8,128)(2,1)S(1)}, u32[]{:S(2)}, u32[]{:S(2)}) async-start(bf16[32,16,1408]{2,1,0:T(8,128)(2,1)} %bitcast.11), calls=%async_computation | async-start | bytes 2883584 | tf_op jit(solution)/shard_map/all_to_all | solution.py:341
  15.6 3.4 %constant_dynamic-slice_fusion.3 = bf16[640,3,640]{2,0,1:T(8,128)(2,1)} fusion(bf16[640,3,2560]{2,0,1:T(8,128)(2,1)} %param.14, s32[]{:T(128)S(6)} %select_n.70), kind=kLoop, calls=%fused_computation.9 | loop fusion | bytes 4915204 | tf_op jit(solution)/shard_map/dynamic_slice | solution.py:315
  19.0 5.1 %copy.11 = bf16[640,3,640]{0,2,1:T(8,128)(2,1)} copy(bf16[640,3,640]{2,0,1:T(8,128)(2,1)} %constant_dynamic-slice_fusion.3) | data formatting | bytes 4915200
  24.1 26.3 %all-to-all-done = bf16[32,16,1408]{2,1,0:T(8,128)(2,1)S(1)} async-done(((bf16[32,16,1408]{2,1,0:T(8,128)(2,1)}), bf16[32,16,1408]{2,1,0:T(8,128)(2,1)S(1)}, u32[]{:S(2)}, u32[]{:S(2)}) %all-to-all-start) | async-done | bytes 1441824 | tf_op jit(solution)/shard_map/all_to_all | solution.py:341
  50.4 8.4 %shard_map.85 = (bf16[320,1920]{1,0:T(8,128)(2,1)S(1)}, bf16[320,1920]{1,0:T(8,128)(2,1)}) custom-call(s32[9]{0:T(128)S(1)} %stack.39.place_ref, bf16[512,1408]{1,0:T(8,128)(2,1)S(1)} %bitcast.26, bf16[3,640,640]{2,1,0:T(8,128)(2,1)} %bitcast.29), custom_call_target="tpu_custom_call" | custom-call | flops 2516582400 | bytes 6357028 | tf_op jit(solution)/shard_map/pallas_call | solution.py:53
  59.9 3.7 %all-to-all-start.1 = ((bf16[32,16,640]{2,1,0:T(8,128)(2,1)}), bf16[32,16,640]{2,1,0:T(8,128)(2,1)S(1)}, u32[]{:S(2)}, u32[]{:S(2)}) async-start(bf16[32,16,640]{2,1,0:T(8,128)(2,1)} %bitcast.13), calls=%async_computation.1 | async-start | bytes 1310720 | tf_op jit(solution)/shard_map/all_to_all | solution.py:341
  63.7 1.4 copy-done.1
  67.6 3.1 %collective-permute-start = (bf16[512,1280]{1,0:T(8,128)(2,1)S(1)}, bf16[512,1280]{1,0:T(8,128)(2,1)S(1)}, u32[]{:S(2)}, u32[]{:S(2)}) collective-permute-start(bf16[512,1280]{1,0:T(8,128)(2,1)S(1)} %get-tuple-element.16.key_ref.value_ref), channel_id=1, source_target_pairs={{0,1},{1,8},{2,3},{3,10},{4,5},{5,12},{6,7},{7,14},{8,9},{9,16},{1... | collective-permute-start | bytes 3932168 | tf_op jit(solution)/shard_map/ppermute | solution.py:309
  70.7 1.9 %add_convert_fusion = bf16[320,1920]{1,0:T(8,128)(2,1)S(1)} fusion(bf16[320,1920]{1,0:T(8,128)(2,1)} %collective-permute-done.2, bf16[320,1920]{1,0:T(8,128)(2,1)} %copy-done.2), kind=kLoop, calls=%fused_computation | loop fusion | flops 2457600 | bytes 3686400 | tf_op jit(solution)/shard_map/convert_element_type | solution.py:371
  74.0 1.7 collective-permute-start.3
  75.7 2.9 %collective-permute-start.5 = (bf16[80,1920]{1,0:T(8,128)(2,1)}, bf16[80,1920]{1,0:T(8,128)(2,1)}, u32[]{:S(2)}, u32[]{:S(2)}) collective-permute-start(bf16[80,1920]{1,0:T(8,128)(2,1)} %get-tuple-element.22), channel_id=1, source_target_pairs={{0,24},{1,25},{2,26},{3,27},{4,28},{5,29},{6,30},{7,31},{8,0},{9,1... | collective-permute-start | bytes 921608 | tf_op jit(solution)/shard_map/ppermute | solution.py:309
  79.2 27.1 %collective-permute-done.3 = bf16[80,1920]{1,0:T(8,128)(2,1)} collective-permute-done((bf16[80,1920]{1,0:T(8,128)(2,1)}, bf16[80,1920]{1,0:T(8,128)(2,1)}, u32[]{:S(2)}, u32[]{:S(2)}) %collective-permute-start.3) | collective-permute-done | bytes 307232 | tf_op jit(solution)/shard_map/ppermute | solution.py:309
  107.6 14.3 %collective-permute-done.4 = bf16[80,1920]{1,0:T(8,128)(2,1)} collective-permute-done((bf16[80,1920]{1,0:T(8,128)(2,1)}, bf16[80,1920]{1,0:T(8,128)(2,1)}, u32[]{:S(2)}, u32[]{:S(2)}) %collective-permute-start.4) | collective-permute-done | bytes 307232 | tf_op jit(solution)/shard_map/ppermute | solution.py:309
  121.9 2.1 %add_convert_fusion.1.refs_0_ = bf16[80,1920]{1,0:T(8,128)(2,1)} fusion(bf16[80,1920]{1,0:T(8,128)(2,1)} %collective-permute-done.5, bf16[80,1920]{1,0:T(8,128)(2,1)} %collective-permute-done.4, bf16[80,1920]{1,0:T(8,128)(2,1)} %collective-permute-done.3, bf16[320,1920]{1,0:T(8,128)(2,1)} %copy-done.9, s32[]{:T(128)S(6)} %select_n.71), kind=kLoop, calls=%fused_computation.1 | loop fusion | flops 1228800 | bytes 1536004 | tf_op jit(solution)/shard_map/convert_element_type | solution.py:385
  124.1 2.0 %collective-permute-start.6 = (bf16[80,1920]{1,0:T(8,128)(2,1)}, bf16[80,1920]{1,0:T(8,128)(2,1)}, u32[]{:S(2)}, u32[]{:S(2)}) collective-permute-start(bf16[80,1920]{1,0:T(8,128)(2,1)} %add_convert_fusion.1.refs_0_), channel_id=1, source_target_pairs={{0,8},{1,9},{2,10},{3,11},{4,12},{5,13},{6,14},{7,15},{8,16},{9,17... | collective-permute-start | bytes 921608 | tf_op jit(solution)/shard_map/ppermute | solution.py:309
  126.1 5.9 %collective-permute-done.8.refs_3_ = bf16[80,1920]{1,0:T(8,128)(2,1)} collective-permute-done((bf16[80,1920]{1,0:T(8,128)(2,1)}, bf16[80,1920]{1,0:T(8,128)(2,1)}, u32[]{:S(2)}, u32[]{:S(2)}) %collective-permute-start.8) | collective-permute-done | bytes 307232 | tf_op jit(solution)/shard_map/ppermute | solution.py:309
  132.4 18.9 %collective-permute-done.7.refs_2_ = bf16[80,1920]{1,0:T(8,128)(2,1)} collective-permute-done((bf16[80,1920]{1,0:T(8,128)(2,1)}, bf16[80,1920]{1,0:T(8,128)(2,1)}, u32[]{:S(2)}, u32[]{:S(2)}) %collective-permute-start.7) | collective-permute-done | bytes 307232 | tf_op jit(solution)/shard_map/ppermute | solution.py:309
  152.9 12.5 %shard_map.84 = (f32[512,640]{1,0:T(8,128)S(1)}, bf16[512,640]{1,0:T(8,128)(2,1)S(1)}) custom-call(s32[9]{0:T(128)S(1)} %stack.39.place_ref, bf16[512,512]{1,0:T(8,128)(2,1)S(1)} %copy-done.7, bf16[512,640]{1,0:T(8,128)(2,1)S(1)} %bitcast.24, s32[8,512]{1,0:T(8,128)S(1)} %reshape.29.ids_ref, bf16[512,1280]{1,0:T(8,128)(2,1)S(1)} %get-tuple-element.16.key_ref.value_ref, ...), custom_call_target="tpu_custom_call" | custom-call | flops 1509949440 | bytes 11026468 | tf_op jit(solution)/shard_map/pallas_call | solution.py:53
  165.4 7.3 %shard_map.86 = bf16[512,640]{1,0:T(8,128)(2,1)S(1)} custom-call(s32[9]{0:T(128)S(1)} %stack.39.place_ref, bf16[3,640,640]{2,1,0:T(8,128)(2,1)} %bitcast.30, bf16[512,640]{1,0:T(8,128)(2,1)S(1)} %get-tuple-element.17.query_ref, f32[512,640]{1,0:T(8,128)S(1)} %get-tuple-element.18.attended_ref, bf16[80,1920]{1,0:T(8,128)(2,1)} %add_convert_fusion.1.refs_0_, ...), custom_call_target="tpu_custom_call" | custom-call | flops 1258291200 | bytes 7536676 | tf_op jit(solution)/shard_map/pallas_call | solution.py:53
  172.9 1.3 collective-permute-start.16
  176.5 4.4 %collective-permute-done.16.refs_3_ = bf16[128,640]{1,0:T(8,128)(2,1)S(1)} collective-permute-done((bf16[128,640]{1,0:T(8,128)(2,1)S(1)}, bf16[128,640]{1,0:T(8,128)(2,1)S(1)}, u32[]{:S(2)}, u32[]{:S(2)}) %collective-permute-start.16) | collective-permute-done | bytes 163872 | tf_op jit(solution)/shard_map/ppermute | solution.py:309
  181.3 1.4 collective-permute-done.14.refs_1_
  182.6 1.7 shard_map.87
  (54 shorter events, 16.3 us)
Async XLA Ops:
  8.3 42.2 %all-to-all-start = ((bf16[32,16,1408]{2,1,0:T(8,128)(2,1)}), bf16[32,16,1408]{2,1,0:T(8,128)(2,1)S(1)}, u32[]{:S(2)}, u32[]{:S(2)}) async-start(bf16[32,16,1408]{2,1,0:T(8,128)(2,1)} %bitcast.11), calls=%async_computation | async-start | bytes 2883584 | tf_op jit(solution)/shard_map/all_to_all | solution.py:341
  50.4 8.4 %copy-start = (bf16[32,16,1408]{2,1,0:T(8,128)(2,1)}, bf16[32,16,1408]{2,1,0:T(8,128)(2,1)S(1)}, u32[]{:S(2)}) copy-start(bf16[32,16,1408]{2,1,0:T(8,128)(2,1)S(1)} %all-to-all-done) | copy-start | bytes 4325380
  59.9 10.8 %collective-permute-start.2 = (bf16[320,1920]{1,0:T(8,128)(2,1)}, bf16[320,1920]{1,0:T(8,128)(2,1)}, u32[]{:S(2)}, u32[]{:S(2)}) collective-permute-start(bf16[320,1920]{1,0:T(8,128)(2,1)} %get-tuple-element.20), channel_id=1, source_target_pairs={{0,1},{1,0},{2,3},{3,2},{4,5},{5,4},{6,7},{7,6},{8,9},{9,8},{10,11... | collective-permute-start | bytes 3686408 | tf_op jit(solution)/shard_map/ppermute | solution.py:309
  59.9 91.9 %all-to-all-start.1 = ((bf16[32,16,640]{2,1,0:T(8,128)(2,1)}), bf16[32,16,640]{2,1,0:T(8,128)(2,1)S(1)}, u32[]{:S(2)}, u32[]{:S(2)}) async-start(bf16[32,16,640]{2,1,0:T(8,128)(2,1)} %bitcast.13), calls=%async_computation.1 | async-start | bytes 1310720 | tf_op jit(solution)/shard_map/all_to_all | solution.py:341
  63.7 1.4 copy-start.1
  66.3 6.4 %copy-start.6 = (bf16[512,512]{1,0:T(8,128)(2,1)}, bf16[512,512]{1,0:T(8,128)(2,1)S(1)}, u32[]{:S(2)}) copy-start(bf16[512,512]{1,0:T(8,128)(2,1)S(1)} %get-tuple-element.14.choose_ref) | copy-start | bytes 1572868
  66.3 59.8 %collective-permute-start.1 = (bf16[512,1280]{1,0:T(8,128)(2,1)S(1)}, bf16[512,1280]{1,0:T(8,128)(2,1)}, u32[]{:S(2)}, u32[]{:S(2)}) collective-permute-start(bf16[512,1280]{1,0:T(8,128)(2,1)S(1)} %get-tuple-element.16.key_ref.value_ref), channel_id=1, source_target_pairs={{1,0},{3,2},{5,4},{7,6},{8,1},{9,8},{10,3},{11,10},{12,5},{13,12},... | collective-permute-start | bytes 3932168 | tf_op jit(solution)/shard_map/ppermute | solution.py:309
  67.6 84.2 %collective-permute-start = (bf16[512,1280]{1,0:T(8,128)(2,1)S(1)}, bf16[512,1280]{1,0:T(8,128)(2,1)S(1)}, u32[]{:S(2)}, u32[]{:S(2)}) collective-permute-start(bf16[512,1280]{1,0:T(8,128)(2,1)S(1)} %get-tuple-element.16.key_ref.value_ref), channel_id=1, source_target_pairs={{0,1},{1,8},{2,3},{3,10},{4,5},{5,12},{6,7},{7,14},{8,9},{9,16},{1... | collective-permute-start | bytes 3932168 | tf_op jit(solution)/shard_map/ppermute | solution.py:309
  72.7 79.1 %copy-start.10 = (s32[4096]{0:T(1024)S(1)}, s32[4096]{0:T(1024)}, u32[]{:S(2)}) copy-start(s32[4096]{0:T(1024)} %param.13) | copy-start | bytes 49156
  74.0 32.3 %collective-permute-start.3 = (bf16[80,1920]{1,0:T(8,128)(2,1)}, bf16[80,1920]{1,0:T(8,128)(2,1)}, u32[]{:S(2)}, u32[]{:S(2)}) collective-permute-start(bf16[80,1920]{1,0:T(8,128)(2,1)} %get-tuple-element.21), channel_id=1, source_target_pairs={{0,8},{1,9},{2,10},{3,11},{4,12},{5,13},{6,14},{7,15},{8,16},{9,17... | collective-permute-start | bytes 921608 | tf_op jit(solution)/shard_map/ppermute | solution.py:309
  75.7 31.9 %collective-permute-start.5 = (bf16[80,1920]{1,0:T(8,128)(2,1)}, bf16[80,1920]{1,0:T(8,128)(2,1)}, u32[]{:S(2)}, u32[]{:S(2)}) collective-permute-start(bf16[80,1920]{1,0:T(8,128)(2,1)} %get-tuple-element.22), channel_id=1, source_target_pairs={{0,24},{1,25},{2,26},{3,27},{4,28},{5,29},{6,30},{7,31},{8,0},{9,1... | collective-permute-start | bytes 921608 | tf_op jit(solution)/shard_map/ppermute | solution.py:309
  78.6 43.3 %collective-permute-start.4 = (bf16[80,1920]{1,0:T(8,128)(2,1)}, bf16[80,1920]{1,0:T(8,128)(2,1)}, u32[]{:S(2)}, u32[]{:S(2)}) collective-permute-start(bf16[80,1920]{1,0:T(8,128)(2,1)} %get-tuple-element.23), channel_id=1, source_target_pairs={{0,16},{1,17},{2,18},{3,19},{4,20},{5,21},{6,22},{7,23},{8,24},{9,... | collective-permute-start | bytes 921608 | tf_op jit(solution)/shard_map/ppermute | solution.py:309
  124.0 7.9 %collective-permute-start.8 = (bf16[80,1920]{1,0:T(8,128)(2,1)}, bf16[80,1920]{1,0:T(8,128)(2,1)}, u32[]{:S(2)}, u32[]{:S(2)}) collective-permute-start(bf16[80,1920]{1,0:T(8,128)(2,1)} %add_convert_fusion.1.refs_0_), channel_id=1, source_target_pairs={{0,24},{1,25},{2,26},{3,27},{4,28},{5,29},{6,30},{7,31},{8,0},{9,1... | collective-permute-start | bytes 921608 | tf_op jit(solution)/shard_map/ppermute | solution.py:309
  124.1 27.3 %collective-permute-start.7 = (bf16[80,1920]{1,0:T(8,128)(2,1)}, bf16[80,1920]{1,0:T(8,128)(2,1)}, u32[]{:S(2)}, u32[]{:S(2)}) collective-permute-start(bf16[80,1920]{1,0:T(8,128)(2,1)} %add_convert_fusion.1.refs_0_), channel_id=1, source_target_pairs={{0,16},{1,17},{2,18},{3,19},{4,20},{5,21},{6,22},{7,23},{8,24},{9,... | collective-permute-start | bytes 921608 | tf_op jit(solution)/shard_map/ppermute | solution.py:309
  124.1 27.3 %collective-permute-start.6 = (bf16[80,1920]{1,0:T(8,128)(2,1)}, bf16[80,1920]{1,0:T(8,128)(2,1)}, u32[]{:S(2)}, u32[]{:S(2)}) collective-permute-start(bf16[80,1920]{1,0:T(8,128)(2,1)} %add_convert_fusion.1.refs_0_), channel_id=1, source_target_pairs={{0,8},{1,9},{2,10},{3,11},{4,12},{5,13},{6,14},{7,15},{8,16},{9,17... | collective-permute-start | bytes 921608 | tf_op jit(solution)/shard_map/ppermute | solution.py:309
  126.1 39.3 %collective-permute-start.9 = (bf16[80,1920]{1,0:T(8,128)(2,1)}, bf16[80,1920]{1,0:T(8,128)(2,1)}, u32[]{:S(2)}, u32[]{:S(2)}) collective-permute-start(bf16[80,1920]{1,0:T(8,128)(2,1)} %add_convert_fusion.1.refs_0_), channel_id=1, source_target_pairs={{0,1},{1,0},{2,3},{3,2},{4,5},{5,4},{6,7},{7,6},{8,9},{9,8},{10,11... | collective-permute-start | bytes 921608 | tf_op jit(solution)/shard_map/ppermute | solution.py:309
  132.0 33.4 %collective-permute-start.12 = (bf16[80,1920]{1,0:T(8,128)(2,1)}, bf16[80,1920]{1,0:T(8,128)(2,1)}, u32[]{:S(2)}, u32[]{:S(2)}) collective-permute-start(bf16[80,1920]{1,0:T(8,128)(2,1)} %collective-permute-done.8.refs_3_), channel_id=1, source_target_pairs={{0,1},{1,0},{2,3},{3,2},{4,5},{5,4},{6,7},{7,6},{8,9},{9,8},{10,11... | collective-permute-start | bytes 921608 | tf_op jit(solution)/shard_map/ppermute | solution.py:309
  151.3 14.1 %collective-permute-start.11 = (bf16[80,1920]{1,0:T(8,128)(2,1)}, bf16[80,1920]{1,0:T(8,128)(2,1)}, u32[]{:S(2)}, u32[]{:S(2)}) collective-permute-start(bf16[80,1920]{1,0:T(8,128)(2,1)} %collective-permute-done.7.refs_2_), channel_id=1, source_target_pairs={{0,1},{1,0},{2,3},{3,2},{4,5},{5,4},{6,7},{7,6},{8,9},{9,8},{10,11... | collective-permute-start | bytes 921608 | tf_op jit(solution)/shard_map/ppermute | solution.py:309
  151.3 14.1 %collective-permute-start.10 = (bf16[80,1920]{1,0:T(8,128)(2,1)}, bf16[80,1920]{1,0:T(8,128)(2,1)}, u32[]{:S(2)}, u32[]{:S(2)}) collective-permute-start(bf16[80,1920]{1,0:T(8,128)(2,1)} %collective-permute-done.6.refs_1_), channel_id=1, source_target_pairs={{0,1},{1,0},{2,3},{3,2},{4,5},{5,4},{6,7},{7,6},{8,9},{9,8},{10,11... | collective-permute-start | bytes 921608 | tf_op jit(solution)/shard_map/ppermute | solution.py:309
  172.8 3.7 %copy-start.11 = (f32[2560]{0:T(1024)S(1)}, f32[2560]{0:T(1024)}, u32[]{:S(2)}) copy-start(f32[2560]{0:T(1024)} %param.15) | copy-start | bytes 30724
  172.9 8.0 %collective-permute-start.16 = (bf16[128,640]{1,0:T(8,128)(2,1)S(1)}, bf16[128,640]{1,0:T(8,128)(2,1)S(1)}, u32[]{:S(2)}, u32[]{:S(2)}) collective-permute-start(bf16[128,640]{1,0:T(8,128)(2,1)S(1)} %get-tuple-element.24), channel_id=1, source_target_pairs={{0,3},{1,7},{2,1},{3,5},{4,2},{5,6},{6,0},{7,4},{8,11},{9,15},{10,... | collective-permute-start | bytes 491528 | tf_op jit(solution)/shard_map/ppermute | solution.py:309
  174.2 7.1 %collective-permute-start.15 = (bf16[128,640]{1,0:T(8,128)(2,1)S(1)}, bf16[128,640]{1,0:T(8,128)(2,1)S(1)}, u32[]{:S(2)}, u32[]{:S(2)}) collective-permute-start(bf16[128,640]{1,0:T(8,128)(2,1)S(1)} %get-tuple-element.25), channel_id=1, source_target_pairs={{0,1},{1,5},{2,3},{3,7},{4,0},{5,4},{6,2},{7,6},{8,9},{9,13},{10,1... | collective-permute-start | bytes 491528 | tf_op jit(solution)/shard_map/ppermute | solution.py:309
  175.2 7.4 %collective-permute-start.14 = (bf16[128,640]{1,0:T(8,128)(2,1)S(1)}, bf16[128,640]{1,0:T(8,128)(2,1)S(1)}, u32[]{:S(2)}, u32[]{:S(2)}) collective-permute-start(bf16[128,640]{1,0:T(8,128)(2,1)S(1)} %get-tuple-element.26), channel_id=1, source_target_pairs={{0,2},{1,6},{2,0},{3,4},{4,3},{5,7},{6,1},{7,5},{8,10},{9,14},{10,... | collective-permute-start | bytes 491528 | tf_op jit(solution)/shard_map/ppermute | solution.py:309
  175.8 6.9 %collective-permute-start.13 = (bf16[128,640]{1,0:T(8,128)(2,1)S(1)}, bf16[128,640]{1,0:T(8,128)(2,1)S(1)}, u32[]{:S(2)}, u32[]{:S(2)}) collective-permute-start(bf16[128,640]{1,0:T(8,128)(2,1)S(1)} %get-tuple-element.27), channel_id=1, source_target_pairs={{0,0},{1,4},{2,2},{3,6},{4,1},{5,5},{6,3},{7,7},{8,8},{9,12},{10,1... | collective-permute-start | bytes 491528 | tf_op jit(solution)/shard_map/ppermute | solution.py:309
  (7 other events, 7.4 us)
where the time goes:
time: 187 us; the launch traced here: 184 us
  waiting for transfers between devices  100 us (53%)
  Pallas kernels  34.5 us (18%)
  starting transfers between devices  27.2 us (15%)
  local copies, waits for them, and re-layouts  18.2 us (10%)
  other arithmetic  4.06 us (2%)
    ppermute x17, waiting for transfers between devices, permute(): return lax.ppermute(array, 'tok', route)  73.7 us
    pallas_call x6, Pallas kernels, call(): pl.pallas_call(kernel, out_shape=list(outs), in_specs=specs, out_specs=ou...  34.5 us
    all_to_all x2, waiting for transfers between devices, exchange(): lax.all_to_all(flat, 'tok', split_axis=0, concat_axis=0, tiled=True)  26.3 us
    ppermute x17, starting transfers between devices, permute(): return lax.ppermute(array, 'tok', route)  16.1 us
    unnamed x26, local copies, waits for them, and re-layouts  13.6 us
    all_to_all x2, starting transfers between devices, exchange(): lax.all_to_all(flat, 'tok', split_axis=0, concat_axis=0, tiled=True)  11.1 us
  transfers between devices with their start and end apart: 19, of which 9 were waited for; matrix products, arithmetic and copies ran while one was open for 7% of the time, Pallas kernels for 7%

commit v1 on v0

v1 whole, which is shorter than its diff:
```python
import functools
import math

import jax
import jax.numpy as jnp
from jax import lax
from jax.experimental import pallas as pl
from jax.experimental.pallas import tpu as pltpu
from jax.sharding import PartitionSpec as P


HEADS = 8
HEAD_DIM = 320
ATT_DIM = 128
WINDOW = 1024
WIDTH = 2560
ATT_HEADS = 20
LANES = 128
EPS = 1e-06

PARTS = math.gcd(HEADS, ATT_HEADS)
PART_WIDTH = WIDTH // PARTS
PART_FAST = HEADS // PARTS
PART_ATT = ATT_HEADS // PARTS
SPAN = -(-HEAD_DIM // LANES) * LANES


F32 = jnp.float32
BF16 = jnp.bfloat16
VMEM = pltpu.VMEM


def iota(shape, dim):
    return lax.broadcasted_iota(jnp.int32, shape, dim)


def dot(a, b, dims=((1,), (0,))):
    return lax.dot_general(a, b, (dims, ((), ())), preferred_element_type=F32)


def column_of(row):
    n = row.shape[1]
    square = jnp.broadcast_to(row.astype(F32), (n, n))
    diagonal = iota((n, n), 0) == iota((n, n), 1)
    return jnp.sum(jnp.where(diagonal, square, 0.0), axis=1, keepdims=True)


def call(kernel, outs, ins, scratch=(), smem=0, flops=0, grid=None, in_specs=None, out_specs=None):
    specs = [pl.BlockSpec(memory_space=pltpu.SMEM)] * smem
    specs += in_specs or [pl.BlockSpec(memory_space=VMEM)] * (len(ins) - smem)
    moved = sum(x.size * x.dtype.itemsize for x in list(ins) + list(outs))
    extra = {} if grid is None else {"grid": grid}
    return pl.pallas_call(
        kernel,
        out_shape=list(outs),
        in_specs=specs,
        out_specs=out_specs or [pl.BlockSpec(memory_space=VMEM)] * len(outs),
        scratch_shapes=list(scratch),
        compiler_params=pltpu.CompilerParams(vmem_limit_bytes=60 << 20),
        cost_estimate=pl.CostEstimate(flops=flops, bytes_accessed=moved, transcendentals=0),
        **extra,
    )(*ins)


def window_of(head):
    begin = min(head * HEAD_DIM // LANES * LANES, PART_WIDTH - SPAN)
    return begin, head * HEAD_DIM - begin


def heads_kernel(place_ref, rate_ref, key_ref, value_ref, *out_refs):
    n = key_ref.shape[0]
    step, part, core = pl.program_id(0), place_ref[1], place_ref[2]
    rates = rate_ref[...]
    lane = iota((n, SPAN), 1)
    rows = []
    for head in range(PART_FAST):
        begin, offset = window_of(head)

        def window(ref):
            rows = ref[:, begin : begin + SPAN].astype(F32)
            rows = pltpu.roll(rows, SPAN - offset, 1) if offset else rows
            return jnp.where(lane < HEAD_DIM, rows, 0.0)

        own = (step ^ part) * PART_FAST + head
        rate = jnp.sum(jnp.where(iota(rates.shape, 1) == own, rates, 0.0), axis=1, keepdims=True)
        keys = window(key_ref)
        for index in range(3):
            piece = rate.astype(BF16).astype(F32)
            rate = rate - piece
            keys = jnp.where(lane == HEAD_DIM + index, piece, keys)
        rows.append((keys, window(value_ref)))
    for flip in range(PART_FAST):
        chosen = [jnp.where(core == flip, first, second).astype(BF16) for first, second in zip(*rows)]
        for index in range(PARTS):
            @pl.when(step == index)
            def _():
                out_refs[index * PART_FAST + flip][:, :SPAN] = chosen[0]
                out_refs[index * PART_FAST + flip][:, SPAN:] = chosen[1]


def pack_kernel(group_shift, slots, place_ref, order_ref, query_ref, key_ref, value_ref, kv_ref, q_ref, choose_buf):
    n = query_ref.shape[0]
    planes, _, cores = kv_ref.shape[:3]

    @pl.when(pl.program_id(0) == 0)
    def _():
        pos = order_ref[pl.ds(place_ref[0], 1), :]
        group = lax.shift_right_logical(pos, group_shift)
        group_col = column_of(group).astype(jnp.int32)
        earlier = (group_col == group) & (iota((n, n), 0) < iota((n, n), 1))
        rank = jnp.sum(jnp.where(earlier, 1.0, 0.0), axis=0, keepdims=True)
        slot = group * slots + rank.astype(jnp.int32)
        choose_buf[...] = jnp.where(iota((n, n), 0) == slot, 1.0, 0.0).astype(BF16)

    def put_rows(ref, rows, begin):
        width = rows.shape[1]
        for plane in range(planes):
            for core in range(cores):
                at = (plane * cores + core) * slots
                ref[plane, 0, core, :, begin : begin + width] = rows[at : at + slots]

    choose = choose_buf[...]
    put_rows(kv_ref, dot(choose, key_ref[...]).astype(BF16), 0)
    put_rows(kv_ref, dot(choose, value_ref[...]).astype(BF16), PART_WIDTH)
    put_rows(q_ref, dot(choose, query_ref[...]).astype(BF16), 0)


def arrival_choice(group_shift, slots, orders, group, n):
    sources, rows = orders.shape
    low_shift = group_shift // 2
    mine = lax.shift_right_logical(orders, group_shift) == group
    before = jnp.where(iota((rows, rows), 0) < iota((rows, rows), 1), 1.0, 0.0).astype(BF16)
    rank = dot(jnp.where(mine, 1.0, 0.0).astype(BF16), before)
    within = orders & ((1 << group_shift) - 1)
    digits = (lax.shift_right_logical(within, low_shift).astype(F32), (within & ((1 << low_shift) - 1)).astype(F32))
    spread = jnp.where(iota((sources, n), 1) // slots == iota((sources, n), 0), 1.0, 0.0).astype(BF16)
    keep = iota((slots, n), 1) % slots == iota((slots, n), 0)
    column = iota((sources, slots), 1)
    pos = jnp.zeros((1, n), F32)
    for digit, weight in zip(digits, (float(1 << low_shift), 1.0)):
        table = jnp.zeros((sources, slots), F32)
        for k in range(slots):
            one = jnp.sum(jnp.where(mine & (rank == float(k)), digit, 0.0), axis=1, keepdims=True)
            table = jnp.where(column == k, one, table)
        wide = dot(table.astype(BF16), spread, ((0,), (0,)))
        pos += weight * jnp.sum(jnp.where(keep, wide, 0.0), axis=0, keepdims=True)
    return jnp.where(iota((n, n), 0) == pos.astype(jnp.int32), 1.0, 0.0).astype(BF16)


def place_kernel(group_shift, slots, place_ref, order_ref, kv_in_ref, kv_ref, choose_ref):
    choose = arrival_choice(group_shift, slots, order_ref[...], place_ref[3], choose_ref.shape[0])
    choose_ref[...] = choose
    for part in range(2):
        lanes = slice(part * PART_WIDTH, (part + 1) * PART_WIDTH)
        kv_ref[:, lanes] = dot(choose, kv_in_ref[:, lanes]).astype(BF16)


def grads_kernel(chunk, place_ref, weight_ref, *refs):
    kv_refs, (out_ref, weight_buf, key_buf, target_buf, dg_buf, du_buf, pr_buf) = refs[:-7], refs[-7:]
    block = kv_refs[0].shape[0]
    n = key_buf.shape[0]
    hidden = weight_ref.shape[2]
    first = pl.multiple_of(place_ref[2] * HEAD_DIM, 16)
    for index in range(3):
        weight_buf[index, :HEAD_DIM, :] = weight_ref[index, pl.ds(first, HEAD_DIM), :]
        weight_buf[index, HEAD_DIM:, :] = jnp.zeros((SPAN - HEAD_DIM, hidden), BF16)
    lane = iota((1, SPAN), 1)
    wanted = (lane >= HEAD_DIM) & (lane < HEAD_DIM + 3)
    for index, ref in enumerate(kv_refs):
        here = pl.ds(index * block, block)
        key = ref[:, :SPAN]
        rate = jnp.sum(jnp.where(wanted, key.astype(F32), 0.0), axis=1, keepdims=True)
        key_buf[here, :] = key
        target_buf[here, :] = (ref[:, SPAN:].astype(F32) * rate).astype(BF16)
    for at in range(0, n, chunk):
        here = pl.ds(at, chunk)
        gate = dot(key_buf[here, :], weight_buf[0])
        upward = dot(key_buf[here, :], weight_buf[1])
        backward = dot(target_buf[here, :], weight_buf[2])
        sigmoid = jax.nn.sigmoid(gate)
        active = gate * sigmoid
        pr_buf[here, :] = (active * upward).astype(BF16)
        du_buf[here, :] = (backward * active).astype(BF16)
        dg_buf[here, :] = (backward * upward * sigmoid * (1.0 + gate * (1.0 - sigmoid))).astype(BF16)
    for index, (left, right) in enumerate(((key_buf, dg_buf), (key_buf, du_buf), (target_buf, pr_buf))):
        total = dot(left[...], right[...], ((0,), (0,)))
        out_ref[:, index * hidden : (index + 1) * hidden] = total[:HEAD_DIM].astype(BF16)


def attention_kernel(block, place_ref, choose_ref, query_in_ref, ids_ref, key_ref, key_low_ref, key_high_ref, value_ref, value_low_ref, value_high_ref, out_ref, query_ref, bias):
    n = choose_ref.shape[0]
    half = WINDOW // 2
    group = place_ref[3]
    last = ids_ref.shape[0] - 1

    @pl.when(pl.program_id(0) == 0)
    def _():
        mid = ids_ref[pl.ds(group, 1), :]
        low = ids_ref[pl.ds(jnp.maximum(group - 1, 0), 1), :]
        high = ids_ref[pl.ds(jnp.minimum(group + 1, last), 1), :]
        low = jnp.where(group > 0, low, -1)
        high = jnp.where(group < last, high, -1)
        for at in range(0, n, block):
            own = column_of(mid[:, at : at + block]).astype(jnp.int32)
            ids = jnp.concatenate([low[:, at:], mid, high[:, : at + block]], axis=1)
            span = ids.shape[1]
            gap = iota((block, span), 1) - iota((block, span), 0) - half
            allowed = (gap < half) & (gap > -half) & (own == ids)
            bias[at // block, :, :] = jnp.where(allowed, 0.0, -1e30)

    query = dot(choose_ref[...], query_in_ref[...]).astype(BF16)
    query_ref[...] = query
    factor = ATT_DIM ** (-0.5) * math.log2(math.e)
    for at in range(0, n, block):
        part = query[at : at + block]
        stops = (0, half - at, half - at + n, half + n + block - half)
        keys = (key_low_ref[at:, :], key_ref[...], key_high_ref[: at + block, :])
        values = (value_low_ref[at:, :], value_ref[...], value_high_ref[: at + block, :])
        scores = []
        for index in range(3):
            lanes = slice(stops[index], stops[index] + keys[index].shape[0])
            scores.append(dot(part, keys[index], ((1,), (1,))) + bias[at // block, :, lanes])
        peak = functools.reduce(jnp.maximum, [jnp.max(s, axis=1, keepdims=True) for s in scores])
        total = jnp.zeros_like(peak)
        mixed = jnp.zeros((block, ATT_DIM), F32)
        for score, value in zip(scores, values):
            weight = jnp.exp2((score - peak) * factor)
            total += jnp.sum(weight, axis=1, keepdims=True)
            mixed += dot(weight.astype(BF16), value)
        out_ref[pl.ds(at, block), :] = mixed / total


def apply_kernel(place_ref, weight_ref, query_ref, attended_ref, *refs):
    hidden = weight_ref.shape[2]
    count = (len(refs) - 3) // 2
    mine_refs, other_refs, (out_ref, fresh, scales) = refs[:count], refs[count : 2 * count], refs[2 * count :]
    piece = mine_refs[0].shape[0]
    core = place_ref[2]
    for head in range(PART_FAST):
        _, offset = window_of(head)
        for index in range(3):
            lanes = slice(index * hidden, (index + 1) * hidden)
            anchor = jnp.full((1, hidden), EPS, F32)
            length = jnp.full((1, hidden), EPS, F32)
            for step in range(count):
                at = pl.multiple_of(place_ref[4 + PARTS + step], 16)
                base = weight_ref[index, pl.ds(at + head * HEAD_DIM, piece), :].astype(F32)
                grad = jnp.where(core == head, mine_refs[step][:, lanes], other_refs[step][:, lanes]).astype(F32)
                update = base + grad
                anchor += jnp.sum(base * base, axis=0, keepdims=True)
                length += jnp.sum(update * update, axis=0, keepdims=True)
                fresh[head, index, pl.ds(at + offset, piece), :] = update.astype(BF16)
            scales[head * 3 + index, :] = (jnp.sqrt(anchor) / jnp.sqrt(length))[0]
            if offset:
                fresh[head, index, :offset, :] = jnp.zeros((offset, hidden), BF16)
            if offset + HEAD_DIM < SPAN:
                fresh[head, index, offset + HEAD_DIM :, :] = jnp.zeros((SPAN - offset - HEAD_DIM, hidden), BF16)
    parts = []
    for head in range(PART_FAST):
        begin, _ = window_of(head)
        query = query_ref[:, begin : begin + SPAN]
        scale = [scales[head * 3 + index : head * 3 + index + 1, :] for index in range(3)]
        gate = dot(query, fresh[head, 0]) * scale[0]
        upward = dot(query, fresh[head, 1]) * (scale[1] * scale[2])
        product = (gate * jax.nn.sigmoid(gate) * upward).astype(BF16)
        parts.append((begin, dot(product, fresh[head, 2], ((1,), (1,)))))
    for lane in range(0, PART_WIDTH, LANES):
        total = attended_ref[:, lane : lane + LANES]
        for begin, value in parts:
            if begin <= lane < begin + SPAN:
                total += value[:, lane - begin : lane - begin + LANES]
        out_ref[:, lane : lane + LANES] = total.astype(BF16)


def norm_kernel(place_ref, *refs):
    part_refs, gain_ref, out_ref, buf = refs[:PARTS], refs[PARTS], refs[PARTS + 1], refs[PARTS + 2]
    square = jnp.zeros((out_ref.shape[0], 1), F32)
    for index, ref in enumerate(part_refs):
        rows = ref[...]
        buf[place_ref[4 + index]] = rows
        wide = rows.astype(F32)
        square += jnp.sum(wide * wide, axis=1, keepdims=True)
    factor = lax.rsqrt(square / WIDTH + EPS)
    for part in range(PARTS):
        lanes = slice(part * PART_WIDTH, (part + 1) * PART_WIDTH)
        out_ref[:, lanes] = (buf[part].astype(F32) * factor * gain_ref[:, lanes]).astype(BF16)


def shards(queries, key_rows, value_rows, learn_rates, frame_order, window_ids, fast_init, norm_gain):
    tok_dev = queries.shape[0]
    hidden = fast_init.shape[0]
    sections = lax.axis_size("tok")
    plane_size = PARTS * PART_FAST
    planes = sections // plane_size
    group_rows = tok_dev * PARTS
    groups = planes * PART_FAST
    slots = tok_dev // groups
    half = WINDOW // 2
    assert PART_FAST == 2 and half == group_rows and group_rows & (group_rows - 1) == 0
    group_shift = group_rows.bit_length() - 1

    rank = lax.axis_index("tok")
    plane = rank // plane_size
    part = rank // PART_FAST % PARTS
    core = rank % PART_FAST
    row, column = part // 2, part % 2
    group = plane * PART_FAST + core

    def at(plane, row, column, core):
        return plane * plane_size + (row * 2 + column) * PART_FAST + core

    everyone = [(z, y, x, c) for z in range(planes) for y in range(2) for x in range(2) for c in range(2)]

    def permute(array, target):
        route = []
        for source in everyone:
            goal = target(*source)
            if goal is not None:
                route.append((at(*source), at(*goal)))
        return lax.ppermute(array, "tok", route)

    sources = [2 * (core ^ j // 2) + (column ^ j % 2) for j in range(PARTS)]
    bits = planes.bit_length() - 1
    piece = HEAD_DIM >> bits
    assert planes == 1 << bits and piece << bits == HEAD_DIM and piece % 16 == 0

    def owned(plane):
        return sum((plane >> bit & 1) * (HEAD_DIM >> bit + 1) for bit in range(bits))

    masks = [0]
    for bit in reversed(range(bits)):
        masks += [mask ^ 1 << bit for mask in masks]
    starts = [owned(plane ^ mask) for mask in masks]
    place = jnp.stack([rank, part, core, group] + sources + starts).astype(jnp.int32)

    def weight_part():
        own = lax.dynamic_slice_in_dim(fast_init, part * PART_WIDTH, PART_WIDTH, 2)
        return jnp.transpose(own, (1, 2, 0))

    weights = weight_part()

    full = lambda a: pl.BlockSpec(a.shape, lambda h: (0,) * a.ndim)
    cut = pl.BlockSpec((tok_dev, PART_WIDTH), lambda h: (0, h))
    other_cut = pl.BlockSpec((tok_dev, PART_WIDTH), lambda h, place: (0, h ^ place[1]))
    whole = lambda shape: pl.BlockSpec(shape, lambda h, place: (0,) * len(shape))
    heads_out = pl.pallas_call(
        heads_kernel,
        out_shape=[jax.ShapeDtypeStruct((tok_dev, 2 * SPAN), BF16)] * plane_size,
        grid_spec=pltpu.PrefetchScalarGridSpec(
            num_scalar_prefetch=1,
            grid=(PARTS,),
            in_specs=[whole(learn_rates.shape), other_cut, other_cut],
            out_specs=[whole((tok_dev, 2 * SPAN))] * plane_size,
        ),
        compiler_params=pltpu.CompilerParams(vmem_limit_bytes=60 << 20),
        cost_estimate=pl.CostEstimate(flops=tok_dev * WIDTH, bytes_accessed=8 * tok_dev * WIDTH, transcendentals=0),
        name="heads",
    )(place, learn_rates, key_rows, value_rows)
    heads_in = [heads_out[0]]
    for j in range(1, plane_size):
        heads_in.append(permute(heads_out[j], lambda z, y, x, c, j=j: (z, y ^ j >> 2, x ^ j >> 1 & 1, c ^ j & 1)))

    shape = (planes, PARTS, PART_FAST, slots)
    orders = frame_order.reshape(sections, tok_dev)
    kv_out, q_out = call(
        functools.partial(pack_kernel, group_shift, slots),
        [jax.ShapeDtypeStruct(shape + (width,), BF16) for width in (2 * PART_WIDTH, PART_WIDTH)],
        [place, orders, queries, key_rows, value_rows],
        in_specs=[full(orders), cut, cut, cut],
        out_specs=[
            pl.BlockSpec((planes, 1, PART_FAST, slots, width), lambda h: (0, h, 0, 0, 0))
            for width in (2 * PART_WIDTH, PART_WIDTH)
        ],
        grid=(PARTS,),
        scratch=[VMEM((tok_dev, tok_dev), BF16)],
        smem=1, flops=2 * tok_dev * tok_dev * 3 * WIDTH,
    )

    def exchange(array):
        flat = array.reshape(sections, slots, array.shape[-1])
        return lax.all_to_all(flat, "tok", split_axis=0, concat_axis=0, tiled=True).reshape(group_rows, array.shape[-1])

    kv_in = exchange(kv_out)
    q_in = exchange(q_out)

    kv_seq, choose = call(
        functools.partial(place_kernel, group_shift, slots),
        [jax.ShapeDtypeStruct((group_rows, 2 * PART_WIDTH), BF16), jax.ShapeDtypeStruct((group_rows, group_rows), BF16)],
        [place, orders, kv_in], smem=1, flops=2 * group_rows * group_rows * 2 * PART_WIDTH,
    )

    def neighbour(step):
        def target(z, y, x, c):
            goal = z * PART_FAST + c + step
            return (goal // PART_FAST, y, x, goal % PART_FAST) if 0 <= goal < groups else None

        return target

    kv_low = permute(kv_seq, neighbour(1))
    kv_high = permute(kv_seq, neighbour(-1))

    tokens = plane_size * tok_dev
    (total,) = call(
        functools.partial(grads_kernel, tokens // 2),
        [jax.ShapeDtypeStruct((HEAD_DIM, 3 * hidden), BF16)], [place, weights] + heads_in,
        scratch=[VMEM((3, SPAN, hidden), BF16)] + [VMEM((tokens, SPAN), BF16)] * 2 + [VMEM((tokens, hidden), BF16)] * 3,
        smem=1, flops=12 * tokens * HEAD_DIM * hidden,
    )

    def across(bit):
        return lambda z, y, x, c: (z ^ 1 << bit, y, x, c)

    for bit in range(bits):
        size = HEAD_DIM >> bit + 1
        side = plane >> bit & 1
        came = permute(lax.dynamic_slice_in_dim(total, (1 - side) * size, size, 0), across(bit))
        kept = lax.dynamic_slice_in_dim(total, side * size, size, 0)
        total = (kept.astype(F32) + came.astype(F32)).astype(BF16)
    pieces = [total]
    for bit in reversed(range(bits)):
        fresh_pieces = []
        for held in pieces:
            fresh_pieces.append(permute(held, across(bit)))
        pieces += fresh_pieces
    swap = lambda z, y, x, c: (z, y, x, 1 - c)
    pieces_other = []
    for held in pieces:
        pieces_other.append(permute(held, swap))

    block = min(LANES, group_rows)
    lane_block = lambda rows, shift: pl.BlockSpec((rows, ATT_DIM), lambda h: (0, h + shift))
    ids = window_ids.reshape(groups, group_rows)
    attended, query_seq = call(
        functools.partial(attention_kernel, block),
        [jax.ShapeDtypeStruct((group_rows, PART_WIDTH), F32), jax.ShapeDtypeStruct((group_rows, PART_WIDTH), BF16)],
        [place, choose, q_in, ids, kv_seq, kv_low, kv_high, kv_seq, kv_low, kv_high],
        in_specs=[full(choose), lane_block(group_rows, 0), full(ids)]
        + [lane_block(group_rows, 0)] * 3 + [lane_block(group_rows, PART_ATT)] * 3,
        out_specs=[lane_block(group_rows, 0)] * 2,
        grid=(PART_ATT,),
        scratch=[VMEM((group_rows // block, block, WINDOW + block), F32)],
        smem=1, flops=4 * group_rows * (WINDOW + block) * PART_WIDTH,
    )

    (combined,) = call(
        apply_kernel,
        [jax.ShapeDtypeStruct((group_rows, PART_WIDTH), BF16)],
        [place, weights, query_seq, attended] + pieces + pieces_other,
        scratch=[VMEM((PART_FAST, 3, SPAN, hidden), BF16), VMEM((PART_FAST * 3, hidden), F32)],
        smem=1, flops=6 * group_rows * PART_WIDTH * hidden,
    )

    blocks = combined.reshape(PARTS, tok_dev, PART_WIDTH)
    parts = []
    for j in range(PARTS):
        goal = 2 * (column ^ j % 2) + (row ^ j // 2)
        send = lax.dynamic_index_in_dim(blocks, goal, 0, keepdims=False)
        parts.append(permute(send, lambda z, y, x, c, j=j: (z, c, x ^ j % 2, y ^ j // 2)))

    (out,) = call(
        norm_kernel,
        [jax.ShapeDtypeStruct((tok_dev, WIDTH), BF16)],
        [place] + parts + [norm_gain.reshape(1, WIDTH)],
        scratch=[VMEM((PARTS, tok_dev, PART_WIDTH), BF16)],
        smem=1, flops=6 * tok_dev * WIDTH,
    )
    return out


def solution(mesh):
    rows = P(("groups", "tok"), None)
    return jax.shard_map(
        shards,
        mesh=mesh,
        in_specs=(rows, rows, rows, rows, P("groups"), P("groups"), P(), P()),
        out_specs=rows,
        check_vma=False,
    )
```

time: 187 us -> 180 us (0.963)
  waiting for transfers between devices: 100 us -> 83 us
  Pallas kernels: 34.5 us -> 44.5 us
  starting transfers between devices: 27.2 us -> 34 us
  local copies, waits for them, and re-layouts: 18.2 us -> 15.1 us
  other arithmetic: 4.06 us -> 2 us
    all_to_all x2, waiting for transfers between devices: 26.3 us -> 0.01 us  [exchange(): lax.all_to_all(flat, 'tok', split_axis=0, concat_axis=0, tiled=True)]
    ppermute x17 -> x22, waiting for transfers between devices: 73.7 us -> 83 us  [permute(): return lax.ppermute(array, 'tok', route)]
    ppermute x17 -> x22, starting transfers between devices: 16.1 us -> 23.7 us  [permute(): return lax.ppermute(array, 'tok', route)]
    unnamed x26 -> x36, local copies, waits for them, and re-layouts: 13.6 us -> 8.12 us
    pallas_call x6, Pallas kernels: 34.5 us -> 39.6 us  [call(): pl.pallas_call(kernel, out_shape=list(outs), in_specs=specs, out_specs=ou...]
    pallas_call x0 -> x1, Pallas kernels: none -> 4.87 us  [shards(): pl.pallas_call(heads_kernel, out_shape=[jax.ShapeDtypeStruct((tok_dev, 2...]
    convert_element_type x2, other arithmetic: 4.06 us -> 2 us  [shards(): total = (kept.astype(F32) + came.astype(F32)).astype(BF16)]
  transfers between devices with their start and end apart: 19 -> 24, of which waited for: 9 -> 8; matrix products, arithmetic and copies ran while one was open for 7% -> 6% of each run, Pallas kernels for 7% -> 17%
where the time goes in v1:
time: 180 us; the launch traced here: 179 us
  waiting for transfers between devices  83 us (46%)
  Pallas kernels  44.5 us (25%)
  starting transfers between devices  34 us (19%)
  local copies, waits for them, and re-layouts  15.1 us (8%)
  other arithmetic  2 us (1%)
    ppermute x22, waiting for transfers between devices, permute(): return lax.ppermute(array, 'tok', route)  83 us
    pallas_call x6, Pallas kernels, call(): pl.pallas_call(kernel, out_shape=list(outs), in_specs=specs, out_specs=ou...  39.6 us
    ppermute x22, starting transfers between devices, permute(): return lax.ppermute(array, 'tok', route)  23.7 us
    all_to_all x2, starting transfers between devices, exchange(): lax.all_to_all(flat, 'tok', split_axis=0, concat_axis=0, tiled=True)  10.3 us
    unnamed x36, local copies, waits for them, and re-layouts  8.12 us
    pallas_call x1, Pallas kernels, shards(): pl.pallas_call(heads_kernel, out_shape=[jax.ShapeDtypeStruct((tok_dev, 2...  4.87 us
  transfers between devices with their start and end apart: 24, of which 8 were waited for; matrix products, arithmetic and copies ran while one was open for 6% of the time, Pallas kernels for 17%

profile of v1, /device:TPU:0, one launch (start us, length us, event | category | flops | bytes accessed | tf_op | source)
XLA Modules:
  0.0 178.8 jit_solution(10876831738852014916)
XLA Ops:
  0.7 4.4 %shard_map.82 = (bf16[4,4,2,16,1280]{4,3,2,1,0:T(8,128)(2,1)}, bf16[4,4,2,16,640]{4,3,2,1,0:T(8,128)(2,1)}) custom-call(s32[12]{0:T(128)} %stack.51.place_ref, s32[32,128]{1,0:T(8,128)} %bitcast.33, bf16[128,2560]{1,0:T(8,128)(2,1)} %query_ref.1, bf16[128,2560]{1,0:T(8,128)(2,1)} %key_ref.3, bf16[128,2560]{1,0:T(8,128)(2,1)} %value_ref.3), custom_call_target="tpu_custom_call" | custom-call | flops 251658240 | bytes 3948592 | tf_op jit(solution)/shard_map/pallas_call | solution.py:53
  5.1 7.4 %all-to-all-start = ((bf16[32,16,1280]{2,1,0:T(8,128)(2,1)}), bf16[32,16,1280]{2,1,0:T(8,128)(2,1)}, u32[]{:S(2)}, u32[]{:S(2)}) async-start(bf16[32,16,1280]{2,1,0:T(8,128)(2,1)} %bitcast.31), calls=%async_computation | async-start | bytes 2621440 | tf_op jit(solution)/shard_map/all_to_all | solution.py:381
  13.3 4.9 %heads.1 = (bf16[128,768]{1,0:T(8,128)(2,1)}, bf16[128,768]{1,0:T(8,128)(2,1)}, bf16[128,768]{1,0:T(8,128)(2,1)}, bf16[128,768]{1,0:T(8,128)(2,1)}, bf16[128,768...) custom-call(s32[12]{0:T(128)} %stack.51.place_ref, ...), custom_call_target="tpu_custom_call" | custom-call | flops 327680 | bytes 2621440 | tf_op jit(solution)/shard_map/heads/pallas_call | solution.py:346
  21.9 2.5 %collective-permute-start.7 = (bf16[128,768]{1,0:T(8,128)(2,1)}, bf16[128,768]{1,0:T(8,128)(2,1)}, u32[]{:S(2)}, u32[]{:S(2)}) collective-permute-start(bf16[128,768]{1,0:T(8,128)(2,1)} %get-tuple-element.31), channel_id=1, source_target_pairs={{0,6},{1,7},{2,4},{3,5},{4,2},{5,3},{6,0},{7,1},{8,14},{9,15},{10,... | collective-permute-start | bytes 589832 | tf_op jit(solution)/shard_map/ppermute | solution.py:320
  24.4 6.3 %collective-permute-done.3.refs_2_ = bf16[128,768]{1,0:T(8,128)(2,1)S(1)} collective-permute-done((bf16[128,768]{1,0:T(8,128)(2,1)}, bf16[128,768]{1,0:T(8,128)(2,1)S(1)}, u32[]{:S(2)}, u32[]{:S(2)}) %collective-permute-start.3) | collective-permute-done | bytes 196640 | tf_op jit(solution)/shard_map/ppermute | solution.py:320
  31.9 1.9 %constant_dynamic-slice_fusion.2 = bf16[640,3,640]{2,0,1:T(8,128)(2,1)S(1)} fusion(bf16[640,3,2560]{2,0,1:T(8,128)(2,1)} %param.14, s32[]{:T(128)S(6)} %select_n.58), kind=kLoop, calls=%fused_computation.8 | loop fusion | bytes 4915204 | tf_op jit(solution)/shard_map/dynamic_slice | solution.py:337
  33.8 3.3 %copy.11 = bf16[640,3,640]{0,2,1:T(8,128)(2,1)} copy(bf16[640,3,640]{2,0,1:T(8,128)(2,1)S(1)} %constant_dynamic-slice_fusion.2) | data formatting | bytes 4915200
  37.1 10.7 %collective-permute-done.6.refs_5_ = bf16[128,768]{1,0:T(8,128)(2,1)S(1)} collective-permute-done((bf16[128,768]{1,0:T(8,128)(2,1)}, bf16[128,768]{1,0:T(8,128)(2,1)S(1)}, u32[]{:S(2)}, u32[]{:S(2)}) %collective-permute-start.6) | collective-permute-done | bytes 196640 | tf_op jit(solution)/shard_map/ppermute | solution.py:320
  48.5 8.0 %shard_map.85 = bf16[320,1920]{1,0:T(8,128)(2,1)} custom-call(s32[12]{0:T(128)} %stack.51.place_ref, bf16[3,640,640]{2,1,0:T(8,128)(2,1)} %bitcast.27, bf16[128,768]{1,0:T(8,128)(2,1)} %get-tuple-element.25.refs_0_, bf16[128,768]{1,0:T(8,128)(2,1)} %copy-done.12, bf16[128,768]{1,0:T(8,128)(2,1)} %copy-done.13, bf16[128,768]{1,0:T(8,128)(2,1)} %copy-done.14, ...), custom_call_target="tpu_custom_call" | custom-call | flops 2516582400 | bytes 5259312 | tf_op jit(solution)/shard_map/pallas_call | solution.py:53
  58.6 15.0 %collective-permute-done.9 = bf16[160,1920]{1,0:T(8,128)(2,1)S(1)} collective-permute-done((bf16[160,1920]{1,0:T(8,128)(2,1)S(1)}, bf16[160,1920]{1,0:T(8,128)(2,1)S(1)}, u32[]{:S(2)}, u32[]{:S(2)}) %collective-permute-start.9) | collective-permute-done | bytes 614432 | tf_op jit(solution)/shard_map/ppermute | solution.py:320
  75.4 2.3 %collective-permute-start.10 = (bf16[80,1920]{1,0:T(8,128)(2,1)}, bf16[80,1920]{1,0:T(8,128)(2,1)}, u32[]{:S(2)}, u32[]{:S(2)}) collective-permute-start(bf16[80,1920]{1,0:T(8,128)(2,1)} %constant_dynamic-slice_fusion), channel_id=1, source_target_pairs={{0,16},{1,17},{2,18},{3,19},{4,20},{5,21},{6,22},{7,23},{8,24},{9,... | collective-permute-start | bytes 921608 | tf_op jit(solution)/shard_map/ppermute | solution.py:320
  77.6 4.0 %shard_map.83 = (bf16[512,1280]{1,0:T(8,128)(2,1)}, bf16[512,512]{1,0:T(8,128)(2,1)}) custom-call(s32[12]{0:T(128)} %stack.51.place_ref, s32[32,128]{1,0:T(8,128)} %bitcast.34, bf16[512,1280]{1,0:T(8,128)(2,1)} %bitcast.15.kv_in_ref), custom_call_target="tpu_custom_call" | custom-call | flops 671088640 | bytes 3162160 | tf_op jit(solution)/shard_map/pallas_call | solution.py:53
  83.0 3.1 %collective-permute-start = (bf16[512,1280]{1,0:T(8,128)(2,1)}, bf16[512,1280]{1,0:T(8,128)(2,1)S(1)}, u32[]{:S(2)}, u32[]{:S(2)}) collective-permute-start(bf16[512,1280]{1,0:T(8,128)(2,1)} %get-tuple-element.22.key_ref.value_ref), channel_id=1, source_target_pairs={{0,1},{1,8},{2,3},{3,10},{4,5},{5,12},{6,7},{7,14},{8,9},{9,16},{1... | collective-permute-start | bytes 3932168 | tf_op jit(solution)/shard_map/ppermute | solution.py:320
  86.2 2.8 %all-to-all-start.1 = ((bf16[32,16,640]{2,1,0:T(8,128)(2,1)}), bf16[32,16,640]{2,1,0:T(8,128)(2,1)S(1)}, u32[]{:S(2)}, u32[]{:S(2)}) async-start(bf16[32,16,640]{2,1,0:T(8,128)(2,1)} %bitcast.32), calls=%async_computation.1 | async-start | bytes 1310720 | tf_op jit(solution)/shard_map/all_to_all | solution.py:381
  89.0 2.9 %collective-permute-done.10 = bf16[80,1920]{1,0:T(8,128)(2,1)} collective-permute-done((bf16[80,1920]{1,0:T(8,128)(2,1)}, bf16[80,1920]{1,0:T(8,128)(2,1)}, u32[]{:S(2)}, u32[]{:S(2)}) %collective-permute-start.10) | collective-permute-done | bytes 307232 | tf_op jit(solution)/shard_map/ppermute | solution.py:320
  91.9 1.9 %add_convert_fusion.1.refs_0_ = bf16[80,1920]{1,0:T(8,128)(2,1)} fusion(bf16[80,1920]{1,0:T(8,128)(2,1)} %collective-permute-done.10, bf16[160,1920]{1,0:T(8,128)(2,1)} %copy-done.3, s32[]{:T(128)S(6)} %select_n.61), kind=kLoop, calls=%fused_computation.1 | loop fusion | flops 614400 | bytes 921604 | tf_op jit(solution)/shard_map/convert_element_type | solution.py:418
  93.8 5.0 %collective-permute-start.12 = (bf16[80,1920]{1,0:T(8,128)(2,1)}, bf16[80,1920]{1,0:T(8,128)(2,1)}, u32[]{:S(2)}, u32[]{:S(2)}) collective-permute-start(bf16[80,1920]{1,0:T(8,128)(2,1)} %add_convert_fusion.1.refs_0_), channel_id=1, source_target_pairs={{0,8},{1,9},{2,10},{3,11},{4,12},{5,13},{6,14},{7,15},{8,0},{9,1},... | collective-permute-start | bytes 921608 | tf_op jit(solution)/shard_map/ppermute | solution.py:320
  98.7 34.4 %collective-permute-done.11.refs_1_ = bf16[80,1920]{1,0:T(8,128)(2,1)} collective-permute-done((bf16[80,1920]{1,0:T(8,128)(2,1)}, bf16[80,1920]{1,0:T(8,128)(2,1)}, u32[]{:S(2)}, u32[]{:S(2)}) %collective-permute-start.11) | collective-permute-done | bytes 307232 | tf_op jit(solution)/shard_map/ppermute | solution.py:320
  133.6 7.2 %collective-permute-done.13.refs_3_ = bf16[80,1920]{1,0:T(8,128)(2,1)} collective-permute-done((bf16[80,1920]{1,0:T(8,128)(2,1)}, bf16[80,1920]{1,0:T(8,128)(2,1)}, u32[]{:S(2)}, u32[]{:S(2)}) %collective-permute-start.13) | collective-permute-done | bytes 307232 | tf_op jit(solution)/shard_map/ppermute | solution.py:320
  143.2 13.2 %shard_map.84 = (f32[512,640]{1,0:T(8,128)}, bf16[512,640]{1,0:T(8,128)(2,1)}) custom-call(s32[12]{0:T(128)} %stack.51.place_ref, bf16[512,512]{1,0:T(8,128)(2,1)} %get-tuple-element.20.choose_ref, bf16[512,640]{1,0:T(8,128)(2,1)} %bitcast.29, s32[8,512]{1,0:T(8,128)} %reshape.29.ids_ref, bf16[512,1280]{1,0:T(8,128)(2,1)} %get-tuple-element.22.key_ref.value_ref, ...), custom_call_target="tpu_custom_call" | custom-call | flops 1509949440 | bytes 11026480 | tf_op jit(solution)/shard_map/pallas_call | solution.py:53
  156.5 7.7 %shard_map.86 = bf16[512,640]{1,0:T(8,128)(2,1)} custom-call(s32[12]{0:T(128)} %stack.51.place_ref, bf16[3,640,640]{2,1,0:T(8,128)(2,1)} %bitcast.28, bf16[512,640]{1,0:T(8,128)(2,1)} %get-tuple-element.23.query_ref, f32[512,640]{1,0:T(8,128)} %get-tuple-element.24.attended_ref, bf16[80,1920]{1,0:T(8,128)(2,1)} %add_convert_fusion.1.refs_0_, ...), custom_call_target="tpu_custom_call" | custom-call | flops 1258291200 | bytes 7536688 | tf_op jit(solution)/shard_map/pallas_call | solution.py:53
  168.6 4.8 %collective-permute-done.21.refs_3_ = bf16[128,640]{1,0:T(8,128)(2,1)S(1)} collective-permute-done((bf16[128,640]{1,0:T(8,128)(2,1)S(1)}, bf16[128,640]{1,0:T(8,128)(2,1)S(1)}, u32[]{:S(2)}, u32[]{:S(2)}) %collective-permute-start.21) | collective-permute-done | bytes 163872 | tf_op jit(solution)/shard_map/ppermute | solution.py:320
  173.4 1.7 collective-permute-done.19.refs_1_
  176.5 2.4 %shard_map.87 = bf16[128,2560]{1,0:T(8,128)(2,1)} custom-call(s32[12]{0:T(128)} %stack.51.place_ref, bf16[128,640]{1,0:T(8,128)(2,1)} %copy-done.8, bf16[128,640]{1,0:T(8,128)(2,1)} %copy-done.7, bf16[128,640]{1,0:T(8,128)(2,1)} %copy-done.6, bf16[128,640]{1,0:T(8,128)(2,1)} %copy-done.5, f32[1,2560]{1,0:T(1,128)} %reshape.31.refs_4_), custom_call_target="tpu_custom_call" | custom-call | flops 1966080 | bytes 1321008 | tf_op jit(solution)/shard_map/pallas_call | solution.py:53
  (76 shorter events, 21.0 us)
Async XLA Ops:
  5.1 72.5 %all-to-all-start = ((bf16[32,16,1280]{2,1,0:T(8,128)(2,1)}), bf16[32,16,1280]{2,1,0:T(8,128)(2,1)}, u32[]{:S(2)}, u32[]{:S(2)}) async-start(bf16[32,16,1280]{2,1,0:T(8,128)(2,1)} %bitcast.31), calls=%async_computation | async-start | bytes 2621440 | tf_op jit(solution)/shard_map/all_to_all | solution.py:381
  18.2 3.7 %collective-permute-start.2 = (bf16[128,768]{1,0:T(8,128)(2,1)}, bf16[128,768]{1,0:T(8,128)(2,1)S(1)}, u32[]{:S(2)}, u32[]{:S(2)}) collective-permute-start(bf16[128,768]{1,0:T(8,128)(2,1)} %get-tuple-element.26), channel_id=1, source_target_pairs={{0,1},{1,0},{2,3},{3,2},{4,5},{5,4},{6,7},{7,6},{8,9},{9,8},{10,11... | collective-permute-start | bytes 589832 | tf_op jit(solution)/shard_map/ppermute | solution.py:320
  18.4 12.3 %collective-permute-start.3 = (bf16[128,768]{1,0:T(8,128)(2,1)}, bf16[128,768]{1,0:T(8,128)(2,1)S(1)}, u32[]{:S(2)}, u32[]{:S(2)}) collective-permute-start(bf16[128,768]{1,0:T(8,128)(2,1)} %get-tuple-element.27), channel_id=1, source_target_pairs={{0,2},{1,3},{2,0},{3,1},{4,6},{5,7},{6,4},{7,5},{8,10},{9,11},{10,... | collective-permute-start | bytes 589832 | tf_op jit(solution)/shard_map/ppermute | solution.py:320
  20.0 17.1 %collective-permute-start.4 = (bf16[128,768]{1,0:T(8,128)(2,1)}, bf16[128,768]{1,0:T(8,128)(2,1)S(1)}, u32[]{:S(2)}, u32[]{:S(2)}) collective-permute-start(bf16[128,768]{1,0:T(8,128)(2,1)} %get-tuple-element.28), channel_id=1, source_target_pairs={{0,3},{1,2},{2,1},{3,0},{4,7},{5,6},{6,5},{7,4},{8,11},{9,10},{10,... | collective-permute-start | bytes 589832 | tf_op jit(solution)/shard_map/ppermute | solution.py:320
  20.0 17.1 %collective-permute-start.5 = (bf16[128,768]{1,0:T(8,128)(2,1)}, bf16[128,768]{1,0:T(8,128)(2,1)S(1)}, u32[]{:S(2)}, u32[]{:S(2)}) collective-permute-start(bf16[128,768]{1,0:T(8,128)(2,1)} %get-tuple-element.29), channel_id=1, source_target_pairs={{0,4},{1,5},{2,6},{3,7},{4,0},{5,1},{6,2},{7,3},{8,12},{9,13},{10,... | collective-permute-start | bytes 589832 | tf_op jit(solution)/shard_map/ppermute | solution.py:320
  21.7 26.1 %collective-permute-start.6 = (bf16[128,768]{1,0:T(8,128)(2,1)}, bf16[128,768]{1,0:T(8,128)(2,1)S(1)}, u32[]{:S(2)}, u32[]{:S(2)}) collective-permute-start(bf16[128,768]{1,0:T(8,128)(2,1)} %get-tuple-element.30), channel_id=1, source_target_pairs={{0,5},{1,4},{2,7},{3,6},{4,1},{5,0},{6,3},{7,2},{8,13},{9,12},{10,... | collective-permute-start | bytes 589832 | tf_op jit(solution)/shard_map/ppermute | solution.py:320
  21.9 26.0 %collective-permute-start.7 = (bf16[128,768]{1,0:T(8,128)(2,1)}, bf16[128,768]{1,0:T(8,128)(2,1)}, u32[]{:S(2)}, u32[]{:S(2)}) collective-permute-start(bf16[128,768]{1,0:T(8,128)(2,1)} %get-tuple-element.31), channel_id=1, source_target_pairs={{0,6},{1,7},{2,4},{3,5},{4,2},{5,3},{6,0},{7,1},{8,14},{9,15},{10,... | collective-permute-start | bytes 589832 | tf_op jit(solution)/shard_map/ppermute | solution.py:320
  30.7 17.1 %collective-permute-start.8 = (bf16[128,768]{1,0:T(8,128)(2,1)}, bf16[128,768]{1,0:T(8,128)(2,1)}, u32[]{:S(2)}, u32[]{:S(2)}) collective-permute-start(bf16[128,768]{1,0:T(8,128)(2,1)} %get-tuple-element.32), channel_id=1, source_target_pairs={{0,7},{1,6},{2,5},{3,4},{4,3},{5,2},{6,1},{7,0},{8,15},{9,14},{10,... | collective-permute-start | bytes 589832 | tf_op jit(solution)/shard_map/ppermute | solution.py:320
  57.7 15.9 %collective-permute-start.9 = (bf16[160,1920]{1,0:T(8,128)(2,1)S(1)}, bf16[160,1920]{1,0:T(8,128)(2,1)S(1)}, u32[]{:S(2)}, u32[]{:S(2)}) collective-permute-start(bf16[160,1920]{1,0:T(8,128)(2,1)S(1)} %constant_dynamic-slice_fusion.1), channel_id=1, source_target_pairs={{0,8},{1,9},{2,10},{3,11},{4,12},{5,13},{6,14},{7,15},{8,0},{9,1},... | collective-permute-start | bytes 1843208 | tf_op jit(solution)/shard_map/ppermute | solution.py:320
  75.4 16.5 %collective-permute-start.10 = (bf16[80,1920]{1,0:T(8,128)(2,1)}, bf16[80,1920]{1,0:T(8,128)(2,1)}, u32[]{:S(2)}, u32[]{:S(2)}) collective-permute-start(bf16[80,1920]{1,0:T(8,128)(2,1)} %constant_dynamic-slice_fusion), channel_id=1, source_target_pairs={{0,16},{1,17},{2,18},{3,19},{4,20},{5,21},{6,22},{7,23},{8,24},{9,... | collective-permute-start | bytes 921608 | tf_op jit(solution)/shard_map/ppermute | solution.py:320
  81.6 59.1 %collective-permute-start.1 = (bf16[512,1280]{1,0:T(8,128)(2,1)}, bf16[512,1280]{1,0:T(8,128)(2,1)S(1)}, u32[]{:S(2)}, u32[]{:S(2)}) collective-permute-start(bf16[512,1280]{1,0:T(8,128)(2,1)} %get-tuple-element.22.key_ref.value_ref), channel_id=1, source_target_pairs={{1,0},{3,2},{5,4},{7,6},{8,1},{9,8},{10,3},{11,10},{12,5},{13,12},... | collective-permute-start | bytes 3932168 | tf_op jit(solution)/shard_map/ppermute | solution.py:320
  83.0 58.9 %collective-permute-start = (bf16[512,1280]{1,0:T(8,128)(2,1)}, bf16[512,1280]{1,0:T(8,128)(2,1)S(1)}, u32[]{:S(2)}, u32[]{:S(2)}) collective-permute-start(bf16[512,1280]{1,0:T(8,128)(2,1)} %get-tuple-element.22.key_ref.value_ref), channel_id=1, source_target_pairs={{0,1},{1,8},{2,3},{3,10},{4,5},{5,12},{6,7},{7,14},{8,9},{9,16},{1... | collective-permute-start | bytes 3932168 | tf_op jit(solution)/shard_map/ppermute | solution.py:320
  86.2 55.7 %all-to-all-start.1 = ((bf16[32,16,640]{2,1,0:T(8,128)(2,1)}), bf16[32,16,640]{2,1,0:T(8,128)(2,1)S(1)}, u32[]{:S(2)}, u32[]{:S(2)}) async-start(bf16[32,16,640]{2,1,0:T(8,128)(2,1)} %bitcast.32), calls=%async_computation.1 | async-start | bytes 1310720 | tf_op jit(solution)/shard_map/all_to_all | solution.py:381
  93.7 39.3 %collective-permute-start.11 = (bf16[80,1920]{1,0:T(8,128)(2,1)}, bf16[80,1920]{1,0:T(8,128)(2,1)}, u32[]{:S(2)}, u32[]{:S(2)}) collective-permute-start(bf16[80,1920]{1,0:T(8,128)(2,1)} %add_convert_fusion.1.refs_0_), channel_id=1, source_target_pairs={{0,16},{1,17},{2,18},{3,19},{4,20},{5,21},{6,22},{7,23},{8,24},{9,... | collective-permute-start | bytes 921608 | tf_op jit(solution)/shard_map/ppermute | solution.py:320
  93.8 39.3 %collective-permute-start.12 = (bf16[80,1920]{1,0:T(8,128)(2,1)}, bf16[80,1920]{1,0:T(8,128)(2,1)}, u32[]{:S(2)}, u32[]{:S(2)}) collective-permute-start(bf16[80,1920]{1,0:T(8,128)(2,1)} %add_convert_fusion.1.refs_0_), channel_id=1, source_target_pairs={{0,8},{1,9},{2,10},{3,11},{4,12},{5,13},{6,14},{7,15},{8,0},{9,1},... | collective-permute-start | bytes 921608 | tf_op jit(solution)/shard_map/ppermute | solution.py:320
  133.1 7.7 %collective-permute-start.13 = (bf16[80,1920]{1,0:T(8,128)(2,1)}, bf16[80,1920]{1,0:T(8,128)(2,1)}, u32[]{:S(2)}, u32[]{:S(2)}) collective-permute-start(bf16[80,1920]{1,0:T(8,128)(2,1)} %collective-permute-done.11.refs_1_), channel_id=1, source_target_pairs={{0,8},{1,9},{2,10},{3,11},{4,12},{5,13},{6,14},{7,15},{8,0},{9,1},... | collective-permute-start | bytes 921608 | tf_op jit(solution)/shard_map/ppermute | solution.py:320
  133.1 23.4 %collective-permute-start.14 = (bf16[80,1920]{1,0:T(8,128)(2,1)}, bf16[80,1920]{1,0:T(8,128)(2,1)}, u32[]{:S(2)}, u32[]{:S(2)}) collective-permute-start(bf16[80,1920]{1,0:T(8,128)(2,1)} %add_convert_fusion.1.refs_0_), channel_id=1, source_target_pairs={{0,1},{1,0},{2,3},{3,2},{4,5},{5,4},{6,7},{7,6},{8,9},{9,8},{10,11... | collective-permute-start | bytes 921608 | tf_op jit(solution)/shard_map/ppermute | solution.py:320
  133.1 23.4 %collective-permute-start.15 = (bf16[80,1920]{1,0:T(8,128)(2,1)}, bf16[80,1920]{1,0:T(8,128)(2,1)}, u32[]{:S(2)}, u32[]{:S(2)}) collective-permute-start(bf16[80,1920]{1,0:T(8,128)(2,1)} %collective-permute-done.11.refs_1_), channel_id=1, source_target_pairs={{0,1},{1,0},{2,3},{3,2},{4,5},{5,4},{6,7},{7,6},{8,9},{9,8},{10,11... | collective-permute-start | bytes 921608 | tf_op jit(solution)/shard_map/ppermute | solution.py:320
  140.8 15.7 %collective-permute-start.16 = (bf16[80,1920]{1,0:T(8,128)(2,1)}, bf16[80,1920]{1,0:T(8,128)(2,1)}, u32[]{:S(2)}, u32[]{:S(2)}) collective-permute-start(bf16[80,1920]{1,0:T(8,128)(2,1)} %collective-permute-done.12.refs_2_), channel_id=1, source_target_pairs={{0,1},{1,0},{2,3},{3,2},{4,5},{5,4},{6,7},{7,6},{8,9},{9,8},{10,11... | collective-permute-start | bytes 921608 | tf_op jit(solution)/shard_map/ppermute | solution.py:320
  140.8 15.7 %collective-permute-start.17 = (bf16[80,1920]{1,0:T(8,128)(2,1)}, bf16[80,1920]{1,0:T(8,128)(2,1)}, u32[]{:S(2)}, u32[]{:S(2)}) collective-permute-start(bf16[80,1920]{1,0:T(8,128)(2,1)} %collective-permute-done.13.refs_3_), channel_id=1, source_target_pairs={{0,1},{1,0},{2,3},{3,2},{4,5},{5,4},{6,7},{7,6},{8,9},{9,8},{10,11... | collective-permute-start | bytes 921608 | tf_op jit(solution)/shard_map/ppermute | solution.py:320
  165.4 8.0 %collective-permute-start.21 = (bf16[128,640]{1,0:T(8,128)(2,1)S(1)}, bf16[128,640]{1,0:T(8,128)(2,1)S(1)}, u32[]{:S(2)}, u32[]{:S(2)}) collective-permute-start(bf16[128,640]{1,0:T(8,128)(2,1)S(1)} %get-tuple-element.33), channel_id=1, source_target_pairs={{0,3},{1,7},{2,1},{3,5},{4,2},{5,6},{6,0},{7,4},{8,11},{9,15},{10,... | collective-permute-start | bytes 491528 | tf_op jit(solution)/shard_map/ppermute | solution.py:320
  165.7 7.7 %collective-permute-start.20 = (bf16[128,640]{1,0:T(8,128)(2,1)S(1)}, bf16[128,640]{1,0:T(8,128)(2,1)S(1)}, u32[]{:S(2)}, u32[]{:S(2)}) collective-permute-start(bf16[128,640]{1,0:T(8,128)(2,1)S(1)} %get-tuple-element.34), channel_id=1, source_target_pairs={{0,1},{1,5},{2,3},{3,7},{4,0},{5,4},{6,2},{7,6},{8,9},{9,13},{10,1... | collective-permute-start | bytes 491528 | tf_op jit(solution)/shard_map/ppermute | solution.py:320
  166.1 9.1 %collective-permute-start.19 = (bf16[128,640]{1,0:T(8,128)(2,1)S(1)}, bf16[128,640]{1,0:T(8,128)(2,1)S(1)}, u32[]{:S(2)}, u32[]{:S(2)}) collective-permute-start(bf16[128,640]{1,0:T(8,128)(2,1)S(1)} %get-tuple-element.35), channel_id=1, source_target_pairs={{0,2},{1,6},{2,0},{3,4},{4,3},{5,7},{6,1},{7,5},{8,10},{9,14},{10,... | collective-permute-start | bytes 491528 | tf_op jit(solution)/shard_map/ppermute | solution.py:320
  167.3 7.9 %collective-permute-start.18 = (bf16[128,640]{1,0:T(8,128)(2,1)S(1)}, bf16[128,640]{1,0:T(8,128)(2,1)S(1)}, u32[]{:S(2)}, u32[]{:S(2)}) collective-permute-start(bf16[128,640]{1,0:T(8,128)(2,1)S(1)} %get-tuple-element.36), channel_id=1, source_target_pairs={{0,0},{1,4},{2,2},{3,6},{4,1},{5,5},{6,3},{7,7},{8,8},{9,12},{10,1... | collective-permute-start | bytes 491528 | tf_op jit(solution)/shard_map/ppermute | solution.py:320
  (17 other events, 134.3 us)

commit v2 on v1

--- a/solution.py
+++ b/solution.py
@@ -232,8 +232,9 @@
 
 def apply_kernel(place_ref, weight_ref, query_ref, attended_ref, *refs):
     hidden = weight_ref.shape[2]
-    count = (len(refs) - 3) // 2
-    mine_refs, other_refs, (out_ref, fresh, scales) = refs[:count], refs[count : 2 * count], refs[2 * count :]
+    out_refs, (fresh, scales, rows_buf) = refs[-3 - PARTS : -3], refs[-3:]
+    count = (len(refs) - 3 - PARTS) // 2
+    mine_refs, other_refs = refs[:count], refs[count : 2 * count]
     piece = mine_refs[0].shape[0]
     core = place_ref[2]
     for head in range(PART_FAST):
@@ -269,7 +270,11 @@
         for begin, value in parts:
             if begin <= lane < begin + SPAN:
                 total += value[:, lane - begin : lane - begin + LANES]
-        out_ref[:, lane : lane + LANES] = total.astype(BF16)
+        rows_buf[:, lane : lane + LANES] = total.astype(BF16)
+    block = out_refs[0].shape[0]
+    for index, ref in enumerate(out_refs):
+        begin = pl.multiple_of(place_ref[4 + PARTS + count + index] * block, block)
+        ref[...] = rows_buf[pl.ds(begin, block), :]
 
 
 def norm_kernel(place_ref, *refs):
@@ -331,7 +336,8 @@
     for bit in reversed(range(bits)):
         masks += [mask ^ 1 << bit for mask in masks]
     starts = [owned(plane ^ mask) for mask in masks]
-    place = jnp.stack([rank, part, core, group] + sources + starts).astype(jnp.int32)
+    goals = [2 * (column ^ j % 2) + (row ^ j // 2) for j in range(PARTS)]
+    place = jnp.stack([rank, part, core, group] + sources + starts + goals).astype(jnp.int32)
 
     def weight_part():
         own = lax.dynamic_slice_in_dim(fast_init, part * PART_WIDTH, PART_WIDTH, 2)
@@ -442,20 +448,21 @@
         smem=1, flops=4 * group_rows * (WINDOW + block) * PART_WIDTH,
     )
 
-    (combined,) = call(
+    blocks = call(
         apply_kernel,
-        [jax.ShapeDtypeStruct((group_rows, PART_WIDTH), BF16)],
+        [jax.ShapeDtypeStruct((tok_dev, PART_WIDTH), BF16)] * PARTS,
         [place, weights, query_seq, attended] + pieces + pieces_other,
-        scratch=[VMEM((PART_FAST, 3, SPAN, hidden), BF16), VMEM((PART_FAST * 3, hidden), F32)],
+        scratch=[
+            VMEM((PART_FAST, 3, SPAN, hidden), BF16),
+            VMEM((PART_FAST * 3, hidden), F32),
+            VMEM((group_rows, PART_WIDTH), BF16),
+        ],
         smem=1, flops=6 * group_rows * PART_WIDTH * hidden,
     )
 
-    blocks = combined.reshape(PARTS, tok_dev, PART_WIDTH)
     parts = []
     for j in range(PARTS):
-        goal = 2 * (column ^ j % 2) + (row ^ j // 2)
-        send = lax.dynamic_index_in_dim(blocks, goal, 0, keepdims=False)
-        parts.append(permute(send, lambda z, y, x, c, j=j: (z, c, x ^ j % 2, y ^ j // 2)))
+        parts.append(permute(blocks[j], lambda z, y, x, c, j=j: (z, c, x ^ j % 2, y ^ j // 2)))
 
     (out,) = call(
         norm_kernel,

time: 180 us -> 181 us (level)
  starting transfers between devices: 34 us -> 36.3 us
    ppermute x22, starting transfers between devices: 23.7 us -> 26.1 us  [permute(): return lax.ppermute(array, 'tok', route)]
where the time goes in v2:
time: 181 us; the launch traced here: 180 us
  waiting for transfers between devices  83.3 us (46%)
  Pallas kernels  44.5 us (25%)
  starting transfers between devices  36.3 us (20%)
  local copies, waits for them, and re-layouts  13.9 us (8%)
  other arithmetic  2 us (1%)
    ppermute x22, waiting for transfers between devices, permute(): return lax.ppermute(array, 'tok', route)  83.3 us
    pallas_call x6, Pallas kernels, call(): pl.pallas_call(kernel, out_shape=list(outs), in_specs=specs, out_specs=ou...  39.6 us
    ppermute x22, starting transfers between devices, permute(): return lax.ppermute(array, 'tok', route)  26.1 us
    all_to_all x2, starting transfers between devices, exchange(): lax.all_to_all(flat, 'tok', split_axis=0, concat_axis=0, tiled=True)  10.2 us
    unnamed x36, local copies, waits for them, and re-layouts  8.12 us
    pallas_call x1, Pallas kernels, shards(): pl.pallas_call(heads_kernel, out_shape=[jax.ShapeDtypeStruct((tok_dev, 2...  4.87 us
  transfers between devices with their start and end apart: 24, of which 8 were waited for; matrix products, arithmetic and copies ran while one was open for 6% of the time, Pallas kernels for 17%

profile of v2, /device:TPU:0, one launch (start us, length us, event | category | flops | bytes accessed | tf_op | source)
XLA Modules:
  0.0 180.3 jit_solution(6199181831953937993)
XLA Ops:
  0.7 4.4 %shard_map.82 = (bf16[4,4,2,16,1280]{4,3,2,1,0:T(8,128)(2,1)}, bf16[4,4,2,16,640]{4,3,2,1,0:T(8,128)(2,1)}) custom-call(s32[16]{0:T(128)} %stack.67.place_ref, s32[32,128]{1,0:T(8,128)} %bitcast.27, bf16[128,2560]{1,0:T(8,128)(2,1)} %query_ref.1, bf16[128,2560]{1,0:T(8,128)(2,1)} %key_ref.3, bf16[128,2560]{1,0:T(8,128)(2,1)} %value_ref.3), custom_call_target="tpu_custom_call" | custom-call | flops 251658240 | bytes 3948608 | tf_op jit(solution)/shard_map/pallas_call | solution.py:53
  5.1 7.4 %all-to-all-start = ((bf16[32,16,1280]{2,1,0:T(8,128)(2,1)}), bf16[32,16,1280]{2,1,0:T(8,128)(2,1)}, u32[]{:S(2)}, u32[]{:S(2)}) async-start(bf16[32,16,1280]{2,1,0:T(8,128)(2,1)} %bitcast.25), calls=%async_computation | async-start | bytes 2621440 | tf_op jit(solution)/shard_map/all_to_all | solution.py:387
  13.3 4.9 %heads.1 = (bf16[128,768]{1,0:T(8,128)(2,1)}, bf16[128,768]{1,0:T(8,128)(2,1)}, bf16[128,768]{1,0:T(8,128)(2,1)}, bf16[128,768]{1,0:T(8,128)(2,1)}, bf16[128,768...) custom-call(s32[16]{0:T(128)} %stack.67.place_ref, ...), custom_call_target="tpu_custom_call" | custom-call | flops 327680 | bytes 2621440 | tf_op jit(solution)/shard_map/heads/pallas_call | solution.py:352
  21.9 2.5 %collective-permute-start.7 = (bf16[128,768]{1,0:T(8,128)(2,1)}, bf16[128,768]{1,0:T(8,128)(2,1)}, u32[]{:S(2)}, u32[]{:S(2)}) collective-permute-start(bf16[128,768]{1,0:T(8,128)(2,1)} %get-tuple-element.35), channel_id=1, source_target_pairs={{0,6},{1,7},{2,4},{3,5},{4,2},{5,3},{6,0},{7,1},{8,14},{9,15},{10,... | collective-permute-start | bytes 589832 | tf_op jit(solution)/shard_map/ppermute | solution.py:325
  24.4 6.3 %collective-permute-done.3.refs_2_ = bf16[128,768]{1,0:T(8,128)(2,1)S(1)} collective-permute-done((bf16[128,768]{1,0:T(8,128)(2,1)}, bf16[128,768]{1,0:T(8,128)(2,1)S(1)}, u32[]{:S(2)}, u32[]{:S(2)}) %collective-permute-start.3) | collective-permute-done | bytes 196640 | tf_op jit(solution)/shard_map/ppermute | solution.py:325
  31.9 1.9 %constant_dynamic-slice_fusion.2 = bf16[640,3,640]{2,0,1:T(8,128)(2,1)S(1)} fusion(bf16[640,3,2560]{2,0,1:T(8,128)(2,1)} %param.14, s32[]{:T(128)S(6)} %select_n.46), kind=kLoop, calls=%fused_computation.4 | loop fusion | bytes 4915204 | tf_op jit(solution)/shard_map/dynamic_slice | solution.py:343
  33.8 3.3 %copy.11 = bf16[640,3,640]{0,2,1:T(8,128)(2,1)} copy(bf16[640,3,640]{2,0,1:T(8,128)(2,1)S(1)} %constant_dynamic-slice_fusion.2) | data formatting | bytes 4915200
  37.1 10.7 %collective-permute-done.6.refs_5_ = bf16[128,768]{1,0:T(8,128)(2,1)S(1)} collective-permute-done((bf16[128,768]{1,0:T(8,128)(2,1)}, bf16[128,768]{1,0:T(8,128)(2,1)S(1)}, u32[]{:S(2)}, u32[]{:S(2)}) %collective-permute-start.6) | collective-permute-done | bytes 196640 | tf_op jit(solution)/shard_map/ppermute | solution.py:325
  48.5 7.9 %shard_map.85 = bf16[320,1920]{1,0:T(8,128)(2,1)} custom-call(s32[16]{0:T(128)} %stack.67.place_ref, bf16[3,640,640]{2,1,0:T(8,128)(2,1)} %bitcast.22, bf16[128,768]{1,0:T(8,128)(2,1)} %get-tuple-element.29.refs_0_, bf16[128,768]{1,0:T(8,128)(2,1)} %copy-done.12, bf16[128,768]{1,0:T(8,128)(2,1)} %copy-done.13, bf16[128,768]{1,0:T(8,128)(2,1)} %copy-done.14, ...), custom_call_target="tpu_custom_call" | custom-call | flops 2516582400 | bytes 5259328 | tf_op jit(solution)/shard_map/pallas_call | solution.py:53
  58.6 15.0 %collective-permute-done.9 = bf16[160,1920]{1,0:T(8,128)(2,1)S(1)} collective-permute-done((bf16[160,1920]{1,0:T(8,128)(2,1)S(1)}, bf16[160,1920]{1,0:T(8,128)(2,1)S(1)}, u32[]{:S(2)}, u32[]{:S(2)}) %collective-permute-start.9) | collective-permute-done | bytes 614432 | tf_op jit(solution)/shard_map/ppermute | solution.py:325
  75.4 2.3 %collective-permute-start.10 = (bf16[80,1920]{1,0:T(8,128)(2,1)}, bf16[80,1920]{1,0:T(8,128)(2,1)}, u32[]{:S(2)}, u32[]{:S(2)}) collective-permute-start(bf16[80,1920]{1,0:T(8,128)(2,1)} %constant_dynamic-slice_fusion), channel_id=1, source_target_pairs={{0,16},{1,17},{2,18},{3,19},{4,20},{5,21},{6,22},{7,23},{8,24},{9,... | collective-permute-start | bytes 921608 | tf_op jit(solution)/shard_map/ppermute | solution.py:325
  77.6 4.0 %shard_map.83 = (bf16[512,1280]{1,0:T(8,128)(2,1)}, bf16[512,512]{1,0:T(8,128)(2,1)}) custom-call(s32[16]{0:T(128)} %stack.67.place_ref, s32[32,128]{1,0:T(8,128)} %bitcast.28, bf16[512,1280]{1,0:T(8,128)(2,1)} %bitcast.19.kv_in_ref), custom_call_target="tpu_custom_call" | custom-call | flops 671088640 | bytes 3162176 | tf_op jit(solution)/shard_map/pallas_call | solution.py:53
  83.1 3.1 %collective-permute-start = (bf16[512,1280]{1,0:T(8,128)(2,1)}, bf16[512,1280]{1,0:T(8,128)(2,1)S(1)}, u32[]{:S(2)}, u32[]{:S(2)}) collective-permute-start(bf16[512,1280]{1,0:T(8,128)(2,1)} %get-tuple-element.26.key_ref.value_ref), channel_id=1, source_target_pairs={{0,1},{1,8},{2,3},{3,10},{4,5},{5,12},{6,7},{7,14},{8,9},{9,16},{1... | collective-permute-start | bytes 3932168 | tf_op jit(solution)/shard_map/ppermute | solution.py:325
  86.2 2.8 %all-to-all-start.1 = ((bf16[32,16,640]{2,1,0:T(8,128)(2,1)}), bf16[32,16,640]{2,1,0:T(8,128)(2,1)S(1)}, u32[]{:S(2)}, u32[]{:S(2)}) async-start(bf16[32,16,640]{2,1,0:T(8,128)(2,1)} %bitcast.26), calls=%async_computation.1 | async-start | bytes 1310720 | tf_op jit(solution)/shard_map/all_to_all | solution.py:387
  89.0 2.9 %collective-permute-done.10 = bf16[80,1920]{1,0:T(8,128)(2,1)} collective-permute-done((bf16[80,1920]{1,0:T(8,128)(2,1)}, bf16[80,1920]{1,0:T(8,128)(2,1)}, u32[]{:S(2)}, u32[]{:S(2)}) %collective-permute-start.10) | collective-permute-done | bytes 307232 | tf_op jit(solution)/shard_map/ppermute | solution.py:325
  91.9 1.9 %add_convert_fusion.1.refs_0_ = bf16[80,1920]{1,0:T(8,128)(2,1)} fusion(bf16[80,1920]{1,0:T(8,128)(2,1)} %collective-permute-done.10, bf16[160,1920]{1,0:T(8,128)(2,1)} %copy-done.3, s32[]{:T(128)S(6)} %select_n.49), kind=kLoop, calls=%fused_computation.1 | loop fusion | flops 614400 | bytes 921604 | tf_op jit(solution)/shard_map/convert_element_type | solution.py:424
  93.8 5.0 %collective-permute-start.12 = (bf16[80,1920]{1,0:T(8,128)(2,1)}, bf16[80,1920]{1,0:T(8,128)(2,1)}, u32[]{:S(2)}, u32[]{:S(2)}) collective-permute-start(bf16[80,1920]{1,0:T(8,128)(2,1)} %add_convert_fusion.1.refs_0_), channel_id=1, source_target_pairs={{0,8},{1,9},{2,10},{3,11},{4,12},{5,13},{6,14},{7,15},{8,0},{9,1},... | collective-permute-start | bytes 921608 | tf_op jit(solution)/shard_map/ppermute | solution.py:325
  98.7 34.4 %collective-permute-done.11.refs_1_ = bf16[80,1920]{1,0:T(8,128)(2,1)} collective-permute-done((bf16[80,1920]{1,0:T(8,128)(2,1)}, bf16[80,1920]{1,0:T(8,128)(2,1)}, u32[]{:S(2)}, u32[]{:S(2)}) %collective-permute-start.11) | collective-permute-done | bytes 307232 | tf_op jit(solution)/shard_map/ppermute | solution.py:325
  133.6 7.1 %collective-permute-done.13.refs_3_ = bf16[80,1920]{1,0:T(8,128)(2,1)} collective-permute-done((bf16[80,1920]{1,0:T(8,128)(2,1)}, bf16[80,1920]{1,0:T(8,128)(2,1)}, u32[]{:S(2)}, u32[]{:S(2)}) %collective-permute-start.13) | collective-permute-done | bytes 307232 | tf_op jit(solution)/shard_map/ppermute | solution.py:325
  143.2 13.2 %shard_map.84 = (f32[512,640]{1,0:T(8,128)}, bf16[512,640]{1,0:T(8,128)(2,1)}) custom-call(s32[16]{0:T(128)} %stack.67.place_ref, bf16[512,512]{1,0:T(8,128)(2,1)} %get-tuple-element.24.choose_ref, bf16[512,640]{1,0:T(8,128)(2,1)} %bitcast.24, s32[8,512]{1,0:T(8,128)} %reshape.26.ids_ref, bf16[512,1280]{1,0:T(8,128)(2,1)} %get-tuple-element.26.key_ref.value_ref, ...), custom_call_target="tpu_custom_call" | custom-call | flops 1509949440 | bytes 11026496 | tf_op jit(solution)/shard_map/pallas_call | solution.py:53
  156.5 7.7 %shard_map.86 = (bf16[128,640]{1,0:T(8,128)(2,1)}, bf16[128,640]{1,0:T(8,128)(2,1)}, bf16[128,640]{1,0:T(8,128)(2,1)}, bf16[128,640]{1,0:T(8,128)(2,1)}) custom-call(s32[16]{0:T(128)} %stack.67.place_ref, bf16[3,640,640]{2,1,0:T(8,128)(2,1)} %bitcast.23, bf16[512,640]{1,0:T(8,128)(2,1)} %get-tuple-element.27.query_ref, ...), custom_call_target="tpu_custom_call" | custom-call | flops 1258291200 | bytes 7536704 | tf_op jit(solution)/shard_map/pallas_call | solution.py:53
  169.7 2.2 %collective-permute-done.19.refs_1_ = bf16[128,640]{1,0:T(8,128)(2,1)S(1)} collective-permute-done((bf16[128,640]{1,0:T(8,128)(2,1)}, bf16[128,640]{1,0:T(8,128)(2,1)S(1)}, u32[]{:S(2)}, u32[]{:S(2)}) %collective-permute-start.19) | collective-permute-done | bytes 163872 | tf_op jit(solution)/shard_map/ppermute | solution.py:325
  171.9 4.7 %collective-permute-done.20.refs_2_ = bf16[128,640]{1,0:T(8,128)(2,1)S(1)} collective-permute-done((bf16[128,640]{1,0:T(8,128)(2,1)}, bf16[128,640]{1,0:T(8,128)(2,1)S(1)}, u32[]{:S(2)}, u32[]{:S(2)}) %collective-permute-start.20) | collective-permute-done | bytes 163872 | tf_op jit(solution)/shard_map/ppermute | solution.py:325
  177.9 2.4 %shard_map.87 = bf16[128,2560]{1,0:T(8,128)(2,1)} custom-call(s32[16]{0:T(128)} %stack.67.place_ref, bf16[128,640]{1,0:T(8,128)(2,1)} %copy-done.5, bf16[128,640]{1,0:T(8,128)(2,1)} %copy-done.6, bf16[128,640]{1,0:T(8,128)(2,1)} %copy-done.7, bf16[128,640]{1,0:T(8,128)(2,1)} %copy-done.8, f32[1,2560]{1,0:T(1,128)} %reshape.27.refs_4_), custom_call_target="tpu_custom_call" | custom-call | flops 1966080 | bytes 1321024 | tf_op jit(solution)/shard_map/pallas_call | solution.py:53
  (75 shorter events, 22.1 us)
Async XLA Ops:
  5.1 72.5 %all-to-all-start = ((bf16[32,16,1280]{2,1,0:T(8,128)(2,1)}), bf16[32,16,1280]{2,1,0:T(8,128)(2,1)}, u32[]{:S(2)}, u32[]{:S(2)}) async-start(bf16[32,16,1280]{2,1,0:T(8,128)(2,1)} %bitcast.25), calls=%async_computation | async-start | bytes 2621440 | tf_op jit(solution)/shard_map/all_to_all | solution.py:387
  18.2 3.7 %collective-permute-start.2 = (bf16[128,768]{1,0:T(8,128)(2,1)}, bf16[128,768]{1,0:T(8,128)(2,1)S(1)}, u32[]{:S(2)}, u32[]{:S(2)}) collective-permute-start(bf16[128,768]{1,0:T(8,128)(2,1)} %get-tuple-element.30), channel_id=1, source_target_pairs={{0,1},{1,0},{2,3},{3,2},{4,5},{5,4},{6,7},{7,6},{8,9},{9,8},{10,11... | collective-permute-start | bytes 589832 | tf_op jit(solution)/shard_map/ppermute | solution.py:325
  18.4 12.3 %collective-permute-start.3 = (bf16[128,768]{1,0:T(8,128)(2,1)}, bf16[128,768]{1,0:T(8,128)(2,1)S(1)}, u32[]{:S(2)}, u32[]{:S(2)}) collective-permute-start(bf16[128,768]{1,0:T(8,128)(2,1)} %get-tuple-element.31), channel_id=1, source_target_pairs={{0,2},{1,3},{2,0},{3,1},{4,6},{5,7},{6,4},{7,5},{8,10},{9,11},{10,... | collective-permute-start | bytes 589832 | tf_op jit(solution)/shard_map/ppermute | solution.py:325
  20.0 17.1 %collective-permute-start.4 = (bf16[128,768]{1,0:T(8,128)(2,1)}, bf16[128,768]{1,0:T(8,128)(2,1)S(1)}, u32[]{:S(2)}, u32[]{:S(2)}) collective-permute-start(bf16[128,768]{1,0:T(8,128)(2,1)} %get-tuple-element.32), channel_id=1, source_target_pairs={{0,3},{1,2},{2,1},{3,0},{4,7},{5,6},{6,5},{7,4},{8,11},{9,10},{10,... | collective-permute-start | bytes 589832 | tf_op jit(solution)/shard_map/ppermute | solution.py:325
  20.0 17.1 %collective-permute-start.5 = (bf16[128,768]{1,0:T(8,128)(2,1)}, bf16[128,768]{1,0:T(8,128)(2,1)S(1)}, u32[]{:S(2)}, u32[]{:S(2)}) collective-permute-start(bf16[128,768]{1,0:T(8,128)(2,1)} %get-tuple-element.33), channel_id=1, source_target_pairs={{0,4},{1,5},{2,6},{3,7},{4,0},{5,1},{6,2},{7,3},{8,12},{9,13},{10,... | collective-permute-start | bytes 589832 | tf_op jit(solution)/shard_map/ppermute | solution.py:325
  21.7 26.1 %collective-permute-start.6 = (bf16[128,768]{1,0:T(8,128)(2,1)}, bf16[128,768]{1,0:T(8,128)(2,1)S(1)}, u32[]{:S(2)}, u32[]{:S(2)}) collective-permute-start(bf16[128,768]{1,0:T(8,128)(2,1)} %get-tuple-element.34), channel_id=1, source_target_pairs={{0,5},{1,4},{2,7},{3,6},{4,1},{5,0},{6,3},{7,2},{8,13},{9,12},{10,... | collective-permute-start | bytes 589832 | tf_op jit(solution)/shard_map/ppermute | solution.py:325
  21.9 26.0 %collective-permute-start.7 = (bf16[128,768]{1,0:T(8,128)(2,1)}, bf16[128,768]{1,0:T(8,128)(2,1)}, u32[]{:S(2)}, u32[]{:S(2)}) collective-permute-start(bf16[128,768]{1,0:T(8,128)(2,1)} %get-tuple-element.35), channel_id=1, source_target_pairs={{0,6},{1,7},{2,4},{3,5},{4,2},{5,3},{6,0},{7,1},{8,14},{9,15},{10,... | collective-permute-start | bytes 589832 | tf_op jit(solution)/shard_map/ppermute | solution.py:325
  30.7 17.1 %collective-permute-start.8 = (bf16[128,768]{1,0:T(8,128)(2,1)}, bf16[128,768]{1,0:T(8,128)(2,1)}, u32[]{:S(2)}, u32[]{:S(2)}) collective-permute-start(bf16[128,768]{1,0:T(8,128)(2,1)} %get-tuple-element.36), channel_id=1, source_target_pairs={{0,7},{1,6},{2,5},{3,4},{4,3},{5,2},{6,1},{7,0},{8,15},{9,14},{10,... | collective-permute-start | bytes 589832 | tf_op jit(solution)/shard_map/ppermute | solution.py:325
  57.7 15.9 %collective-permute-start.9 = (bf16[160,1920]{1,0:T(8,128)(2,1)S(1)}, bf16[160,1920]{1,0:T(8,128)(2,1)S(1)}, u32[]{:S(2)}, u32[]{:S(2)}) collective-permute-start(bf16[160,1920]{1,0:T(8,128)(2,1)S(1)} %constant_dynamic-slice_fusion.1), channel_id=1, source_target_pairs={{0,8},{1,9},{2,10},{3,11},{4,12},{5,13},{6,14},{7,15},{8,0},{9,1},... | collective-permute-start | bytes 1843208 | tf_op jit(solution)/shard_map/ppermute | solution.py:325
  75.4 16.5 %collective-permute-start.10 = (bf16[80,1920]{1,0:T(8,128)(2,1)}, bf16[80,1920]{1,0:T(8,128)(2,1)}, u32[]{:S(2)}, u32[]{:S(2)}) collective-permute-start(bf16[80,1920]{1,0:T(8,128)(2,1)} %constant_dynamic-slice_fusion), channel_id=1, source_target_pairs={{0,16},{1,17},{2,18},{3,19},{4,20},{5,21},{6,22},{7,23},{8,24},{9,... | collective-permute-start | bytes 921608 | tf_op jit(solution)/shard_map/ppermute | solution.py:325
  81.6 59.1 %collective-permute-start.1 = (bf16[512,1280]{1,0:T(8,128)(2,1)}, bf16[512,1280]{1,0:T(8,128)(2,1)S(1)}, u32[]{:S(2)}, u32[]{:S(2)}) collective-permute-start(bf16[512,1280]{1,0:T(8,128)(2,1)} %get-tuple-element.26.key_ref.value_ref), channel_id=1, source_target_pairs={{1,0},{3,2},{5,4},{7,6},{8,1},{9,8},{10,3},{11,10},{12,5},{13,12},... | collective-permute-start | bytes 3932168 | tf_op jit(solution)/shard_map/ppermute | solution.py:325
  83.1 58.8 %collective-permute-start = (bf16[512,1280]{1,0:T(8,128)(2,1)}, bf16[512,1280]{1,0:T(8,128)(2,1)S(1)}, u32[]{:S(2)}, u32[]{:S(2)}) collective-permute-start(bf16[512,1280]{1,0:T(8,128)(2,1)} %get-tuple-element.26.key_ref.value_ref), channel_id=1, source_target_pairs={{0,1},{1,8},{2,3},{3,10},{4,5},{5,12},{6,7},{7,14},{8,9},{9,16},{1... | collective-permute-start | bytes 3932168 | tf_op jit(solution)/shard_map/ppermute | solution.py:325
  86.2 55.7 %all-to-all-start.1 = ((bf16[32,16,640]{2,1,0:T(8,128)(2,1)}), bf16[32,16,640]{2,1,0:T(8,128)(2,1)S(1)}, u32[]{:S(2)}, u32[]{:S(2)}) async-start(bf16[32,16,640]{2,1,0:T(8,128)(2,1)} %bitcast.26), calls=%async_computation.1 | async-start | bytes 1310720 | tf_op jit(solution)/shard_map/all_to_all | solution.py:387
  93.8 39.3 %collective-permute-start.11 = (bf16[80,1920]{1,0:T(8,128)(2,1)}, bf16[80,1920]{1,0:T(8,128)(2,1)}, u32[]{:S(2)}, u32[]{:S(2)}) collective-permute-start(bf16[80,1920]{1,0:T(8,128)(2,1)} %add_convert_fusion.1.refs_0_), channel_id=1, source_target_pairs={{0,16},{1,17},{2,18},{3,19},{4,20},{5,21},{6,22},{7,23},{8,24},{9,... | collective-permute-start | bytes 921608 | tf_op jit(solution)/shard_map/ppermute | solution.py:325
  93.8 39.3 %collective-permute-start.12 = (bf16[80,1920]{1,0:T(8,128)(2,1)}, bf16[80,1920]{1,0:T(8,128)(2,1)}, u32[]{:S(2)}, u32[]{:S(2)}) collective-permute-start(bf16[80,1920]{1,0:T(8,128)(2,1)} %add_convert_fusion.1.refs_0_), channel_id=1, source_target_pairs={{0,8},{1,9},{2,10},{3,11},{4,12},{5,13},{6,14},{7,15},{8,0},{9,1},... | collective-permute-start | bytes 921608 | tf_op jit(solution)/shard_map/ppermute | solution.py:325
  133.1 7.7 %collective-permute-start.13 = (bf16[80,1920]{1,0:T(8,128)(2,1)}, bf16[80,1920]{1,0:T(8,128)(2,1)}, u32[]{:S(2)}, u32[]{:S(2)}) collective-permute-start(bf16[80,1920]{1,0:T(8,128)(2,1)} %collective-permute-done.11.refs_1_), channel_id=1, source_target_pairs={{0,8},{1,9},{2,10},{3,11},{4,12},{5,13},{6,14},{7,15},{8,0},{9,1},... | collective-permute-start | bytes 921608 | tf_op jit(solution)/shard_map/ppermute | solution.py:325
  133.1 23.3 %collective-permute-start.14 = (bf16[80,1920]{1,0:T(8,128)(2,1)}, bf16[80,1920]{1,0:T(8,128)(2,1)}, u32[]{:S(2)}, u32[]{:S(2)}) collective-permute-start(bf16[80,1920]{1,0:T(8,128)(2,1)} %add_convert_fusion.1.refs_0_), channel_id=1, source_target_pairs={{0,1},{1,0},{2,3},{3,2},{4,5},{5,4},{6,7},{7,6},{8,9},{9,8},{10,11... | collective-permute-start | bytes 921608 | tf_op jit(solution)/shard_map/ppermute | solution.py:325
  133.1 23.4 %collective-permute-start.15 = (bf16[80,1920]{1,0:T(8,128)(2,1)}, bf16[80,1920]{1,0:T(8,128)(2,1)}, u32[]{:S(2)}, u32[]{:S(2)}) collective-permute-start(bf16[80,1920]{1,0:T(8,128)(2,1)} %collective-permute-done.11.refs_1_), channel_id=1, source_target_pairs={{0,1},{1,0},{2,3},{3,2},{4,5},{5,4},{6,7},{7,6},{8,9},{9,8},{10,11... | collective-permute-start | bytes 921608 | tf_op jit(solution)/shard_map/ppermute | solution.py:325
  140.8 15.7 %collective-permute-start.16 = (bf16[80,1920]{1,0:T(8,128)(2,1)}, bf16[80,1920]{1,0:T(8,128)(2,1)}, u32[]{:S(2)}, u32[]{:S(2)}) collective-permute-start(bf16[80,1920]{1,0:T(8,128)(2,1)} %collective-permute-done.12.refs_2_), channel_id=1, source_target_pairs={{0,1},{1,0},{2,3},{3,2},{4,5},{5,4},{6,7},{7,6},{8,9},{9,8},{10,11... | collective-permute-start | bytes 921608 | tf_op jit(solution)/shard_map/ppermute | solution.py:325
  140.8 15.7 %collective-permute-start.17 = (bf16[80,1920]{1,0:T(8,128)(2,1)}, bf16[80,1920]{1,0:T(8,128)(2,1)}, u32[]{:S(2)}, u32[]{:S(2)}) collective-permute-start(bf16[80,1920]{1,0:T(8,128)(2,1)} %collective-permute-done.13.refs_3_), channel_id=1, source_target_pairs={{0,1},{1,0},{2,3},{3,2},{4,5},{5,4},{6,7},{7,6},{8,9},{9,8},{10,11... | collective-permute-start | bytes 921608 | tf_op jit(solution)/shard_map/ppermute | solution.py:325
  164.2 5.6 %collective-permute-start.18 = (bf16[128,640]{1,0:T(8,128)(2,1)}, bf16[128,640]{1,0:T(8,128)(2,1)S(1)}, u32[]{:S(2)}, u32[]{:S(2)}) collective-permute-start(bf16[128,640]{1,0:T(8,128)(2,1)} %get-tuple-element.37), channel_id=1, source_target_pairs={{0,0},{1,4},{2,2},{3,6},{4,1},{5,5},{6,3},{7,7},{8,8},{9,12},{10,1... | collective-permute-start | bytes 491528 | tf_op jit(solution)/shard_map/ppermute | solution.py:325
  165.7 6.2 %collective-permute-start.19 = (bf16[128,640]{1,0:T(8,128)(2,1)}, bf16[128,640]{1,0:T(8,128)(2,1)S(1)}, u32[]{:S(2)}, u32[]{:S(2)}) collective-permute-start(bf16[128,640]{1,0:T(8,128)(2,1)} %get-tuple-element.38), channel_id=1, source_target_pairs={{0,2},{1,6},{2,0},{3,4},{4,3},{5,7},{6,1},{7,5},{8,10},{9,14},{10,... | collective-permute-start | bytes 491528 | tf_op jit(solution)/shard_map/ppermute | solution.py:325
  166.2 10.4 %collective-permute-start.20 = (bf16[128,640]{1,0:T(8,128)(2,1)}, bf16[128,640]{1,0:T(8,128)(2,1)S(1)}, u32[]{:S(2)}, u32[]{:S(2)}) collective-permute-start(bf16[128,640]{1,0:T(8,128)(2,1)} %get-tuple-element.39), channel_id=1, source_target_pairs={{0,1},{1,5},{2,3},{3,7},{4,0},{5,4},{6,2},{7,6},{8,9},{9,13},{10,1... | collective-permute-start | bytes 491528 | tf_op jit(solution)/shard_map/ppermute | solution.py:325
  167.9 8.7 %collective-permute-start.21 = (bf16[128,640]{1,0:T(8,128)(2,1)}, bf16[128,640]{1,0:T(8,128)(2,1)S(1)}, u32[]{:S(2)}, u32[]{:S(2)}) collective-permute-start(bf16[128,640]{1,0:T(8,128)(2,1)} %get-tuple-element.40), channel_id=1, source_target_pairs={{0,3},{1,7},{2,1},{3,5},{4,2},{5,6},{6,0},{7,4},{8,11},{9,15},{10,... | collective-permute-start | bytes 491528 | tf_op jit(solution)/shard_map/ppermute | solution.py:325
  (17 other events, 151.1 us)

commit v3 on v2

--- a/solution.py
+++ b/solution.py
@@ -68,39 +68,43 @@
 
 
 def heads_kernel(place_ref, rate_ref, key_ref, value_ref, *out_refs):
-    n = key_ref.shape[0]
+    n, width = key_ref.shape
     step, part, core = pl.program_id(0), place_ref[1], place_ref[2]
     rates = rate_ref[...]
     lane = iota((n, SPAN), 1)
-    rows = []
-    for head in range(PART_FAST):
-        begin, offset = window_of(head)
-
-        def window(ref):
-            rows = ref[:, begin : begin + SPAN].astype(F32)
-            rows = pltpu.roll(rows, SPAN - offset, 1) if offset else rows
-            return jnp.where(lane < HEAD_DIM, rows, 0.0)
-
-        own = (step ^ part) * PART_FAST + head
-        rate = jnp.sum(jnp.where(iota(rates.shape, 1) == own, rates, 0.0), axis=1, keepdims=True)
-        keys = window(key_ref)
-        for index in range(3):
-            piece = rate.astype(BF16).astype(F32)
-            rate = rate - piece
-            keys = jnp.where(lane == HEAD_DIM + index, piece, keys)
-        rows.append((keys, window(value_ref)))
-    for flip in range(PART_FAST):
-        chosen = [jnp.where(core == flip, first, second).astype(BF16) for first, second in zip(*rows)]
-        for index in range(PARTS):
-            @pl.when(step == index)
-            def _():
-                out_refs[index * PART_FAST + flip][:, :SPAN] = chosen[0]
-                out_refs[index * PART_FAST + flip][:, SPAN:] = chosen[1]
-
-
-def pack_kernel(group_shift, slots, place_ref, order_ref, query_ref, key_ref, value_ref, kv_ref, q_ref, choose_buf):
+    for local in range(width // PART_WIDTH):
+        index = step * (width // PART_WIDTH) + local
+        own_part = index ^ part
+        edge = lax.rem(own_part, width // PART_WIDTH) * PART_WIDTH
+        rows = []
+        for head in range(PART_FAST):
+            begin, offset = window_of(head)
+
+            def window(ref):
+                rows = ref[:, pl.ds(pl.multiple_of(edge + begin, LANES), SPAN)].astype(F32)
+                rows = pltpu.roll(rows, SPAN - offset, 1) if offset else rows
+                return jnp.where(lane < HEAD_DIM, rows, 0.0)
+
+            own = own_part * PART_FAST + head
+            rate = jnp.sum(jnp.where(iota(rates.shape, 1) == own, rates, 0.0), axis=1, keepdims=True)
+            keys = window(key_ref)
+            for third in range(3):
+                piece = rate.astype(BF16).astype(F32)
+                rate = rate - piece
+                keys = jnp.where(lane == HEAD_DIM + third, piece, keys)
+            rows.append((keys, window(value_ref)))
+        for flip in range(PART_FAST):
+            chosen = [jnp.where(core == flip, first, second).astype(BF16) for first, second in zip(*rows)]
+            for at in range(local, PARTS, width // PART_WIDTH):
+                @pl.when(step == at // (width // PART_WIDTH))
+                def _():
+                    out_refs[at * PART_FAST + flip][:, :SPAN] = chosen[0]
+                    out_refs[at * PART_FAST + flip][:, SPAN:] = chosen[1]
+
+
+def pack_kernel(group_shift, slots, place_ref, order_ref, query_ref, key_ref, value_ref, out_ref, choose_buf):
     n = query_ref.shape[0]
-    planes, _, cores = kv_ref.shape[:3]
+    planes, parts, cores = out_ref.shape[:3]
 
     @pl.when(pl.program_id(0) == 0)
     def _():
@@ -112,17 +116,15 @@
         slot = group * slots + rank.astype(jnp.int32)
         choose_buf[...] = jnp.where(iota((n, n), 0) == slot, 1.0, 0.0).astype(BF16)
 
-    def put_rows(ref, rows, begin):
-        width = rows.shape[1]
-        for plane in range(planes):
-            for core in range(cores):
-                at = (plane * cores + core) * slots
-                ref[plane, 0, core, :, begin : begin + width] = rows[at : at + slots]
-
     choose = choose_buf[...]
-    put_rows(kv_ref, dot(choose, key_ref[...]).astype(BF16), 0)
-    put_rows(kv_ref, dot(choose, value_ref[...]).astype(BF16), PART_WIDTH)
-    put_rows(q_ref, dot(choose, query_ref[...]).astype(BF16), 0)
+    for index, ref in enumerate((key_ref, value_ref, query_ref)):
+        lanes = slice(index * PART_WIDTH, (index + 1) * PART_WIDTH)
+        for part in range(parts):
+            rows = dot(choose, ref[:, part * PART_WIDTH : (part + 1) * PART_WIDTH]).astype(BF16)
+            for plane in range(planes):
+                for core in range(cores):
+                    at = (plane * cores + core) * slots
+                    out_ref[plane, part, core, :, lanes] = rows[at : at + slots]
 
 
 def arrival_choice(group_shift, slots, orders, group, n):
@@ -147,16 +149,14 @@
     return jnp.where(iota((n, n), 0) == pos.astype(jnp.int32), 1.0, 0.0).astype(BF16)
 
 
-def place_kernel(group_shift, slots, place_ref, order_ref, kv_in_ref, kv_ref, choose_ref):
-    choose = arrival_choice(group_shift, slots, order_ref[...], place_ref[3], choose_ref.shape[0])
-    choose_ref[...] = choose
-    for part in range(2):
-        lanes = slice(part * PART_WIDTH, (part + 1) * PART_WIDTH)
-        kv_ref[:, lanes] = dot(choose, kv_in_ref[:, lanes]).astype(BF16)
+def place_kernel(group_shift, slots, place_ref, order_ref, in_ref, kv_ref, q_ref):
+    choose = arrival_choice(group_shift, slots, order_ref[...], place_ref[3], in_ref.shape[0])
+    kv_ref[...] = dot(choose, in_ref[:, : 2 * PART_WIDTH]).astype(BF16)
+    q_ref[...] = dot(choose, in_ref[:, 2 * PART_WIDTH :]).astype(BF16)
 
 
 def grads_kernel(chunk, place_ref, weight_ref, *refs):
-    kv_refs, (out_ref, weight_buf, key_buf, target_buf, dg_buf, du_buf, pr_buf) = refs[:-7], refs[-7:]
+    kv_refs, (send_ref, keep_ref, weight_buf, key_buf, target_buf, dg_buf, du_buf, pr_buf, sums) = refs[:-9], refs[-9:]
     block = kv_refs[0].shape[0]
     n = key_buf.shape[0]
     hidden = weight_ref.shape[2]
@@ -184,11 +184,15 @@
         dg_buf[here, :] = (backward * upward * sigmoid * (1.0 + gate * (1.0 - sigmoid))).astype(BF16)
     for index, (left, right) in enumerate(((key_buf, dg_buf), (key_buf, du_buf), (target_buf, pr_buf))):
         total = dot(left[...], right[...], ((0,), (0,)))
-        out_ref[:, index * hidden : (index + 1) * hidden] = total[:HEAD_DIM].astype(BF16)
-
-
-def attention_kernel(block, place_ref, choose_ref, query_in_ref, ids_ref, key_ref, key_low_ref, key_high_ref, value_ref, value_low_ref, value_high_ref, out_ref, query_ref, bias):
-    n = choose_ref.shape[0]
+        sums[:, index * hidden : (index + 1) * hidden] = total[:HEAD_DIM].astype(BF16)
+    half = send_ref.shape[0]
+    side = place_ref[3] // PART_FAST & 1
+    send_ref[...] = sums[pl.ds(pl.multiple_of((1 - side) * half, 16), half), :]
+    keep_ref[...] = sums[pl.ds(pl.multiple_of(side * half, 16), half), :]
+
+
+def attention_kernel(block, place_ref, query_ref, ids_ref, key_ref, key_low_ref, key_high_ref, value_ref, value_low_ref, value_high_ref, out_ref, bias):
+    n = query_ref.shape[0]
     half = WINDOW // 2
     group = place_ref[3]
     last = ids_ref.shape[0] - 1
@@ -208,11 +212,9 @@
             allowed = (gap < half) & (gap > -half) & (own == ids)
             bias[at // block, :, :] = jnp.where(allowed, 0.0, -1e30)
 
-    query = dot(choose_ref[...], query_in_ref[...]).astype(BF16)
-    query_ref[...] = query
     factor = ATT_DIM ** (-0.5) * math.log2(math.e)
     for at in range(0, n, block):
-        part = query[at : at + block]
+        part = query_ref[at : at + block, :]
         stops = (0, half - at, half - at + n, half + n + block - half)
         keys = (key_low_ref[at:, :], key_ref[...], key_high_ref[: at + block, :])
         values = (value_low_ref[at:, :], value_ref[...], value_high_ref[: at + block, :])
@@ -346,15 +348,16 @@
     weights = weight_part()
 
     full = lambda a: pl.BlockSpec(a.shape, lambda h: (0,) * a.ndim)
-    cut = pl.BlockSpec((tok_dev, PART_WIDTH), lambda h: (0, h))
-    other_cut = pl.BlockSpec((tok_dev, PART_WIDTH), lambda h, place: (0, h ^ place[1]))
+    steps = 2
+    together = PARTS // steps
+    other_cut = pl.BlockSpec((tok_dev, WIDTH // steps), lambda h, place: (0, h ^ place[1] // together))
     whole = lambda shape: pl.BlockSpec(shape, lambda h, place: (0,) * len(shape))
     heads_out = pl.pallas_call(
         heads_kernel,
         out_shape=[jax.ShapeDtypeStruct((tok_dev, 2 * SPAN), BF16)] * plane_size,
         grid_spec=pltpu.PrefetchScalarGridSpec(
             num_scalar_prefetch=1,
-            grid=(PARTS,),
+            grid=(steps,),
             in_specs=[whole(learn_rates.shape), other_cut, other_cut],
             out_specs=[whole((tok_dev, 2 * SPAN))] * plane_size,
         ),
@@ -366,33 +369,26 @@
     for j in range(1, plane_size):
         heads_in.append(permute(heads_out[j], lambda z, y, x, c, j=j: (z, y ^ j >> 2, x ^ j >> 1 & 1, c ^ j & 1)))
 
-    shape = (planes, PARTS, PART_FAST, slots)
     orders = frame_order.reshape(sections, tok_dev)
-    kv_out, q_out = call(
+    cut = pl.BlockSpec((tok_dev, WIDTH // steps), lambda h: (0, h))
+    (packed,) = call(
         functools.partial(pack_kernel, group_shift, slots),
-        [jax.ShapeDtypeStruct(shape + (width,), BF16) for width in (2 * PART_WIDTH, PART_WIDTH)],
+        [jax.ShapeDtypeStruct((planes, PARTS, PART_FAST, slots, 3 * PART_WIDTH), BF16)],
         [place, orders, queries, key_rows, value_rows],
         in_specs=[full(orders), cut, cut, cut],
-        out_specs=[
-            pl.BlockSpec((planes, 1, PART_FAST, slots, width), lambda h: (0, h, 0, 0, 0))
-            for width in (2 * PART_WIDTH, PART_WIDTH)
-        ],
-        grid=(PARTS,),
+        out_specs=[pl.BlockSpec((planes, together, PART_FAST, slots, 3 * PART_WIDTH), lambda h: (0, h, 0, 0, 0))],
+        grid=(steps,),
         scratch=[VMEM((tok_dev, tok_dev), BF16)],
         smem=1, flops=2 * tok_dev * tok_dev * 3 * WIDTH,
     )
-
-    def exchange(array):
-        flat = array.reshape(sections, slots, array.shape[-1])
-        return lax.all_to_all(flat, "tok", split_axis=0, concat_axis=0, tiled=True).reshape(group_rows, array.shape[-1])
-
-    kv_in = exchange(kv_out)
-    q_in = exchange(q_out)
-
-    kv_seq, choose = call(
+    arrived = lax.all_to_all(
+        packed.reshape(sections, slots, 3 * PART_WIDTH), "tok", split_axis=0, concat_axis=0, tiled=True
+    ).reshape(group_rows, 3 * PART_WIDTH)
+
+    kv_seq, query_seq = call(
         functools.partial(place_kernel, group_shift, slots),
-        [jax.ShapeDtypeStruct((group_rows, 2 * PART_WIDTH), BF16), jax.ShapeDtypeStruct((group_rows, group_rows), BF16)],
-        [place, orders, kv_in], smem=1, flops=2 * group_rows * group_rows * 2 * PART_WIDTH,
+        [jax.ShapeDtypeStruct((group_rows, width), BF16) for width in (2 * PART_WIDTH, PART_WIDTH)],
+        [place, orders, arrived], smem=1, flops=2 * group_rows * group_rows * 3 * PART_WIDTH,
     )
 
     def neighbour(step):
@@ -406,22 +402,30 @@
     kv_high = permute(kv_seq, neighbour(-1))
 
     tokens = plane_size * tok_dev
-    (total,) = call(
+    send, keep = call(
         functools.partial(grads_kernel, tokens // 2),
-        [jax.ShapeDtypeStruct((HEAD_DIM, 3 * hidden), BF16)], [place, weights] + heads_in,
-        scratch=[VMEM((3, SPAN, hidden), BF16)] + [VMEM((tokens, SPAN), BF16)] * 2 + [VMEM((tokens, hidden), BF16)] * 3,
+        [jax.ShapeDtypeStruct((HEAD_DIM // 2, 3 * hidden), BF16)] * 2, [place, weights] + heads_in,
+        scratch=[VMEM((3, SPAN, hidden), BF16)] + [VMEM((tokens, SPAN), BF16)] * 2
+        + [VMEM((tokens, hidden), BF16)] * 3 + [VMEM((HEAD_DIM, 3 * hidden), BF16)],
         smem=1, flops=12 * tokens * HEAD_DIM * hidden,
     )
 
     def across(bit):
         return lambda z, y, x, c: (z ^ 1 << bit, y, x, c)
 
+    def added(first, second):
+        return (first.astype(F32) + second.astype(F32)).astype(BF16)
+
     for bit in range(bits):
-        size = HEAD_DIM >> bit + 1
-        side = plane >> bit & 1
-        came = permute(lax.dynamic_slice_in_dim(total, (1 - side) * size, size, 0), across(bit))
-        kept = lax.dynamic_slice_in_dim(total, side * size, size, 0)
-        total = (kept.astype(F32) + came.astype(F32)).astype(BF16)
+        came = permute(send, across(bit))
+        if bit + 1 < bits:
+            size = HEAD_DIM >> bit + 2
+            side = plane >> bit + 1 & 1
+            cuts = [[lax.dynamic_slice_in_dim(a, at * size, size, 0) for a in (keep, came)] for at in (1 - side, side)]
+            send = added(*cuts[0])
+            keep = added(*cuts[1])
+        else:
+            total = added(keep, came)
     pieces = [total]
     for bit in reversed(range(bits)):
         fresh_pieces = []
@@ -436,13 +440,13 @@
     block = min(LANES, group_rows)
     lane_block = lambda rows, shift: pl.BlockSpec((rows, ATT_DIM), lambda h: (0, h + shift))
     ids = window_ids.reshape(groups, group_rows)
-    attended, query_seq = call(
+    (attended,) = call(
         functools.partial(attention_kernel, block),
-        [jax.ShapeDtypeStruct((group_rows, PART_WIDTH), F32), jax.ShapeDtypeStruct((group_rows, PART_WIDTH), BF16)],
-        [place, choose, q_in, ids, kv_seq, kv_low, kv_high, kv_seq, kv_low, kv_high],
-        in_specs=[full(choose), lane_block(group_rows, 0), full(ids)]
+        [jax.ShapeDtypeStruct((group_rows, PART_WIDTH), F32)],
+        [place, query_seq, ids, kv_seq, kv_low, kv_high, kv_seq, kv_low, kv_high],
+        in_specs=[lane_block(group_rows, 0), full(ids)]
         + [lane_block(group_rows, 0)] * 3 + [lane_block(group_rows, PART_ATT)] * 3,
-        out_specs=[lane_block(group_rows, 0)] * 2,
+        out_specs=[lane_block(group_rows, 0)],
         grid=(PART_ATT,),
         scratch=[VMEM((group_rows // block, block, WINDOW + block), F32)],
         smem=1, flops=4 * group_rows * (WINDOW + block) * PART_WIDTH,

time: 181 us -> 168 us (0.928)
  waiting for transfers between devices: 83.3 us -> 76.8 us
  local copies, waits for them, and re-layouts: 13.9 us -> 10.3 us
  Pallas kernels: 44.5 us -> 41 us
    ppermute x22, waiting for transfers between devices: 83.3 us -> 76.8 us  [permute(): return lax.ppermute(array, 'tok', route)]
    ppermute x22, starting transfers between devices: 26.1 us -> 29.4 us  [permute(): return lax.ppermute(array, 'tok', route)]
    all_to_all x2 -> x1, starting transfers between devices: 10.2 us -> 7.44 us  [shards(): lax.all_to_all(packed.reshape(sections, slots, 3 * PART_WIDTH), 'tok', sp...]
    pallas_call x6, Pallas kernels: 39.6 us -> 37 us  [call(): pl.pallas_call(kernel, out_shape=list(outs), in_specs=specs, out_specs=ou...]
    unnamed x36 -> x38, local copies, waits for them, and re-layouts: 8.12 us -> 5.8 us
    dynamic_slice x2 -> x0, local copies, waits for them, and re-layouts: 1.98 us -> none  [shards(): lax.dynamic_slice_in_dim(total, (1 - side) * size, size, 0)]
  transfers between devices with their start and end apart: 24 -> 23, of which waited for: 8 -> 11; matrix products, arithmetic and copies ran while one was open for 6% -> 6% of each run, Pallas kernels for 17% -> 17%
where the time goes in v3:
time: 168 us
  waiting for transfers between devices  76.8 us (46%)
  Pallas kernels  41 us (24%)
  starting transfers between devices  36.8 us (22%)
  local copies, waits for them, and re-layouts  10.3 us (6%)
  other arithmetic  2.42 us (1%)
    ppermute x22, waiting for transfers between devices, permute(): return lax.ppermute(array, 'tok', route)  76.8 us
    pallas_call x6, Pallas kernels, call(): pl.pallas_call(kernel, out_shape=list(outs), in_specs=specs, out_specs=ou...  37 us
    ppermute x22, starting transfers between devices, permute(): return lax.ppermute(array, 'tok', route)  29.4 us
    all_to_all x1, starting transfers between devices, shards(): lax.all_to_all(packed.reshape(sections, slots, 3 * PART_WIDTH), 'tok', sp...  7.44 us
    unnamed x38, local copies, waits for them, and re-layouts  5.8 us
    pallas_call x1, Pallas kernels, shards(): pl.pallas_call(heads_kernel, out_shape=[jax.ShapeDtypeStruct((tok_dev, 2...  4.05 us
  transfers between devices with their start and end apart: 23, of which 11 were waited for; matrix products, arithmetic and copies ran while one was open for 6% of the time, Pallas kernels for 17%

profile of v3, /device:TPU:0, one launch (start us, length us, event | category | flops | bytes accessed | tf_op | source)
XLA Modules:
  0.0 167.5 jit_solution(237428856644717970)
XLA Ops:
  0.7 3.2 %shard_map.82 = bf16[4,4,2,16,1920]{4,3,2,1,0:T(8,128)(2,1)} custom-call(s32[16]{0:T(128)} %stack.67.place_ref, s32[32,128]{1,0:T(8,128)} %bitcast.23, bf16[128,2560]{1,0:T(8,128)(2,1)} %query_ref.1, bf16[128,2560]{1,0:T(8,128)(2,1)} %key_ref.3, bf16[128,2560]{1,0:T(8,128)(2,1)} %value_ref.3), custom_call_target="tpu_custom_call" | custom-call | flops 251658240 | bytes 3948608 | tf_op jit(solution)/shard_map/pallas_call | solution.py:53
  3.9 7.4 %all-to-all-start = ((bf16[32,16,1920]{2,1,0:T(8,128)(2,1)}), bf16[32,16,1920]{2,1,0:T(8,128)(2,1)}, u32[]{:S(2)}, u32[]{:S(2)}) async-start(bf16[32,16,1920]{2,1,0:T(8,128)(2,1)} %bitcast.22), calls=%async_computation | async-start | bytes 3932160 | tf_op jit(solution)/shard_map/all_to_all | solution.py:384
  12.0 4.0 %heads.1 = (bf16[128,768]{1,0:T(8,128)(2,1)}, bf16[128,768]{1,0:T(8,128)(2,1)}, bf16[128,768]{1,0:T(8,128)(2,1)}, bf16[128,768]{1,0:T(8,128)(2,1)}, bf16[128,768...) custom-call(s32[16]{0:T(128)} %stack.67.place_ref, ...), custom_call_target="tpu_custom_call" | custom-call | flops 327680 | bytes 2621440 | tf_op jit(solution)/shard_map/heads/pallas_call | solution.py:355
  19.8 2.5 %collective-permute-start.7 = (bf16[128,768]{1,0:T(8,128)(2,1)}, bf16[128,768]{1,0:T(8,128)(2,1)}, u32[]{:S(2)}, u32[]{:S(2)}) collective-permute-start(bf16[128,768]{1,0:T(8,128)(2,1)} %get-tuple-element.29), channel_id=1, source_target_pairs={{0,6},{1,7},{2,4},{3,5},{4,2},{5,3},{6,0},{7,1},{8,14},{9,15},{10,... | collective-permute-start | bytes 589832 | tf_op jit(solution)/shard_map/ppermute | solution.py:327
  22.3 9.2 %collective-permute-done.3.refs_2_ = bf16[128,768]{1,0:T(8,128)(2,1)S(1)} collective-permute-done((bf16[128,768]{1,0:T(8,128)(2,1)}, bf16[128,768]{1,0:T(8,128)(2,1)S(1)}, u32[]{:S(2)}, u32[]{:S(2)}) %collective-permute-start.3) | collective-permute-done | bytes 196640 | tf_op jit(solution)/shard_map/ppermute | solution.py:327
  31.5 3.1 %collective-permute-start.8 = (bf16[128,768]{1,0:T(8,128)(2,1)}, bf16[128,768]{1,0:T(8,128)(2,1)}, u32[]{:S(2)}, u32[]{:S(2)}) collective-permute-start(bf16[128,768]{1,0:T(8,128)(2,1)} %get-tuple-element.30), channel_id=1, source_target_pairs={{0,7},{1,6},{2,5},{3,4},{4,3},{5,2},{6,1},{7,0},{8,15},{9,14},{10,... | collective-permute-start | bytes 589832 | tf_op jit(solution)/shard_map/ppermute | solution.py:327
  34.6 1.9 %constant_dynamic-slice_fusion = bf16[640,3,640]{2,0,1:T(8,128)(2,1)S(1)} fusion(bf16[640,3,2560]{2,0,1:T(8,128)(2,1)} %param.14, s32[]{:T(128)S(6)} %select_n.42), kind=kLoop, calls=%fused_computation.3 | loop fusion | bytes 4915204 | tf_op jit(solution)/shard_map/dynamic_slice | solution.py:345
  36.5 3.3 %copy.11 = bf16[640,3,640]{0,2,1:T(8,128)(2,1)} copy(bf16[640,3,640]{2,0,1:T(8,128)(2,1)S(1)} %constant_dynamic-slice_fusion) | data formatting | bytes 4915200
  40.5 6.0 %collective-permute-done.7.refs_6_ = bf16[128,768]{1,0:T(8,128)(2,1)} collective-permute-done((bf16[128,768]{1,0:T(8,128)(2,1)}, bf16[128,768]{1,0:T(8,128)(2,1)}, u32[]{:S(2)}, u32[]{:S(2)}) %collective-permute-start.7) | collective-permute-done | bytes 196640 | tf_op jit(solution)/shard_map/ppermute | solution.py:327
  46.5 4.2 %collective-permute-done.8.refs_7_ = bf16[128,768]{1,0:T(8,128)(2,1)} collective-permute-done((bf16[128,768]{1,0:T(8,128)(2,1)}, bf16[128,768]{1,0:T(8,128)(2,1)}, u32[]{:S(2)}, u32[]{:S(2)}) %collective-permute-start.8) | collective-permute-done | bytes 196640 | tf_op jit(solution)/shard_map/ppermute | solution.py:327
  50.7 8.3 %shard_map.85 = (bf16[160,1920]{1,0:T(8,128)(2,1)}, bf16[160,1920]{1,0:T(8,128)(2,1)}) custom-call(s32[16]{0:T(128)} %stack.67.place_ref, bf16[3,640,640]{2,1,0:T(8,128)(2,1)} %bitcast.20, bf16[128,768]{1,0:T(8,128)(2,1)} %get-tuple-element.23.refs_0_, bf16[128,768]{1,0:T(8,128)(2,1)} %copy-done.13, bf16[128,768]{1,0:T(8,128)(2,1)} %copy-done.14, ...), custom_call_target="tpu_custom_call" | custom-call | flops 2516582400 | bytes 5259328 | tf_op jit(solution)/shard_map/pallas_call | solution.py:53
  59.0 2.6 %collective-permute-start.9 = (bf16[160,1920]{1,0:T(8,128)(2,1)}, bf16[160,1920]{1,0:T(8,128)(2,1)S(1)}, u32[]{:S(2)}, u32[]{:S(2)}) collective-permute-start(bf16[160,1920]{1,0:T(8,128)(2,1)} %get-tuple-element.32), channel_id=1, source_target_pairs={{0,8},{1,9},{2,10},{3,11},{4,12},{5,13},{6,14},{7,15},{8,0},{9,1},... | collective-permute-start | bytes 1843208 | tf_op jit(solution)/shard_map/ppermute | solution.py:327
  61.6 14.0 %collective-permute-done.9 = bf16[160,1920]{1,0:T(8,128)(2,1)S(1)} collective-permute-done((bf16[160,1920]{1,0:T(8,128)(2,1)}, bf16[160,1920]{1,0:T(8,128)(2,1)S(1)}, u32[]{:S(2)}, u32[]{:S(2)}) %collective-permute-start.9) | collective-permute-done | bytes 614432 | tf_op jit(solution)/shard_map/ppermute | solution.py:327
  76.9 4.2 %collective-permute-start.10 = (bf16[80,1920]{1,0:T(8,128)(2,1)S(1)}, bf16[80,1920]{1,0:T(8,128)(2,1)}, u32[]{:S(2)}, u32[]{:S(2)}) collective-permute-start(bf16[80,1920]{1,0:T(8,128)(2,1)S(1)} %add_convert_fusion.1), channel_id=1, source_target_pairs={{0,16},{1,17},{2,18},{3,19},{4,20},{5,21},{6,22},{7,23},{8,24},{9,... | collective-permute-start | bytes 921608 | tf_op jit(solution)/shard_map/ppermute | solution.py:327
  81.2 4.4 %shard_map.83 = (bf16[512,1280]{1,0:T(8,128)(2,1)}, bf16[512,640]{1,0:T(8,128)(2,1)}) custom-call(s32[16]{0:T(128)} %stack.67.place_ref, s32[32,128]{1,0:T(8,128)} %bitcast.24, bf16[512,1920]{1,0:T(8,128)(2,1)} %bitcast.19.in_ref), custom_call_target="tpu_custom_call" | custom-call | flops 1006632960 | bytes 3948608 | tf_op jit(solution)/shard_map/pallas_call | solution.py:53
  88.4 6.4 %collective-permute-done.10 = bf16[80,1920]{1,0:T(8,128)(2,1)} collective-permute-done((bf16[80,1920]{1,0:T(8,128)(2,1)S(1)}, bf16[80,1920]{1,0:T(8,128)(2,1)}, u32[]{:S(2)}, u32[]{:S(2)}) %collective-permute-start.10) | collective-permute-done | bytes 307232 | tf_op jit(solution)/shard_map/ppermute | solution.py:327
  96.0 4.2 %collective-permute-start.12 = (bf16[80,1920]{1,0:T(8,128)(2,1)S(1)}, bf16[80,1920]{1,0:T(8,128)(2,1)S(1)}, u32[]{:S(2)}, u32[]{:S(2)}) collective-permute-start(bf16[80,1920]{1,0:T(8,128)(2,1)S(1)} %add_convert_fusion.refs_0_), channel_id=1, source_target_pairs={{0,8},{1,9},{2,10},{3,11},{4,12},{5,13},{6,14},{7,15},{8,0},{9,1},... | collective-permute-start | bytes 921608 | tf_op jit(solution)/shard_map/ppermute | solution.py:327
  100.2 21.6 %collective-permute-done.11.refs_1_ = bf16[80,1920]{1,0:T(8,128)(2,1)S(1)} collective-permute-done((bf16[80,1920]{1,0:T(8,128)(2,1)S(1)}, bf16[80,1920]{1,0:T(8,128)(2,1)S(1)}, u32[]{:S(2)}, u32[]{:S(2)}) %collective-permute-start.11) | collective-permute-done | bytes 307232 | tf_op jit(solution)/shard_map/ppermute | solution.py:327
  122.5 7.7 %collective-permute-done.13.refs_3_ = bf16[80,1920]{1,0:T(8,128)(2,1)} collective-permute-done((bf16[80,1920]{1,0:T(8,128)(2,1)S(1)}, bf16[80,1920]{1,0:T(8,128)(2,1)}, u32[]{:S(2)}, u32[]{:S(2)}) %collective-permute-start.13) | collective-permute-done | bytes 307232 | tf_op jit(solution)/shard_map/ppermute | solution.py:327
  133.2 11.1 %shard_map.84.attended_ref = f32[512,640]{1,0:T(8,128)} custom-call(s32[16]{0:T(128)} %stack.67.place_ref, bf16[512,640]{1,0:T(8,128)(2,1)} %get-tuple-element.21.query_ref, s32[8,512]{1,0:T(8,128)} %reshape.18.ids_ref, bf16[512,1280]{1,0:T(8,128)(2,1)} %get-tuple-element.22.key_ref.value_ref, bf16[512,1280]{1,0:T(8,128)(2,1)} %copy-done, ...), custom_call_target="tpu_custom_call" | custom-call | flops 1509949440 | bytes 9846848 | tf_op jit(solution)/shard_map/pallas_call | solution.py:53
  144.4 7.7 %shard_map.86 = (bf16[128,640]{1,0:T(8,128)(2,1)}, bf16[128,640]{1,0:T(8,128)(2,1)}, bf16[128,640]{1,0:T(8,128)(2,1)}, bf16[128,640]{1,0:T(8,128)(2,1)}) custom-call(s32[16]{0:T(128)} %stack.67.place_ref, bf16[3,640,640]{2,1,0:T(8,128)(2,1)} %bitcast.21, bf16[512,640]{1,0:T(8,128)(2,1)} %get-tuple-element.21.query_ref, f32[512,640]{1,0:T(8,128)} %shard_map.84.attended_ref, ...), custom_call_target="tpu_custom_call" | custom-call | flops 1258291200 | bytes 7536704 | tf_op jit(solution)/shard_map/pallas_call | solution.py:53
  157.6 2.3 %collective-permute-done.19.refs_1_ = bf16[128,640]{1,0:T(8,128)(2,1)S(1)} collective-permute-done((bf16[128,640]{1,0:T(8,128)(2,1)}, bf16[128,640]{1,0:T(8,128)(2,1)S(1)}, u32[]{:S(2)}, u32[]{:S(2)}) %collective-permute-start.19) | collective-permute-done | bytes 163872 | tf_op jit(solution)/shard_map/ppermute | solution.py:327
  159.9 3.0 %collective-permute-done.20.refs_2_ = bf16[128,640]{1,0:T(8,128)(2,1)S(1)} collective-permute-done((bf16[128,640]{1,0:T(8,128)(2,1)}, bf16[128,640]{1,0:T(8,128)(2,1)S(1)}, u32[]{:S(2)}, u32[]{:S(2)}) %collective-permute-start.20) | collective-permute-done | bytes 163872 | tf_op jit(solution)/shard_map/ppermute | solution.py:327
  165.2 2.4 %shard_map.87 = bf16[128,2560]{1,0:T(8,128)(2,1)} custom-call(s32[16]{0:T(128)} %stack.67.place_ref, bf16[128,640]{1,0:T(8,128)(2,1)} %copy-done.7, bf16[128,640]{1,0:T(8,128)(2,1)} %copy-done.8, bf16[128,640]{1,0:T(8,128)(2,1)} %copy-done.9, bf16[128,640]{1,0:T(8,128)(2,1)} %copy-done.10, f32[1,2560]{1,0:T(1,128)} %reshape.19.refs_4_), custom_call_target="tpu_custom_call" | custom-call | flops 1966080 | bytes 1321024 | tf_op jit(solution)/shard_map/pallas_call | solution.py:53
  (73 shorter events, 22.5 us)
Async XLA Ops:
  3.9 77.3 %all-to-all-start = ((bf16[32,16,1920]{2,1,0:T(8,128)(2,1)}), bf16[32,16,1920]{2,1,0:T(8,128)(2,1)}, u32[]{:S(2)}, u32[]{:S(2)}) async-start(bf16[32,16,1920]{2,1,0:T(8,128)(2,1)} %bitcast.22), calls=%async_computation | async-start | bytes 3932160 | tf_op jit(solution)/shard_map/all_to_all | solution.py:384
  16.1 3.7 %collective-permute-start.2 = (bf16[128,768]{1,0:T(8,128)(2,1)}, bf16[128,768]{1,0:T(8,128)(2,1)S(1)}, u32[]{:S(2)}, u32[]{:S(2)}) collective-permute-start(bf16[128,768]{1,0:T(8,128)(2,1)} %get-tuple-element.24), channel_id=1, source_target_pairs={{0,1},{1,0},{2,3},{3,2},{4,5},{5,4},{6,7},{7,6},{8,9},{9,8},{10,11... | collective-permute-start | bytes 589832 | tf_op jit(solution)/shard_map/ppermute | solution.py:327
  16.3 15.2 %collective-permute-start.3 = (bf16[128,768]{1,0:T(8,128)(2,1)}, bf16[128,768]{1,0:T(8,128)(2,1)S(1)}, u32[]{:S(2)}, u32[]{:S(2)}) collective-permute-start(bf16[128,768]{1,0:T(8,128)(2,1)} %get-tuple-element.25), channel_id=1, source_target_pairs={{0,2},{1,3},{2,0},{3,1},{4,6},{5,7},{6,4},{7,5},{8,10},{9,11},{10,... | collective-permute-start | bytes 589832 | tf_op jit(solution)/shard_map/ppermute | solution.py:327
  17.9 22.6 %collective-permute-start.4 = (bf16[128,768]{1,0:T(8,128)(2,1)}, bf16[128,768]{1,0:T(8,128)(2,1)S(1)}, u32[]{:S(2)}, u32[]{:S(2)}) collective-permute-start(bf16[128,768]{1,0:T(8,128)(2,1)} %get-tuple-element.26), channel_id=1, source_target_pairs={{0,3},{1,2},{2,1},{3,0},{4,7},{5,6},{6,5},{7,4},{8,11},{9,10},{10,... | collective-permute-start | bytes 589832 | tf_op jit(solution)/shard_map/ppermute | solution.py:327
  17.9 22.5 %collective-permute-start.5 = (bf16[128,768]{1,0:T(8,128)(2,1)}, bf16[128,768]{1,0:T(8,128)(2,1)S(1)}, u32[]{:S(2)}, u32[]{:S(2)}) collective-permute-start(bf16[128,768]{1,0:T(8,128)(2,1)} %get-tuple-element.27), channel_id=1, source_target_pairs={{0,4},{1,5},{2,6},{3,7},{4,0},{5,1},{6,2},{7,3},{8,12},{9,13},{10,... | collective-permute-start | bytes 589832 | tf_op jit(solution)/shard_map/ppermute | solution.py:327
  19.6 20.8 %collective-permute-start.6 = (bf16[128,768]{1,0:T(8,128)(2,1)}, bf16[128,768]{1,0:T(8,128)(2,1)S(1)}, u32[]{:S(2)}, u32[]{:S(2)}) collective-permute-start(bf16[128,768]{1,0:T(8,128)(2,1)} %get-tuple-element.28), channel_id=1, source_target_pairs={{0,5},{1,4},{2,7},{3,6},{4,1},{5,0},{6,3},{7,2},{8,13},{9,12},{10,... | collective-permute-start | bytes 589832 | tf_op jit(solution)/shard_map/ppermute | solution.py:327
  19.8 26.8 %collective-permute-start.7 = (bf16[128,768]{1,0:T(8,128)(2,1)}, bf16[128,768]{1,0:T(8,128)(2,1)}, u32[]{:S(2)}, u32[]{:S(2)}) collective-permute-start(bf16[128,768]{1,0:T(8,128)(2,1)} %get-tuple-element.29), channel_id=1, source_target_pairs={{0,6},{1,7},{2,4},{3,5},{4,2},{5,3},{6,0},{7,1},{8,14},{9,15},{10,... | collective-permute-start | bytes 589832 | tf_op jit(solution)/shard_map/ppermute | solution.py:327
  31.5 19.2 %collective-permute-start.8 = (bf16[128,768]{1,0:T(8,128)(2,1)}, bf16[128,768]{1,0:T(8,128)(2,1)}, u32[]{:S(2)}, u32[]{:S(2)}) collective-permute-start(bf16[128,768]{1,0:T(8,128)(2,1)} %get-tuple-element.30), channel_id=1, source_target_pairs={{0,7},{1,6},{2,5},{3,4},{4,3},{5,2},{6,1},{7,0},{8,15},{9,14},{10,... | collective-permute-start | bytes 589832 | tf_op jit(solution)/shard_map/ppermute | solution.py:327
  59.0 16.7 %collective-permute-start.9 = (bf16[160,1920]{1,0:T(8,128)(2,1)}, bf16[160,1920]{1,0:T(8,128)(2,1)S(1)}, u32[]{:S(2)}, u32[]{:S(2)}) collective-permute-start(bf16[160,1920]{1,0:T(8,128)(2,1)} %get-tuple-element.32), channel_id=1, source_target_pairs={{0,8},{1,9},{2,10},{3,11},{4,12},{5,13},{6,14},{7,15},{8,0},{9,1},... | collective-permute-start | bytes 1843208 | tf_op jit(solution)/shard_map/ppermute | solution.py:327
  76.9 17.8 %collective-permute-start.10 = (bf16[80,1920]{1,0:T(8,128)(2,1)S(1)}, bf16[80,1920]{1,0:T(8,128)(2,1)}, u32[]{:S(2)}, u32[]{:S(2)}) collective-permute-start(bf16[80,1920]{1,0:T(8,128)(2,1)S(1)} %add_convert_fusion.1), channel_id=1, source_target_pairs={{0,16},{1,17},{2,18},{3,19},{4,20},{5,21},{6,22},{7,23},{8,24},{9,... | collective-permute-start | bytes 921608 | tf_op jit(solution)/shard_map/ppermute | solution.py:327
  85.5 44.8 %collective-permute-start = (bf16[512,1280]{1,0:T(8,128)(2,1)}, bf16[512,1280]{1,0:T(8,128)(2,1)S(1)}, u32[]{:S(2)}, u32[]{:S(2)}) collective-permute-start(bf16[512,1280]{1,0:T(8,128)(2,1)} %get-tuple-element.22.key_ref.value_ref), channel_id=1, source_target_pairs={{0,1},{1,8},{2,3},{3,10},{4,5},{5,12},{6,7},{7,14},{8,9},{9,16},{1... | collective-permute-start | bytes 3932168 | tf_op jit(solution)/shard_map/ppermute | solution.py:327
  86.9 45.2 %collective-permute-start.1 = (bf16[512,1280]{1,0:T(8,128)(2,1)}, bf16[512,1280]{1,0:T(8,128)(2,1)S(1)}, u32[]{:S(2)}, u32[]{:S(2)}) collective-permute-start(bf16[512,1280]{1,0:T(8,128)(2,1)} %get-tuple-element.22.key_ref.value_ref), channel_id=1, source_target_pairs={{1,0},{3,2},{5,4},{7,6},{8,1},{9,8},{10,3},{11,10},{12,5},{13,12},... | collective-permute-start | bytes 3932168 | tf_op jit(solution)/shard_map/ppermute | solution.py:327
  95.9 48.4 %copy-start.2 = (bf16[80,1920]{1,0:T(8,128)(2,1)}, bf16[80,1920]{1,0:T(8,128)(2,1)S(1)}, u32[]{:S(2)}) copy-start(bf16[80,1920]{1,0:T(8,128)(2,1)S(1)} %add_convert_fusion.refs_0_) | copy-start | bytes 921604
  95.9 25.9 %collective-permute-start.11 = (bf16[80,1920]{1,0:T(8,128)(2,1)S(1)}, bf16[80,1920]{1,0:T(8,128)(2,1)S(1)}, u32[]{:S(2)}, u32[]{:S(2)}) collective-permute-start(bf16[80,1920]{1,0:T(8,128)(2,1)S(1)} %add_convert_fusion.refs_0_), channel_id=1, source_target_pairs={{0,16},{1,17},{2,18},{3,19},{4,20},{5,21},{6,22},{7,23},{8,24},{9,... | collective-permute-start | bytes 921608 | tf_op jit(solution)/shard_map/ppermute | solution.py:327
  96.0 26.4 %collective-permute-start.12 = (bf16[80,1920]{1,0:T(8,128)(2,1)S(1)}, bf16[80,1920]{1,0:T(8,128)(2,1)S(1)}, u32[]{:S(2)}, u32[]{:S(2)}) collective-permute-start(bf16[80,1920]{1,0:T(8,128)(2,1)S(1)} %add_convert_fusion.refs_0_), channel_id=1, source_target_pairs={{0,8},{1,9},{2,10},{3,11},{4,12},{5,13},{6,14},{7,15},{8,0},{9,1},... | collective-permute-start | bytes 921608 | tf_op jit(solution)/shard_map/ppermute | solution.py:327
  121.8 8.4 %collective-permute-start.13 = (bf16[80,1920]{1,0:T(8,128)(2,1)S(1)}, bf16[80,1920]{1,0:T(8,128)(2,1)}, u32[]{:S(2)}, u32[]{:S(2)}) collective-permute-start(bf16[80,1920]{1,0:T(8,128)(2,1)S(1)} %collective-permute-done.11.refs_1_), channel_id=1, source_target_pairs={{0,8},{1,9},{2,10},{3,11},{4,12},{5,13},{6,14},{7,15},{8,0},{9,1},... | collective-permute-start | bytes 921608 | tf_op jit(solution)/shard_map/ppermute | solution.py:327
  121.9 22.5 %collective-permute-start.14 = (bf16[80,1920]{1,0:T(8,128)(2,1)S(1)}, bf16[80,1920]{1,0:T(8,128)(2,1)}, u32[]{:S(2)}, u32[]{:S(2)}) collective-permute-start(bf16[80,1920]{1,0:T(8,128)(2,1)S(1)} %add_convert_fusion.refs_0_), channel_id=1, source_target_pairs={{0,1},{1,0},{2,3},{3,2},{4,5},{5,4},{6,7},{7,6},{8,9},{9,8},{10,11... | collective-permute-start | bytes 921608 | tf_op jit(solution)/shard_map/ppermute | solution.py:327
  122.5 21.9 %collective-permute-start.15 = (bf16[80,1920]{1,0:T(8,128)(2,1)S(1)}, bf16[80,1920]{1,0:T(8,128)(2,1)}, u32[]{:S(2)}, u32[]{:S(2)}) collective-permute-start(bf16[80,1920]{1,0:T(8,128)(2,1)S(1)} %collective-permute-done.11.refs_1_), channel_id=1, source_target_pairs={{0,1},{1,0},{2,3},{3,2},{4,5},{5,4},{6,7},{7,6},{8,9},{9,8},{10,11... | collective-permute-start | bytes 921608 | tf_op jit(solution)/shard_map/ppermute | solution.py:327
  130.3 14.1 %collective-permute-start.16 = (bf16[80,1920]{1,0:T(8,128)(2,1)S(1)}, bf16[80,1920]{1,0:T(8,128)(2,1)}, u32[]{:S(2)}, u32[]{:S(2)}) collective-permute-start(bf16[80,1920]{1,0:T(8,128)(2,1)S(1)} %collective-permute-done.12.refs_2_), channel_id=1, source_target_pairs={{0,1},{1,0},{2,3},{3,2},{4,5},{5,4},{6,7},{7,6},{8,9},{9,8},{10,11... | collective-permute-start | bytes 921608 | tf_op jit(solution)/shard_map/ppermute | solution.py:327
  130.3 14.1 %collective-permute-start.17 = (bf16[80,1920]{1,0:T(8,128)(2,1)}, bf16[80,1920]{1,0:T(8,128)(2,1)}, u32[]{:S(2)}, u32[]{:S(2)}) collective-permute-start(bf16[80,1920]{1,0:T(8,128)(2,1)} %collective-permute-done.13.refs_3_), channel_id=1, source_target_pairs={{0,1},{1,0},{2,3},{3,2},{4,5},{5,4},{6,7},{7,6},{8,9},{9,8},{10,11... | collective-permute-start | bytes 921608 | tf_op jit(solution)/shard_map/ppermute | solution.py:327
  152.1 5.5 %collective-permute-start.18 = (bf16[128,640]{1,0:T(8,128)(2,1)}, bf16[128,640]{1,0:T(8,128)(2,1)S(1)}, u32[]{:S(2)}, u32[]{:S(2)}) collective-permute-start(bf16[128,640]{1,0:T(8,128)(2,1)} %get-tuple-element.33), channel_id=1, source_target_pairs={{0,0},{1,4},{2,2},{3,6},{4,1},{5,5},{6,3},{7,7},{8,8},{9,12},{10,1... | collective-permute-start | bytes 491528 | tf_op jit(solution)/shard_map/ppermute | solution.py:327
  153.6 6.3 %collective-permute-start.19 = (bf16[128,640]{1,0:T(8,128)(2,1)}, bf16[128,640]{1,0:T(8,128)(2,1)S(1)}, u32[]{:S(2)}, u32[]{:S(2)}) collective-permute-start(bf16[128,640]{1,0:T(8,128)(2,1)} %get-tuple-element.34), channel_id=1, source_target_pairs={{0,2},{1,6},{2,0},{3,4},{4,3},{5,7},{6,1},{7,5},{8,10},{9,14},{10,... | collective-permute-start | bytes 491528 | tf_op jit(solution)/shard_map/ppermute | solution.py:327
  154.9 8.1 %collective-permute-start.20 = (bf16[128,640]{1,0:T(8,128)(2,1)}, bf16[128,640]{1,0:T(8,128)(2,1)S(1)}, u32[]{:S(2)}, u32[]{:S(2)}) collective-permute-start(bf16[128,640]{1,0:T(8,128)(2,1)} %get-tuple-element.35), channel_id=1, source_target_pairs={{0,1},{1,5},{2,3},{3,7},{4,0},{5,4},{6,2},{7,6},{8,9},{9,13},{10,1... | collective-permute-start | bytes 491528 | tf_op jit(solution)/shard_map/ppermute | solution.py:327
  156.6 7.9 %collective-permute-start.21 = (bf16[128,640]{1,0:T(8,128)(2,1)}, bf16[128,640]{1,0:T(8,128)(2,1)S(1)}, u32[]{:S(2)}, u32[]{:S(2)}) collective-permute-start(bf16[128,640]{1,0:T(8,128)(2,1)} %get-tuple-element.36), channel_id=1, source_target_pairs={{0,3},{1,7},{2,1},{3,5},{4,2},{5,6},{6,0},{7,4},{8,11},{9,15},{10,... | collective-permute-start | bytes 491528 | tf_op jit(solution)/shard_map/ppermute | solution.py:327
  (17 other events, 161.4 us)

commit v4 on v3

--- a/solution.py
+++ b/solution.py
@@ -70,7 +70,6 @@
 def heads_kernel(place_ref, rate_ref, key_ref, value_ref, *out_refs):
     n, width = key_ref.shape
     step, part, core = pl.program_id(0), place_ref[1], place_ref[2]
-    rates = rate_ref[...]
     lane = iota((n, SPAN), 1)
     for local in range(width // PART_WIDTH):
         index = step * (width // PART_WIDTH) + local
@@ -85,8 +84,7 @@
                 rows = pltpu.roll(rows, SPAN - offset, 1) if offset else rows
                 return jnp.where(lane < HEAD_DIM, rows, 0.0)
 
-            own = own_part * PART_FAST + head
-            rate = jnp.sum(jnp.where(iota(rates.shape, 1) == own, rates, 0.0), axis=1, keepdims=True)
+            rate = column_of(rate_ref[pl.ds(own_part * PART_FAST + head, 1), :])
             keys = window(key_ref)
             for third in range(3):
                 piece = rate.astype(BF16).astype(F32)
@@ -149,21 +147,29 @@
     return jnp.where(iota((n, n), 0) == pos.astype(jnp.int32), 1.0, 0.0).astype(BF16)
 
 
-def place_kernel(group_shift, slots, place_ref, order_ref, in_ref, kv_ref, q_ref):
-    choose = arrival_choice(group_shift, slots, order_ref[...], place_ref[3], in_ref.shape[0])
+def choose_kernel(group_shift, slots, place_ref, order_ref, choose_ref):
+    choose_ref[...] = arrival_choice(group_shift, slots, order_ref[...], place_ref[3], choose_ref.shape[0])
+
+
+def place_kernel(choose_ref, in_ref, kv_ref, q_ref):
+    choose = choose_ref[...]
     kv_ref[...] = dot(choose, in_ref[:, : 2 * PART_WIDTH]).astype(BF16)
     q_ref[...] = dot(choose, in_ref[:, 2 * PART_WIDTH :]).astype(BF16)
 
 
-def grads_kernel(chunk, place_ref, weight_ref, *refs):
-    kv_refs, (send_ref, keep_ref, weight_buf, key_buf, target_buf, dg_buf, du_buf, pr_buf, sums) = refs[:-9], refs[-9:]
+def grads_kernel(chunk, last, place_ref, weight_ref, *refs):
+    outs = 2 if last else 1
+    weight_buf, key_buf, target_buf, delta_buf, pr_buf, sums = refs[-6:]
+    out_refs, in_refs = refs[-6 - outs : -6], refs[: -6 - outs]
+    kv_refs, early_ref = (in_refs[:-1], in_refs[-1]) if last else (in_refs, None)
     block = kv_refs[0].shape[0]
     n = key_buf.shape[0]
     hidden = weight_ref.shape[2]
     first = pl.multiple_of(place_ref[2] * HEAD_DIM, 16)
     for index in range(3):
-        weight_buf[index, :HEAD_DIM, :] = weight_ref[index, pl.ds(first, HEAD_DIM), :]
-        weight_buf[index, HEAD_DIM:, :] = jnp.zeros((SPAN - HEAD_DIM, hidden), BF16)
+        lanes = slice(index * hidden, (index + 1) * hidden)
+        weight_buf[:HEAD_DIM, lanes] = weight_ref[index, pl.ds(first, HEAD_DIM), :]
+    weight_buf[HEAD_DIM:, :] = jnp.zeros((SPAN - HEAD_DIM, 3 * hidden), BF16)
     lane = iota((1, SPAN), 1)
     wanted = (lane >= HEAD_DIM) & (lane < HEAD_DIM + 3)
     for index, ref in enumerate(kv_refs):
@@ -174,62 +180,96 @@
         target_buf[here, :] = (ref[:, SPAN:].astype(F32) * rate).astype(BF16)
     for at in range(0, n, chunk):
         here = pl.ds(at, chunk)
-        gate = dot(key_buf[here, :], weight_buf[0])
-        upward = dot(key_buf[here, :], weight_buf[1])
-        backward = dot(target_buf[here, :], weight_buf[2])
+        both = dot(key_buf[here, :], weight_buf[:, : 2 * hidden])
+        gate, upward = both[:, :hidden], both[:, hidden:]
+        backward = dot(target_buf[here, :], weight_buf[:, 2 * hidden :])
         sigmoid = jax.nn.sigmoid(gate)
         active = gate * sigmoid
         pr_buf[here, :] = (active * upward).astype(BF16)
-        du_buf[here, :] = (backward * active).astype(BF16)
-        dg_buf[here, :] = (backward * upward * sigmoid * (1.0 + gate * (1.0 - sigmoid))).astype(BF16)
-    for index, (left, right) in enumerate(((key_buf, dg_buf), (key_buf, du_buf), (target_buf, pr_buf))):
-        total = dot(left[...], right[...], ((0,), (0,)))
-        sums[:, index * hidden : (index + 1) * hidden] = total[:HEAD_DIM].astype(BF16)
-    half = send_ref.shape[0]
-    side = place_ref[3] // PART_FAST & 1
-    send_ref[...] = sums[pl.ds(pl.multiple_of((1 - side) * half, 16), half), :]
-    keep_ref[...] = sums[pl.ds(pl.multiple_of(side * half, 16), half), :]
-
-
-def attention_kernel(block, place_ref, query_ref, ids_ref, key_ref, key_low_ref, key_high_ref, value_ref, value_low_ref, value_high_ref, out_ref, bias):
+        delta_buf[here, hidden:] = (backward * active).astype(BF16)
+        delta_buf[here, :hidden] = (backward * upward * sigmoid * (1.0 + gate * (1.0 - sigmoid))).astype(BF16)
+    for left, right, begin in ((key_buf, delta_buf, 0), (target_buf, pr_buf, 2 * hidden)):
+        lanes = slice(begin, begin + right.shape[1])
+        total = dot(left[...], right[...], ((0,), (0,)))[:HEAD_DIM]
+        if last:
+            sums[:, lanes] = (total + early_ref[:, lanes].astype(F32)).astype(BF16)
+        else:
+            out_refs[0][:, lanes] = total.astype(BF16)
+    if last:
+        half = out_refs[0].shape[0]
+        side = place_ref[3] // PART_FAST & 1
+        out_refs[0][...] = sums[pl.ds(pl.multiple_of((1 - side) * half, 16), half), :]
+        out_refs[1][...] = sums[pl.ds(pl.multiple_of(side * half, 16), half), :]
+
+
+FACTOR = ATT_DIM ** (-0.5) * math.log2(math.e)
+
+
+def near_kernel(block, place_ref, query_ref, ids_ref, key_ref, value_ref, out_ref, stat_ref, bias):
+    n = query_ref.shape[0]
+    head = pl.program_id(0)
+
+    @pl.when(head == 0)
+    def _():
+        ids = ids_ref[pl.ds(place_ref[3], 1), :]
+        for at in range(0, n, block):
+            own = column_of(ids[:, at : at + block]).astype(jnp.int32)
+            gap = iota((block, n), 1) - iota((block, n), 0) - at
+            allowed = (gap < WINDOW // 2) & (gap > -(WINDOW // 2)) & (own == ids)
+            bias[at : at + block, :] = jnp.where(allowed, 0.0, -1e30)
+        stat_ref[...] = jnp.zeros_like(stat_ref)
+
+    lane = iota((block, LANES), 1)
+    for at in range(0, n, block):
+        here = slice(at, at + block)
+        score = dot(query_ref[here, :], key_ref[...], ((1,), (1,))) + bias[here, :]
+        peak = jnp.max(score, axis=1, keepdims=True)
+        weight = jnp.exp2((score - peak) * FACTOR)
+        total = jnp.sum(weight, axis=1, keepdims=True)
+        out_ref[here, :] = dot(weight.astype(BF16), value_ref[...])
+        stat = jnp.where(lane == 2 * head, peak, stat_ref[here, :])
+        stat_ref[here, :] = jnp.where(lane == 2 * head + 1, total, stat)
+
+
+def far_kernel(block, place_ref, query_ref, ids_ref, near_ref, stat_ref, key_low_ref, key_high_ref, value_low_ref, value_high_ref, out_ref, bias):
     n = query_ref.shape[0]
     half = WINDOW // 2
+    head = pl.program_id(0)
     group = place_ref[3]
     last = ids_ref.shape[0] - 1
 
-    @pl.when(pl.program_id(0) == 0)
+    @pl.when(head == 0)
     def _():
         mid = ids_ref[pl.ds(group, 1), :]
-        low = ids_ref[pl.ds(jnp.maximum(group - 1, 0), 1), :]
-        high = ids_ref[pl.ds(jnp.minimum(group + 1, last), 1), :]
-        low = jnp.where(group > 0, low, -1)
-        high = jnp.where(group < last, high, -1)
+        low = jnp.where(group > 0, ids_ref[pl.ds(jnp.maximum(group - 1, 0), 1), :], -1)
+        high = jnp.where(group < last, ids_ref[pl.ds(jnp.minimum(group + 1, last), 1), :], -1)
         for at in range(0, n, block):
             own = column_of(mid[:, at : at + block]).astype(jnp.int32)
-            ids = jnp.concatenate([low[:, at:], mid, high[:, : at + block]], axis=1)
-            span = ids.shape[1]
-            gap = iota((block, span), 1) - iota((block, span), 0) - half
-            allowed = (gap < half) & (gap > -half) & (own == ids)
-            bias[at // block, :, :] = jnp.where(allowed, 0.0, -1e30)
-
-    factor = ATT_DIM ** (-0.5) * math.log2(math.e)
+            for ids, begin, end, shift in ((low, at, n, -n), (high, 0, at + block, n)):
+                size = end - begin
+                gap = iota((block, size), 1) + (begin + shift - at) - iota((block, size), 0)
+                allowed = (gap < half) & (gap > -half) & (own == ids[:, begin:end])
+                lanes = slice(begin - at, end - at) if shift < 0 else slice(n - at, n - at + size)
+                bias[at : at + block, lanes] = jnp.where(allowed, 0.0, -1e30)
+
+    lane = iota((block, LANES), 1)
     for at in range(0, n, block):
-        part = query_ref[at : at + block, :]
-        stops = (0, half - at, half - at + n, half + n + block - half)
-        keys = (key_low_ref[at:, :], key_ref[...], key_high_ref[: at + block, :])
-        values = (value_low_ref[at:, :], value_ref[...], value_high_ref[: at + block, :])
-        scores = []
-        for index in range(3):
-            lanes = slice(stops[index], stops[index] + keys[index].shape[0])
-            scores.append(dot(part, keys[index], ((1,), (1,))) + bias[at // block, :, lanes])
-        peak = functools.reduce(jnp.maximum, [jnp.max(s, axis=1, keepdims=True) for s in scores])
-        total = jnp.zeros_like(peak)
-        mixed = jnp.zeros((block, ATT_DIM), F32)
-        for score, value in zip(scores, values):
-            weight = jnp.exp2((score - peak) * factor)
-            total += jnp.sum(weight, axis=1, keepdims=True)
-            mixed += dot(weight.astype(BF16), value)
-        out_ref[pl.ds(at, block), :] = mixed / total
+        here = slice(at, at + block)
+        query = query_ref[here, :]
+        low = dot(query, key_low_ref[at:, :], ((1,), (1,))) + bias[here, : n - at]
+        high = dot(query, key_high_ref[: at + block, :], ((1,), (1,))) + bias[here, n - at :]
+        stat = stat_ref[here, :]
+        old_peak = jnp.sum(jnp.where(lane == 2 * head, stat, 0.0), axis=1, keepdims=True)
+        old_total = jnp.sum(jnp.where(lane == 2 * head + 1, stat, 0.0), axis=1, keepdims=True)
+        peak = jnp.maximum(jnp.max(low, axis=1, keepdims=True), jnp.max(high, axis=1, keepdims=True))
+        peak = jnp.maximum(peak, old_peak)
+        keep = jnp.exp2((old_peak - peak) * FACTOR)
+        low = jnp.exp2((low - peak) * FACTOR)
+        high = jnp.exp2((high - peak) * FACTOR)
+        total = old_total * keep + jnp.sum(low, axis=1, keepdims=True) + jnp.sum(high, axis=1, keepdims=True)
+        mixed = near_ref[here, :] * keep + dot(low.astype(BF16), value_low_ref[at:, :])
+        mixed += dot(high.astype(BF16), value_high_ref[: at + block, :])
+        out_ref[here, :] = mixed / total
 
 
 def apply_kernel(place_ref, weight_ref, query_ref, attended_ref, *refs):
@@ -358,13 +398,13 @@
         grid_spec=pltpu.PrefetchScalarGridSpec(
             num_scalar_prefetch=1,
             grid=(steps,),
-            in_specs=[whole(learn_rates.shape), other_cut, other_cut],
+            in_specs=[whole(learn_rates.shape[::-1]), other_cut, other_cut],
             out_specs=[whole((tok_dev, 2 * SPAN))] * plane_size,
         ),
         compiler_params=pltpu.CompilerParams(vmem_limit_bytes=60 << 20),
         cost_estimate=pl.CostEstimate(flops=tok_dev * WIDTH, bytes_accessed=8 * tok_dev * WIDTH, transcendentals=0),
         name="heads",
-    )(place, learn_rates, key_rows, value_rows)
+    )(place, learn_rates.T, key_rows, value_rows)
     heads_in = [heads_out[0]]
     for j in range(1, plane_size):
         heads_in.append(permute(heads_out[j], lambda z, y, x, c, j=j: (z, y ^ j >> 2, x ^ j >> 1 & 1, c ^ j & 1)))
@@ -385,10 +425,15 @@
         packed.reshape(sections, slots, 3 * PART_WIDTH), "tok", split_axis=0, concat_axis=0, tiled=True
     ).reshape(group_rows, 3 * PART_WIDTH)
 
+    (choose,) = call(
+        functools.partial(choose_kernel, group_shift, slots),
+        [jax.ShapeDtypeStruct((group_rows, group_rows), BF16)],
+        [place, orders], smem=1, flops=2 * group_rows * group_rows,
+    )
     kv_seq, query_seq = call(
-        functools.partial(place_kernel, group_shift, slots),
+        place_kernel,
         [jax.ShapeDtypeStruct((group_rows, width), BF16) for width in (2 * PART_WIDTH, PART_WIDTH)],
-        [place, orders, arrived], smem=1, flops=2 * group_rows * group_rows * 3 * PART_WIDTH,
+        [choose, arrived], flops=2 * group_rows * group_rows * 3 * PART_WIDTH,
     )
 
     def neighbour(step):
@@ -401,13 +446,21 @@
     kv_low = permute(kv_seq, neighbour(1))
     kv_high = permute(kv_seq, neighbour(-1))
 
-    tokens = plane_size * tok_dev
+    near = plane_size // 2
+    tokens = near * tok_dev
+    grad_scratch = [VMEM((SPAN, 3 * hidden), BF16)] + [VMEM((tokens, SPAN), BF16)] * 2
+    grad_scratch += [VMEM((tokens, 2 * hidden), BF16), VMEM((tokens, hidden), BF16), VMEM((HEAD_DIM, 3 * hidden), BF16)]
+    grad_flops = 12 * tokens * HEAD_DIM * hidden
+    (early,) = call(
+        functools.partial(grads_kernel, tokens, False),
+        [jax.ShapeDtypeStruct((HEAD_DIM, 3 * hidden), BF16)], [place, weights] + heads_in[:near],
+        scratch=grad_scratch, smem=1, flops=grad_flops,
+    )
     send, keep = call(
-        functools.partial(grads_kernel, tokens // 2),
-        [jax.ShapeDtypeStruct((HEAD_DIM // 2, 3 * hidden), BF16)] * 2, [place, weights] + heads_in,
-        scratch=[VMEM((3, SPAN, hidden), BF16)] + [VMEM((tokens, SPAN), BF16)] * 2
-        + [VMEM((tokens, hidden), BF16)] * 3 + [VMEM((HEAD_DIM, 3 * hidden), BF16)],
-        smem=1, flops=12 * tokens * HEAD_DIM * hidden,
+        functools.partial(grads_kernel, tokens, True),
+        [jax.ShapeDtypeStruct((HEAD_DIM // 2, 3 * hidden), BF16)] * 2,
+        [place, weights] + heads_in[near:] + [early],
+        scratch=grad_scratch, smem=1, flops=grad_flops,
     )
 
     def across(bit):
@@ -440,16 +493,27 @@
     block = min(LANES, group_rows)
     lane_block = lambda rows, shift: pl.BlockSpec((rows, ATT_DIM), lambda h: (0, h + shift))
     ids = window_ids.reshape(groups, group_rows)
+    wide = jax.ShapeDtypeStruct((group_rows, PART_WIDTH), F32)
+    stat_shape = jax.ShapeDtypeStruct((group_rows, LANES), F32)
+    assert block + group_rows == WINDOW // 2 + block and 2 * PART_ATT <= LANES
+    near_mixed, stats = call(
+        functools.partial(near_kernel, block),
+        [wide, stat_shape],
+        [place, query_seq, ids, kv_seq, kv_seq],
+        in_specs=[lane_block(group_rows, 0), full(ids), lane_block(group_rows, 0), lane_block(group_rows, PART_ATT)],
+        out_specs=[lane_block(group_rows, 0), full(stat_shape)],
+        grid=(PART_ATT,), scratch=[VMEM((group_rows, group_rows), F32)],
+        smem=1, flops=4 * group_rows * group_rows * PART_WIDTH,
+    )
     (attended,) = call(
-        functools.partial(attention_kernel, block),
-        [jax.ShapeDtypeStruct((group_rows, PART_WIDTH), F32)],
-        [place, query_seq, ids, kv_seq, kv_low, kv_high, kv_seq, kv_low, kv_high],
-        in_specs=[lane_block(group_rows, 0), full(ids)]
-        + [lane_block(group_rows, 0)] * 3 + [lane_block(group_rows, PART_ATT)] * 3,
+        functools.partial(far_kernel, block),
+        [wide],
+        [place, query_seq, ids, near_mixed, stats, kv_low, kv_high, kv_low, kv_high],
+        in_specs=[lane_block(group_rows, 0), full(ids), lane_block(group_rows, 0), full(stats)]
+        + [lane_block(group_rows, 0)] * 2 + [lane_block(group_rows, PART_ATT)] * 2,
         out_specs=[lane_block(group_rows, 0)],
-        grid=(PART_ATT,),
-        scratch=[VMEM((group_rows // block, block, WINDOW + block), F32)],
-        smem=1, flops=4 * group_rows * (WINDOW + block) * PART_WIDTH,
+        grid=(PART_ATT,), scratch=[VMEM((group_rows, group_rows + block), F32)],
+        smem=1, flops=4 * group_rows * (group_rows + block) * PART_WIDTH,
     )
 
     blocks = call(

time: 168 us -> 173 us (1.030)
  Pallas kernels: 41 us -> 52.9 us
  waiting for transfers between devices: 76.8 us -> 67.9 us
    pallas_call x6 -> x9, Pallas kernels: 37 us -> 48.8 us  [call(): pl.pallas_call(kernel, out_shape=list(outs), in_specs=specs, out_specs=ou...]
    ppermute x22, waiting for transfers between devices: 76.8 us -> 67.9 us  [permute(): return lax.ppermute(array, 'tok', route)]
    unnamed x38 -> x35, local copies, waits for them, and re-layouts: 5.8 us -> 5.7 us
  transfers between devices with their start and end apart: 23 -> 23, of which waited for: 11 -> 10; matrix products, arithmetic and copies ran while one was open for 6% -> 6% of each run, Pallas kernels for 17% -> 23%
where the time goes in v4:
time: 173 us; the launch traced here: 172 us
  waiting for transfers between devices  67.9 us (39%)
  Pallas kernels  52.9 us (31%)
  starting transfers between devices  38.3 us (22%)
  local copies, waits for them, and re-layouts  10.2 us (6%)
  other arithmetic  2.42 us (1%)
    ppermute x22, waiting for transfers between devices, permute(): return lax.ppermute(array, 'tok', route)  67.9 us
    pallas_call x9, Pallas kernels, call(): pl.pallas_call(kernel, out_shape=list(outs), in_specs=specs, out_specs=ou...  48.8 us
    ppermute x22, starting transfers between devices, permute(): return lax.ppermute(array, 'tok', route)  30.9 us
    all_to_all x1, starting transfers between devices, shards(): lax.all_to_all(packed.reshape(sections, slots, 3 * PART_WIDTH), 'tok', sp...  7.44 us
    unnamed x35, local copies, waits for them, and re-layouts  5.7 us
    pallas_call x1, Pallas kernels, shards(): pl.pallas_call(heads_kernel, out_shape=[jax.ShapeDtypeStruct((tok_dev, 2...  4.14 us
  transfers between devices with their start and end apart: 23, of which 10 were waited for; matrix products, arithmetic and copies ran while one was open for 6% of the time, Pallas kernels for 23%

profile of v4, /device:TPU:0, one launch (start us, length us, event | category | flops | bytes accessed | tf_op | source)
XLA Modules:
  0.0 172.0 jit_solution(14853818854958430524)
XLA Ops:
  0.7 3.2 %shard_map.83 = bf16[4,4,2,16,1920]{4,3,2,1,0:T(8,128)(2,1)} custom-call(s32[16]{0:T(128)} %stack.67.place_ref, s32[32,128]{1,0:T(8,128)} %bitcast.25, bf16[128,2560]{1,0:T(8,128)(2,1)} %query_ref.1, bf16[128,2560]{1,0:T(8,128)(2,1)} %key_ref.3, bf16[128,2560]{1,0:T(8,128)(2,1)} %value_ref.3), custom_call_target="tpu_custom_call" | custom-call | flops 251658240 | bytes 3948608 | tf_op jit(solution)/shard_map/pallas_call | solution.py:53
  3.9 7.4 %all-to-all-start = ((bf16[32,16,1920]{2,1,0:T(8,128)(2,1)}), bf16[32,16,1920]{2,1,0:T(8,128)(2,1)}, u32[]{:S(2)}, u32[]{:S(2)}) async-start(bf16[32,16,1920]{2,1,0:T(8,128)(2,1)} %bitcast.24), calls=%async_computation | async-start | bytes 3932160 | tf_op jit(solution)/shard_map/all_to_all | solution.py:424
  11.3 4.1 %heads.1 = (bf16[128,768]{1,0:T(8,128)(2,1)}, bf16[128,768]{1,0:T(8,128)(2,1)}, bf16[128,768]{1,0:T(8,128)(2,1)}, bf16[128,768]{1,0:T(8,128)(2,1)}, bf16[128,768...) custom-call(s32[16]{0:T(128)} %stack.67.place_ref, ...), custom_call_target="tpu_custom_call" | custom-call | flops 327680 | bytes 2621440 | tf_op jit(solution)/shard_map/heads/pallas_call | solution.py:395
  19.1 2.5 %collective-permute-start.4 = (bf16[128,768]{1,0:T(8,128)(2,1)}, bf16[128,768]{1,0:T(8,128)(2,1)}, u32[]{:S(2)}, u32[]{:S(2)}) collective-permute-start(bf16[128,768]{1,0:T(8,128)(2,1)} %get-tuple-element.29), channel_id=1, source_target_pairs={{0,6},{1,7},{2,4},{3,5},{4,2},{5,3},{6,0},{7,1},{8,14},{9,15},{10,... | collective-permute-start | bytes 589832 | tf_op jit(solution)/shard_map/ppermute | solution.py:367
  21.7 9.9 %collective-permute-done.7.refs_2_ = bf16[128,768]{1,0:T(8,128)(2,1)S(1)} collective-permute-done((bf16[128,768]{1,0:T(8,128)(2,1)}, bf16[128,768]{1,0:T(8,128)(2,1)S(1)}, u32[]{:S(2)}, u32[]{:S(2)}) %collective-permute-start.7) | collective-permute-done | bytes 196640 | tf_op jit(solution)/shard_map/ppermute | solution.py:367
  31.6 3.0 %collective-permute-start.5 = (bf16[128,768]{1,0:T(8,128)(2,1)}, bf16[128,768]{1,0:T(8,128)(2,1)}, u32[]{:S(2)}, u32[]{:S(2)}) collective-permute-start(bf16[128,768]{1,0:T(8,128)(2,1)} %get-tuple-element.30), channel_id=1, source_target_pairs={{0,7},{1,6},{2,5},{3,4},{4,3},{5,2},{6,1},{7,0},{8,15},{9,14},{10,... | collective-permute-start | bytes 589832 | tf_op jit(solution)/shard_map/ppermute | solution.py:367
  36.5 3.3 %copy.10 = bf16[640,3,640]{0,2,1:T(8,128)(2,1)} copy(bf16[640,3,640]{2,0,1:T(8,128)(2,1)S(1)} %constant_dynamic-slice_fusion) | data formatting | bytes 4915200
  41.0 5.4 %shard_map.87.refs_4_ = bf16[320,1920]{1,0:T(8,128)(2,1)} custom-call(s32[16]{0:T(128)} %stack.67.place_ref, bf16[3,640,640]{2,1,0:T(8,128)(2,1)} %bitcast.21, bf16[128,768]{1,0:T(8,128)(2,1)} %get-tuple-element.31.refs_0_, bf16[128,768]{1,0:T(8,128)(2,1)} %copy-done.14, bf16[128,768]{1,0:T(8,128)(2,1)} %copy-done.15, bf16[128,768]{1,0:T(8,128)(2,1)} %copy-done.16), custom_call_target="tpu_custom_call" | custom-call | flops 1258291200 | bytes 4472896 | tf_op jit(solution)/shard_map/pallas_call | solution.py:53
  46.5 4.2 %collective-permute-done.5.refs_3_ = bf16[128,768]{1,0:T(8,128)(2,1)} collective-permute-done((bf16[128,768]{1,0:T(8,128)(2,1)}, bf16[128,768]{1,0:T(8,128)(2,1)}, u32[]{:S(2)}, u32[]{:S(2)}) %collective-permute-start.5) | collective-permute-done | bytes 196640 | tf_op jit(solution)/shard_map/ppermute | solution.py:367
  50.7 6.1 %shard_map.88 = (bf16[160,1920]{1,0:T(8,128)(2,1)}, bf16[160,1920]{1,0:T(8,128)(2,1)}) custom-call(s32[16]{0:T(128)} %stack.67.place_ref, bf16[3,640,640]{2,1,0:T(8,128)(2,1)} %bitcast.22, bf16[128,768]{1,0:T(8,128)(2,1)} %copy-done.12, bf16[128,768]{1,0:T(8,128)(2,1)} %copy-done.13, bf16[128,768]{1,0:T(8,128)(2,1)} %collective-permute-done.4.refs_2_, ...), custom_call_target="tpu_custom_call" | custom-call | flops 1258291200 | bytes 5701696 | tf_op jit(solution)/shard_map/pallas_call | solution.py:53
  56.8 2.6 %collective-permute-start.9 = (bf16[160,1920]{1,0:T(8,128)(2,1)}, bf16[160,1920]{1,0:T(8,128)(2,1)S(1)}, u32[]{:S(2)}, u32[]{:S(2)}) collective-permute-start(bf16[160,1920]{1,0:T(8,128)(2,1)} %get-tuple-element.36), channel_id=1, source_target_pairs={{0,8},{1,9},{2,10},{3,11},{4,12},{5,13},{6,14},{7,15},{8,0},{9,1},... | collective-permute-start | bytes 1843208 | tf_op jit(solution)/shard_map/ppermute | solution.py:367
  61.7 11.7 %collective-permute-done.9 = bf16[160,1920]{1,0:T(8,128)(2,1)S(1)} collective-permute-done((bf16[160,1920]{1,0:T(8,128)(2,1)}, bf16[160,1920]{1,0:T(8,128)(2,1)S(1)}, u32[]{:S(2)}, u32[]{:S(2)}) %collective-permute-start.9) | collective-permute-done | bytes 614432 | tf_op jit(solution)/shard_map/ppermute | solution.py:367
  74.7 4.2 %collective-permute-start.10 = (bf16[80,1920]{1,0:T(8,128)(2,1)S(1)}, bf16[80,1920]{1,0:T(8,128)(2,1)}, u32[]{:S(2)}, u32[]{:S(2)}) collective-permute-start(bf16[80,1920]{1,0:T(8,128)(2,1)S(1)} %add_convert_fusion.1), channel_id=1, source_target_pairs={{0,16},{1,17},{2,18},{3,19},{4,20},{5,21},{6,22},{7,23},{8,24},{9,... | collective-permute-start | bytes 921608 | tf_op jit(solution)/shard_map/ppermute | solution.py:367
  79.0 4.0 %shard_map.84 = (bf16[512,1280]{1,0:T(8,128)(2,1)}, bf16[512,640]{1,0:T(8,128)(2,1)}) custom-call(bf16[512,512]{1,0:T(8,128)(2,1)} %shard_map.82.choose_ref, bf16[512,1920]{1,0:T(8,128)(2,1)} %bitcast.19.in_ref), custom_call_target="tpu_custom_call" | custom-call | flops 1006632960 | bytes 4456448 | tf_op jit(solution)/shard_map/pallas_call | solution.py:53
  84.2 3.3 %collective-permute-start = (bf16[512,1280]{1,0:T(8,128)(2,1)}, bf16[512,1280]{1,0:T(8,128)(2,1)S(1)}, u32[]{:S(2)}, u32[]{:S(2)}) collective-permute-start(bf16[512,1280]{1,0:T(8,128)(2,1)} %get-tuple-element.24.key_ref.value_ref), channel_id=1, source_target_pairs={{0,1},{1,8},{2,3},{3,10},{4,5},{5,12},{6,7},{7,14},{8,9},{9,16},{1... | collective-permute-start | bytes 3932168 | tf_op jit(solution)/shard_map/ppermute | solution.py:367
  87.5 5.1 %collective-permute-done.10 = bf16[80,1920]{1,0:T(8,128)(2,1)} collective-permute-done((bf16[80,1920]{1,0:T(8,128)(2,1)S(1)}, bf16[80,1920]{1,0:T(8,128)(2,1)}, u32[]{:S(2)}, u32[]{:S(2)}) %collective-permute-start.10) | collective-permute-done | bytes 307232 | tf_op jit(solution)/shard_map/ppermute | solution.py:367
  93.9 4.1 %collective-permute-start.12 = (bf16[80,1920]{1,0:T(8,128)(2,1)S(1)}, bf16[80,1920]{1,0:T(8,128)(2,1)S(1)}, u32[]{:S(2)}, u32[]{:S(2)}) collective-permute-start(bf16[80,1920]{1,0:T(8,128)(2,1)S(1)} %add_convert_fusion.refs_0_), channel_id=1, source_target_pairs={{0,8},{1,9},{2,10},{3,11},{4,12},{5,13},{6,14},{7,15},{8,0},{9,1},... | collective-permute-start | bytes 921608 | tf_op jit(solution)/shard_map/ppermute | solution.py:367
  98.1 21.6 %collective-permute-done.11.refs_1_ = bf16[80,1920]{1,0:T(8,128)(2,1)S(1)} collective-permute-done((bf16[80,1920]{1,0:T(8,128)(2,1)S(1)}, bf16[80,1920]{1,0:T(8,128)(2,1)S(1)}, u32[]{:S(2)}, u32[]{:S(2)}) %collective-permute-start.11) | collective-permute-done | bytes 307232 | tf_op jit(solution)/shard_map/ppermute | solution.py:367
  120.3 7.7 %collective-permute-done.13.refs_3_ = bf16[80,1920]{1,0:T(8,128)(2,1)} collective-permute-done((bf16[80,1920]{1,0:T(8,128)(2,1)S(1)}, bf16[80,1920]{1,0:T(8,128)(2,1)}, u32[]{:S(2)}, u32[]{:S(2)}) %collective-permute-start.13) | collective-permute-done | bytes 307232 | tf_op jit(solution)/shard_map/ppermute | solution.py:367
  129.9 8.2 %shard_map.85 = (f32[512,640]{1,0:T(8,128)}, f32[512,128]{1,0:T(8,128)}) custom-call(s32[16]{0:T(128)} %stack.67.place_ref, bf16[512,640]{1,0:T(8,128)(2,1)} %get-tuple-element.23.query_ref, s32[8,512]{1,0:T(8,128)} %reshape.18.ids_ref, bf16[512,1280]{1,0:T(8,128)(2,1)} %get-tuple-element.24.key_ref.value_ref, ...), custom_call_target="tpu_custom_call" | custom-call | flops 671088640 | bytes 4866112 | tf_op jit(solution)/shard_map/pallas_call | solution.py:53
  139.1 9.6 %shard_map.86.attended_ref = f32[512,640]{1,0:T(8,128)} custom-call(s32[16]{0:T(128)} %stack.67.place_ref, bf16[512,640]{1,0:T(8,128)(2,1)} %get-tuple-element.23.query_ref, s32[8,512]{1,0:T(8,128)} %reshape.18.ids_ref, f32[512,640]{1,0:T(8,128)} %get-tuple-element.25.near_ref, f32[512,128]{1,0:T(8,128)} %get-tuple-element.26.stat_ref, ...), custom_call_target="tpu_custom_call" | custom-call | flops 838860800 | bytes 8798272 | tf_op jit(solution)/shard_map/pallas_call | solution.py:53
  148.8 7.7 %shard_map.89 = (bf16[128,640]{1,0:T(8,128)(2,1)}, bf16[128,640]{1,0:T(8,128)(2,1)}, bf16[128,640]{1,0:T(8,128)(2,1)}, bf16[128,640]{1,0:T(8,128)(2,1)}) custom-call(s32[16]{0:T(128)} %stack.67.place_ref, bf16[3,640,640]{2,1,0:T(8,128)(2,1)} %bitcast.23, bf16[512,640]{1,0:T(8,128)(2,1)} %get-tuple-element.23.query_ref, f32[512,640]{1,0:T(8,128)} %shard_map.86.attended_ref, ...), custom_call_target="tpu_custom_call" | custom-call | flops 1258291200 | bytes 7536704 | tf_op jit(solution)/shard_map/pallas_call | solution.py:53
  162.0 2.4 %collective-permute-done.19.refs_1_ = bf16[128,640]{1,0:T(8,128)(2,1)S(1)} collective-permute-done((bf16[128,640]{1,0:T(8,128)(2,1)}, bf16[128,640]{1,0:T(8,128)(2,1)S(1)}, u32[]{:S(2)}, u32[]{:S(2)}) %collective-permute-start.19) | collective-permute-done | bytes 163872 | tf_op jit(solution)/shard_map/ppermute | solution.py:367
  164.4 3.0 %collective-permute-done.20.refs_2_ = bf16[128,640]{1,0:T(8,128)(2,1)S(1)} collective-permute-done((bf16[128,640]{1,0:T(8,128)(2,1)}, bf16[128,640]{1,0:T(8,128)(2,1)S(1)}, u32[]{:S(2)}, u32[]{:S(2)}) %collective-permute-start.20) | collective-permute-done | bytes 163872 | tf_op jit(solution)/shard_map/ppermute | solution.py:367
  (73 shorter events, 27.3 us)
Async XLA Ops:
  3.9 75.1 %all-to-all-start = ((bf16[32,16,1920]{2,1,0:T(8,128)(2,1)}), bf16[32,16,1920]{2,1,0:T(8,128)(2,1)}, u32[]{:S(2)}, u32[]{:S(2)}) async-start(bf16[32,16,1920]{2,1,0:T(8,128)(2,1)} %bitcast.24), calls=%async_computation | async-start | bytes 3932160 | tf_op jit(solution)/shard_map/all_to_all | solution.py:424
  15.4 3.7 %collective-permute-start.6 = (bf16[128,768]{1,0:T(8,128)(2,1)}, bf16[128,768]{1,0:T(8,128)(2,1)S(1)}, u32[]{:S(2)}, u32[]{:S(2)}) collective-permute-start(bf16[128,768]{1,0:T(8,128)(2,1)} %get-tuple-element.32), channel_id=1, source_target_pairs={{0,1},{1,0},{2,3},{3,2},{4,5},{5,4},{6,7},{7,6},{8,9},{9,8},{10,11... | collective-permute-start | bytes 589832 | tf_op jit(solution)/shard_map/ppermute | solution.py:367
  15.6 16.0 %collective-permute-start.7 = (bf16[128,768]{1,0:T(8,128)(2,1)}, bf16[128,768]{1,0:T(8,128)(2,1)S(1)}, u32[]{:S(2)}, u32[]{:S(2)}) collective-permute-start(bf16[128,768]{1,0:T(8,128)(2,1)} %get-tuple-element.33), channel_id=1, source_target_pairs={{0,2},{1,3},{2,0},{3,1},{4,6},{5,7},{6,4},{7,5},{8,10},{9,11},{10,... | collective-permute-start | bytes 589832 | tf_op jit(solution)/shard_map/ppermute | solution.py:367
  17.3 23.1 %collective-permute-start.8 = (bf16[128,768]{1,0:T(8,128)(2,1)}, bf16[128,768]{1,0:T(8,128)(2,1)S(1)}, u32[]{:S(2)}, u32[]{:S(2)}) collective-permute-start(bf16[128,768]{1,0:T(8,128)(2,1)} %get-tuple-element.34), channel_id=1, source_target_pairs={{0,3},{1,2},{2,1},{3,0},{4,7},{5,6},{6,5},{7,4},{8,11},{9,10},{10,... | collective-permute-start | bytes 589832 | tf_op jit(solution)/shard_map/ppermute | solution.py:367
  17.3 29.2 %collective-permute-start.2 = (bf16[128,768]{1,0:T(8,128)(2,1)}, bf16[128,768]{1,0:T(8,128)(2,1)S(1)}, u32[]{:S(2)}, u32[]{:S(2)}) collective-permute-start(bf16[128,768]{1,0:T(8,128)(2,1)} %get-tuple-element.27), channel_id=1, source_target_pairs={{0,4},{1,5},{2,6},{3,7},{4,0},{5,1},{6,2},{7,3},{8,12},{9,13},{10,... | collective-permute-start | bytes 589832 | tf_op jit(solution)/shard_map/ppermute | solution.py:367
  19.0 27.5 %collective-permute-start.3 = (bf16[128,768]{1,0:T(8,128)(2,1)}, bf16[128,768]{1,0:T(8,128)(2,1)S(1)}, u32[]{:S(2)}, u32[]{:S(2)}) collective-permute-start(bf16[128,768]{1,0:T(8,128)(2,1)} %get-tuple-element.28), channel_id=1, source_target_pairs={{0,5},{1,4},{2,7},{3,6},{4,1},{5,0},{6,3},{7,2},{8,13},{9,12},{10,... | collective-permute-start | bytes 589832 | tf_op jit(solution)/shard_map/ppermute | solution.py:367
  19.1 27.4 %collective-permute-start.4 = (bf16[128,768]{1,0:T(8,128)(2,1)}, bf16[128,768]{1,0:T(8,128)(2,1)}, u32[]{:S(2)}, u32[]{:S(2)}) collective-permute-start(bf16[128,768]{1,0:T(8,128)(2,1)} %get-tuple-element.29), channel_id=1, source_target_pairs={{0,6},{1,7},{2,4},{3,5},{4,2},{5,3},{6,0},{7,1},{8,14},{9,15},{10,... | collective-permute-start | bytes 589832 | tf_op jit(solution)/shard_map/ppermute | solution.py:367
  31.6 19.1 %collective-permute-start.5 = (bf16[128,768]{1,0:T(8,128)(2,1)}, bf16[128,768]{1,0:T(8,128)(2,1)}, u32[]{:S(2)}, u32[]{:S(2)}) collective-permute-start(bf16[128,768]{1,0:T(8,128)(2,1)} %get-tuple-element.30), channel_id=1, source_target_pairs={{0,7},{1,6},{2,5},{3,4},{4,3},{5,2},{6,1},{7,0},{8,15},{9,14},{10,... | collective-permute-start | bytes 589832 | tf_op jit(solution)/shard_map/ppermute | solution.py:367
  56.8 16.7 %collective-permute-start.9 = (bf16[160,1920]{1,0:T(8,128)(2,1)}, bf16[160,1920]{1,0:T(8,128)(2,1)S(1)}, u32[]{:S(2)}, u32[]{:S(2)}) collective-permute-start(bf16[160,1920]{1,0:T(8,128)(2,1)} %get-tuple-element.36), channel_id=1, source_target_pairs={{0,8},{1,9},{2,10},{3,11},{4,12},{5,13},{6,14},{7,15},{8,0},{9,1},... | collective-permute-start | bytes 1843208 | tf_op jit(solution)/shard_map/ppermute | solution.py:367
  74.7 17.9 %collective-permute-start.10 = (bf16[80,1920]{1,0:T(8,128)(2,1)S(1)}, bf16[80,1920]{1,0:T(8,128)(2,1)}, u32[]{:S(2)}, u32[]{:S(2)}) collective-permute-start(bf16[80,1920]{1,0:T(8,128)(2,1)S(1)} %add_convert_fusion.1), channel_id=1, source_target_pairs={{0,16},{1,17},{2,18},{3,19},{4,20},{5,21},{6,22},{7,23},{8,24},{9,... | collective-permute-start | bytes 921608 | tf_op jit(solution)/shard_map/ppermute | solution.py:367
  82.9 45.1 %collective-permute-start.1 = (bf16[512,1280]{1,0:T(8,128)(2,1)}, bf16[512,1280]{1,0:T(8,128)(2,1)S(1)}, u32[]{:S(2)}, u32[]{:S(2)}) collective-permute-start(bf16[512,1280]{1,0:T(8,128)(2,1)} %get-tuple-element.24.key_ref.value_ref), channel_id=1, source_target_pairs={{1,0},{3,2},{5,4},{7,6},{8,1},{9,8},{10,3},{11,10},{12,5},{13,12},... | collective-permute-start | bytes 3932168 | tf_op jit(solution)/shard_map/ppermute | solution.py:367
  84.2 53.8 %collective-permute-start = (bf16[512,1280]{1,0:T(8,128)(2,1)}, bf16[512,1280]{1,0:T(8,128)(2,1)S(1)}, u32[]{:S(2)}, u32[]{:S(2)}) collective-permute-start(bf16[512,1280]{1,0:T(8,128)(2,1)} %get-tuple-element.24.key_ref.value_ref), channel_id=1, source_target_pairs={{0,1},{1,8},{2,3},{3,10},{4,5},{5,12},{6,7},{7,14},{8,9},{9,16},{1... | collective-permute-start | bytes 3932168 | tf_op jit(solution)/shard_map/ppermute | solution.py:367
  93.8 54.9 %copy-start.2 = (bf16[80,1920]{1,0:T(8,128)(2,1)}, bf16[80,1920]{1,0:T(8,128)(2,1)S(1)}, u32[]{:S(2)}) copy-start(bf16[80,1920]{1,0:T(8,128)(2,1)S(1)} %add_convert_fusion.refs_0_) | copy-start | bytes 921604
  93.9 25.9 %collective-permute-start.11 = (bf16[80,1920]{1,0:T(8,128)(2,1)S(1)}, bf16[80,1920]{1,0:T(8,128)(2,1)S(1)}, u32[]{:S(2)}, u32[]{:S(2)}) collective-permute-start(bf16[80,1920]{1,0:T(8,128)(2,1)S(1)} %add_convert_fusion.refs_0_), channel_id=1, source_target_pairs={{0,16},{1,17},{2,18},{3,19},{4,20},{5,21},{6,22},{7,23},{8,24},{9,... | collective-permute-start | bytes 921608 | tf_op jit(solution)/shard_map/ppermute | solution.py:367
  93.9 26.3 %collective-permute-start.12 = (bf16[80,1920]{1,0:T(8,128)(2,1)S(1)}, bf16[80,1920]{1,0:T(8,128)(2,1)S(1)}, u32[]{:S(2)}, u32[]{:S(2)}) collective-permute-start(bf16[80,1920]{1,0:T(8,128)(2,1)S(1)} %add_convert_fusion.refs_0_), channel_id=1, source_target_pairs={{0,8},{1,9},{2,10},{3,11},{4,12},{5,13},{6,14},{7,15},{8,0},{9,1},... | collective-permute-start | bytes 921608 | tf_op jit(solution)/shard_map/ppermute | solution.py:367
  119.7 8.4 %collective-permute-start.13 = (bf16[80,1920]{1,0:T(8,128)(2,1)S(1)}, bf16[80,1920]{1,0:T(8,128)(2,1)}, u32[]{:S(2)}, u32[]{:S(2)}) collective-permute-start(bf16[80,1920]{1,0:T(8,128)(2,1)S(1)} %collective-permute-done.11.refs_1_), channel_id=1, source_target_pairs={{0,8},{1,9},{2,10},{3,11},{4,12},{5,13},{6,14},{7,15},{8,0},{9,1},... | collective-permute-start | bytes 921608 | tf_op jit(solution)/shard_map/ppermute | solution.py:367
  119.7 29.1 %collective-permute-start.14 = (bf16[80,1920]{1,0:T(8,128)(2,1)S(1)}, bf16[80,1920]{1,0:T(8,128)(2,1)}, u32[]{:S(2)}, u32[]{:S(2)}) collective-permute-start(bf16[80,1920]{1,0:T(8,128)(2,1)S(1)} %add_convert_fusion.refs_0_), channel_id=1, source_target_pairs={{0,1},{1,0},{2,3},{3,2},{4,5},{5,4},{6,7},{7,6},{8,9},{9,8},{10,11... | collective-permute-start | bytes 921608 | tf_op jit(solution)/shard_map/ppermute | solution.py:367
  120.3 28.6 %collective-permute-start.15 = (bf16[80,1920]{1,0:T(8,128)(2,1)S(1)}, bf16[80,1920]{1,0:T(8,128)(2,1)}, u32[]{:S(2)}, u32[]{:S(2)}) collective-permute-start(bf16[80,1920]{1,0:T(8,128)(2,1)S(1)} %collective-permute-done.11.refs_1_), channel_id=1, source_target_pairs={{0,1},{1,0},{2,3},{3,2},{4,5},{5,4},{6,7},{7,6},{8,9},{9,8},{10,11... | collective-permute-start | bytes 921608 | tf_op jit(solution)/shard_map/ppermute | solution.py:367
  128.1 20.7 %collective-permute-start.16 = (bf16[80,1920]{1,0:T(8,128)(2,1)S(1)}, bf16[80,1920]{1,0:T(8,128)(2,1)}, u32[]{:S(2)}, u32[]{:S(2)}) collective-permute-start(bf16[80,1920]{1,0:T(8,128)(2,1)S(1)} %collective-permute-done.12.refs_2_), channel_id=1, source_target_pairs={{0,1},{1,0},{2,3},{3,2},{4,5},{5,4},{6,7},{7,6},{8,9},{9,8},{10,11... | collective-permute-start | bytes 921608 | tf_op jit(solution)/shard_map/ppermute | solution.py:367
  128.1 20.7 %collective-permute-start.17 = (bf16[80,1920]{1,0:T(8,128)(2,1)}, bf16[80,1920]{1,0:T(8,128)(2,1)}, u32[]{:S(2)}, u32[]{:S(2)}) collective-permute-start(bf16[80,1920]{1,0:T(8,128)(2,1)} %collective-permute-done.13.refs_3_), channel_id=1, source_target_pairs={{0,1},{1,0},{2,3},{3,2},{4,5},{5,4},{6,7},{7,6},{8,9},{9,8},{10,11... | collective-permute-start | bytes 921608 | tf_op jit(solution)/shard_map/ppermute | solution.py:367
  156.5 5.5 %collective-permute-start.18 = (bf16[128,640]{1,0:T(8,128)(2,1)}, bf16[128,640]{1,0:T(8,128)(2,1)S(1)}, u32[]{:S(2)}, u32[]{:S(2)}) collective-permute-start(bf16[128,640]{1,0:T(8,128)(2,1)} %get-tuple-element.37), channel_id=1, source_target_pairs={{0,0},{1,4},{2,2},{3,6},{4,1},{5,5},{6,3},{7,7},{8,8},{9,12},{10,1... | collective-permute-start | bytes 491528 | tf_op jit(solution)/shard_map/ppermute | solution.py:367
  158.1 6.3 %collective-permute-start.19 = (bf16[128,640]{1,0:T(8,128)(2,1)}, bf16[128,640]{1,0:T(8,128)(2,1)S(1)}, u32[]{:S(2)}, u32[]{:S(2)}) collective-permute-start(bf16[128,640]{1,0:T(8,128)(2,1)} %get-tuple-element.38), channel_id=1, source_target_pairs={{0,2},{1,6},{2,0},{3,4},{4,3},{5,7},{6,1},{7,5},{8,10},{9,14},{10,... | collective-permute-start | bytes 491528 | tf_op jit(solution)/shard_map/ppermute | solution.py:367
  159.3 8.0 %collective-permute-start.20 = (bf16[128,640]{1,0:T(8,128)(2,1)}, bf16[128,640]{1,0:T(8,128)(2,1)S(1)}, u32[]{:S(2)}, u32[]{:S(2)}) collective-permute-start(bf16[128,640]{1,0:T(8,128)(2,1)} %get-tuple-element.39), channel_id=1, source_target_pairs={{0,1},{1,5},{2,3},{3,7},{4,0},{5,4},{6,2},{7,6},{8,9},{9,13},{10,1... | collective-permute-start | bytes 491528 | tf_op jit(solution)/shard_map/ppermute | solution.py:367
  161.0 8.0 %collective-permute-start.21 = (bf16[128,640]{1,0:T(8,128)(2,1)}, bf16[128,640]{1,0:T(8,128)(2,1)S(1)}, u32[]{:S(2)}, u32[]{:S(2)}) collective-permute-start(bf16[128,640]{1,0:T(8,128)(2,1)} %get-tuple-element.40), channel_id=1, source_target_pairs={{0,3},{1,7},{2,1},{3,5},{4,2},{5,6},{6,0},{7,4},{8,11},{9,15},{10,... | collective-permute-start | bytes 491528 | tf_op jit(solution)/shard_map/ppermute | solution.py:367
  (16 other events, 153.9 us)

commit v5 on v4

--- a/solution.py
+++ b/solution.py
@@ -205,77 +205,108 @@
 FACTOR = ATT_DIM ** (-0.5) * math.log2(math.e)
 
 
-def near_kernel(block, place_ref, query_ref, ids_ref, key_ref, value_ref, out_ref, stat_ref, bias):
+def reach(before, index, count, block):
+    at = pl.multiple_of(jnp.where(before, index, count - 1 - index) * block, block)
+    return at, pl.multiple_of(jnp.where(before, at, 0), block), jnp.where(before, -count * block, count * block - at)
+
+
+def block_ids(ids, index, count, block, turned):
+    turn = count - 1 - index
+    row = jnp.where(turned, ids[:, turn * block : (turn + 1) * block], ids[:, index * block : (index + 1) * block])
+    return column_of(row).astype(jnp.int32)
+
+
+def mask_of(own, ids, shift):
+    gap = iota((own.shape[0], ids.shape[1]), 1) - iota((own.shape[0], ids.shape[1]), 0) + shift
+    return jnp.where((gap < WINDOW // 2) & (gap > -(WINDOW // 2)) & (own == ids), 0.0, -1e30)
+
+
+def near_kernel(block, place_ref, query_ref, ids_ref, key_ref, value_ref, chip_key_ref, chip_value_ref, out_ref, stat_ref, bias, chip_bias):
     n = query_ref.shape[0]
+    count = n // block
     head = pl.program_id(0)
+    core, group = place_ref[2], place_ref[3]
+    second = core == 1
 
     @pl.when(head == 0)
     def _():
-        ids = ids_ref[pl.ds(place_ref[3], 1), :]
-        for at in range(0, n, block):
-            own = column_of(ids[:, at : at + block]).astype(jnp.int32)
-            gap = iota((block, n), 1) - iota((block, n), 0) - at
-            allowed = (gap < WINDOW // 2) & (gap > -(WINDOW // 2)) & (own == ids)
-            bias[at : at + block, :] = jnp.where(allowed, 0.0, -1e30)
+        ids = ids_ref[pl.ds(group, 1), :]
+        for index in range(count):
+            at = index * block
+            bias[at : at + block, :] = mask_of(column_of(ids[:, at : at + block]).astype(jnp.int32), ids, -at)
+        for index in range(count):
+            _, _, shift = reach(second, count - 1 - index, count, block)
+            size = (index + 1) * block
+            own = block_ids(ids, index, count, block, second)
+            other = ids_ref[pl.ds(group + 1 - 2 * core, 1), :]
+            other = jnp.where(second, other[:, n - size :], other[:, :size])
+            chip_bias[index, :, :size] = mask_of(own, other, shift)
         stat_ref[...] = jnp.zeros_like(stat_ref)
 
     lane = iota((block, LANES), 1)
-    for at in range(0, n, block):
-        here = slice(at, at + block)
-        score = dot(query_ref[here, :], key_ref[...], ((1,), (1,))) + bias[here, :]
-        peak = jnp.max(score, axis=1, keepdims=True)
-        weight = jnp.exp2((score - peak) * FACTOR)
-        total = jnp.sum(weight, axis=1, keepdims=True)
-        out_ref[here, :] = dot(weight.astype(BF16), value_ref[...])
+    for index in range(count):
+        at, start, _ = reach(second, count - 1 - index, count, block)
+        size = (index + 1) * block
+        here, there = pl.ds(at, block), pl.ds(start, size)
+        query = query_ref[here, :]
+        score = dot(query, key_ref[...], ((1,), (1,))) + bias[here, :]
+        chip = dot(query, chip_key_ref[there, :], ((1,), (1,))) + chip_bias[index, :, :size]
+        peak = jnp.maximum(jnp.max(score, axis=1, keepdims=True), jnp.max(chip, axis=1, keepdims=True))
+        score = jnp.exp2((score - peak) * FACTOR)
+        chip = jnp.exp2((chip - peak) * FACTOR)
+        total = jnp.sum(score, axis=1, keepdims=True) + jnp.sum(chip, axis=1, keepdims=True)
+        out_ref[here, :] = dot(score.astype(BF16), value_ref[...]) + dot(chip.astype(BF16), chip_value_ref[there, :])
         stat = jnp.where(lane == 2 * head, peak, stat_ref[here, :])
         stat_ref[here, :] = jnp.where(lane == 2 * head + 1, total, stat)
 
 
-def far_kernel(block, place_ref, query_ref, ids_ref, near_ref, stat_ref, key_low_ref, key_high_ref, value_low_ref, value_high_ref, out_ref, bias):
+def far_kernel(block, first_goal, place_ref, query_ref, ids_ref, near_ref, stat_ref, fast_ref, key_ref, value_ref, *refs):
+    out_refs, (bias, rows_buf) = refs[:-2], refs[-2:]
     n = query_ref.shape[0]
-    half = WINDOW // 2
+    count = n // block
     head = pl.program_id(0)
-    group = place_ref[3]
+    core, group = place_ref[2], place_ref[3]
     last = ids_ref.shape[0] - 1
+    first = core == 0
 
     @pl.when(head == 0)
     def _():
-        mid = ids_ref[pl.ds(group, 1), :]
-        low = jnp.where(group > 0, ids_ref[pl.ds(jnp.maximum(group - 1, 0), 1), :], -1)
-        high = jnp.where(group < last, ids_ref[pl.ds(jnp.minimum(group + 1, last), 1), :], -1)
-        for at in range(0, n, block):
-            own = column_of(mid[:, at : at + block]).astype(jnp.int32)
-            for ids, begin, end, shift in ((low, at, n, -n), (high, 0, at + block, n)):
-                size = end - begin
-                gap = iota((block, size), 1) + (begin + shift - at) - iota((block, size), 0)
-                allowed = (gap < half) & (gap > -half) & (own == ids[:, begin:end])
-                lanes = slice(begin - at, end - at) if shift < 0 else slice(n - at, n - at + size)
-                bias[at : at + block, lanes] = jnp.where(allowed, 0.0, -1e30)
+        beyond = group - 1 + 2 * core
+        exists = (beyond >= 0) & (beyond <= last)
+        ids = ids_ref[pl.ds(group, 1), :]
+        for index in range(count):
+            _, _, shift = reach(first, index, count, block)
+            size = n - index * block
+            own = block_ids(ids, index, count, block, core == 1)
+            other = ids_ref[pl.ds(jnp.clip(beyond, 0, last), 1), :]
+            other = jnp.where(first, other[:, n - size :], other[:, :size])
+            bias[index, :, :size] = mask_of(own, jnp.where(exists, other, -1), shift)
 
     lane = iota((block, LANES), 1)
-    for at in range(0, n, block):
-        here = slice(at, at + block)
-        query = query_ref[here, :]
-        low = dot(query, key_low_ref[at:, :], ((1,), (1,))) + bias[here, : n - at]
-        high = dot(query, key_high_ref[: at + block, :], ((1,), (1,))) + bias[here, n - at :]
+    for index in range(count):
+        at, start, _ = reach(first, index, count, block)
+        size = n - index * block
+        here, there = pl.ds(at, block), pl.ds(start, size)
+        score = dot(query_ref[here, :], key_ref[there, :], ((1,), (1,))) + bias[index, :, :size]
         stat = stat_ref[here, :]
         old_peak = jnp.sum(jnp.where(lane == 2 * head, stat, 0.0), axis=1, keepdims=True)
         old_total = jnp.sum(jnp.where(lane == 2 * head + 1, stat, 0.0), axis=1, keepdims=True)
-        peak = jnp.maximum(jnp.max(low, axis=1, keepdims=True), jnp.max(high, axis=1, keepdims=True))
-        peak = jnp.maximum(peak, old_peak)
+        peak = jnp.maximum(jnp.max(score, axis=1, keepdims=True), old_peak)
         keep = jnp.exp2((old_peak - peak) * FACTOR)
-        low = jnp.exp2((low - peak) * FACTOR)
-        high = jnp.exp2((high - peak) * FACTOR)
-        total = old_total * keep + jnp.sum(low, axis=1, keepdims=True) + jnp.sum(high, axis=1, keepdims=True)
-        mixed = near_ref[here, :] * keep + dot(low.astype(BF16), value_low_ref[at:, :])
-        mixed += dot(high.astype(BF16), value_high_ref[: at + block, :])
-        out_ref[here, :] = mixed / total
-
-
-def apply_kernel(place_ref, weight_ref, query_ref, attended_ref, *refs):
+        score = jnp.exp2((score - peak) * FACTOR)
+        total = old_total * keep + jnp.sum(score, axis=1, keepdims=True)
+        mixed = near_ref[here, :] * keep + dot(score.astype(BF16), value_ref[there, :])
+        rows_buf[here, :] = (mixed / total + fast_ref[here, :]).astype(BF16)
+    rows = out_refs[0].shape[0]
+    for index, ref in enumerate(out_refs):
+        begin = pl.multiple_of(place_ref[first_goal + index] * rows, rows)
+        ref[...] = rows_buf[pl.ds(begin, rows), :]
+
+
+def apply_kernel(place_ref, weight_ref, query_ref, *refs):
     hidden = weight_ref.shape[2]
-    out_refs, (fresh, scales, rows_buf) = refs[-3 - PARTS : -3], refs[-3:]
-    count = (len(refs) - 3 - PARTS) // 2
+    out_ref, fresh, scales = refs[-3:]
+    count = (len(refs) - 3) // 2
     mine_refs, other_refs = refs[:count], refs[count : 2 * count]
     piece = mine_refs[0].shape[0]
     core = place_ref[2]
@@ -308,15 +339,8 @@
         product = (gate * jax.nn.sigmoid(gate) * upward).astype(BF16)
         parts.append((begin, dot(product, fresh[head, 2], ((1,), (1,)))))
     for lane in range(0, PART_WIDTH, LANES):
-        total = attended_ref[:, lane : lane + LANES]
-        for begin, value in parts:
-            if begin <= lane < begin + SPAN:
-                total += value[:, lane - begin : lane - begin + LANES]
-        rows_buf[:, lane : lane + LANES] = total.astype(BF16)
-    block = out_refs[0].shape[0]
-    for index, ref in enumerate(out_refs):
-        begin = pl.multiple_of(place_ref[4 + PARTS + count + index] * block, block)
-        ref[...] = rows_buf[pl.ds(begin, block), :]
+        inside = [value[:, lane - begin : lane - begin + LANES] for begin, value in parts if begin <= lane < begin + SPAN]
+        out_ref[:, lane : lane + LANES] = functools.reduce(jnp.add, inside)
 
 
 def norm_kernel(place_ref, *refs):
@@ -436,15 +460,14 @@
         [choose, arrived], flops=2 * group_rows * group_rows * 3 * PART_WIDTH,
     )
 
-    def neighbour(step):
-        def target(z, y, x, c):
-            goal = z * PART_FAST + c + step
-            return (goal // PART_FAST, y, x, goal % PART_FAST) if 0 <= goal < groups else None
-
-        return target
-
-    kv_low = permute(kv_seq, neighbour(1))
-    kv_high = permute(kv_seq, neighbour(-1))
+    swap = lambda z, y, x, c: (z, y, x, 1 - c)
+
+    def beyond(z, y, x, c):
+        goal = z + 2 * c - 1
+        return (goal, y, x, 1 - c) if 0 <= goal < planes else None
+
+    kv_chip = permute(kv_seq, swap)
+    kv_far = permute(kv_seq, beyond)
 
     near = plane_size // 2
     tokens = near * tok_dev
@@ -485,7 +508,6 @@
         for held in pieces:
             fresh_pieces.append(permute(held, across(bit)))
         pieces += fresh_pieces
-    swap = lambda z, y, x, c: (z, y, x, 1 - c)
     pieces_other = []
     for held in pieces:
         pieces_other.append(permute(held, swap))
@@ -495,37 +517,38 @@
     ids = window_ids.reshape(groups, group_rows)
     wide = jax.ShapeDtypeStruct((group_rows, PART_WIDTH), F32)
     stat_shape = jax.ShapeDtypeStruct((group_rows, LANES), F32)
-    assert block + group_rows == WINDOW // 2 + block and 2 * PART_ATT <= LANES
+    count = group_rows // block
+    assert 2 * PART_ATT <= LANES
+    keys, values = lane_block(group_rows, 0), lane_block(group_rows, PART_ATT)
     near_mixed, stats = call(
         functools.partial(near_kernel, block),
         [wide, stat_shape],
-        [place, query_seq, ids, kv_seq, kv_seq],
-        in_specs=[lane_block(group_rows, 0), full(ids), lane_block(group_rows, 0), lane_block(group_rows, PART_ATT)],
+        [place, query_seq, ids, kv_seq, kv_seq, kv_chip, kv_chip],
+        in_specs=[lane_block(group_rows, 0), full(ids), keys, values, keys, values],
         out_specs=[lane_block(group_rows, 0), full(stat_shape)],
-        grid=(PART_ATT,), scratch=[VMEM((group_rows, group_rows), F32)],
-        smem=1, flops=4 * group_rows * group_rows * PART_WIDTH,
-    )
-    (attended,) = call(
-        functools.partial(far_kernel, block),
+        grid=(PART_ATT,),
+        scratch=[VMEM((group_rows, group_rows), F32), VMEM((count, block, group_rows), F32)],
+        smem=1, flops=6 * group_rows * group_rows * PART_WIDTH,
+    )
+
+    (fast_out,) = call(
+        apply_kernel,
         [wide],
-        [place, query_seq, ids, near_mixed, stats, kv_low, kv_high, kv_low, kv_high],
+        [place, weights, query_seq] + pieces + pieces_other,
+        scratch=[VMEM((PART_FAST, 3, SPAN, hidden), BF16), VMEM((PART_FAST * 3, hidden), F32)],
+        smem=1, flops=6 * group_rows * PART_WIDTH * hidden,
+    )
+
+    blocks = call(
+        functools.partial(far_kernel, block, 4 + PARTS + len(starts)),
+        [jax.ShapeDtypeStruct((tok_dev, PART_WIDTH), BF16)] * PARTS,
+        [place, query_seq, ids, near_mixed, stats, fast_out, kv_far, kv_far],
         in_specs=[lane_block(group_rows, 0), full(ids), lane_block(group_rows, 0), full(stats)]
-        + [lane_block(group_rows, 0)] * 2 + [lane_block(group_rows, PART_ATT)] * 2,
-        out_specs=[lane_block(group_rows, 0)],
-        grid=(PART_ATT,), scratch=[VMEM((group_rows, group_rows + block), F32)],
-        smem=1, flops=4 * group_rows * (group_rows + block) * PART_WIDTH,
-    )
-
-    blocks = call(
-        apply_kernel,
-        [jax.ShapeDtypeStruct((tok_dev, PART_WIDTH), BF16)] * PARTS,
-        [place, weights, query_seq, attended] + pieces + pieces_other,
-        scratch=[
-            VMEM((PART_FAST, 3, SPAN, hidden), BF16),
-            VMEM((PART_FAST * 3, hidden), F32),
-            VMEM((group_rows, PART_WIDTH), BF16),
-        ],
-        smem=1, flops=6 * group_rows * PART_WIDTH * hidden,
+        + [lane_block(group_rows, 0), keys, values],
+        out_specs=[lane_block(tok_dev, 0)] * PARTS,
+        grid=(PART_ATT,),
+        scratch=[VMEM((count, block, group_rows), F32), VMEM((group_rows, ATT_DIM), BF16)],
+        smem=1, flops=3 * group_rows * group_rows * PART_WIDTH,
     )
 
     parts = []

time: 173 us -> 174 us (level)
  waiting for transfers between devices: 67.9 us -> 72.2 us
  starting transfers between devices: 38.3 us -> 34.2 us
    ppermute x22, waiting for transfers between devices: 67.9 us -> 72.2 us  [permute(): return lax.ppermute(array, 'tok', route)]
    ppermute x22, starting transfers between devices: 30.9 us -> 26.8 us  [permute(): return lax.ppermute(array, 'tok', route)]
    unnamed x35 -> x37, local copies, waits for them, and re-layouts: 5.7 us -> 6.81 us
  transfers between devices with their start and end apart: 23 -> 23, of which waited for: 10 -> 12; matrix products, arithmetic and copies ran while one was open for 6% -> 5% of each run, Pallas kernels for 23% -> 23%
where the time goes in v5:
time: 174 us
  waiting for transfers between devices  72.2 us (41%)
  Pallas kernels  53.5 us (31%)
  starting transfers between devices  34.2 us (20%)
  local copies, waits for them, and re-layouts  11.3 us (6%)
  other arithmetic  2.42 us (1%)
    ppermute x22, waiting for transfers between devices, permute(): return lax.ppermute(array, 'tok', route)  72.2 us
    pallas_call x9, Pallas kernels, call(): pl.pallas_call(kernel, out_shape=list(outs), in_specs=specs, out_specs=ou...  49.3 us
    ppermute x22, starting transfers between devices, permute(): return lax.ppermute(array, 'tok', route)  26.8 us
    all_to_all x1, starting transfers between devices, shards(): lax.all_to_all(packed.reshape(sections, slots, 3 * PART_WIDTH), 'tok', sp...  7.43 us
    unnamed x37, local copies, waits for them, and re-layouts  6.81 us
    pallas_call x1, Pallas kernels, shards(): pl.pallas_call(heads_kernel, out_shape=[jax.ShapeDtypeStruct((tok_dev, 2...  4.15 us
  transfers between devices with their start and end apart: 23, of which 12 were waited for; matrix products, arithmetic and copies ran while one was open for 5% of the time, Pallas kernels for 23%

profile of v5, /device:TPU:0, one launch (start us, length us, event | category | flops | bytes accessed | tf_op | source)
XLA Modules:
  0.0 173.7 jit_solution(10816789816591361287)
XLA Ops:
  0.6 3.2 %shard_map.83 = bf16[4,4,2,16,1920]{4,3,2,1,0:T(8,128)(2,1)} custom-call(s32[16]{0:T(128)} %stack.67.place_ref, s32[32,128]{1,0:T(8,128)} %bitcast.25, bf16[128,2560]{1,0:T(8,128)(2,1)} %query_ref.1, bf16[128,2560]{1,0:T(8,128)(2,1)} %key_ref.3, bf16[128,2560]{1,0:T(8,128)(2,1)} %value_ref.3), custom_call_target="tpu_custom_call" | custom-call | flops 251658240 | bytes 3948608 | tf_op jit(solution)/shard_map/pallas_call | solution.py:53
  3.8 7.4 %all-to-all-start = ((bf16[32,16,1920]{2,1,0:T(8,128)(2,1)}), bf16[32,16,1920]{2,1,0:T(8,128)(2,1)}, u32[]{:S(2)}, u32[]{:S(2)}) async-start(bf16[32,16,1920]{2,1,0:T(8,128)(2,1)} %bitcast.24), calls=%async_computation | async-start | bytes 3932160 | tf_op jit(solution)/shard_map/all_to_all | solution.py:448
  11.3 4.1 %heads.1 = (bf16[128,768]{1,0:T(8,128)(2,1)}, bf16[128,768]{1,0:T(8,128)(2,1)}, bf16[128,768]{1,0:T(8,128)(2,1)}, bf16[128,768]{1,0:T(8,128)(2,1)}, bf16[128,768...) custom-call(s32[16]{0:T(128)} %stack.67.place_ref, ...), custom_call_target="tpu_custom_call" | custom-call | flops 327680 | bytes 2621440 | tf_op jit(solution)/shard_map/heads/pallas_call | solution.py:419
  19.1 2.5 %collective-permute-start.3 = (bf16[128,768]{1,0:T(8,128)(2,1)}, bf16[128,768]{1,0:T(8,128)(2,1)}, u32[]{:S(2)}, u32[]{:S(2)}) collective-permute-start(bf16[128,768]{1,0:T(8,128)(2,1)} %get-tuple-element.29), channel_id=1, source_target_pairs={{0,6},{1,7},{2,4},{3,5},{4,2},{5,3},{6,0},{7,1},{8,14},{9,15},{10,... | collective-permute-start | bytes 589832 | tf_op jit(solution)/shard_map/ppermute | solution.py:391
  21.6 9.9 %collective-permute-done.6.refs_2_ = bf16[128,768]{1,0:T(8,128)(2,1)S(1)} collective-permute-done((bf16[128,768]{1,0:T(8,128)(2,1)}, bf16[128,768]{1,0:T(8,128)(2,1)S(1)}, u32[]{:S(2)}, u32[]{:S(2)}) %collective-permute-start.6) | collective-permute-done | bytes 196640 | tf_op jit(solution)/shard_map/ppermute | solution.py:391
  31.5 3.0 %collective-permute-start.4 = (bf16[128,768]{1,0:T(8,128)(2,1)}, bf16[128,768]{1,0:T(8,128)(2,1)}, u32[]{:S(2)}, u32[]{:S(2)}) collective-permute-start(bf16[128,768]{1,0:T(8,128)(2,1)} %get-tuple-element.30), channel_id=1, source_target_pairs={{0,7},{1,6},{2,5},{3,4},{4,3},{5,2},{6,1},{7,0},{8,15},{9,14},{10,... | collective-permute-start | bytes 589832 | tf_op jit(solution)/shard_map/ppermute | solution.py:391
  36.5 3.3 %copy.10 = bf16[640,3,640]{0,2,1:T(8,128)(2,1)} copy(bf16[640,3,640]{2,0,1:T(8,128)(2,1)S(1)} %constant_dynamic-slice_fusion) | data formatting | bytes 4915200
  41.0 5.4 %shard_map.86.refs_4_ = bf16[320,1920]{1,0:T(8,128)(2,1)} custom-call(s32[16]{0:T(128)} %stack.67.place_ref, bf16[3,640,640]{2,1,0:T(8,128)(2,1)} %bitcast.21, bf16[128,768]{1,0:T(8,128)(2,1)} %get-tuple-element.31.refs_0_, bf16[128,768]{1,0:T(8,128)(2,1)} %copy-done.15, bf16[128,768]{1,0:T(8,128)(2,1)} %copy-done.16, bf16[128,768]{1,0:T(8,128)(2,1)} %copy-done.17), custom_call_target="tpu_custom_call" | custom-call | flops 1258291200 | bytes 4472896 | tf_op jit(solution)/shard_map/pallas_call | solution.py:53
  46.5 4.2 %collective-permute-done.4.refs_3_ = bf16[128,768]{1,0:T(8,128)(2,1)} collective-permute-done((bf16[128,768]{1,0:T(8,128)(2,1)}, bf16[128,768]{1,0:T(8,128)(2,1)}, u32[]{:S(2)}, u32[]{:S(2)}) %collective-permute-start.4) | collective-permute-done | bytes 196640 | tf_op jit(solution)/shard_map/ppermute | solution.py:391
  50.7 6.1 %shard_map.87 = (bf16[160,1920]{1,0:T(8,128)(2,1)}, bf16[160,1920]{1,0:T(8,128)(2,1)}) custom-call(s32[16]{0:T(128)} %stack.67.place_ref, bf16[3,640,640]{2,1,0:T(8,128)(2,1)} %bitcast.22, bf16[128,768]{1,0:T(8,128)(2,1)} %copy-done.13, bf16[128,768]{1,0:T(8,128)(2,1)} %copy-done.14, bf16[128,768]{1,0:T(8,128)(2,1)} %collective-permute-done.3.refs_2_, ...), custom_call_target="tpu_custom_call" | custom-call | flops 1258291200 | bytes 5701696 | tf_op jit(solution)/shard_map/pallas_call | solution.py:53
  56.8 2.6 %collective-permute-start.8 = (bf16[160,1920]{1,0:T(8,128)(2,1)}, bf16[160,1920]{1,0:T(8,128)(2,1)S(1)}, u32[]{:S(2)}, u32[]{:S(2)}) collective-permute-start(bf16[160,1920]{1,0:T(8,128)(2,1)} %get-tuple-element.36), channel_id=1, source_target_pairs={{0,8},{1,9},{2,10},{3,11},{4,12},{5,13},{6,14},{7,15},{8,0},{9,1},... | collective-permute-start | bytes 1843208 | tf_op jit(solution)/shard_map/ppermute | solution.py:391
  59.5 14.0 %collective-permute-done.8 = bf16[160,1920]{1,0:T(8,128)(2,1)S(1)} collective-permute-done((bf16[160,1920]{1,0:T(8,128)(2,1)}, bf16[160,1920]{1,0:T(8,128)(2,1)S(1)}, u32[]{:S(2)}, u32[]{:S(2)}) %collective-permute-start.8) | collective-permute-done | bytes 614432 | tf_op jit(solution)/shard_map/ppermute | solution.py:391
  74.7 4.2 %collective-permute-start.9 = (bf16[80,1920]{1,0:T(8,128)(2,1)S(1)}, bf16[80,1920]{1,0:T(8,128)(2,1)}, u32[]{:S(2)}, u32[]{:S(2)}) collective-permute-start(bf16[80,1920]{1,0:T(8,128)(2,1)S(1)} %add_convert_fusion.1), channel_id=1, source_target_pairs={{0,16},{1,17},{2,18},{3,19},{4,20},{5,21},{6,22},{7,23},{8,24},{9,... | collective-permute-start | bytes 921608 | tf_op jit(solution)/shard_map/ppermute | solution.py:391
  81.2 4.0 %shard_map.84 = (bf16[512,1280]{1,0:T(8,128)(2,1)}, bf16[512,640]{1,0:T(8,128)(2,1)}) custom-call(bf16[512,512]{1,0:T(8,128)(2,1)} %shard_map.82.choose_ref, bf16[512,1920]{1,0:T(8,128)(2,1)} %bitcast.18.in_ref), custom_call_target="tpu_custom_call" | custom-call | flops 1006632960 | bytes 4456448 | tf_op jit(solution)/shard_map/pallas_call | solution.py:53
  86.2 6.5 %collective-permute-done.9 = bf16[80,1920]{1,0:T(8,128)(2,1)} collective-permute-done((bf16[80,1920]{1,0:T(8,128)(2,1)S(1)}, bf16[80,1920]{1,0:T(8,128)(2,1)}, u32[]{:S(2)}, u32[]{:S(2)}) %collective-permute-start.9) | collective-permute-done | bytes 307232 | tf_op jit(solution)/shard_map/ppermute | solution.py:391
  93.9 4.1 %collective-permute-start.11 = (bf16[80,1920]{1,0:T(8,128)(2,1)S(1)}, bf16[80,1920]{1,0:T(8,128)(2,1)S(1)}, u32[]{:S(2)}, u32[]{:S(2)}) collective-permute-start(bf16[80,1920]{1,0:T(8,128)(2,1)S(1)} %add_convert_fusion.refs_0_), channel_id=1, source_target_pairs={{0,8},{1,9},{2,10},{3,11},{4,12},{5,13},{6,14},{7,15},{8,0},{9,1},... | collective-permute-start | bytes 921608 | tf_op jit(solution)/shard_map/ppermute | solution.py:391
  98.1 21.6 %collective-permute-done.10.refs_1_ = bf16[80,1920]{1,0:T(8,128)(2,1)S(1)} collective-permute-done((bf16[80,1920]{1,0:T(8,128)(2,1)S(1)}, bf16[80,1920]{1,0:T(8,128)(2,1)S(1)}, u32[]{:S(2)}, u32[]{:S(2)}) %collective-permute-start.10) | collective-permute-done | bytes 307232 | tf_op jit(solution)/shard_map/ppermute | solution.py:391
  120.4 7.7 %collective-permute-done.12.refs_3_ = bf16[80,1920]{1,0:T(8,128)(2,1)} collective-permute-done((bf16[80,1920]{1,0:T(8,128)(2,1)S(1)}, bf16[80,1920]{1,0:T(8,128)(2,1)}, u32[]{:S(2)}, u32[]{:S(2)}) %collective-permute-start.12) | collective-permute-done | bytes 307232 | tf_op jit(solution)/shard_map/ppermute | solution.py:391
  130.0 7.5 %shard_map.88.fast_ref = f32[512,640]{1,0:T(8,128)} custom-call(s32[16]{0:T(128)} %stack.67.place_ref, bf16[3,640,640]{2,1,0:T(8,128)(2,1)} %bitcast.23, bf16[512,640]{1,0:T(8,128)(2,1)} %get-tuple-element.23.query_ref, bf16[80,1920]{1,0:T(8,128)(2,1)} %copy-done.2, bf16[80,1920]{1,0:T(8,128)(2,1)} %copy-done.5, bf16[80,1920]{1,0:T(8,128)(2,1)} %copy-done.6, ...), custom_call_target="tpu_custom_call" | custom-call | flops 1258291200 | bytes 6881344 | tf_op jit(solution)/shard_map/pallas_call | solution.py:53
  138.6 10.0 %shard_map.85 = (f32[512,640]{1,0:T(8,128)}, f32[512,128]{1,0:T(8,128)}) custom-call(s32[16]{0:T(128)} %stack.67.place_ref, bf16[512,640]{1,0:T(8,128)(2,1)} %get-tuple-element.23.query_ref, s32[8,512]{1,0:T(8,128)} %reshape.18.ids_ref, bf16[512,1280]{1,0:T(8,128)(2,1)} %get-tuple-element.24.key_ref.value_ref, ...), custom_call_target="tpu_custom_call" | custom-call | flops 1006632960 | bytes 7487552 | tf_op jit(solution)/shard_map/pallas_call | solution.py:53
  149.8 8.5 %shard_map.89 = (bf16[128,640]{1,0:T(8,128)(2,1)}, bf16[128,640]{1,0:T(8,128)(2,1)}, bf16[128,640]{1,0:T(8,128)(2,1)}, bf16[128,640]{1,0:T(8,128)(2,1)}) custom-call(s32[16]{0:T(128)} %stack.67.place_ref, bf16[512,640]{1,0:T(8,128)(2,1)} %get-tuple-element.23.query_ref, s32[8,512]{1,0:T(8,128)} %reshape.18.ids_ref, f32[512,640]{1,0:T(8,128)} %get-tuple-element.25.near_ref, ...), custom_call_target="tpu_custom_call" | custom-call | flops 503316480 | bytes 6832192 | tf_op jit(solution)/shard_map/pallas_call | solution.py:53
  163.8 2.3 %collective-permute-done.19.refs_1_ = bf16[128,640]{1,0:T(8,128)(2,1)S(1)} collective-permute-done((bf16[128,640]{1,0:T(8,128)(2,1)}, bf16[128,640]{1,0:T(8,128)(2,1)S(1)}, u32[]{:S(2)}, u32[]{:S(2)}) %collective-permute-start.19) | collective-permute-done | bytes 163872 | tf_op jit(solution)/shard_map/ppermute | solution.py:391
  166.0 3.1 %collective-permute-done.20.refs_2_ = bf16[128,640]{1,0:T(8,128)(2,1)S(1)} collective-permute-done((bf16[128,640]{1,0:T(8,128)(2,1)}, bf16[128,640]{1,0:T(8,128)(2,1)S(1)}, u32[]{:S(2)}, u32[]{:S(2)}) %collective-permute-start.20) | collective-permute-done | bytes 163872 | tf_op jit(solution)/shard_map/ppermute | solution.py:391
  171.4 2.4 %shard_map.90 = bf16[128,2560]{1,0:T(8,128)(2,1)} custom-call(s32[16]{0:T(128)} %stack.67.place_ref, bf16[128,640]{1,0:T(8,128)(2,1)} %copy-done.8, bf16[128,640]{1,0:T(8,128)(2,1)} %copy-done.9, bf16[128,640]{1,0:T(8,128)(2,1)} %copy-done.10, bf16[128,640]{1,0:T(8,128)(2,1)} %copy-done.11, f32[1,2560]{1,0:T(1,128)} %reshape.19.refs_4_), custom_call_target="tpu_custom_call" | custom-call | flops 1966080 | bytes 1321024 | tf_op jit(solution)/shard_map/pallas_call | solution.py:53
  (75 shorter events, 25.8 us)
Async XLA Ops:
  3.8 77.4 %all-to-all-start = ((bf16[32,16,1920]{2,1,0:T(8,128)(2,1)}), bf16[32,16,1920]{2,1,0:T(8,128)(2,1)}, u32[]{:S(2)}, u32[]{:S(2)}) async-start(bf16[32,16,1920]{2,1,0:T(8,128)(2,1)} %bitcast.24), calls=%async_computation | async-start | bytes 3932160 | tf_op jit(solution)/shard_map/all_to_all | solution.py:448
  15.4 3.7 %collective-permute-start.5 = (bf16[128,768]{1,0:T(8,128)(2,1)}, bf16[128,768]{1,0:T(8,128)(2,1)S(1)}, u32[]{:S(2)}, u32[]{:S(2)}) collective-permute-start(bf16[128,768]{1,0:T(8,128)(2,1)} %get-tuple-element.32), channel_id=1, source_target_pairs={{0,1},{1,0},{2,3},{3,2},{4,5},{5,4},{6,7},{7,6},{8,9},{9,8},{10,11... | collective-permute-start | bytes 589832 | tf_op jit(solution)/shard_map/ppermute | solution.py:391
  15.6 15.9 %collective-permute-start.6 = (bf16[128,768]{1,0:T(8,128)(2,1)}, bf16[128,768]{1,0:T(8,128)(2,1)S(1)}, u32[]{:S(2)}, u32[]{:S(2)}) collective-permute-start(bf16[128,768]{1,0:T(8,128)(2,1)} %get-tuple-element.33), channel_id=1, source_target_pairs={{0,2},{1,3},{2,0},{3,1},{4,6},{5,7},{6,4},{7,5},{8,10},{9,11},{10,... | collective-permute-start | bytes 589832 | tf_op jit(solution)/shard_map/ppermute | solution.py:391
  17.2 23.1 %collective-permute-start.7 = (bf16[128,768]{1,0:T(8,128)(2,1)}, bf16[128,768]{1,0:T(8,128)(2,1)S(1)}, u32[]{:S(2)}, u32[]{:S(2)}) collective-permute-start(bf16[128,768]{1,0:T(8,128)(2,1)} %get-tuple-element.34), channel_id=1, source_target_pairs={{0,3},{1,2},{2,1},{3,0},{4,7},{5,6},{6,5},{7,4},{8,11},{9,10},{10,... | collective-permute-start | bytes 589832 | tf_op jit(solution)/shard_map/ppermute | solution.py:391
  17.3 29.1 %collective-permute-start.1 = (bf16[128,768]{1,0:T(8,128)(2,1)}, bf16[128,768]{1,0:T(8,128)(2,1)S(1)}, u32[]{:S(2)}, u32[]{:S(2)}) collective-permute-start(bf16[128,768]{1,0:T(8,128)(2,1)} %get-tuple-element.27), channel_id=1, source_target_pairs={{0,4},{1,5},{2,6},{3,7},{4,0},{5,1},{6,2},{7,3},{8,12},{9,13},{10,... | collective-permute-start | bytes 589832 | tf_op jit(solution)/shard_map/ppermute | solution.py:391
  19.0 27.4 %collective-permute-start.2 = (bf16[128,768]{1,0:T(8,128)(2,1)}, bf16[128,768]{1,0:T(8,128)(2,1)S(1)}, u32[]{:S(2)}, u32[]{:S(2)}) collective-permute-start(bf16[128,768]{1,0:T(8,128)(2,1)} %get-tuple-element.28), channel_id=1, source_target_pairs={{0,5},{1,4},{2,7},{3,6},{4,1},{5,0},{6,3},{7,2},{8,13},{9,12},{10,... | collective-permute-start | bytes 589832 | tf_op jit(solution)/shard_map/ppermute | solution.py:391
  19.1 27.4 %collective-permute-start.3 = (bf16[128,768]{1,0:T(8,128)(2,1)}, bf16[128,768]{1,0:T(8,128)(2,1)}, u32[]{:S(2)}, u32[]{:S(2)}) collective-permute-start(bf16[128,768]{1,0:T(8,128)(2,1)} %get-tuple-element.29), channel_id=1, source_target_pairs={{0,6},{1,7},{2,4},{3,5},{4,2},{5,3},{6,0},{7,1},{8,14},{9,15},{10,... | collective-permute-start | bytes 589832 | tf_op jit(solution)/shard_map/ppermute | solution.py:391
  31.5 19.1 %collective-permute-start.4 = (bf16[128,768]{1,0:T(8,128)(2,1)}, bf16[128,768]{1,0:T(8,128)(2,1)}, u32[]{:S(2)}, u32[]{:S(2)}) collective-permute-start(bf16[128,768]{1,0:T(8,128)(2,1)} %get-tuple-element.30), channel_id=1, source_target_pairs={{0,7},{1,6},{2,5},{3,4},{4,3},{5,2},{6,1},{7,0},{8,15},{9,14},{10,... | collective-permute-start | bytes 589832 | tf_op jit(solution)/shard_map/ppermute | solution.py:391
  56.8 16.7 %collective-permute-start.8 = (bf16[160,1920]{1,0:T(8,128)(2,1)}, bf16[160,1920]{1,0:T(8,128)(2,1)S(1)}, u32[]{:S(2)}, u32[]{:S(2)}) collective-permute-start(bf16[160,1920]{1,0:T(8,128)(2,1)} %get-tuple-element.36), channel_id=1, source_target_pairs={{0,8},{1,9},{2,10},{3,11},{4,12},{5,13},{6,14},{7,15},{8,0},{9,1},... | collective-permute-start | bytes 1843208 | tf_op jit(solution)/shard_map/ppermute | solution.py:391
  74.7 17.9 %collective-permute-start.9 = (bf16[80,1920]{1,0:T(8,128)(2,1)S(1)}, bf16[80,1920]{1,0:T(8,128)(2,1)}, u32[]{:S(2)}, u32[]{:S(2)}) collective-permute-start(bf16[80,1920]{1,0:T(8,128)(2,1)S(1)} %add_convert_fusion.1), channel_id=1, source_target_pairs={{0,16},{1,17},{2,18},{3,19},{4,20},{5,21},{6,22},{7,23},{8,24},{9,... | collective-permute-start | bytes 921608 | tf_op jit(solution)/shard_map/ppermute | solution.py:391
  85.2 52.3 %collective-permute-start = (bf16[512,1280]{1,0:T(8,128)(2,1)}, bf16[512,1280]{1,0:T(8,128)(2,1)S(1)}, u32[]{:S(2)}, u32[]{:S(2)}) collective-permute-start(bf16[512,1280]{1,0:T(8,128)(2,1)} %get-tuple-element.24.key_ref.value_ref), channel_id=1, source_target_pairs={{0,1},{1,0},{2,3},{3,2},{4,5},{5,4},{6,7},{7,6},{8,9},{9,8},{10,11... | collective-permute-start | bytes 3932168 | tf_op jit(solution)/shard_map/ppermute | solution.py:391
  85.3 63.4 %collective-permute-start.17 = (bf16[512,1280]{1,0:T(8,128)(2,1)}, bf16[512,1280]{1,0:T(8,128)(2,1)S(1)}, u32[]{:S(2)}, u32[]{:S(2)}) collective-permute-start(bf16[512,1280]{1,0:T(8,128)(2,1)} %get-tuple-element.24.key_ref.value_ref), channel_id=1, source_target_pairs={{1,8},{3,10},{5,12},{7,14},{8,1},{9,16},{10,3},{11,18},{12,5},{13,... | collective-permute-start | bytes 3932168 | tf_op jit(solution)/shard_map/ppermute | solution.py:391
  93.8 36.2 %copy-start.2 = (bf16[80,1920]{1,0:T(8,128)(2,1)}, bf16[80,1920]{1,0:T(8,128)(2,1)S(1)}, u32[]{:S(2)}) copy-start(bf16[80,1920]{1,0:T(8,128)(2,1)S(1)} %add_convert_fusion.refs_0_) | copy-start | bytes 921604
  93.9 25.8 %collective-permute-start.10 = (bf16[80,1920]{1,0:T(8,128)(2,1)S(1)}, bf16[80,1920]{1,0:T(8,128)(2,1)S(1)}, u32[]{:S(2)}, u32[]{:S(2)}) collective-permute-start(bf16[80,1920]{1,0:T(8,128)(2,1)S(1)} %add_convert_fusion.refs_0_), channel_id=1, source_target_pairs={{0,16},{1,17},{2,18},{3,19},{4,20},{5,21},{6,22},{7,23},{8,24},{9,... | collective-permute-start | bytes 921608 | tf_op jit(solution)/shard_map/ppermute | solution.py:391
  93.9 25.7 %collective-permute-start.11 = (bf16[80,1920]{1,0:T(8,128)(2,1)S(1)}, bf16[80,1920]{1,0:T(8,128)(2,1)S(1)}, u32[]{:S(2)}, u32[]{:S(2)}) collective-permute-start(bf16[80,1920]{1,0:T(8,128)(2,1)S(1)} %add_convert_fusion.refs_0_), channel_id=1, source_target_pairs={{0,8},{1,9},{2,10},{3,11},{4,12},{5,13},{6,14},{7,15},{8,0},{9,1},... | collective-permute-start | bytes 921608 | tf_op jit(solution)/shard_map/ppermute | solution.py:391
  98.1 22.2 %collective-permute-start.13 = (bf16[80,1920]{1,0:T(8,128)(2,1)S(1)}, bf16[80,1920]{1,0:T(8,128)(2,1)S(1)}, u32[]{:S(2)}, u32[]{:S(2)}) collective-permute-start(bf16[80,1920]{1,0:T(8,128)(2,1)S(1)} %add_convert_fusion.refs_0_), channel_id=1, source_target_pairs={{0,1},{1,0},{2,3},{3,2},{4,5},{5,4},{6,7},{7,6},{8,9},{9,8},{10,11... | collective-permute-start | bytes 921608 | tf_op jit(solution)/shard_map/ppermute | solution.py:391
  119.7 8.4 %collective-permute-start.12 = (bf16[80,1920]{1,0:T(8,128)(2,1)S(1)}, bf16[80,1920]{1,0:T(8,128)(2,1)}, u32[]{:S(2)}, u32[]{:S(2)}) collective-permute-start(bf16[80,1920]{1,0:T(8,128)(2,1)S(1)} %collective-permute-done.10.refs_1_), channel_id=1, source_target_pairs={{0,8},{1,9},{2,10},{3,11},{4,12},{5,13},{6,14},{7,15},{8,0},{9,1},... | collective-permute-start | bytes 921608 | tf_op jit(solution)/shard_map/ppermute | solution.py:391
  119.7 9.7 %collective-permute-start.14 = (bf16[80,1920]{1,0:T(8,128)(2,1)S(1)}, bf16[80,1920]{1,0:T(8,128)(2,1)}, u32[]{:S(2)}, u32[]{:S(2)}) collective-permute-start(bf16[80,1920]{1,0:T(8,128)(2,1)S(1)} %collective-permute-done.10.refs_1_), channel_id=1, source_target_pairs={{0,1},{1,0},{2,3},{3,2},{4,5},{5,4},{6,7},{7,6},{8,9},{9,8},{10,11... | collective-permute-start | bytes 921608 | tf_op jit(solution)/shard_map/ppermute | solution.py:391
  120.3 9.1 %collective-permute-start.15 = (bf16[80,1920]{1,0:T(8,128)(2,1)S(1)}, bf16[80,1920]{1,0:T(8,128)(2,1)}, u32[]{:S(2)}, u32[]{:S(2)}) collective-permute-start(bf16[80,1920]{1,0:T(8,128)(2,1)S(1)} %collective-permute-done.11.refs_2_), channel_id=1, source_target_pairs={{0,1},{1,0},{2,3},{3,2},{4,5},{5,4},{6,7},{7,6},{8,9},{9,8},{10,11... | collective-permute-start | bytes 921608 | tf_op jit(solution)/shard_map/ppermute | solution.py:391
  128.1 1.9 %collective-permute-start.16 = (bf16[80,1920]{1,0:T(8,128)(2,1)}, bf16[80,1920]{1,0:T(8,128)(2,1)}, u32[]{:S(2)}, u32[]{:S(2)}) collective-permute-start(bf16[80,1920]{1,0:T(8,128)(2,1)} %collective-permute-done.12.refs_3_), channel_id=1, source_target_pairs={{0,1},{1,0},{2,3},{3,2},{4,5},{5,4},{6,7},{7,6},{8,9},{9,8},{10,11... | collective-permute-start | bytes 921608 | tf_op jit(solution)/shard_map/ppermute | solution.py:391
  158.2 5.5 %collective-permute-start.18 = (bf16[128,640]{1,0:T(8,128)(2,1)}, bf16[128,640]{1,0:T(8,128)(2,1)S(1)}, u32[]{:S(2)}, u32[]{:S(2)}) collective-permute-start(bf16[128,640]{1,0:T(8,128)(2,1)} %get-tuple-element.37), channel_id=1, source_target_pairs={{0,0},{1,4},{2,2},{3,6},{4,1},{5,5},{6,3},{7,7},{8,8},{9,12},{10,1... | collective-permute-start | bytes 491528 | tf_op jit(solution)/shard_map/ppermute | solution.py:391
  159.8 6.2 %collective-permute-start.19 = (bf16[128,640]{1,0:T(8,128)(2,1)}, bf16[128,640]{1,0:T(8,128)(2,1)S(1)}, u32[]{:S(2)}, u32[]{:S(2)}) collective-permute-start(bf16[128,640]{1,0:T(8,128)(2,1)} %get-tuple-element.38), channel_id=1, source_target_pairs={{0,2},{1,6},{2,0},{3,4},{4,3},{5,7},{6,1},{7,5},{8,10},{9,14},{10,... | collective-permute-start | bytes 491528 | tf_op jit(solution)/shard_map/ppermute | solution.py:391
  161.0 8.1 %collective-permute-start.20 = (bf16[128,640]{1,0:T(8,128)(2,1)}, bf16[128,640]{1,0:T(8,128)(2,1)S(1)}, u32[]{:S(2)}, u32[]{:S(2)}) collective-permute-start(bf16[128,640]{1,0:T(8,128)(2,1)} %get-tuple-element.39), channel_id=1, source_target_pairs={{0,1},{1,5},{2,3},{3,7},{4,0},{5,4},{6,2},{7,6},{8,9},{9,13},{10,1... | collective-permute-start | bytes 491528 | tf_op jit(solution)/shard_map/ppermute | solution.py:391
  162.8 7.9 %collective-permute-start.21 = (bf16[128,640]{1,0:T(8,128)(2,1)}, bf16[128,640]{1,0:T(8,128)(2,1)S(1)}, u32[]{:S(2)}, u32[]{:S(2)}) collective-permute-start(bf16[128,640]{1,0:T(8,128)(2,1)} %get-tuple-element.40), channel_id=1, source_target_pairs={{0,3},{1,7},{2,1},{3,5},{4,2},{5,6},{6,0},{7,4},{8,11},{9,15},{10,... | collective-permute-start | bytes 491528 | tf_op jit(solution)/shard_map/ppermute | solution.py:391
  (17 other events, 112.6 us)

commit v6 on v5

--- a/solution.py
+++ b/solution.py
@@ -45,7 +45,7 @@
     return jnp.sum(jnp.where(diagonal, square, 0.0), axis=1, keepdims=True)
 
 
-def call(kernel, outs, ins, scratch=(), smem=0, flops=0, grid=None, in_specs=None, out_specs=None):
+def call(kernel, outs, ins, scratch=(), smem=0, flops=0, grid=None, in_specs=None, out_specs=None, limit=60):
     specs = [pl.BlockSpec(memory_space=pltpu.SMEM)] * smem
     specs += in_specs or [pl.BlockSpec(memory_space=VMEM)] * (len(ins) - smem)
     moved = sum(x.size * x.dtype.itemsize for x in list(ins) + list(outs))
@@ -56,7 +56,7 @@
         in_specs=specs,
         out_specs=out_specs or [pl.BlockSpec(memory_space=VMEM)] * len(outs),
         scratch_shapes=list(scratch),
-        compiler_params=pltpu.CompilerParams(vmem_limit_bytes=60 << 20),
+        compiler_params=pltpu.CompilerParams(vmem_limit_bytes=limit << 20),
         cost_estimate=pl.CostEstimate(flops=flops, bytes_accessed=moved, transcendentals=0),
         **extra,
     )(*ins)
@@ -67,44 +67,13 @@
     return begin, head * HEAD_DIM - begin
 
 
-def heads_kernel(place_ref, rate_ref, key_ref, value_ref, *out_refs):
-    n, width = key_ref.shape
+def front_kernel(group_shift, slots, place_ref, order_ref, rate_ref, query_ref, key_ref, value_ref, *refs):
+    out_ref, head_refs, choose_buf = refs[0], refs[1:-1], refs[-1]
+    n, _ = key_ref.shape
+    planes, together, cores = out_ref.shape[:3]
     step, part, core = pl.program_id(0), place_ref[1], place_ref[2]
-    lane = iota((n, SPAN), 1)
-    for local in range(width // PART_WIDTH):
-        index = step * (width // PART_WIDTH) + local
-        own_part = index ^ part
-        edge = lax.rem(own_part, width // PART_WIDTH) * PART_WIDTH
-        rows = []
-        for head in range(PART_FAST):
-            begin, offset = window_of(head)
-
-            def window(ref):
-                rows = ref[:, pl.ds(pl.multiple_of(edge + begin, LANES), SPAN)].astype(F32)
-                rows = pltpu.roll(rows, SPAN - offset, 1) if offset else rows
-                return jnp.where(lane < HEAD_DIM, rows, 0.0)
-
-            rate = column_of(rate_ref[pl.ds(own_part * PART_FAST + head, 1), :])
-            keys = window(key_ref)
-            for third in range(3):
-                piece = rate.astype(BF16).astype(F32)
-                rate = rate - piece
-                keys = jnp.where(lane == HEAD_DIM + third, piece, keys)
-            rows.append((keys, window(value_ref)))
-        for flip in range(PART_FAST):
-            chosen = [jnp.where(core == flip, first, second).astype(BF16) for first, second in zip(*rows)]
-            for at in range(local, PARTS, width // PART_WIDTH):
-                @pl.when(step == at // (width // PART_WIDTH))
-                def _():
-                    out_refs[at * PART_FAST + flip][:, :SPAN] = chosen[0]
-                    out_refs[at * PART_FAST + flip][:, SPAN:] = chosen[1]
-
-
-def pack_kernel(group_shift, slots, place_ref, order_ref, query_ref, key_ref, value_ref, out_ref, choose_buf):
-    n = query_ref.shape[0]
-    planes, parts, cores = out_ref.shape[:3]
-
-    @pl.when(pl.program_id(0) == 0)
+
+    @pl.when(step == 0)
     def _():
         pos = order_ref[pl.ds(place_ref[0], 1), :]
         group = lax.shift_right_logical(pos, group_shift)
@@ -117,12 +86,40 @@
     choose = choose_buf[...]
     for index, ref in enumerate((key_ref, value_ref, query_ref)):
         lanes = slice(index * PART_WIDTH, (index + 1) * PART_WIDTH)
-        for part in range(parts):
-            rows = dot(choose, ref[:, part * PART_WIDTH : (part + 1) * PART_WIDTH]).astype(BF16)
+        for local in range(together):
+            rows = dot(choose, ref[:, local * PART_WIDTH : (local + 1) * PART_WIDTH]).astype(BF16)
             for plane in range(planes):
-                for core in range(cores):
-                    at = (plane * cores + core) * slots
-                    out_ref[plane, part, core, :, lanes] = rows[at : at + slots]
+                for at in range(cores):
+                    first = (plane * cores + at) * slots
+                    out_ref[plane, local, at, :, lanes] = rows[first : first + slots]
+
+    lane = iota((n, SPAN), 1)
+    tail = PART_WIDTH - SPAN
+    for local in range(together):
+        target_part = step * together + local
+        rows = []
+        for head in range(PART_FAST):
+            begin, offset = window_of(head)
+            span = slice(local * PART_WIDTH + begin, local * PART_WIDTH + begin + SPAN)
+            rate = column_of(rate_ref[pl.ds(target_part * PART_FAST + head, 1), :])
+            keys = key_ref[:, span].astype(F32)
+            targets = value_ref[:, span].astype(F32) * rate
+            turn = SPAN - HEAD_DIM
+            if offset:
+                keys = pltpu.roll(keys, SPAN - offset, 1)
+            if offset != turn:
+                targets = pltpu.roll(targets, turn - offset, 1)
+            rows.append((keys.astype(BF16), targets.astype(BF16)))
+        for flip in range(PART_FAST):
+            keys, targets = (jnp.where(core == flip, one, two) for one, two in zip(*rows))
+            middle = jnp.where(iota((n, LANES), 1) < HEAD_DIM - tail, keys[:, tail:], targets[:, : SPAN - tail])
+            for index in range(PARTS):
+                @pl.when((target_part ^ part) == index)
+                def _():
+                    ref = head_refs[index * PART_FAST + flip]
+                    ref[:, :tail] = keys[:, :tail]
+                    ref[:, tail:SPAN] = middle
+                    ref[:, SPAN:] = targets[:, SPAN - tail :]
 
 
 def arrival_choice(group_shift, slots, orders, group, n):
@@ -166,18 +163,16 @@
     n = key_buf.shape[0]
     hidden = weight_ref.shape[2]
     first = pl.multiple_of(place_ref[2] * HEAD_DIM, 16)
+    spare = SPAN - HEAD_DIM
     for index in range(3):
         lanes = slice(index * hidden, (index + 1) * hidden)
-        weight_buf[:HEAD_DIM, lanes] = weight_ref[index, pl.ds(first, HEAD_DIM), :]
-    weight_buf[HEAD_DIM:, :] = jnp.zeros((SPAN - HEAD_DIM, 3 * hidden), BF16)
-    lane = iota((1, SPAN), 1)
-    wanted = (lane >= HEAD_DIM) & (lane < HEAD_DIM + 3)
+        begin, blank = (0, HEAD_DIM) if index < 2 else (spare, 0)
+        weight_buf[begin : begin + HEAD_DIM, lanes] = weight_ref[index, pl.ds(first, HEAD_DIM), :]
+        weight_buf[blank : blank + spare, lanes] = jnp.zeros((spare, hidden), BF16)
     for index, ref in enumerate(kv_refs):
         here = pl.ds(index * block, block)
-        key = ref[:, :SPAN]
-        rate = jnp.sum(jnp.where(wanted, key.astype(F32), 0.0), axis=1, keepdims=True)
-        key_buf[here, :] = key
-        target_buf[here, :] = (ref[:, SPAN:].astype(F32) * rate).astype(BF16)
+        key_buf[here, :] = ref[:, :SPAN]
+        target_buf[here, :] = ref[:, PART_WIDTH - SPAN :]
     for at in range(0, n, chunk):
         here = pl.ds(at, chunk)
         both = dot(key_buf[here, :], weight_buf[:, : 2 * hidden])
@@ -188,9 +183,9 @@
         pr_buf[here, :] = (active * upward).astype(BF16)
         delta_buf[here, hidden:] = (backward * active).astype(BF16)
         delta_buf[here, :hidden] = (backward * upward * sigmoid * (1.0 + gate * (1.0 - sigmoid))).astype(BF16)
-    for left, right, begin in ((key_buf, delta_buf, 0), (target_buf, pr_buf, 2 * hidden)):
+    for left, right, begin, row in ((key_buf, delta_buf, 0, 0), (target_buf, pr_buf, 2 * hidden, spare)):
         lanes = slice(begin, begin + right.shape[1])
-        total = dot(left[...], right[...], ((0,), (0,)))[:HEAD_DIM]
+        total = dot(left[...], right[...], ((0,), (0,)))[row : row + HEAD_DIM]
         if last:
             sums[:, lanes] = (total + early_ref[:, lanes].astype(F32)).astype(BF16)
         else:
@@ -221,92 +216,89 @@
     return jnp.where((gap < WINDOW // 2) & (gap > -(WINDOW // 2)) & (own == ids), 0.0, -1e30)
 
 
-def near_kernel(block, place_ref, query_ref, ids_ref, key_ref, value_ref, chip_key_ref, chip_value_ref, out_ref, stat_ref, bias, chip_bias):
+def head_lanes(head):
+    return pl.ds(pl.multiple_of(head * ATT_DIM, ATT_DIM), ATT_DIM), pl.ds(pl.multiple_of(PART_WIDTH + head * ATT_DIM, ATT_DIM), ATT_DIM)
+
+
+def near_kernel(block, place_ref, query_ref, ids_ref, kv_ref, chip_ref, out_ref, stat_ref, bias, chip_bias):
     n = query_ref.shape[0]
     count = n // block
-    head = pl.program_id(0)
     core, group = place_ref[2], place_ref[3]
     second = core == 1
-
-    @pl.when(head == 0)
-    def _():
-        ids = ids_ref[pl.ds(group, 1), :]
+    ids = ids_ref[pl.ds(group, 1), :]
+    for index in range(count):
+        at = index * block
+        bias[at : at + block, :] = mask_of(column_of(ids[:, at : at + block]).astype(jnp.int32), ids, -at)
+    for index in range(count):
+        _, _, shift = reach(second, count - 1 - index, count, block)
+        size = (index + 1) * block
+        own = block_ids(ids, index, count, block, second)
+        other = ids_ref[pl.ds(group + 1 - 2 * core, 1), :]
+        other = jnp.where(second, other[:, n - size :], other[:, :size])
+        chip_bias[index, :, :size] = mask_of(own, other, shift)
+    stat_ref[...] = jnp.zeros_like(stat_ref)
+    lane = iota((block, LANES), 1)
+
+    @pl.loop(0, PART_ATT)
+    def _(head):
+        keys, values = head_lanes(head)
         for index in range(count):
-            at = index * block
-            bias[at : at + block, :] = mask_of(column_of(ids[:, at : at + block]).astype(jnp.int32), ids, -at)
-        for index in range(count):
-            _, _, shift = reach(second, count - 1 - index, count, block)
+            at, start, _ = reach(second, count - 1 - index, count, block)
             size = (index + 1) * block
-            own = block_ids(ids, index, count, block, second)
-            other = ids_ref[pl.ds(group + 1 - 2 * core, 1), :]
-            other = jnp.where(second, other[:, n - size :], other[:, :size])
-            chip_bias[index, :, :size] = mask_of(own, other, shift)
-        stat_ref[...] = jnp.zeros_like(stat_ref)
-
-    lane = iota((block, LANES), 1)
-    for index in range(count):
-        at, start, _ = reach(second, count - 1 - index, count, block)
-        size = (index + 1) * block
-        here, there = pl.ds(at, block), pl.ds(start, size)
-        query = query_ref[here, :]
-        score = dot(query, key_ref[...], ((1,), (1,))) + bias[here, :]
-        chip = dot(query, chip_key_ref[there, :], ((1,), (1,))) + chip_bias[index, :, :size]
-        peak = jnp.maximum(jnp.max(score, axis=1, keepdims=True), jnp.max(chip, axis=1, keepdims=True))
-        score = jnp.exp2((score - peak) * FACTOR)
-        chip = jnp.exp2((chip - peak) * FACTOR)
-        total = jnp.sum(score, axis=1, keepdims=True) + jnp.sum(chip, axis=1, keepdims=True)
-        out_ref[here, :] = dot(score.astype(BF16), value_ref[...]) + dot(chip.astype(BF16), chip_value_ref[there, :])
-        stat = jnp.where(lane == 2 * head, peak, stat_ref[here, :])
-        stat_ref[here, :] = jnp.where(lane == 2 * head + 1, total, stat)
-
-
-def far_kernel(block, first_goal, place_ref, query_ref, ids_ref, near_ref, stat_ref, fast_ref, key_ref, value_ref, *refs):
-    out_refs, (bias, rows_buf) = refs[:-2], refs[-2:]
+            here, there = pl.ds(at, block), pl.ds(start, size)
+            query = query_ref[here, keys]
+            score = dot(query, kv_ref[:, keys], ((1,), (1,))) + bias[here, :]
+            chip = dot(query, chip_ref[there, keys], ((1,), (1,))) + chip_bias[index, :, :size]
+            peak = jnp.maximum(jnp.max(score, axis=1, keepdims=True), jnp.max(chip, axis=1, keepdims=True))
+            score = jnp.exp2((score - peak) * FACTOR)
+            chip = jnp.exp2((chip - peak) * FACTOR)
+            total = jnp.sum(score, axis=1, keepdims=True) + jnp.sum(chip, axis=1, keepdims=True)
+            out_ref[here, keys] = dot(score.astype(BF16), kv_ref[:, values]) + dot(chip.astype(BF16), chip_ref[there, values])
+            stat = jnp.where(lane == 2 * head, peak, stat_ref[here, :])
+            stat_ref[here, :] = jnp.where(lane == 2 * head + 1, total, stat)
+
+
+def far_kernel(block, place_ref, query_ref, ids_ref, near_ref, stat_ref, kv_ref, out_ref, bias):
     n = query_ref.shape[0]
     count = n // block
-    head = pl.program_id(0)
     core, group = place_ref[2], place_ref[3]
     last = ids_ref.shape[0] - 1
     first = core == 0
-
-    @pl.when(head == 0)
-    def _():
-        beyond = group - 1 + 2 * core
-        exists = (beyond >= 0) & (beyond <= last)
-        ids = ids_ref[pl.ds(group, 1), :]
+    beyond = group - 1 + 2 * core
+    exists = (beyond >= 0) & (beyond <= last)
+    ids = ids_ref[pl.ds(group, 1), :]
+    for index in range(count):
+        _, _, shift = reach(first, index, count, block)
+        size = n - index * block
+        own = block_ids(ids, index, count, block, core == 1)
+        other = ids_ref[pl.ds(jnp.clip(beyond, 0, last), 1), :]
+        other = jnp.where(first, other[:, n - size :], other[:, :size])
+        bias[index, :, :size] = mask_of(own, jnp.where(exists, other, -1), shift)
+    lane = iota((block, LANES), 1)
+
+    @pl.loop(0, PART_ATT)
+    def _(head):
+        keys, values = head_lanes(head)
         for index in range(count):
-            _, _, shift = reach(first, index, count, block)
+            at, start, _ = reach(first, index, count, block)
             size = n - index * block
-            own = block_ids(ids, index, count, block, core == 1)
-            other = ids_ref[pl.ds(jnp.clip(beyond, 0, last), 1), :]
-            other = jnp.where(first, other[:, n - size :], other[:, :size])
-            bias[index, :, :size] = mask_of(own, jnp.where(exists, other, -1), shift)
-
-    lane = iota((block, LANES), 1)
-    for index in range(count):
-        at, start, _ = reach(first, index, count, block)
-        size = n - index * block
-        here, there = pl.ds(at, block), pl.ds(start, size)
-        score = dot(query_ref[here, :], key_ref[there, :], ((1,), (1,))) + bias[index, :, :size]
-        stat = stat_ref[here, :]
-        old_peak = jnp.sum(jnp.where(lane == 2 * head, stat, 0.0), axis=1, keepdims=True)
-        old_total = jnp.sum(jnp.where(lane == 2 * head + 1, stat, 0.0), axis=1, keepdims=True)
-        peak = jnp.maximum(jnp.max(score, axis=1, keepdims=True), old_peak)
-        keep = jnp.exp2((old_peak - peak) * FACTOR)
-        score = jnp.exp2((score - peak) * FACTOR)
-        total = old_total * keep + jnp.sum(score, axis=1, keepdims=True)
-        mixed = near_ref[here, :] * keep + dot(score.astype(BF16), value_ref[there, :])
-        rows_buf[here, :] = (mixed / total + fast_ref[here, :]).astype(BF16)
-    rows = out_refs[0].shape[0]
-    for index, ref in enumerate(out_refs):
-        begin = pl.multiple_of(place_ref[first_goal + index] * rows, rows)
-        ref[...] = rows_buf[pl.ds(begin, rows), :]
-
-
-def apply_kernel(place_ref, weight_ref, query_ref, *refs):
+            here, there = pl.ds(at, block), pl.ds(start, size)
+            score = dot(query_ref[here, keys], kv_ref[there, keys], ((1,), (1,))) + bias[index, :, :size]
+            stat = stat_ref[here, :]
+            old_peak = jnp.sum(jnp.where(lane == 2 * head, stat, 0.0), axis=1, keepdims=True)
+            old_total = jnp.sum(jnp.where(lane == 2 * head + 1, stat, 0.0), axis=1, keepdims=True)
+            peak = jnp.maximum(jnp.max(score, axis=1, keepdims=True), old_peak)
+            keep = jnp.exp2((old_peak - peak) * FACTOR)
+            score = jnp.exp2((score - peak) * FACTOR)
+            total = old_total * keep + jnp.sum(score, axis=1, keepdims=True)
+            mixed = near_ref[here, keys] * keep + dot(score.astype(BF16), kv_ref[there, values])
+            out_ref[here, keys] = mixed / total
+
+
+def apply_kernel(place_ref, weight_ref, query_ref, attended_ref, *refs):
     hidden = weight_ref.shape[2]
-    out_ref, fresh, scales = refs[-3:]
-    count = (len(refs) - 3) // 2
+    out_refs, (fresh, scales, rows_buf) = refs[-3 - PARTS : -3], refs[-3:]
+    count = (len(refs) - 3 - PARTS) // 2
     mine_refs, other_refs = refs[:count], refs[count : 2 * count]
     piece = mine_refs[0].shape[0]
     core = place_ref[2]
@@ -340,7 +332,11 @@
         parts.append((begin, dot(product, fresh[head, 2], ((1,), (1,)))))
     for lane in range(0, PART_WIDTH, LANES):
         inside = [value[:, lane - begin : lane - begin + LANES] for begin, value in parts if begin <= lane < begin + SPAN]
-        out_ref[:, lane : lane + LANES] = functools.reduce(jnp.add, inside)
+        rows_buf[:, lane : lane + LANES] = functools.reduce(jnp.add, inside, attended_ref[:, lane : lane + LANES]).astype(BF16)
+    block = out_refs[0].shape[0]
+    for index, ref in enumerate(out_refs):
+        begin = pl.multiple_of(place_ref[4 + PARTS + count + index] * block, block)
+        ref[...] = rows_buf[pl.ds(begin, block), :]
 
 
 def norm_kernel(place_ref, *refs):
@@ -414,37 +410,25 @@
     full = lambda a: pl.BlockSpec(a.shape, lambda h: (0,) * a.ndim)
     steps = 2
     together = PARTS // steps
-    other_cut = pl.BlockSpec((tok_dev, WIDTH // steps), lambda h, place: (0, h ^ place[1] // together))
-    whole = lambda shape: pl.BlockSpec(shape, lambda h, place: (0,) * len(shape))
-    heads_out = pl.pallas_call(
-        heads_kernel,
-        out_shape=[jax.ShapeDtypeStruct((tok_dev, 2 * SPAN), BF16)] * plane_size,
-        grid_spec=pltpu.PrefetchScalarGridSpec(
-            num_scalar_prefetch=1,
-            grid=(steps,),
-            in_specs=[whole(learn_rates.shape[::-1]), other_cut, other_cut],
-            out_specs=[whole((tok_dev, 2 * SPAN))] * plane_size,
-        ),
-        compiler_params=pltpu.CompilerParams(vmem_limit_bytes=60 << 20),
-        cost_estimate=pl.CostEstimate(flops=tok_dev * WIDTH, bytes_accessed=8 * tok_dev * WIDTH, transcendentals=0),
-        name="heads",
-    )(place, learn_rates.T, key_rows, value_rows)
+    orders = frame_order.reshape(sections, tok_dev)
+    rates = learn_rates.T
+    cut = pl.BlockSpec((tok_dev, WIDTH // steps), lambda h: (0, h))
+    head_shape = jax.ShapeDtypeStruct((tok_dev, 2 * HEAD_DIM), BF16)
+    packed, *heads_out = call(
+        functools.partial(front_kernel, group_shift, slots),
+        [jax.ShapeDtypeStruct((planes, PARTS, PART_FAST, slots, 3 * PART_WIDTH), BF16)] + [head_shape] * plane_size,
+        [place, orders, rates, queries, key_rows, value_rows],
+        in_specs=[full(orders), full(rates), cut, cut, cut],
+        out_specs=[pl.BlockSpec((planes, together, PART_FAST, slots, 3 * PART_WIDTH), lambda h: (0, h, 0, 0, 0))]
+        + [full(head_shape)] * plane_size,
+        grid=(steps,),
+        scratch=[VMEM((tok_dev, tok_dev), BF16)],
+        smem=1, flops=2 * tok_dev * tok_dev * 3 * WIDTH,
+    )
     heads_in = [heads_out[0]]
     for j in range(1, plane_size):
         heads_in.append(permute(heads_out[j], lambda z, y, x, c, j=j: (z, y ^ j >> 2, x ^ j >> 1 & 1, c ^ j & 1)))
 
-    orders = frame_order.reshape(sections, tok_dev)
-    cut = pl.BlockSpec((tok_dev, WIDTH // steps), lambda h: (0, h))
-    (packed,) = call(
-        functools.partial(pack_kernel, group_shift, slots),
-        [jax.ShapeDtypeStruct((planes, PARTS, PART_FAST, slots, 3 * PART_WIDTH), BF16)],
-        [place, orders, queries, key_rows, value_rows],
-        in_specs=[full(orders), cut, cut, cut],
-        out_specs=[pl.BlockSpec((planes, together, PART_FAST, slots, 3 * PART_WIDTH), lambda h: (0, h, 0, 0, 0))],
-        grid=(steps,),
-        scratch=[VMEM((tok_dev, tok_dev), BF16)],
-        smem=1, flops=2 * tok_dev * tok_dev * 3 * WIDTH,
-    )
     arrived = lax.all_to_all(
         packed.reshape(sections, slots, 3 * PART_WIDTH), "tok", split_axis=0, concat_axis=0, tiled=True
     ).reshape(group_rows, 3 * PART_WIDTH)
@@ -513,42 +497,35 @@
         pieces_other.append(permute(held, swap))
 
     block = min(LANES, group_rows)
-    lane_block = lambda rows, shift: pl.BlockSpec((rows, ATT_DIM), lambda h: (0, h + shift))
+    count = group_rows // block
     ids = window_ids.reshape(groups, group_rows)
     wide = jax.ShapeDtypeStruct((group_rows, PART_WIDTH), F32)
-    stat_shape = jax.ShapeDtypeStruct((group_rows, LANES), F32)
-    count = group_rows // block
     assert 2 * PART_ATT <= LANES
-    keys, values = lane_block(group_rows, 0), lane_block(group_rows, PART_ATT)
     near_mixed, stats = call(
         functools.partial(near_kernel, block),
-        [wide, stat_shape],
-        [place, query_seq, ids, kv_seq, kv_seq, kv_chip, kv_chip],
-        in_specs=[lane_block(group_rows, 0), full(ids), keys, values, keys, values],
-        out_specs=[lane_block(group_rows, 0), full(stat_shape)],
-        grid=(PART_ATT,),
+        [wide, jax.ShapeDtypeStruct((group_rows, LANES), F32)],
+        [place, query_seq, ids, kv_seq, kv_chip],
         scratch=[VMEM((group_rows, group_rows), F32), VMEM((count, block, group_rows), F32)],
-        smem=1, flops=6 * group_rows * group_rows * PART_WIDTH,
-    )
-
-    (fast_out,) = call(
+        smem=1, flops=6 * group_rows * group_rows * PART_WIDTH, limit=24,
+    )
+    (attended,) = call(
+        functools.partial(far_kernel, block),
+        [wide],
+        [place, query_seq, ids, near_mixed, stats, kv_far],
+        scratch=[VMEM((count, block, group_rows), F32)],
+        smem=1, flops=3 * group_rows * group_rows * PART_WIDTH, limit=24,
+    )
+
+    blocks = call(
         apply_kernel,
-        [wide],
-        [place, weights, query_seq] + pieces + pieces_other,
-        scratch=[VMEM((PART_FAST, 3, SPAN, hidden), BF16), VMEM((PART_FAST * 3, hidden), F32)],
-        smem=1, flops=6 * group_rows * PART_WIDTH * hidden,
-    )
-
-    blocks = call(
-        functools.partial(far_kernel, block, 4 + PARTS + len(starts)),
         [jax.ShapeDtypeStruct((tok_dev, PART_WIDTH), BF16)] * PARTS,
-        [place, query_seq, ids, near_mixed, stats, fast_out, kv_far, kv_far],
-        in_specs=[lane_block(group_rows, 0), full(ids), lane_block(group_rows, 0), full(stats)]
-        + [lane_block(group_rows, 0), keys, values],
-        out_specs=[lane_block(tok_dev, 0)] * PARTS,
-        grid=(PART_ATT,),
-        scratch=[VMEM((count, block, group_rows), F32), VMEM((group_rows, ATT_DIM), BF16)],
-        smem=1, flops=3 * group_rows * group_rows * PART_WIDTH,
+        [place, weights, query_seq, attended] + pieces + pieces_other,
+        scratch=[
+            VMEM((PART_FAST, 3, SPAN, hidden), BF16),
+            VMEM((PART_FAST * 3, hidden), F32),
+            VMEM((group_rows, PART_WIDTH), BF16),
+        ],
+        smem=1, flops=6 * group_rows * PART_WIDTH * hidden, limit=40,
     )
 
     parts = []

time: 174 us -> 171 us (0.983)
  waiting for transfers between devices: 72.2 us -> 80.9 us
  Pallas kernels: 53.5 us -> 45.2 us
  starting transfers between devices: 34.2 us -> 31.1 us
    ppermute x22, waiting for transfers between devices: 72.2 us -> 80.9 us  [permute(): return lax.ppermute(array, 'tok', route)]
    pallas_call x1 -> x0, Pallas kernels: 4.15 us -> none  [shards(): pl.pallas_call(heads_kernel, out_shape=[jax.ShapeDtypeStruct((tok_dev, 2...]
    pallas_call x9, Pallas kernels: 49.3 us -> 45.2 us  [call(): pl.pallas_call(kernel, out_shape=list(outs), in_specs=specs, out_specs=ou...]
    ppermute x22, starting transfers between devices: 26.8 us -> 23.6 us  [permute(): return lax.ppermute(array, 'tok', route)]
    unnamed x37 -> x45, local copies, waits for them, and re-layouts: 6.81 us -> 7.81 us
  transfers between devices with their start and end apart: 23 -> 23, of which waited for: 12 -> 9; matrix products, arithmetic and copies ran while one was open for 5% -> 5% of each run, Pallas kernels for 23% -> 19%
where the time goes in v6:
time: 171 us
  waiting for transfers between devices  80.9 us (47%)
  Pallas kernels  45.2 us (26%)
  starting transfers between devices  31.1 us (18%)
  local copies, waits for them, and re-layouts  10.9 us (6%)
  other arithmetic  2.19 us (1%)
    ppermute x22, waiting for transfers between devices, permute(): return lax.ppermute(array, 'tok', route)  80.9 us
    pallas_call x9, Pallas kernels, call(): pl.pallas_call(kernel, out_shape=list(outs), in_specs=specs, out_specs=ou...  45.2 us
    ppermute x22, starting transfers between devices, permute(): return lax.ppermute(array, 'tok', route)  23.6 us
    unnamed x45, local copies, waits for them, and re-layouts  7.81 us
    all_to_all x1, starting transfers between devices, shards(): lax.all_to_all(packed.reshape(sections, slots, 3 * PART_WIDTH), 'tok', sp...  7.44 us
  transfers between devices with their start and end apart: 23, of which 9 were waited for; matrix products, arithmetic and copies ran while one was open for 5% of the time, Pallas kernels for 19%

profile of v6, /device:TPU:0, one launch (start us, length us, event | category | flops | bytes accessed | tf_op | source)
XLA Modules:
  0.0 170.6 jit_solution(12969629465057642034)
XLA Ops:
  0.6 4.3 %shard_map.83 = (bf16[4,4,2,16,1920]{4,3,2,1,0:T(8,128)(2,1)}, bf16[128,640]{1,0:T(8,128)(2,1)}, bf16[128,640]{1,0:T(8,128)(2,1)}, bf16[128,640]{1,0:T(8,128)(2,...) custom-call(s32[16]{0:T(128)} %stack.67.place_ref, ...), custom_call_target="tpu_custom_call" | custom-call | flops 251658240 | bytes 5263424 | tf_op jit(solution)/shard_map/pallas_call | solution.py:53
  5.0 7.4 %all-to-all-start = ((bf16[32,16,1920]{2,1,0:T(8,128)(2,1)}), bf16[32,16,1920]{2,1,0:T(8,128)(2,1)}, u32[]{:S(2)}, u32[]{:S(2)}) async-start(bf16[32,16,1920]{2,1,0:T(8,128)(2,1)} %bitcast.24), calls=%async_computation | async-start | bytes 3932160 | tf_op jit(solution)/shard_map/all_to_all | solution.py:432
  12.7 1.6 collective-permute-start.7
  18.8 13.3 %collective-permute-done.7.refs_2_ = bf16[128,640]{1,0:T(8,128)(2,1)S(1)} collective-permute-done((bf16[128,640]{1,0:T(8,128)(2,1)S(1)}, bf16[128,640]{1,0:T(8,128)(2,1)S(1)}, u32[]{:S(2)}, u32[]{:S(2)}) %collective-permute-start.7) | collective-permute-done | bytes 163872 | tf_op jit(solution)/shard_map/ppermute | solution.py:387
  32.7 1.9 %constant_dynamic-slice_fusion = bf16[640,3,640]{2,0,1:T(8,128)(2,1)S(1)} fusion(bf16[640,3,2560]{2,0,1:T(8,128)(2,1)} %param.14, s32[]{:T(128)S(6)} %select_n.42), kind=kLoop, calls=%fused_computation.3 | loop fusion | bytes 4915204 | tf_op jit(solution)/shard_map/dynamic_slice | solution.py:405
  34.6 3.3 %copy.10 = bf16[640,3,640]{0,2,1:T(8,128)(2,1)} copy(bf16[640,3,640]{2,0,1:T(8,128)(2,1)S(1)} %constant_dynamic-slice_fusion) | data formatting | bytes 4915200
  37.9 9.4 %collective-permute-done.8.refs_3_ = bf16[128,640]{1,0:T(8,128)(2,1)} collective-permute-done((bf16[128,640]{1,0:T(8,128)(2,1)}, bf16[128,640]{1,0:T(8,128)(2,1)}, u32[]{:S(2)}, u32[]{:S(2)}) %collective-permute-start.8) | collective-permute-done | bytes 163872 | tf_op jit(solution)/shard_map/ppermute | solution.py:387
  47.3 5.4 %shard_map.87.refs_4_ = bf16[320,1920]{1,0:T(8,128)(2,1)} custom-call(s32[16]{0:T(128)} %stack.67.place_ref, bf16[3,640,640]{2,1,0:T(8,128)(2,1)} %bitcast.21, bf16[128,640]{1,0:T(8,128)(2,1)} %get-tuple-element.33.refs_0_, bf16[128,640]{1,0:T(8,128)(2,1)} %copy-done.18, bf16[128,640]{1,0:T(8,128)(2,1)} %copy-done.20, ...), custom_call_target="tpu_custom_call" | custom-call | flops 1258291200 | bytes 4341824 | tf_op jit(solution)/shard_map/pallas_call | solution.py:53
  53.5 6.1 %shard_map.88 = (bf16[160,1920]{1,0:T(8,128)(2,1)}, bf16[160,1920]{1,0:T(8,128)(2,1)}) custom-call(s32[16]{0:T(128)} %stack.67.place_ref, bf16[3,640,640]{2,1,0:T(8,128)(2,1)} %bitcast.22, bf16[128,640]{1,0:T(8,128)(2,1)} %copy-done.16, bf16[128,640]{1,0:T(8,128)(2,1)} %copy-done.17, bf16[128,640]{1,0:T(8,128)(2,1)} %collective-permute-done.4.refs_2_, ...), custom_call_target="tpu_custom_call" | custom-call | flops 1258291200 | bytes 5570624 | tf_op jit(solution)/shard_map/pallas_call | solution.py:53
  59.6 2.4 %collective-permute-start.9 = (bf16[160,1920]{1,0:T(8,128)(2,1)}, bf16[160,1920]{1,0:T(8,128)(2,1)S(1)}, u32[]{:S(2)}, u32[]{:S(2)}) collective-permute-start(bf16[160,1920]{1,0:T(8,128)(2,1)} %get-tuple-element.38), channel_id=1, source_target_pairs={{0,8},{1,9},{2,10},{3,11},{4,12},{5,13},{6,14},{7,15},{8,0},{9,1},... | collective-permute-start | bytes 1843208 | tf_op jit(solution)/shard_map/ppermute | solution.py:387
  62.0 2.2 %shard_map.82.choose_ref = bf16[512,512]{1,0:T(8,128)(2,1)} custom-call(s32[16]{0:T(128)} %stack.67.place_ref, s32[32,128]{1,0:T(8,128)} %bitcast.26), custom_call_target="tpu_custom_call" | custom-call | flops 524288 | bytes 540736 | tf_op jit(solution)/shard_map/pallas_call | solution.py:53
  64.2 12.7 %collective-permute-done.9 = bf16[160,1920]{1,0:T(8,128)(2,1)S(1)} collective-permute-done((bf16[160,1920]{1,0:T(8,128)(2,1)}, bf16[160,1920]{1,0:T(8,128)(2,1)S(1)}, u32[]{:S(2)}, u32[]{:S(2)}) %collective-permute-start.9) | collective-permute-done | bytes 614432 | tf_op jit(solution)/shard_map/ppermute | solution.py:387
  77.9 3.7 %collective-permute-start.10 = (bf16[80,1920]{1,0:T(8,128)(2,1)S(1)}, bf16[80,1920]{1,0:T(8,128)(2,1)}, u32[]{:S(2)}, u32[]{:S(2)}) collective-permute-start(bf16[80,1920]{1,0:T(8,128)(2,1)S(1)} %add_convert_fusion.1), channel_id=1, source_target_pairs={{0,16},{1,17},{2,18},{3,19},{4,20},{5,21},{6,22},{7,23},{8,24},{9,... | collective-permute-start | bytes 921608 | tf_op jit(solution)/shard_map/ppermute | solution.py:387
  81.7 4.0 %shard_map.84 = (bf16[512,1280]{1,0:T(8,128)(2,1)}, bf16[512,640]{1,0:T(8,128)(2,1)}) custom-call(bf16[512,512]{1,0:T(8,128)(2,1)} %shard_map.82.choose_ref, bf16[512,1920]{1,0:T(8,128)(2,1)} %bitcast.20.in_ref), custom_call_target="tpu_custom_call" | custom-call | flops 1006632960 | bytes 4456448 | tf_op jit(solution)/shard_map/pallas_call | solution.py:53
  86.6 9.3 %collective-permute-done.10 = bf16[80,1920]{1,0:T(8,128)(2,1)} collective-permute-done((bf16[80,1920]{1,0:T(8,128)(2,1)S(1)}, bf16[80,1920]{1,0:T(8,128)(2,1)}, u32[]{:S(2)}, u32[]{:S(2)}) %collective-permute-start.10) | collective-permute-done | bytes 307232 | tf_op jit(solution)/shard_map/ppermute | solution.py:387
  97.1 3.9 %collective-permute-start.12 = (bf16[80,1920]{1,0:T(8,128)(2,1)S(1)}, bf16[80,1920]{1,0:T(8,128)(2,1)S(1)}, u32[]{:S(2)}, u32[]{:S(2)}) collective-permute-start(bf16[80,1920]{1,0:T(8,128)(2,1)S(1)} %add_convert_fusion.refs_0_), channel_id=1, source_target_pairs={{0,8},{1,9},{2,10},{3,11},{4,12},{5,13},{6,14},{7,15},{8,0},{9,1},... | collective-permute-start | bytes 921608 | tf_op jit(solution)/shard_map/ppermute | solution.py:387
  100.9 21.9 %collective-permute-done.11.refs_1_ = bf16[80,1920]{1,0:T(8,128)(2,1)S(1)} collective-permute-done((bf16[80,1920]{1,0:T(8,128)(2,1)S(1)}, bf16[80,1920]{1,0:T(8,128)(2,1)S(1)}, u32[]{:S(2)}, u32[]{:S(2)}) %collective-permute-start.11) | collective-permute-done | bytes 307232 | tf_op jit(solution)/shard_map/ppermute | solution.py:387
  123.4 6.7 %collective-permute-done.13.refs_3_ = bf16[80,1920]{1,0:T(8,128)(2,1)S(1)} collective-permute-done((bf16[80,1920]{1,0:T(8,128)(2,1)S(1)}, bf16[80,1920]{1,0:T(8,128)(2,1)S(1)}, u32[]{:S(2)}, u32[]{:S(2)}) %collective-permute-start.13) | collective-permute-done | bytes 307232 | tf_op jit(solution)/shard_map/ppermute | solution.py:387
  133.1 9.0 %shard_map.85 = (f32[512,640]{1,0:T(8,128)S(1)}, f32[512,128]{1,0:T(8,128)S(1)}) custom-call(s32[16]{0:T(128)S(1)} %copy-done.3, bf16[512,640]{1,0:T(8,128)(2,1)S(1)} %copy-done.1, s32[8,512]{1,0:T(8,128)S(1)} %reshape.18.ids_ref, bf16[512,1280]{1,0:T(8,128)(2,1)S(1)} %copy-done.4, bf16[512,1280]{1,0:T(8,128)(2,1)} %collective-permute-done.chip_ref), custom_call_target="tpu_custom_call" | custom-call | flops 1006632960 | bytes 4866112 | tf_op jit(solution)/shard_map/pallas_call | solution.py:53
  142.1 6.5 %shard_map.86.attended_ref = f32[512,640]{1,0:T(8,128)S(1)} custom-call(s32[16]{0:T(128)S(1)} %copy-done.3, bf16[512,640]{1,0:T(8,128)(2,1)S(1)} %copy-done.2, s32[8,512]{1,0:T(8,128)S(1)} %reshape.18.ids_ref, f32[512,640]{1,0:T(8,128)S(1)} %get-tuple-element.27.near_ref, f32[512,128]{1,0:T(8,128)S(1)} %get-tuple-element.28.stat_ref, ...), custom_call_target="tpu_custom_call" | custom-call | flops 503316480 | bytes 4866112 | tf_op jit(solution)/shard_map/pallas_call | solution.py:53
  148.7 5.3 %shard_map.89 = (bf16[128,640]{1,0:T(8,128)(2,1)S(1)}, bf16[128,640]{1,0:T(8,128)(2,1)S(1)}, bf16[128,640]{1,0:T(8,128)(2,1)S(1)}, bf16[128,640]{1,0:T(8,128)(2,1)S(1)}) custom-call(s32[16]{0:T(128)S(1)} %copy-done.3, bf16[3,640,640]{2,1,0:T(8,128)(2,1)S(1)} %bitcast.23, bf16[512,640]{1,0:T(8,128)(2,1)S(1)} %copy-done.2, ...), custom_call_target="tpu_custom_call" | custom-call | flops 1258291200 | bytes 7536704 | tf_op jit(solution)/shard_map/pallas_call | solution.py:53
  155.7 3.3 %collective-permute-start.20 = (bf16[128,640]{1,0:T(8,128)(2,1)S(1)}, bf16[128,640]{1,0:T(8,128)(2,1)S(1)}, u32[]{:S(2)}, u32[]{:S(2)}) collective-permute-start(bf16[128,640]{1,0:T(8,128)(2,1)S(1)} %get-tuple-element.41), channel_id=1, source_target_pairs={{0,1},{1,5},{2,3},{3,7},{4,0},{5,4},{6,2},{7,6},{8,9},{9,13},{10,1... | collective-permute-start | bytes 491528 | tf_op jit(solution)/shard_map/ppermute | solution.py:387
  160.0 6.3 %collective-permute-done.20.refs_2_ = bf16[128,640]{1,0:T(8,128)(2,1)S(1)} collective-permute-done((bf16[128,640]{1,0:T(8,128)(2,1)S(1)}, bf16[128,640]{1,0:T(8,128)(2,1)S(1)}, u32[]{:S(2)}, u32[]{:S(2)}) %collective-permute-start.20) | collective-permute-done | bytes 163872 | tf_op jit(solution)/shard_map/ppermute | solution.py:387
  168.2 2.4 %shard_map.90 = bf16[128,2560]{1,0:T(8,128)(2,1)} custom-call(s32[16]{0:T(128)} %stack.67.place_ref, bf16[128,640]{1,0:T(8,128)(2,1)} %copy-done.6, bf16[128,640]{1,0:T(8,128)(2,1)} %copy-done.7, bf16[128,640]{1,0:T(8,128)(2,1)} %copy-done.8, bf16[128,640]{1,0:T(8,128)(2,1)} %copy-done.9, f32[1,2560]{1,0:T(1,128)} %reshape.19.refs_4_), custom_call_target="tpu_custom_call" | custom-call | flops 1966080 | bytes 1321024 | tf_op jit(solution)/shard_map/pallas_call | solution.py:53
  (82 shorter events, 17.9 us)
Async XLA Ops:
  5.0 76.7 %all-to-all-start = ((bf16[32,16,1920]{2,1,0:T(8,128)(2,1)}), bf16[32,16,1920]{2,1,0:T(8,128)(2,1)}, u32[]{:S(2)}, u32[]{:S(2)}) async-start(bf16[32,16,1920]{2,1,0:T(8,128)(2,1)} %bitcast.24), calls=%async_computation | async-start | bytes 3932160 | tf_op jit(solution)/shard_map/all_to_all | solution.py:432
  12.4 4.8 %collective-permute-start.6 = (bf16[128,640]{1,0:T(8,128)(2,1)S(1)}, bf16[128,640]{1,0:T(8,128)(2,1)S(1)}, u32[]{:S(2)}, u32[]{:S(2)}) collective-permute-start(bf16[128,640]{1,0:T(8,128)(2,1)S(1)} %copy-done.21), channel_id=1, source_target_pairs={{0,1},{1,0},{2,3},{3,2},{4,5},{5,4},{6,7},{7,6},{8,9},{9,8},{10,11... | collective-permute-start | bytes 491528 | tf_op jit(solution)/shard_map/ppermute | solution.py:387
  12.7 19.4 %collective-permute-start.7 = (bf16[128,640]{1,0:T(8,128)(2,1)S(1)}, bf16[128,640]{1,0:T(8,128)(2,1)S(1)}, u32[]{:S(2)}, u32[]{:S(2)}) collective-permute-start(bf16[128,640]{1,0:T(8,128)(2,1)S(1)} %copy-done.19), channel_id=1, source_target_pairs={{0,2},{1,3},{2,0},{3,1},{4,6},{5,7},{6,4},{7,5},{8,10},{9,11},{10,... | collective-permute-start | bytes 491528 | tf_op jit(solution)/shard_map/ppermute | solution.py:387
  14.3 38.4 %collective-permute-start.2 = (bf16[128,640]{1,0:T(8,128)(2,1)S(1)}, bf16[128,640]{1,0:T(8,128)(2,1)S(1)}, u32[]{:S(2)}, u32[]{:S(2)}) collective-permute-start(bf16[128,640]{1,0:T(8,128)(2,1)S(1)} %copy-done.15), channel_id=1, source_target_pairs={{0,4},{1,5},{2,6},{3,7},{4,0},{5,1},{6,2},{7,3},{8,12},{9,13},{10,... | collective-permute-start | bytes 491528 | tf_op jit(solution)/shard_map/ppermute | solution.py:387
  15.8 36.9 %collective-permute-start.3 = (bf16[128,640]{1,0:T(8,128)(2,1)S(1)}, bf16[128,640]{1,0:T(8,128)(2,1)S(1)}, u32[]{:S(2)}, u32[]{:S(2)}) collective-permute-start(bf16[128,640]{1,0:T(8,128)(2,1)S(1)} %copy-done.14), channel_id=1, source_target_pairs={{0,5},{1,4},{2,7},{3,6},{4,1},{5,0},{6,3},{7,2},{8,13},{9,12},{10,... | collective-permute-start | bytes 491528 | tf_op jit(solution)/shard_map/ppermute | solution.py:387
  15.8 36.9 %collective-permute-start.4 = (bf16[128,640]{1,0:T(8,128)(2,1)S(1)}, bf16[128,640]{1,0:T(8,128)(2,1)}, u32[]{:S(2)}, u32[]{:S(2)}) collective-permute-start(bf16[128,640]{1,0:T(8,128)(2,1)S(1)} %copy-done.13), channel_id=1, source_target_pairs={{0,6},{1,7},{2,4},{3,5},{4,2},{5,3},{6,0},{7,1},{8,14},{9,15},{10,... | collective-permute-start | bytes 491528 | tf_op jit(solution)/shard_map/ppermute | solution.py:387
  17.3 35.5 %collective-permute-start.5 = (bf16[128,640]{1,0:T(8,128)(2,1)S(1)}, bf16[128,640]{1,0:T(8,128)(2,1)}, u32[]{:S(2)}, u32[]{:S(2)}) collective-permute-start(bf16[128,640]{1,0:T(8,128)(2,1)S(1)} %copy-done.12), channel_id=1, source_target_pairs={{0,7},{1,6},{2,5},{3,4},{4,3},{5,2},{6,1},{7,0},{8,15},{9,14},{10,... | collective-permute-start | bytes 491528 | tf_op jit(solution)/shard_map/ppermute | solution.py:387
  32.7 14.6 %collective-permute-start.8 = (bf16[128,640]{1,0:T(8,128)(2,1)}, bf16[128,640]{1,0:T(8,128)(2,1)}, u32[]{:S(2)}, u32[]{:S(2)}) collective-permute-start(bf16[128,640]{1,0:T(8,128)(2,1)} %get-tuple-element.36), channel_id=1, source_target_pairs={{0,3},{1,2},{2,1},{3,0},{4,7},{5,6},{6,5},{7,4},{8,11},{9,10},{10,... | collective-permute-start | bytes 491528 | tf_op jit(solution)/shard_map/ppermute | solution.py:387
  59.6 17.3 %collective-permute-start.9 = (bf16[160,1920]{1,0:T(8,128)(2,1)}, bf16[160,1920]{1,0:T(8,128)(2,1)S(1)}, u32[]{:S(2)}, u32[]{:S(2)}) collective-permute-start(bf16[160,1920]{1,0:T(8,128)(2,1)} %get-tuple-element.38), channel_id=1, source_target_pairs={{0,8},{1,9},{2,10},{3,11},{4,12},{5,13},{6,14},{7,15},{8,0},{9,1},... | collective-permute-start | bytes 1843208 | tf_op jit(solution)/shard_map/ppermute | solution.py:387
  77.9 17.9 %collective-permute-start.10 = (bf16[80,1920]{1,0:T(8,128)(2,1)S(1)}, bf16[80,1920]{1,0:T(8,128)(2,1)}, u32[]{:S(2)}, u32[]{:S(2)}) collective-permute-start(bf16[80,1920]{1,0:T(8,128)(2,1)S(1)} %add_convert_fusion.1), channel_id=1, source_target_pairs={{0,16},{1,17},{2,18},{3,19},{4,20},{5,21},{6,22},{7,23},{8,24},{9,... | collective-permute-start | bytes 921608 | tf_op jit(solution)/shard_map/ppermute | solution.py:387
  81.7 49.0 %copy-start.3 = (s32[16]{0:T(128)S(1)}, s32[16]{0:T(128)}, u32[]{:S(2)}) copy-start(s32[16]{0:T(128)} %stack.67.place_ref) | copy-start | bytes 196
  85.7 44.5 %collective-permute-start = (bf16[512,1280]{1,0:T(8,128)(2,1)}, bf16[512,1280]{1,0:T(8,128)(2,1)}, u32[]{:S(2)}, u32[]{:S(2)}) collective-permute-start(bf16[512,1280]{1,0:T(8,128)(2,1)} %get-tuple-element.26.kv_ref), channel_id=1, source_target_pairs={{0,1},{1,0},{2,3},{3,2},{4,5},{5,4},{6,7},{7,6},{8,9},{9,8},{10,11... | collective-permute-start | bytes 3932168 | tf_op jit(solution)/shard_map/ppermute | solution.py:387
  85.7 56.4 %collective-permute-start.1 = (bf16[512,1280]{1,0:T(8,128)(2,1)}, bf16[512,1280]{1,0:T(8,128)(2,1)S(1)}, u32[]{:S(2)}, u32[]{:S(2)}) collective-permute-start(bf16[512,1280]{1,0:T(8,128)(2,1)} %get-tuple-element.26.kv_ref), channel_id=1, source_target_pairs={{1,8},{3,10},{5,12},{7,14},{8,1},{9,16},{10,3},{11,18},{12,5},{13,... | collective-permute-start | bytes 3932168 | tf_op jit(solution)/shard_map/ppermute | solution.py:387
  97.0 25.9 %collective-permute-start.11 = (bf16[80,1920]{1,0:T(8,128)(2,1)S(1)}, bf16[80,1920]{1,0:T(8,128)(2,1)S(1)}, u32[]{:S(2)}, u32[]{:S(2)}) collective-permute-start(bf16[80,1920]{1,0:T(8,128)(2,1)S(1)} %add_convert_fusion.refs_0_), channel_id=1, source_target_pairs={{0,16},{1,17},{2,18},{3,19},{4,20},{5,21},{6,22},{7,23},{8,24},{9,... | collective-permute-start | bytes 921608 | tf_op jit(solution)/shard_map/ppermute | solution.py:387
  97.1 25.8 %collective-permute-start.12 = (bf16[80,1920]{1,0:T(8,128)(2,1)S(1)}, bf16[80,1920]{1,0:T(8,128)(2,1)S(1)}, u32[]{:S(2)}, u32[]{:S(2)}) collective-permute-start(bf16[80,1920]{1,0:T(8,128)(2,1)S(1)} %add_convert_fusion.refs_0_), channel_id=1, source_target_pairs={{0,8},{1,9},{2,10},{3,11},{4,12},{5,13},{6,14},{7,15},{8,0},{9,1},... | collective-permute-start | bytes 921608 | tf_op jit(solution)/shard_map/ppermute | solution.py:387
  122.9 7.2 %collective-permute-start.13 = (bf16[80,1920]{1,0:T(8,128)(2,1)S(1)}, bf16[80,1920]{1,0:T(8,128)(2,1)S(1)}, u32[]{:S(2)}, u32[]{:S(2)}) collective-permute-start(bf16[80,1920]{1,0:T(8,128)(2,1)S(1)} %collective-permute-done.11.refs_1_), channel_id=1, source_target_pairs={{0,8},{1,9},{2,10},{3,11},{4,12},{5,13},{6,14},{7,15},{8,0},{9,1},... | collective-permute-start | bytes 921608 | tf_op jit(solution)/shard_map/ppermute | solution.py:387
  122.9 25.7 %collective-permute-start.14 = (bf16[80,1920]{1,0:T(8,128)(2,1)S(1)}, bf16[80,1920]{1,0:T(8,128)(2,1)S(1)}, u32[]{:S(2)}, u32[]{:S(2)}) collective-permute-start(bf16[80,1920]{1,0:T(8,128)(2,1)S(1)} %add_convert_fusion.refs_0_), channel_id=1, source_target_pairs={{0,1},{1,0},{2,3},{3,2},{4,5},{5,4},{6,7},{7,6},{8,9},{9,8},{10,11... | collective-permute-start | bytes 921608 | tf_op jit(solution)/shard_map/ppermute | solution.py:387
  122.9 25.7 %collective-permute-start.15 = (bf16[80,1920]{1,0:T(8,128)(2,1)S(1)}, bf16[80,1920]{1,0:T(8,128)(2,1)}, u32[]{:S(2)}, u32[]{:S(2)}) collective-permute-start(bf16[80,1920]{1,0:T(8,128)(2,1)S(1)} %collective-permute-done.11.refs_1_), channel_id=1, source_target_pairs={{0,1},{1,0},{2,3},{3,2},{4,5},{5,4},{6,7},{7,6},{8,9},{9,8},{10,11... | collective-permute-start | bytes 921608 | tf_op jit(solution)/shard_map/ppermute | solution.py:387
  130.1 18.5 %collective-permute-start.16 = (bf16[80,1920]{1,0:T(8,128)(2,1)S(1)}, bf16[80,1920]{1,0:T(8,128)(2,1)}, u32[]{:S(2)}, u32[]{:S(2)}) collective-permute-start(bf16[80,1920]{1,0:T(8,128)(2,1)S(1)} %collective-permute-done.12.refs_2_), channel_id=1, source_target_pairs={{0,1},{1,0},{2,3},{3,2},{4,5},{5,4},{6,7},{7,6},{8,9},{9,8},{10,11... | collective-permute-start | bytes 921608 | tf_op jit(solution)/shard_map/ppermute | solution.py:387
  130.1 18.5 %collective-permute-start.17 = (bf16[80,1920]{1,0:T(8,128)(2,1)S(1)}, bf16[80,1920]{1,0:T(8,128)(2,1)}, u32[]{:S(2)}, u32[]{:S(2)}) collective-permute-start(bf16[80,1920]{1,0:T(8,128)(2,1)S(1)} %collective-permute-done.13.refs_3_), channel_id=1, source_target_pairs={{0,1},{1,0},{2,3},{3,2},{4,5},{5,4},{6,7},{7,6},{8,9},{9,8},{10,11... | collective-permute-start | bytes 921608 | tf_op jit(solution)/shard_map/ppermute | solution.py:387
  154.0 5.9 %collective-permute-start.18 = (bf16[128,640]{1,0:T(8,128)(2,1)S(1)}, bf16[128,640]{1,0:T(8,128)(2,1)S(1)}, u32[]{:S(2)}, u32[]{:S(2)}) collective-permute-start(bf16[128,640]{1,0:T(8,128)(2,1)S(1)} %get-tuple-element.39), channel_id=1, source_target_pairs={{0,0},{1,4},{2,2},{3,6},{4,1},{5,5},{6,3},{7,7},{8,8},{9,12},{10,1... | collective-permute-start | bytes 491528 | tf_op jit(solution)/shard_map/ppermute | solution.py:387
  154.6 5.4 %collective-permute-start.19 = (bf16[128,640]{1,0:T(8,128)(2,1)S(1)}, bf16[128,640]{1,0:T(8,128)(2,1)S(1)}, u32[]{:S(2)}, u32[]{:S(2)}) collective-permute-start(bf16[128,640]{1,0:T(8,128)(2,1)S(1)} %get-tuple-element.40), channel_id=1, source_target_pairs={{0,2},{1,6},{2,0},{3,4},{4,3},{5,7},{6,1},{7,5},{8,10},{9,14},{10,... | collective-permute-start | bytes 491528 | tf_op jit(solution)/shard_map/ppermute | solution.py:387
  155.7 10.7 %collective-permute-start.20 = (bf16[128,640]{1,0:T(8,128)(2,1)S(1)}, bf16[128,640]{1,0:T(8,128)(2,1)S(1)}, u32[]{:S(2)}, u32[]{:S(2)}) collective-permute-start(bf16[128,640]{1,0:T(8,128)(2,1)S(1)} %get-tuple-element.41), channel_id=1, source_target_pairs={{0,1},{1,5},{2,3},{3,7},{4,0},{5,4},{6,2},{7,6},{8,9},{9,13},{10,1... | collective-permute-start | bytes 491528 | tf_op jit(solution)/shard_map/ppermute | solution.py:387
  159.0 8.5 %collective-permute-start.21 = (bf16[128,640]{1,0:T(8,128)(2,1)S(1)}, bf16[128,640]{1,0:T(8,128)(2,1)S(1)}, u32[]{:S(2)}, u32[]{:S(2)}) collective-permute-start(bf16[128,640]{1,0:T(8,128)(2,1)S(1)} %get-tuple-element.42), channel_id=1, source_target_pairs={{0,3},{1,7},{2,1},{3,5},{4,2},{5,6},{6,0},{7,4},{8,11},{9,15},{10,... | collective-permute-start | bytes 491528 | tf_op jit(solution)/shard_map/ppermute | solution.py:387
  (21 other events, 225.3 us)

commit v7 on v6

--- a/solution.py
+++ b/solution.py
@@ -154,8 +154,8 @@
     q_ref[...] = dot(choose, in_ref[:, 2 * PART_WIDTH :]).astype(BF16)
 
 
-def grads_kernel(chunk, last, place_ref, weight_ref, *refs):
-    outs = 2 if last else 1
+def grads_kernel(chunk, first_start, outs, place_ref, weight_ref, *refs):
+    last = outs > 1
     weight_buf, key_buf, target_buf, delta_buf, pr_buf, sums = refs[-6:]
     out_refs, in_refs = refs[-6 - outs : -6], refs[: -6 - outs]
     kv_refs, early_ref = (in_refs[:-1], in_refs[-1]) if last else (in_refs, None)
@@ -191,10 +191,9 @@
         else:
             out_refs[0][:, lanes] = total.astype(BF16)
     if last:
-        half = out_refs[0].shape[0]
-        side = place_ref[3] // PART_FAST & 1
-        out_refs[0][...] = sums[pl.ds(pl.multiple_of((1 - side) * half, 16), half), :]
-        out_refs[1][...] = sums[pl.ds(pl.multiple_of(side * half, 16), half), :]
+        for index, ref in enumerate(out_refs):
+            begin = pl.multiple_of(place_ref[first_start + index], 16)
+            ref[...] = sums[pl.ds(begin, ref.shape[0]), :]
 
 
 FACTOR = ATT_DIM ** (-0.5) * math.log2(math.e)
@@ -295,12 +294,11 @@
             out_ref[here, keys] = mixed / total
 
 
-def apply_kernel(place_ref, weight_ref, query_ref, attended_ref, *refs):
+def apply_kernel(first_goal, first_rows, place_ref, weight_ref, query_ref, attended_ref, *refs):
     hidden = weight_ref.shape[2]
     out_refs, (fresh, scales, rows_buf) = refs[-3 - PARTS : -3], refs[-3:]
     count = (len(refs) - 3 - PARTS) // 2
     mine_refs, other_refs = refs[:count], refs[count : 2 * count]
-    piece = mine_refs[0].shape[0]
     core = place_ref[2]
     for head in range(PART_FAST):
         _, offset = window_of(head)
@@ -309,7 +307,8 @@
             anchor = jnp.full((1, hidden), EPS, F32)
             length = jnp.full((1, hidden), EPS, F32)
             for step in range(count):
-                at = pl.multiple_of(place_ref[4 + PARTS + step], 16)
+                piece = mine_refs[step].shape[0]
+                at = pl.multiple_of(place_ref[first_rows + step], 16)
                 base = weight_ref[index, pl.ds(at + head * HEAD_DIM, piece), :].astype(F32)
                 grad = jnp.where(core == head, mine_refs[step][:, lanes], other_refs[step][:, lanes]).astype(F32)
                 update = base + grad
@@ -335,7 +334,7 @@
         rows_buf[:, lane : lane + LANES] = functools.reduce(jnp.add, inside, attended_ref[:, lane : lane + LANES]).astype(BF16)
     block = out_refs[0].shape[0]
     for index, ref in enumerate(out_refs):
-        begin = pl.multiple_of(place_ref[4 + PARTS + count + index] * block, block)
+        begin = pl.multiple_of(place_ref[first_goal + index] * block, block)
         ref[...] = rows_buf[pl.ds(begin, block), :]
 
 
@@ -353,6 +352,17 @@
         out_ref[:, lanes] = (buf[part].astype(F32) * factor * gain_ref[:, lanes]).astype(BF16)
 
 
+def gather_layout(bits, piece, relay):
+    layout = [(0, 0, piece)]
+    for bit in reversed(range(bits)):
+        for mask, begin, size in list(layout):
+            cuts = [(begin, size)]
+            if mask == 0 and bit == bits - 1 and bits > 1:
+                cuts = [(0, relay), (relay, piece - relay)]
+            layout += [(mask ^ 1 << bit, first, count) for first, count in cuts]
+    return layout
+
+
 def shards(queries, key_rows, value_rows, learn_rates, frame_order, window_ids, fast_init, norm_gain):
     tok_dev = queries.shape[0]
     hidden = fast_init.shape[0]
@@ -394,12 +404,15 @@
     def owned(plane):
         return sum((plane >> bit & 1) * (HEAD_DIM >> bit + 1) for bit in range(bits))
 
-    masks = [0]
-    for bit in reversed(range(bits)):
-        masks += [mask ^ 1 << bit for mask in masks]
-    starts = [owned(plane ^ mask) for mask in masks]
+    relay = -(-piece // 32) * 16
+    layout = gather_layout(bits, piece, relay)
+    starts = [owned(plane ^ mask) for mask in range(planes)]
+    rows_from = [starts[mask] + begin for mask, begin, _ in layout]
     goals = [2 * (column ^ j % 2) + (row ^ j // 2) for j in range(PARTS)]
-    place = jnp.stack([rank, part, core, group] + sources + starts + goals).astype(jnp.int32)
+    first_start = 4 + PARTS
+    first_goal = first_start + planes
+    first_rows = first_goal + PARTS
+    place = jnp.stack([rank, part, core, group] + sources + starts + goals + rows_from).astype(jnp.int32)
 
     def weight_part():
         own = lax.dynamic_slice_in_dim(fast_init, part * PART_WIDTH, PART_WIDTH, 2)
@@ -426,6 +439,7 @@
         smem=1, flops=2 * tok_dev * tok_dev * 3 * WIDTH,
     )
     heads_in = [heads_out[0]]
+    send_order = [2, 3, 6, 7, 4, 5, 1]
     for j in range(1, plane_size):
         heads_in.append(permute(heads_out[j], lambda z, y, x, c, j=j: (z, y ^ j >> 2, x ^ j >> 1 & 1, c ^ j & 1)))
 
@@ -455,18 +469,20 @@
 
     near = plane_size // 2
     tokens = near * tok_dev
+    by_arrival = [heads_in[0]] + [heads_in[j] for j in send_order]
+    early_heads, late_heads = by_arrival[:near], by_arrival[near:]
     grad_scratch = [VMEM((SPAN, 3 * hidden), BF16)] + [VMEM((tokens, SPAN), BF16)] * 2
     grad_scratch += [VMEM((tokens, 2 * hidden), BF16), VMEM((tokens, hidden), BF16), VMEM((HEAD_DIM, 3 * hidden), BF16)]
     grad_flops = 12 * tokens * HEAD_DIM * hidden
     (early,) = call(
-        functools.partial(grads_kernel, tokens, False),
-        [jax.ShapeDtypeStruct((HEAD_DIM, 3 * hidden), BF16)], [place, weights] + heads_in[:near],
+        functools.partial(grads_kernel, tokens, first_start, 1),
+        [jax.ShapeDtypeStruct((HEAD_DIM, 3 * hidden), BF16)], [place, weights] + early_heads,
         scratch=grad_scratch, smem=1, flops=grad_flops,
     )
-    send, keep = call(
-        functools.partial(grads_kernel, tokens, True),
-        [jax.ShapeDtypeStruct((HEAD_DIM // 2, 3 * hidden), BF16)] * 2,
-        [place, weights] + heads_in[near:] + [early],
+    quarters = call(
+        functools.partial(grads_kernel, tokens, first_start, planes),
+        [jax.ShapeDtypeStruct((piece, 3 * hidden), BF16)] * planes,
+        [place, weights] + late_heads + [early],
         scratch=grad_scratch, smem=1, flops=grad_flops,
     )
 
@@ -476,25 +492,26 @@
     def added(first, second):
         return (first.astype(F32) + second.astype(F32)).astype(BF16)
 
+    held = dict(enumerate(quarters))
     for bit in range(bits):
-        came = permute(send, across(bit))
-        if bit + 1 < bits:
-            size = HEAD_DIM >> bit + 2
-            side = plane >> bit + 1 & 1
-            cuts = [[lax.dynamic_slice_in_dim(a, at * size, size, 0) for a in (keep, came)] for at in (1 - side, side)]
-            send = added(*cuts[0])
-            keep = added(*cuts[1])
-        else:
-            total = added(keep, came)
+        flip = 1 << bit
+        for mask in sorted([mask for mask in held if mask & flip], reverse=True):
+            came = permute(held.pop(mask), across(bit))
+            kept = held[mask ^ flip]
+            held[mask ^ flip] = added(kept, came)
+    total = held[0]
     pieces = [total]
-    for bit in reversed(range(bits)):
-        fresh_pieces = []
-        for held in pieces:
-            fresh_pieces.append(permute(held, across(bit)))
-        pieces += fresh_pieces
+    sent = {(0, 0, piece): total}
+    for mask, begin, size in layout[1:]:
+        bit = [bit for bit in range(bits) if mask >> bit & 1][0]
+        source = (mask ^ 1 << bit, begin, size)
+        if source not in sent:
+            sent[source] = added(kept[begin : begin + size], came[begin : begin + size])
+        sent[mask, begin, size] = permute(sent[source], across(bit))
+        pieces.append(sent[mask, begin, size])
     pieces_other = []
-    for held in pieces:
-        pieces_other.append(permute(held, swap))
+    for held_piece in pieces:
+        pieces_other.append(permute(held_piece, swap))
 
     block = min(LANES, group_rows)
     count = group_rows // block
@@ -517,7 +534,7 @@
     )
 
     blocks = call(
-        apply_kernel,
+        functools.partial(apply_kernel, first_goal, first_rows),
         [jax.ShapeDtypeStruct((tok_dev, PART_WIDTH), BF16)] * PARTS,
         [place, weights, query_seq, attended] + pieces + pieces_other,
         scratch=[

time: 171 us -> 180 us (1.053)
  local copies, waits for them, and re-layouts: 10.9 us -> 14.7 us
  waiting for transfers between devices: 80.9 us -> 84.3 us
  starting transfers between devices: 31.1 us -> 33.9 us
    unnamed x45 -> x55, local copies, waits for them, and re-layouts: 7.81 us -> 11.5 us
    ppermute x22 -> x27, waiting for transfers between devices: 80.9 us -> 84.3 us  [permute(): return lax.ppermute(array, 'tok', route)]
    ppermute x22 -> x27, starting transfers between devices: 23.6 us -> 26.4 us  [permute(): return lax.ppermute(array, 'tok', route)]
  transfers between devices with their start and end apart: 23 -> 28, of which waited for: 9 -> 11; matrix products, arithmetic and copies ran while one was open for 5% -> 4% of each run, Pallas kernels for 19% -> 16%
where the time goes in v7:
time: 180 us; the launch traced here: 179 us
  waiting for transfers between devices  84.3 us (47%)
  Pallas kernels  43.9 us (24%)
  starting transfers between devices  33.9 us (19%)
  local copies, waits for them, and re-layouts  14.7 us (8%)
  other arithmetic  2.23 us (1%)
    ppermute x27, waiting for transfers between devices, permute(): return lax.ppermute(array, 'tok', route)  84.3 us
    pallas_call x9, Pallas kernels, call(): pl.pallas_call(kernel, out_shape=list(outs), in_specs=specs, out_specs=ou...  43.9 us
    ppermute x27, starting transfers between devices, permute(): return lax.ppermute(array, 'tok', route)  26.4 us
    unnamed x55, local copies, waits for them, and re-layouts  11.5 us
    all_to_all x1, starting transfers between devices, shards(): lax.all_to_all(packed.reshape(sections, slots, 3 * PART_WIDTH), 'tok', sp...  7.45 us
  transfers between devices with their start and end apart: 28, of which 11 were waited for; matrix products, arithmetic and copies ran while one was open for 4% of the time, Pallas kernels for 16%

profile of v7, /device:TPU:0, one launch (start us, length us, event | category | flops | bytes accessed | tf_op | source)
XLA Modules:
  0.0 179.5 jit_solution(12103019917148928951)
XLA Ops:
  0.7 4.3 %shard_map.83 = (bf16[4,4,2,16,1920]{4,3,2,1,0:T(8,128)(2,1)}, bf16[128,640]{1,0:T(8,128)(2,1)}, bf16[128,640]{1,0:T(8,128)(2,1)}, bf16[128,640]{1,0:T(8,128)(2,...) custom-call(s32[22]{0:T(128)} %stack.79.place_ref, ...), custom_call_target="tpu_custom_call" | custom-call | flops 251658240 | bytes 5263448 | tf_op jit(solution)/shard_map/pallas_call | solution.py:53
  5.0 7.5 %all-to-all-start = ((bf16[32,16,1920]{2,1,0:T(8,128)(2,1)}), bf16[32,16,1920]{2,1,0:T(8,128)(2,1)}, u32[]{:S(2)}, u32[]{:S(2)}) async-start(bf16[32,16,1920]{2,1,0:T(8,128)(2,1)} %bitcast.26), calls=%async_computation | async-start | bytes 3932160 | tf_op jit(solution)/shard_map/all_to_all | solution.py:446
  14.3 2.6 %collective-permute-start.2 = (bf16[128,640]{1,0:T(8,128)(2,1)S(1)}, bf16[128,640]{1,0:T(8,128)(2,1)S(1)}, u32[]{:S(2)}, u32[]{:S(2)}) collective-permute-start(bf16[128,640]{1,0:T(8,128)(2,1)S(1)} %copy-done.20), channel_id=1, source_target_pairs={{0,7},{1,6},{2,5},{3,4},{4,3},{5,2},{6,1},{7,0},{8,15},{9,14},{10,... | collective-permute-start | bytes 491528 | tf_op jit(solution)/shard_map/ppermute | solution.py:397
  18.1 14.0 %collective-permute-done.6.refs_1_ = bf16[128,640]{1,0:T(8,128)(2,1)S(1)} collective-permute-done((bf16[128,640]{1,0:T(8,128)(2,1)S(1)}, bf16[128,640]{1,0:T(8,128)(2,1)S(1)}, u32[]{:S(2)}, u32[]{:S(2)}) %collective-permute-start.6) | collective-permute-done | bytes 163872 | tf_op jit(solution)/shard_map/ppermute | solution.py:397
  32.2 6.6 %collective-permute-done.7.refs_2_ = bf16[128,640]{1,0:T(8,128)(2,1)S(1)} collective-permute-done((bf16[128,640]{1,0:T(8,128)(2,1)S(1)}, bf16[128,640]{1,0:T(8,128)(2,1)S(1)}, u32[]{:S(2)}, u32[]{:S(2)}) %collective-permute-start.7) | collective-permute-done | bytes 163872 | tf_op jit(solution)/shard_map/ppermute | solution.py:397
  43.0 3.3 %copy.10 = bf16[640,3,640]{0,2,1:T(8,128)(2,1)} copy(bf16[640,3,640]{2,0,1:T(8,128)(2,1)S(1)} %constant_dynamic-slice_fusion) | data formatting | bytes 4915200
  46.3 2.9 %collective-permute-done.8.refs_3_ = bf16[128,640]{1,0:T(8,128)(2,1)} collective-permute-done((bf16[128,640]{1,0:T(8,128)(2,1)}, bf16[128,640]{1,0:T(8,128)(2,1)}, u32[]{:S(2)}, u32[]{:S(2)}) %collective-permute-start.8) | collective-permute-done | bytes 163872 | tf_op jit(solution)/shard_map/ppermute | solution.py:397
  49.2 5.4 %shard_map.87.refs_4_ = bf16[320,1920]{1,0:T(8,128)(2,1)} custom-call(s32[22]{0:T(128)} %stack.79.place_ref, bf16[3,640,640]{2,1,0:T(8,128)(2,1)} %bitcast.23, bf16[128,640]{1,0:T(8,128)(2,1)} %get-tuple-element.35.refs_0_, bf16[128,640]{1,0:T(8,128)(2,1)} %copy-done.23, bf16[128,640]{1,0:T(8,128)(2,1)} %copy-done.25, ...), custom_call_target="tpu_custom_call" | custom-call | flops 1258291200 | bytes 4341848 | tf_op jit(solution)/shard_map/pallas_call | solution.py:53
  55.3 5.8 %shard_map.88 = (bf16[80,1920]{1,0:T(8,128)(2,1)}, bf16[80,1920]{1,0:T(8,128)(2,1)}, bf16[80,1920]{1,0:T(8,128)(2,1)}, bf16[80,1920]{1,0:T(8,128)(2,1)}) custom-call(s32[22]{0:T(128)} %stack.79.place_ref, bf16[3,640,640]{2,1,0:T(8,128)(2,1)} %bitcast.24, bf16[128,640]{1,0:T(8,128)(2,1)} %copy-done.21, bf16[128,640]{1,0:T(8,128)(2,1)} %copy-done.22, ...), custom_call_target="tpu_custom_call" | custom-call | flops 1258291200 | bytes 5570648 | tf_op jit(solution)/shard_map/pallas_call | solution.py:53
  61.2 3.1 %collective-permute-start.10 = (bf16[80,1920]{1,0:T(8,128)(2,1)}, bf16[80,1920]{1,0:T(8,128)(2,1)S(1)}, u32[]{:S(2)}, u32[]{:S(2)}) collective-permute-start(bf16[80,1920]{1,0:T(8,128)(2,1)} %get-tuple-element.42), channel_id=1, source_target_pairs={{0,8},{1,9},{2,10},{3,11},{4,12},{5,13},{6,14},{7,15},{8,0},{9,1},... | collective-permute-start | bytes 921608 | tf_op jit(solution)/shard_map/ppermute | solution.py:397
  64.3 8.3 %collective-permute-done.10 = bf16[80,1920]{1,0:T(8,128)(2,1)S(1)} collective-permute-done((bf16[80,1920]{1,0:T(8,128)(2,1)}, bf16[80,1920]{1,0:T(8,128)(2,1)S(1)}, u32[]{:S(2)}, u32[]{:S(2)}) %collective-permute-start.10) | collective-permute-done | bytes 307232 | tf_op jit(solution)/shard_map/ppermute | solution.py:397
  78.3 4.2 %collective-permute-done.9 = bf16[80,1920]{1,0:T(8,128)(2,1)S(1)} collective-permute-done((bf16[80,1920]{1,0:T(8,128)(2,1)}, bf16[80,1920]{1,0:T(8,128)(2,1)S(1)}, u32[]{:S(2)}, u32[]{:S(2)}) %collective-permute-start.9) | collective-permute-done | bytes 307232 | tf_op jit(solution)/shard_map/ppermute | solution.py:397
  82.5 5.1 %collective-permute-done.11 = bf16[80,1920]{1,0:T(8,128)(2,1)S(1)} collective-permute-done((bf16[80,1920]{1,0:T(8,128)(2,1)S(1)}, bf16[80,1920]{1,0:T(8,128)(2,1)S(1)}, u32[]{:S(2)}, u32[]{:S(2)}) %collective-permute-start.11) | collective-permute-done | bytes 307232 | tf_op jit(solution)/shard_map/ppermute | solution.py:397
  88.8 4.0 %shard_map.84 = (bf16[512,1280]{1,0:T(8,128)(2,1)}, bf16[512,640]{1,0:T(8,128)(2,1)}) custom-call(bf16[512,512]{1,0:T(8,128)(2,1)} %shard_map.82.choose_ref, bf16[512,1920]{1,0:T(8,128)(2,1)} %bitcast.22.in_ref), custom_call_target="tpu_custom_call" | custom-call | flops 1006632960 | bytes 4456448 | tf_op jit(solution)/shard_map/pallas_call | solution.py:53
  93.8 3.5 %collective-permute-start.12 = (bf16[48,1920]{1,0:T(8,128)(2,1)S(1)}, bf16[48,1920]{1,0:T(8,128)(2,1)S(1)}, u32[]{:S(2)}, u32[]{:S(2)}) collective-permute-start(bf16[48,1920]{1,0:T(8,128)(2,1)S(1)} %add_convert_fusion.3), channel_id=1, source_target_pairs={{0,16},{1,17},{2,18},{3,19},{4,20},{5,21},{6,22},{7,23},{8,24},{9,... | collective-permute-start | bytes 552968 | tf_op jit(solution)/shard_map/ppermute | solution.py:397
  97.4 2.7 %collective-permute-start.14 = (bf16[80,1920]{1,0:T(8,128)(2,1)S(1)}, bf16[80,1920]{1,0:T(8,128)(2,1)S(1)}, u32[]{:S(2)}, u32[]{:S(2)}) collective-permute-start(bf16[80,1920]{1,0:T(8,128)(2,1)S(1)} %get-tuple-element.47.refs_0_), channel_id=1, source_target_pairs={{0,8},{1,9},{2,10},{3,11},{4,12},{5,13},{6,14},{7,15},{8,0},{9,1},... | collective-permute-start | bytes 921608 | tf_op jit(solution)/shard_map/ppermute | solution.py:397
  100.2 25.9 %collective-permute-done.13.refs_2_ = bf16[32,1920]{1,0:T(8,128)(2,1)S(1)} collective-permute-done((bf16[32,1920]{1,0:T(8,128)(2,1)S(1)}, bf16[32,1920]{1,0:T(8,128)(2,1)S(1)}, u32[]{:S(2)}, u32[]{:S(2)}) %collective-permute-start.13) | collective-permute-done | bytes 122912 | tf_op jit(solution)/shard_map/ppermute | solution.py:397
  126.0 6.1 %collective-permute-done.16.refs_5_ = bf16[32,1920]{1,0:T(8,128)(2,1)S(1)} collective-permute-done((bf16[32,1920]{1,0:T(8,128)(2,1)S(1)}, bf16[32,1920]{1,0:T(8,128)(2,1)S(1)}, u32[]{:S(2)}, u32[]{:S(2)}) %collective-permute-start.16) | collective-permute-done | bytes 122912 | tf_op jit(solution)/shard_map/ppermute | solution.py:397
  133.4 4.4 %collective-permute-done.15.refs_4_ = bf16[48,1920]{1,0:T(8,128)(2,1)} collective-permute-done((bf16[48,1920]{1,0:T(8,128)(2,1)S(1)}, bf16[48,1920]{1,0:T(8,128)(2,1)}, u32[]{:S(2)}, u32[]{:S(2)}) %collective-permute-start.15) | collective-permute-done | bytes 184352 | tf_op jit(solution)/shard_map/ppermute | solution.py:397
  143.2 8.2 %shard_map.85 = (f32[512,640]{1,0:T(8,128)S(1)}, f32[512,128]{1,0:T(8,128)S(1)}) custom-call(s32[22]{0:T(128)S(1)} %copy-done.7, bf16[512,640]{1,0:T(8,128)(2,1)S(1)} %copy-done.1, s32[8,512]{1,0:T(8,128)S(1)} %reshape.18.ids_ref, bf16[512,1280]{1,0:T(8,128)(2,1)S(1)} %copy-done.8, bf16[512,1280]{1,0:T(8,128)(2,1)S(1)} %copy-done.10), custom_call_target="tpu_custom_call" | custom-call | flops 1006632960 | bytes 4866136 | tf_op jit(solution)/shard_map/pallas_call | solution.py:53
  151.5 6.5 %shard_map.86.attended_ref = f32[512,640]{1,0:T(8,128)S(1)} custom-call(s32[22]{0:T(128)S(1)} %copy-done.7, bf16[512,640]{1,0:T(8,128)(2,1)S(1)} %copy-done.2, s32[8,512]{1,0:T(8,128)S(1)} %reshape.18.ids_ref, f32[512,640]{1,0:T(8,128)S(1)} %get-tuple-element.29.near_ref, f32[512,128]{1,0:T(8,128)S(1)} %get-tuple-element.30.stat_ref, ...), custom_call_target="tpu_custom_call" | custom-call | flops 503316480 | bytes 4866136 | tf_op jit(solution)/shard_map/pallas_call | solution.py:53
  158.1 5.1 %shard_map.89 = (bf16[128,640]{1,0:T(8,128)(2,1)S(1)}, bf16[128,640]{1,0:T(8,128)(2,1)S(1)}, bf16[128,640]{1,0:T(8,128)(2,1)S(1)}, bf16[128,640]{1,0:T(8,128)(2,1)S(1)}) custom-call(s32[22]{0:T(128)S(1)} %copy-done.7, bf16[3,640,640]{2,1,0:T(8,128)(2,1)S(1)} %bitcast.25, bf16[512,640]{1,0:T(8,128)(2,1)S(1)} %copy-done.2, ...), custom_call_target="tpu_custom_call" | custom-call | flops 1258291200 | bytes 7536728 | tf_op jit(solution)/shard_map/pallas_call | solution.py:53
  165.6 2.9 %collective-permute-start.25 = (bf16[128,640]{1,0:T(8,128)(2,1)S(1)}, bf16[128,640]{1,0:T(8,128)(2,1)S(1)}, u32[]{:S(2)}, u32[]{:S(2)}) collective-permute-start(bf16[128,640]{1,0:T(8,128)(2,1)S(1)} %get-tuple-element.45), channel_id=1, source_target_pairs={{0,1},{1,5},{2,3},{3,7},{4,0},{5,4},{6,2},{7,6},{8,9},{9,13},{10,1... | collective-permute-start | bytes 491528 | tf_op jit(solution)/shard_map/ppermute | solution.py:397
  169.3 6.5 %collective-permute-done.25.refs_2_ = bf16[128,640]{1,0:T(8,128)(2,1)S(1)} collective-permute-done((bf16[128,640]{1,0:T(8,128)(2,1)S(1)}, bf16[128,640]{1,0:T(8,128)(2,1)S(1)}, u32[]{:S(2)}, u32[]{:S(2)}) %collective-permute-start.25) | collective-permute-done | bytes 163872 | tf_op jit(solution)/shard_map/ppermute | solution.py:397
  (104 shorter events, 29.9 us)
Async XLA Ops:
  5.0 83.7 %all-to-all-start = ((bf16[32,16,1920]{2,1,0:T(8,128)(2,1)}), bf16[32,16,1920]{2,1,0:T(8,128)(2,1)}, u32[]{:S(2)}, u32[]{:S(2)}) async-start(bf16[32,16,1920]{2,1,0:T(8,128)(2,1)} %bitcast.26), calls=%async_computation | async-start | bytes 3932160 | tf_op jit(solution)/shard_map/all_to_all | solution.py:446
  12.5 19.6 %collective-permute-start.6 = (bf16[128,640]{1,0:T(8,128)(2,1)S(1)}, bf16[128,640]{1,0:T(8,128)(2,1)S(1)}, u32[]{:S(2)}, u32[]{:S(2)}) collective-permute-start(bf16[128,640]{1,0:T(8,128)(2,1)S(1)} %copy-done.26), channel_id=1, source_target_pairs={{0,2},{1,3},{2,0},{3,1},{4,6},{5,7},{6,4},{7,5},{8,10},{9,11},{10,... | collective-permute-start | bytes 491528 | tf_op jit(solution)/shard_map/ppermute | solution.py:397
  14.3 24.5 %collective-permute-start.7 = (bf16[128,640]{1,0:T(8,128)(2,1)S(1)}, bf16[128,640]{1,0:T(8,128)(2,1)S(1)}, u32[]{:S(2)}, u32[]{:S(2)}) collective-permute-start(bf16[128,640]{1,0:T(8,128)(2,1)S(1)} %copy-done.24), channel_id=1, source_target_pairs={{0,3},{1,2},{2,1},{3,0},{4,7},{5,6},{6,5},{7,4},{8,11},{9,10},{10,... | collective-permute-start | bytes 491528 | tf_op jit(solution)/shard_map/ppermute | solution.py:397
  14.3 40.3 %collective-permute-start.2 = (bf16[128,640]{1,0:T(8,128)(2,1)S(1)}, bf16[128,640]{1,0:T(8,128)(2,1)S(1)}, u32[]{:S(2)}, u32[]{:S(2)}) collective-permute-start(bf16[128,640]{1,0:T(8,128)(2,1)S(1)} %copy-done.20), channel_id=1, source_target_pairs={{0,7},{1,6},{2,5},{3,4},{4,3},{5,2},{6,1},{7,0},{8,15},{9,14},{10,... | collective-permute-start | bytes 491528 | tf_op jit(solution)/shard_map/ppermute | solution.py:397
  16.9 37.7 %collective-permute-start.3 = (bf16[128,640]{1,0:T(8,128)(2,1)S(1)}, bf16[128,640]{1,0:T(8,128)(2,1)S(1)}, u32[]{:S(2)}, u32[]{:S(2)}) collective-permute-start(bf16[128,640]{1,0:T(8,128)(2,1)S(1)} %copy-done.19), channel_id=1, source_target_pairs={{0,4},{1,5},{2,6},{3,7},{4,0},{5,1},{6,2},{7,3},{8,12},{9,13},{10,... | collective-permute-start | bytes 491528 | tf_op jit(solution)/shard_map/ppermute | solution.py:397
  17.5 37.1 %collective-permute-start.4 = (bf16[128,640]{1,0:T(8,128)(2,1)S(1)}, bf16[128,640]{1,0:T(8,128)(2,1)}, u32[]{:S(2)}, u32[]{:S(2)}) collective-permute-start(bf16[128,640]{1,0:T(8,128)(2,1)S(1)} %copy-done.18), channel_id=1, source_target_pairs={{0,5},{1,4},{2,7},{3,6},{4,1},{5,0},{6,3},{7,2},{8,13},{9,12},{10,... | collective-permute-start | bytes 491528 | tf_op jit(solution)/shard_map/ppermute | solution.py:397
  32.2 22.5 %collective-permute-start.5 = (bf16[128,640]{1,0:T(8,128)(2,1)S(1)}, bf16[128,640]{1,0:T(8,128)(2,1)}, u32[]{:S(2)}, u32[]{:S(2)}) collective-permute-start(bf16[128,640]{1,0:T(8,128)(2,1)S(1)} %copy-done.17), channel_id=1, source_target_pairs={{0,1},{1,0},{2,3},{3,2},{4,5},{5,4},{6,7},{7,6},{8,9},{9,8},{10,11... | collective-permute-start | bytes 491528 | tf_op jit(solution)/shard_map/ppermute | solution.py:397
  39.4 9.8 %collective-permute-start.8 = (bf16[128,640]{1,0:T(8,128)(2,1)}, bf16[128,640]{1,0:T(8,128)(2,1)}, u32[]{:S(2)}, u32[]{:S(2)}) collective-permute-start(bf16[128,640]{1,0:T(8,128)(2,1)} %get-tuple-element.38), channel_id=1, source_target_pairs={{0,6},{1,7},{2,4},{3,5},{4,2},{5,3},{6,0},{7,1},{8,14},{9,15},{10,... | collective-permute-start | bytes 491528 | tf_op jit(solution)/shard_map/ppermute | solution.py:397
  61.2 11.5 %collective-permute-start.10 = (bf16[80,1920]{1,0:T(8,128)(2,1)}, bf16[80,1920]{1,0:T(8,128)(2,1)S(1)}, u32[]{:S(2)}, u32[]{:S(2)}) collective-permute-start(bf16[80,1920]{1,0:T(8,128)(2,1)} %get-tuple-element.42), channel_id=1, source_target_pairs={{0,8},{1,9},{2,10},{3,11},{4,12},{5,13},{6,14},{7,15},{8,0},{9,1},... | collective-permute-start | bytes 921608 | tf_op jit(solution)/shard_map/ppermute | solution.py:397
  64.3 18.2 %collective-permute-start.9 = (bf16[80,1920]{1,0:T(8,128)(2,1)}, bf16[80,1920]{1,0:T(8,128)(2,1)S(1)}, u32[]{:S(2)}, u32[]{:S(2)}) collective-permute-start(bf16[80,1920]{1,0:T(8,128)(2,1)} %get-tuple-element.40), channel_id=1, source_target_pairs={{0,8},{1,9},{2,10},{3,11},{4,12},{5,13},{6,14},{7,15},{8,0},{9,1},... | collective-permute-start | bytes 921608 | tf_op jit(solution)/shard_map/ppermute | solution.py:397
  73.7 14.0 %collective-permute-start.11 = (bf16[80,1920]{1,0:T(8,128)(2,1)S(1)}, bf16[80,1920]{1,0:T(8,128)(2,1)S(1)}, u32[]{:S(2)}, u32[]{:S(2)}) collective-permute-start(bf16[80,1920]{1,0:T(8,128)(2,1)S(1)} %add_convert_fusion.1), channel_id=1, source_target_pairs={{0,16},{1,17},{2,18},{3,19},{4,20},{5,21},{6,22},{7,23},{8,24},{9,... | collective-permute-start | bytes 921608 | tf_op jit(solution)/shard_map/ppermute | solution.py:397
  92.8 45.0 %collective-permute-start = (bf16[512,1280]{1,0:T(8,128)(2,1)}, bf16[512,1280]{1,0:T(8,128)(2,1)S(1)}, u32[]{:S(2)}, u32[]{:S(2)}) collective-permute-start(bf16[512,1280]{1,0:T(8,128)(2,1)} %get-tuple-element.28.kv_ref), channel_id=1, source_target_pairs={{0,1},{1,0},{2,3},{3,2},{4,5},{5,4},{6,7},{7,6},{8,9},{9,8},{10,11... | collective-permute-start | bytes 3932168 | tf_op jit(solution)/shard_map/ppermute | solution.py:397
  92.8 46.6 %collective-permute-start.1 = (bf16[512,1280]{1,0:T(8,128)(2,1)}, bf16[512,1280]{1,0:T(8,128)(2,1)S(1)}, u32[]{:S(2)}, u32[]{:S(2)}) collective-permute-start(bf16[512,1280]{1,0:T(8,128)(2,1)} %get-tuple-element.28.kv_ref), channel_id=1, source_target_pairs={{1,8},{3,10},{5,12},{7,14},{8,1},{9,16},{10,3},{11,18},{12,5},{13,... | collective-permute-start | bytes 3932168 | tf_op jit(solution)/shard_map/ppermute | solution.py:397
  93.8 32.3 %collective-permute-start.12 = (bf16[48,1920]{1,0:T(8,128)(2,1)S(1)}, bf16[48,1920]{1,0:T(8,128)(2,1)S(1)}, u32[]{:S(2)}, u32[]{:S(2)}) collective-permute-start(bf16[48,1920]{1,0:T(8,128)(2,1)S(1)} %add_convert_fusion.3), channel_id=1, source_target_pairs={{0,16},{1,17},{2,18},{3,19},{4,20},{5,21},{6,22},{7,23},{8,24},{9,... | collective-permute-start | bytes 552968 | tf_op jit(solution)/shard_map/ppermute | solution.py:397
  97.3 28.7 %collective-permute-start.13 = (bf16[32,1920]{1,0:T(8,128)(2,1)S(1)}, bf16[32,1920]{1,0:T(8,128)(2,1)S(1)}, u32[]{:S(2)}, u32[]{:S(2)}) collective-permute-start(bf16[32,1920]{1,0:T(8,128)(2,1)S(1)} %add_convert_fusion.4), channel_id=1, source_target_pairs={{0,16},{1,17},{2,18},{3,19},{4,20},{5,21},{6,22},{7,23},{8,24},{9,... | collective-permute-start | bytes 368648 | tf_op jit(solution)/shard_map/ppermute | solution.py:397
  97.4 35.4 %collective-permute-start.14 = (bf16[80,1920]{1,0:T(8,128)(2,1)S(1)}, bf16[80,1920]{1,0:T(8,128)(2,1)S(1)}, u32[]{:S(2)}, u32[]{:S(2)}) collective-permute-start(bf16[80,1920]{1,0:T(8,128)(2,1)S(1)} %get-tuple-element.47.refs_0_), channel_id=1, source_target_pairs={{0,8},{1,9},{2,10},{3,11},{4,12},{5,13},{6,14},{7,15},{8,0},{9,1},... | collective-permute-start | bytes 921608 | tf_op jit(solution)/shard_map/ppermute | solution.py:397
  126.0 6.1 %collective-permute-start.19 = (bf16[32,1920]{1,0:T(8,128)(2,1)S(1)}, bf16[32,1920]{1,0:T(8,128)(2,1)S(1)}, u32[]{:S(2)}, u32[]{:S(2)}) collective-permute-start(bf16[32,1920]{1,0:T(8,128)(2,1)S(1)} %collective-permute-done.13.refs_2_), channel_id=1, source_target_pairs={{0,1},{1,0},{2,3},{3,2},{4,5},{5,4},{6,7},{7,6},{8,9},{9,8},{10,11... | collective-permute-start | bytes 368648 | tf_op jit(solution)/shard_map/ppermute | solution.py:397
  132.9 25.2 %collective-permute-start.17 = (bf16[80,1920]{1,0:T(8,128)(2,1)S(1)}, bf16[80,1920]{1,0:T(8,128)(2,1)S(1)}, u32[]{:S(2)}, u32[]{:S(2)}) collective-permute-start(bf16[80,1920]{1,0:T(8,128)(2,1)S(1)} %get-tuple-element.47.refs_0_), channel_id=1, source_target_pairs={{0,1},{1,0},{2,3},{3,2},{4,5},{5,4},{6,7},{7,6},{8,9},{9,8},{10,11... | collective-permute-start | bytes 921608 | tf_op jit(solution)/shard_map/ppermute | solution.py:397
  132.9 25.2 %collective-permute-start.20 = (bf16[80,1920]{1,0:T(8,128)(2,1)S(1)}, bf16[80,1920]{1,0:T(8,128)(2,1)S(1)}, u32[]{:S(2)}, u32[]{:S(2)}) collective-permute-start(bf16[80,1920]{1,0:T(8,128)(2,1)S(1)} %collective-permute-done.14.refs_3_), channel_id=1, source_target_pairs={{0,1},{1,0},{2,3},{3,2},{4,5},{5,4},{6,7},{7,6},{8,9},{9,8},{10,11... | collective-permute-start | bytes 921608 | tf_op jit(solution)/shard_map/ppermute | solution.py:397
  137.8 20.2 %collective-permute-start.18 = (bf16[48,1920]{1,0:T(8,128)(2,1)S(1)}, bf16[48,1920]{1,0:T(8,128)(2,1)}, u32[]{:S(2)}, u32[]{:S(2)}) collective-permute-start(bf16[48,1920]{1,0:T(8,128)(2,1)S(1)} %collective-permute-done.12.refs_1_), channel_id=1, source_target_pairs={{0,1},{1,0},{2,3},{3,2},{4,5},{5,4},{6,7},{7,6},{8,9},{9,8},{10,11... | collective-permute-start | bytes 552968 | tf_op jit(solution)/shard_map/ppermute | solution.py:397
  138.9 19.2 %collective-permute-start.21 = (bf16[48,1920]{1,0:T(8,128)(2,1)}, bf16[48,1920]{1,0:T(8,128)(2,1)}, u32[]{:S(2)}, u32[]{:S(2)}) collective-permute-start(bf16[48,1920]{1,0:T(8,128)(2,1)} %collective-permute-done.15.refs_4_), channel_id=1, source_target_pairs={{0,1},{1,0},{2,3},{3,2},{4,5},{5,4},{6,7},{7,6},{8,9},{9,8},{10,11... | collective-permute-start | bytes 552968 | tf_op jit(solution)/shard_map/ppermute | solution.py:397
  139.4 18.6 %collective-permute-start.22 = (bf16[32,1920]{1,0:T(8,128)(2,1)}, bf16[32,1920]{1,0:T(8,128)(2,1)S(1)}, u32[]{:S(2)}, u32[]{:S(2)}) collective-permute-start(bf16[32,1920]{1,0:T(8,128)(2,1)} %copy-done.3), channel_id=1, source_target_pairs={{0,1},{1,0},{2,3},{3,2},{4,5},{5,4},{6,7},{7,6},{8,9},{9,8},{10,11... | collective-permute-start | bytes 368648 | tf_op jit(solution)/shard_map/ppermute | solution.py:397
  165.6 10.2 %collective-permute-start.25 = (bf16[128,640]{1,0:T(8,128)(2,1)S(1)}, bf16[128,640]{1,0:T(8,128)(2,1)S(1)}, u32[]{:S(2)}, u32[]{:S(2)}) collective-permute-start(bf16[128,640]{1,0:T(8,128)(2,1)S(1)} %get-tuple-element.45), channel_id=1, source_target_pairs={{0,1},{1,5},{2,3},{3,7},{4,0},{5,4},{6,2},{7,6},{8,9},{9,13},{10,1... | collective-permute-start | bytes 491528 | tf_op jit(solution)/shard_map/ppermute | solution.py:397
  168.5 7.3 %collective-permute-start.26 = (bf16[128,640]{1,0:T(8,128)(2,1)S(1)}, bf16[128,640]{1,0:T(8,128)(2,1)S(1)}, u32[]{:S(2)}, u32[]{:S(2)}) collective-permute-start(bf16[128,640]{1,0:T(8,128)(2,1)S(1)} %get-tuple-element.46), channel_id=1, source_target_pairs={{0,3},{1,7},{2,1},{3,5},{4,2},{5,6},{6,0},{7,4},{8,11},{9,15},{10,... | collective-permute-start | bytes 491528 | tf_op jit(solution)/shard_map/ppermute | solution.py:397
  (31 other events, 324.4 us)

commit v8 on v7

--- a/solution.py
+++ b/solution.py
@@ -338,18 +338,19 @@
         ref[...] = rows_buf[pl.ds(begin, block), :]
 
 
-def norm_kernel(place_ref, *refs):
-    part_refs, gain_ref, out_ref, buf = refs[:PARTS], refs[PARTS], refs[PARTS + 1], refs[PARTS + 2]
-    square = jnp.zeros((out_ref.shape[0], 1), F32)
+def norm_kernel(place_ref, gain_ref, *refs):
+    part_refs, (out_ref, buf, sems) = refs[:PARTS], refs[PARTS:]
+    copies = []
     for index, ref in enumerate(part_refs):
-        rows = ref[...]
-        buf[place_ref[4 + index]] = rows
-        wide = rows.astype(F32)
-        square += jnp.sum(wide * wide, axis=1, keepdims=True)
-    factor = lax.rsqrt(square / WIDTH + EPS)
-    for part in range(PARTS):
-        lanes = slice(part * PART_WIDTH, (part + 1) * PART_WIDTH)
-        out_ref[:, lanes] = (buf[part].astype(F32) * factor * gain_ref[:, lanes]).astype(BF16)
+        begin = pl.multiple_of(place_ref[4 + index] * PART_WIDTH, LANES)
+        copies.append(pltpu.make_async_copy(ref, buf.at[:, pl.ds(begin, PART_WIDTH)], sems.at[index]))
+    for copy in copies:
+        copy.start()
+    for copy in copies:
+        copy.wait()
+    rows = buf[...].astype(F32)
+    square = jnp.sum(rows * rows, axis=1, keepdims=True)
+    out_ref[...] = (rows * lax.rsqrt(square / WIDTH + EPS) * gain_ref[...]).astype(BF16)
 
 
 def gather_layout(bits, piece, relay):
@@ -552,8 +553,9 @@
     (out,) = call(
         norm_kernel,
         [jax.ShapeDtypeStruct((tok_dev, WIDTH), BF16)],
-        [place] + parts + [norm_gain.reshape(1, WIDTH)],
-        scratch=[VMEM((PARTS, tok_dev, PART_WIDTH), BF16)],
+        [place, norm_gain.reshape(1, WIDTH)] + parts,
+        in_specs=[pl.BlockSpec(memory_space=VMEM)] + [pl.BlockSpec(memory_space=pltpu.HBM)] * PARTS,
+        scratch=[VMEM((tok_dev, WIDTH), BF16), pltpu.SemaphoreType.DMA((PARTS,))],
         smem=1, flops=6 * tok_dev * WIDTH,
     )
     return out

time: 180 us -> 181 us (level)
  no operation moved by 1% of the time
where the time goes in v8:
time: 181 us; the launch traced here: 180 us
  waiting for transfers between devices  84.3 us (47%)
  Pallas kernels  44.6 us (25%)
  starting transfers between devices  33.9 us (19%)
  local copies, waits for them, and re-layouts  14.7 us (8%)
  other arithmetic  2.23 us (1%)
    ppermute x27, waiting for transfers between devices, permute(): return lax.ppermute(array, 'tok', route)  84.3 us
    pallas_call x9, Pallas kernels, call(): pl.pallas_call(kernel, out_shape=list(outs), in_specs=specs, out_specs=ou...  44.6 us
    ppermute x27, starting transfers between devices, permute(): return lax.ppermute(array, 'tok', route)  26.4 us
    unnamed x55, local copies, waits for them, and re-layouts  11.5 us
    all_to_all x1, starting transfers between devices, shards(): lax.all_to_all(packed.reshape(sections, slots, 3 * PART_WIDTH), 'tok', sp...  7.45 us
  transfers between devices with their start and end apart: 28, of which 11 were waited for; matrix products, arithmetic and copies ran while one was open for 4% of the time, Pallas kernels for 16%

profile of v8, /device:TPU:0, one launch (start us, length us, event | category | flops | bytes accessed | tf_op | source)
XLA Modules:
  0.0 180.3 jit_solution(3911437492889822510)
XLA Ops:
  0.7 4.3 %shard_map.83 = (bf16[4,4,2,16,1920]{4,3,2,1,0:T(8,128)(2,1)}, bf16[128,640]{1,0:T(8,128)(2,1)}, bf16[128,640]{1,0:T(8,128)(2,1)}, bf16[128,640]{1,0:T(8,128)(2,...) custom-call(s32[22]{0:T(128)} %stack.79.place_ref, ...), custom_call_target="tpu_custom_call" | custom-call | flops 251658240 | bytes 5263448 | tf_op jit(solution)/shard_map/pallas_call | solution.py:53
  5.0 7.5 %all-to-all-start = ((bf16[32,16,1920]{2,1,0:T(8,128)(2,1)}), bf16[32,16,1920]{2,1,0:T(8,128)(2,1)}, u32[]{:S(2)}, u32[]{:S(2)}) async-start(bf16[32,16,1920]{2,1,0:T(8,128)(2,1)} %bitcast.26), calls=%async_computation | async-start | bytes 3932160 | tf_op jit(solution)/shard_map/all_to_all | solution.py:447
  18.1 14.0 %collective-permute-done.6.refs_1_ = bf16[128,640]{1,0:T(8,128)(2,1)S(1)} collective-permute-done((bf16[128,640]{1,0:T(8,128)(2,1)S(1)}, bf16[128,640]{1,0:T(8,128)(2,1)S(1)}, u32[]{:S(2)}, u32[]{:S(2)}) %collective-permute-start.6) | collective-permute-done | bytes 163872 | tf_op jit(solution)/shard_map/ppermute | solution.py:398
  32.2 6.6 %collective-permute-done.7.refs_2_ = bf16[128,640]{1,0:T(8,128)(2,1)S(1)} collective-permute-done((bf16[128,640]{1,0:T(8,128)(2,1)S(1)}, bf16[128,640]{1,0:T(8,128)(2,1)S(1)}, u32[]{:S(2)}, u32[]{:S(2)}) %collective-permute-start.7) | collective-permute-done | bytes 163872 | tf_op jit(solution)/shard_map/ppermute | solution.py:398
  43.0 3.3 %copy.10 = bf16[640,3,640]{0,2,1:T(8,128)(2,1)} copy(bf16[640,3,640]{2,0,1:T(8,128)(2,1)S(1)} %constant_dynamic-slice_fusion) | data formatting | bytes 4915200
  46.3 2.9 %collective-permute-done.8.refs_3_ = bf16[128,640]{1,0:T(8,128)(2,1)} collective-permute-done((bf16[128,640]{1,0:T(8,128)(2,1)}, bf16[128,640]{1,0:T(8,128)(2,1)}, u32[]{:S(2)}, u32[]{:S(2)}) %collective-permute-start.8) | collective-permute-done | bytes 163872 | tf_op jit(solution)/shard_map/ppermute | solution.py:398
  49.2 5.4 %shard_map.87.refs_4_ = bf16[320,1920]{1,0:T(8,128)(2,1)} custom-call(s32[22]{0:T(128)} %stack.79.place_ref, bf16[3,640,640]{2,1,0:T(8,128)(2,1)} %bitcast.23, bf16[128,640]{1,0:T(8,128)(2,1)} %get-tuple-element.35.refs_0_, bf16[128,640]{1,0:T(8,128)(2,1)} %copy-done.23, bf16[128,640]{1,0:T(8,128)(2,1)} %copy-done.25, ...), custom_call_target="tpu_custom_call" | custom-call | flops 1258291200 | bytes 4341848 | tf_op jit(solution)/shard_map/pallas_call | solution.py:53
  55.3 5.8 %shard_map.88 = (bf16[80,1920]{1,0:T(8,128)(2,1)}, bf16[80,1920]{1,0:T(8,128)(2,1)}, bf16[80,1920]{1,0:T(8,128)(2,1)}, bf16[80,1920]{1,0:T(8,128)(2,1)}) custom-call(s32[22]{0:T(128)} %stack.79.place_ref, bf16[3,640,640]{2,1,0:T(8,128)(2,1)} %bitcast.24, bf16[128,640]{1,0:T(8,128)(2,1)} %copy-done.21, bf16[128,640]{1,0:T(8,128)(2,1)} %copy-done.22, ...), custom_call_target="tpu_custom_call" | custom-call | flops 1258291200 | bytes 5570648 | tf_op jit(solution)/shard_map/pallas_call | solution.py:53
  61.2 3.1 %collective-permute-start.10 = (bf16[80,1920]{1,0:T(8,128)(2,1)}, bf16[80,1920]{1,0:T(8,128)(2,1)S(1)}, u32[]{:S(2)}, u32[]{:S(2)}) collective-permute-start(bf16[80,1920]{1,0:T(8,128)(2,1)} %get-tuple-element.42), channel_id=1, source_target_pairs={{0,8},{1,9},{2,10},{3,11},{4,12},{5,13},{6,14},{7,15},{8,0},{9,1},... | collective-permute-start | bytes 921608 | tf_op jit(solution)/shard_map/ppermute | solution.py:398
  64.3 8.3 %collective-permute-done.10 = bf16[80,1920]{1,0:T(8,128)(2,1)S(1)} collective-permute-done((bf16[80,1920]{1,0:T(8,128)(2,1)}, bf16[80,1920]{1,0:T(8,128)(2,1)S(1)}, u32[]{:S(2)}, u32[]{:S(2)}) %collective-permute-start.10) | collective-permute-done | bytes 307232 | tf_op jit(solution)/shard_map/ppermute | solution.py:398
  78.3 4.2 %collective-permute-done.9 = bf16[80,1920]{1,0:T(8,128)(2,1)S(1)} collective-permute-done((bf16[80,1920]{1,0:T(8,128)(2,1)}, bf16[80,1920]{1,0:T(8,128)(2,1)S(1)}, u32[]{:S(2)}, u32[]{:S(2)}) %collective-permute-start.9) | collective-permute-done | bytes 307232 | tf_op jit(solution)/shard_map/ppermute | solution.py:398
  82.5 5.1 %collective-permute-done.11 = bf16[80,1920]{1,0:T(8,128)(2,1)S(1)} collective-permute-done((bf16[80,1920]{1,0:T(8,128)(2,1)S(1)}, bf16[80,1920]{1,0:T(8,128)(2,1)S(1)}, u32[]{:S(2)}, u32[]{:S(2)}) %collective-permute-start.11) | collective-permute-done | bytes 307232 | tf_op jit(solution)/shard_map/ppermute | solution.py:398
  88.8 4.0 %shard_map.84 = (bf16[512,1280]{1,0:T(8,128)(2,1)}, bf16[512,640]{1,0:T(8,128)(2,1)}) custom-call(bf16[512,512]{1,0:T(8,128)(2,1)} %shard_map.82.choose_ref, bf16[512,1920]{1,0:T(8,128)(2,1)} %bitcast.22.in_ref), custom_call_target="tpu_custom_call" | custom-call | flops 1006632960 | bytes 4456448 | tf_op jit(solution)/shard_map/pallas_call | solution.py:53
  93.8 3.5 %collective-permute-start.12 = (bf16[48,1920]{1,0:T(8,128)(2,1)S(1)}, bf16[48,1920]{1,0:T(8,128)(2,1)S(1)}, u32[]{:S(2)}, u32[]{:S(2)}) collective-permute-start(bf16[48,1920]{1,0:T(8,128)(2,1)S(1)} %add_convert_fusion.3), channel_id=1, source_target_pairs={{0,16},{1,17},{2,18},{3,19},{4,20},{5,21},{6,22},{7,23},{8,24},{9,... | collective-permute-start | bytes 552968 | tf_op jit(solution)/shard_map/ppermute | solution.py:398
  97.4 2.7 %collective-permute-start.14 = (bf16[80,1920]{1,0:T(8,128)(2,1)S(1)}, bf16[80,1920]{1,0:T(8,128)(2,1)S(1)}, u32[]{:S(2)}, u32[]{:S(2)}) collective-permute-start(bf16[80,1920]{1,0:T(8,128)(2,1)S(1)} %get-tuple-element.47.refs_0_), channel_id=1, source_target_pairs={{0,8},{1,9},{2,10},{3,11},{4,12},{5,13},{6,14},{7,15},{8,0},{9,1},... | collective-permute-start | bytes 921608 | tf_op jit(solution)/shard_map/ppermute | solution.py:398
  100.2 25.9 %collective-permute-done.13.refs_2_ = bf16[32,1920]{1,0:T(8,128)(2,1)S(1)} collective-permute-done((bf16[32,1920]{1,0:T(8,128)(2,1)S(1)}, bf16[32,1920]{1,0:T(8,128)(2,1)S(1)}, u32[]{:S(2)}, u32[]{:S(2)}) %collective-permute-start.13) | collective-permute-done | bytes 122912 | tf_op jit(solution)/shard_map/ppermute | solution.py:398
  126.0 6.1 %collective-permute-done.16.refs_5_ = bf16[32,1920]{1,0:T(8,128)(2,1)S(1)} collective-permute-done((bf16[32,1920]{1,0:T(8,128)(2,1)S(1)}, bf16[32,1920]{1,0:T(8,128)(2,1)S(1)}, u32[]{:S(2)}, u32[]{:S(2)}) %collective-permute-start.16) | collective-permute-done | bytes 122912 | tf_op jit(solution)/shard_map/ppermute | solution.py:398
  133.4 4.4 %collective-permute-done.15.refs_4_ = bf16[48,1920]{1,0:T(8,128)(2,1)} collective-permute-done((bf16[48,1920]{1,0:T(8,128)(2,1)S(1)}, bf16[48,1920]{1,0:T(8,128)(2,1)}, u32[]{:S(2)}, u32[]{:S(2)}) %collective-permute-start.15) | collective-permute-done | bytes 184352 | tf_op jit(solution)/shard_map/ppermute | solution.py:398
  143.2 8.2 %shard_map.85 = (f32[512,640]{1,0:T(8,128)S(1)}, f32[512,128]{1,0:T(8,128)S(1)}) custom-call(s32[22]{0:T(128)S(1)} %copy-done.7, bf16[512,640]{1,0:T(8,128)(2,1)S(1)} %copy-done.1, s32[8,512]{1,0:T(8,128)S(1)} %reshape.19.ids_ref, bf16[512,1280]{1,0:T(8,128)(2,1)S(1)} %copy-done.8, bf16[512,1280]{1,0:T(8,128)(2,1)S(1)} %copy-done.10), custom_call_target="tpu_custom_call" | custom-call | flops 1006632960 | bytes 4866136 | tf_op jit(solution)/shard_map/pallas_call | solution.py:53
  151.5 6.5 %shard_map.86.attended_ref = f32[512,640]{1,0:T(8,128)S(1)} custom-call(s32[22]{0:T(128)S(1)} %copy-done.7, bf16[512,640]{1,0:T(8,128)(2,1)S(1)} %copy-done.2, s32[8,512]{1,0:T(8,128)S(1)} %reshape.19.ids_ref, f32[512,640]{1,0:T(8,128)S(1)} %get-tuple-element.29.near_ref, f32[512,128]{1,0:T(8,128)S(1)} %get-tuple-element.30.stat_ref, ...), custom_call_target="tpu_custom_call" | custom-call | flops 503316480 | bytes 4866136 | tf_op jit(solution)/shard_map/pallas_call | solution.py:53
  158.1 5.1 %shard_map.89 = (bf16[128,640]{1,0:T(8,128)(2,1)S(1)}, bf16[128,640]{1,0:T(8,128)(2,1)S(1)}, bf16[128,640]{1,0:T(8,128)(2,1)S(1)}, bf16[128,640]{1,0:T(8,128)(2,1)S(1)}) custom-call(s32[22]{0:T(128)S(1)} %copy-done.7, bf16[3,640,640]{2,1,0:T(8,128)(2,1)S(1)} %bitcast.25, bf16[512,640]{1,0:T(8,128)(2,1)S(1)} %copy-done.2, ...), custom_call_target="tpu_custom_call" | custom-call | flops 1258291200 | bytes 7536728 | tf_op jit(solution)/shard_map/pallas_call | solution.py:53
  165.6 2.9 %collective-permute-start.25 = (bf16[128,640]{1,0:T(8,128)(2,1)S(1)}, bf16[128,640]{1,0:T(8,128)(2,1)S(1)}, u32[]{:S(2)}, u32[]{:S(2)}) collective-permute-start(bf16[128,640]{1,0:T(8,128)(2,1)S(1)} %get-tuple-element.45), channel_id=1, source_target_pairs={{0,1},{1,5},{2,3},{3,7},{4,0},{5,4},{6,2},{7,6},{8,9},{9,13},{10,1... | collective-permute-start | bytes 491528 | tf_op jit(solution)/shard_map/ppermute | solution.py:398
  169.3 6.5 %collective-permute-done.25.refs_2_ = bf16[128,640]{1,0:T(8,128)(2,1)S(1)} collective-permute-done((bf16[128,640]{1,0:T(8,128)(2,1)S(1)}, bf16[128,640]{1,0:T(8,128)(2,1)S(1)}, u32[]{:S(2)}, u32[]{:S(2)}) %collective-permute-start.25) | collective-permute-done | bytes 163872 | tf_op jit(solution)/shard_map/ppermute | solution.py:398
  177.1 3.0 %shard_map.90 = bf16[128,2560]{1,0:T(8,128)(2,1)} custom-call(s32[22]{0:T(128)} %stack.79.place_ref, f32[1,2560]{1,0:T(1,128)} %reshape.15.gain_ref, bf16[128,640]{1,0:T(8,128)(2,1)} %copy-done.11, bf16[128,640]{1,0:T(8,128)(2,1)} %copy-done.12, bf16[128,640]{1,0:T(8,128)(2,1)} %copy-done.13, bf16[128,640]{1,0:T(8,128)(2,1)} %copy-done.14), custom_call_target="tpu_custom_call" | custom-call | flops 1966080 | bytes 1321048 | tf_op jit(solution)/shard_map/pallas_call | solution.py:53
  (104 shorter events, 30.2 us)
Async XLA Ops:
  5.0 83.7 %all-to-all-start = ((bf16[32,16,1920]{2,1,0:T(8,128)(2,1)}), bf16[32,16,1920]{2,1,0:T(8,128)(2,1)}, u32[]{:S(2)}, u32[]{:S(2)}) async-start(bf16[32,16,1920]{2,1,0:T(8,128)(2,1)} %bitcast.26), calls=%async_computation | async-start | bytes 3932160 | tf_op jit(solution)/shard_map/all_to_all | solution.py:447
  12.5 19.6 %collective-permute-start.6 = (bf16[128,640]{1,0:T(8,128)(2,1)S(1)}, bf16[128,640]{1,0:T(8,128)(2,1)S(1)}, u32[]{:S(2)}, u32[]{:S(2)}) collective-permute-start(bf16[128,640]{1,0:T(8,128)(2,1)S(1)} %copy-done.26), channel_id=1, source_target_pairs={{0,2},{1,3},{2,0},{3,1},{4,6},{5,7},{6,4},{7,5},{8,10},{9,11},{10,... | collective-permute-start | bytes 491528 | tf_op jit(solution)/shard_map/ppermute | solution.py:398
  14.3 24.5 %collective-permute-start.7 = (bf16[128,640]{1,0:T(8,128)(2,1)S(1)}, bf16[128,640]{1,0:T(8,128)(2,1)S(1)}, u32[]{:S(2)}, u32[]{:S(2)}) collective-permute-start(bf16[128,640]{1,0:T(8,128)(2,1)S(1)} %copy-done.24), channel_id=1, source_target_pairs={{0,3},{1,2},{2,1},{3,0},{4,7},{5,6},{6,5},{7,4},{8,11},{9,10},{10,... | collective-permute-start | bytes 491528 | tf_op jit(solution)/shard_map/ppermute | solution.py:398
  14.3 40.3 %collective-permute-start.2 = (bf16[128,640]{1,0:T(8,128)(2,1)S(1)}, bf16[128,640]{1,0:T(8,128)(2,1)S(1)}, u32[]{:S(2)}, u32[]{:S(2)}) collective-permute-start(bf16[128,640]{1,0:T(8,128)(2,1)S(1)} %copy-done.20), channel_id=1, source_target_pairs={{0,7},{1,6},{2,5},{3,4},{4,3},{5,2},{6,1},{7,0},{8,15},{9,14},{10,... | collective-permute-start | bytes 491528 | tf_op jit(solution)/shard_map/ppermute | solution.py:398
  16.9 37.7 %collective-permute-start.3 = (bf16[128,640]{1,0:T(8,128)(2,1)S(1)}, bf16[128,640]{1,0:T(8,128)(2,1)S(1)}, u32[]{:S(2)}, u32[]{:S(2)}) collective-permute-start(bf16[128,640]{1,0:T(8,128)(2,1)S(1)} %copy-done.19), channel_id=1, source_target_pairs={{0,4},{1,5},{2,6},{3,7},{4,0},{5,1},{6,2},{7,3},{8,12},{9,13},{10,... | collective-permute-start | bytes 491528 | tf_op jit(solution)/shard_map/ppermute | solution.py:398
  17.5 37.1 %collective-permute-start.4 = (bf16[128,640]{1,0:T(8,128)(2,1)S(1)}, bf16[128,640]{1,0:T(8,128)(2,1)}, u32[]{:S(2)}, u32[]{:S(2)}) collective-permute-start(bf16[128,640]{1,0:T(8,128)(2,1)S(1)} %copy-done.18), channel_id=1, source_target_pairs={{0,5},{1,4},{2,7},{3,6},{4,1},{5,0},{6,3},{7,2},{8,13},{9,12},{10,... | collective-permute-start | bytes 491528 | tf_op jit(solution)/shard_map/ppermute | solution.py:398
  32.2 22.5 %collective-permute-start.5 = (bf16[128,640]{1,0:T(8,128)(2,1)S(1)}, bf16[128,640]{1,0:T(8,128)(2,1)}, u32[]{:S(2)}, u32[]{:S(2)}) collective-permute-start(bf16[128,640]{1,0:T(8,128)(2,1)S(1)} %copy-done.17), channel_id=1, source_target_pairs={{0,1},{1,0},{2,3},{3,2},{4,5},{5,4},{6,7},{7,6},{8,9},{9,8},{10,11... | collective-permute-start | bytes 491528 | tf_op jit(solution)/shard_map/ppermute | solution.py:398
  39.4 9.8 %collective-permute-start.8 = (bf16[128,640]{1,0:T(8,128)(2,1)}, bf16[128,640]{1,0:T(8,128)(2,1)}, u32[]{:S(2)}, u32[]{:S(2)}) collective-permute-start(bf16[128,640]{1,0:T(8,128)(2,1)} %get-tuple-element.38), channel_id=1, source_target_pairs={{0,6},{1,7},{2,4},{3,5},{4,2},{5,3},{6,0},{7,1},{8,14},{9,15},{10,... | collective-permute-start | bytes 491528 | tf_op jit(solution)/shard_map/ppermute | solution.py:398
  61.2 11.5 %collective-permute-start.10 = (bf16[80,1920]{1,0:T(8,128)(2,1)}, bf16[80,1920]{1,0:T(8,128)(2,1)S(1)}, u32[]{:S(2)}, u32[]{:S(2)}) collective-permute-start(bf16[80,1920]{1,0:T(8,128)(2,1)} %get-tuple-element.42), channel_id=1, source_target_pairs={{0,8},{1,9},{2,10},{3,11},{4,12},{5,13},{6,14},{7,15},{8,0},{9,1},... | collective-permute-start | bytes 921608 | tf_op jit(solution)/shard_map/ppermute | solution.py:398
  64.3 18.2 %collective-permute-start.9 = (bf16[80,1920]{1,0:T(8,128)(2,1)}, bf16[80,1920]{1,0:T(8,128)(2,1)S(1)}, u32[]{:S(2)}, u32[]{:S(2)}) collective-permute-start(bf16[80,1920]{1,0:T(8,128)(2,1)} %get-tuple-element.40), channel_id=1, source_target_pairs={{0,8},{1,9},{2,10},{3,11},{4,12},{5,13},{6,14},{7,15},{8,0},{9,1},... | collective-permute-start | bytes 921608 | tf_op jit(solution)/shard_map/ppermute | solution.py:398
  73.7 14.0 %collective-permute-start.11 = (bf16[80,1920]{1,0:T(8,128)(2,1)S(1)}, bf16[80,1920]{1,0:T(8,128)(2,1)S(1)}, u32[]{:S(2)}, u32[]{:S(2)}) collective-permute-start(bf16[80,1920]{1,0:T(8,128)(2,1)S(1)} %add_convert_fusion.1), channel_id=1, source_target_pairs={{0,16},{1,17},{2,18},{3,19},{4,20},{5,21},{6,22},{7,23},{8,24},{9,... | collective-permute-start | bytes 921608 | tf_op jit(solution)/shard_map/ppermute | solution.py:398
  92.8 45.0 %collective-permute-start = (bf16[512,1280]{1,0:T(8,128)(2,1)}, bf16[512,1280]{1,0:T(8,128)(2,1)S(1)}, u32[]{:S(2)}, u32[]{:S(2)}) collective-permute-start(bf16[512,1280]{1,0:T(8,128)(2,1)} %get-tuple-element.28.kv_ref), channel_id=1, source_target_pairs={{0,1},{1,0},{2,3},{3,2},{4,5},{5,4},{6,7},{7,6},{8,9},{9,8},{10,11... | collective-permute-start | bytes 3932168 | tf_op jit(solution)/shard_map/ppermute | solution.py:398
  92.8 46.6 %collective-permute-start.1 = (bf16[512,1280]{1,0:T(8,128)(2,1)}, bf16[512,1280]{1,0:T(8,128)(2,1)S(1)}, u32[]{:S(2)}, u32[]{:S(2)}) collective-permute-start(bf16[512,1280]{1,0:T(8,128)(2,1)} %get-tuple-element.28.kv_ref), channel_id=1, source_target_pairs={{1,8},{3,10},{5,12},{7,14},{8,1},{9,16},{10,3},{11,18},{12,5},{13,... | collective-permute-start | bytes 3932168 | tf_op jit(solution)/shard_map/ppermute | solution.py:398
  93.8 32.3 %collective-permute-start.12 = (bf16[48,1920]{1,0:T(8,128)(2,1)S(1)}, bf16[48,1920]{1,0:T(8,128)(2,1)S(1)}, u32[]{:S(2)}, u32[]{:S(2)}) collective-permute-start(bf16[48,1920]{1,0:T(8,128)(2,1)S(1)} %add_convert_fusion.3), channel_id=1, source_target_pairs={{0,16},{1,17},{2,18},{3,19},{4,20},{5,21},{6,22},{7,23},{8,24},{9,... | collective-permute-start | bytes 552968 | tf_op jit(solution)/shard_map/ppermute | solution.py:398
  97.3 28.7 %collective-permute-start.13 = (bf16[32,1920]{1,0:T(8,128)(2,1)S(1)}, bf16[32,1920]{1,0:T(8,128)(2,1)S(1)}, u32[]{:S(2)}, u32[]{:S(2)}) collective-permute-start(bf16[32,1920]{1,0:T(8,128)(2,1)S(1)} %add_convert_fusion.4), channel_id=1, source_target_pairs={{0,16},{1,17},{2,18},{3,19},{4,20},{5,21},{6,22},{7,23},{8,24},{9,... | collective-permute-start | bytes 368648 | tf_op jit(solution)/shard_map/ppermute | solution.py:398
  97.4 35.4 %collective-permute-start.14 = (bf16[80,1920]{1,0:T(8,128)(2,1)S(1)}, bf16[80,1920]{1,0:T(8,128)(2,1)S(1)}, u32[]{:S(2)}, u32[]{:S(2)}) collective-permute-start(bf16[80,1920]{1,0:T(8,128)(2,1)S(1)} %get-tuple-element.47.refs_0_), channel_id=1, source_target_pairs={{0,8},{1,9},{2,10},{3,11},{4,12},{5,13},{6,14},{7,15},{8,0},{9,1},... | collective-permute-start | bytes 921608 | tf_op jit(solution)/shard_map/ppermute | solution.py:398
  126.0 6.1 %collective-permute-start.19 = (bf16[32,1920]{1,0:T(8,128)(2,1)S(1)}, bf16[32,1920]{1,0:T(8,128)(2,1)S(1)}, u32[]{:S(2)}, u32[]{:S(2)}) collective-permute-start(bf16[32,1920]{1,0:T(8,128)(2,1)S(1)} %collective-permute-done.13.refs_2_), channel_id=1, source_target_pairs={{0,1},{1,0},{2,3},{3,2},{4,5},{5,4},{6,7},{7,6},{8,9},{9,8},{10,11... | collective-permute-start | bytes 368648 | tf_op jit(solution)/shard_map/ppermute | solution.py:398
  132.9 25.2 %collective-permute-start.17 = (bf16[80,1920]{1,0:T(8,128)(2,1)S(1)}, bf16[80,1920]{1,0:T(8,128)(2,1)S(1)}, u32[]{:S(2)}, u32[]{:S(2)}) collective-permute-start(bf16[80,1920]{1,0:T(8,128)(2,1)S(1)} %get-tuple-element.47.refs_0_), channel_id=1, source_target_pairs={{0,1},{1,0},{2,3},{3,2},{4,5},{5,4},{6,7},{7,6},{8,9},{9,8},{10,11... | collective-permute-start | bytes 921608 | tf_op jit(solution)/shard_map/ppermute | solution.py:398
  132.9 25.2 %collective-permute-start.20 = (bf16[80,1920]{1,0:T(8,128)(2,1)S(1)}, bf16[80,1920]{1,0:T(8,128)(2,1)S(1)}, u32[]{:S(2)}, u32[]{:S(2)}) collective-permute-start(bf16[80,1920]{1,0:T(8,128)(2,1)S(1)} %collective-permute-done.14.refs_3_), channel_id=1, source_target_pairs={{0,1},{1,0},{2,3},{3,2},{4,5},{5,4},{6,7},{7,6},{8,9},{9,8},{10,11... | collective-permute-start | bytes 921608 | tf_op jit(solution)/shard_map/ppermute | solution.py:398
  137.8 20.2 %collective-permute-start.18 = (bf16[48,1920]{1,0:T(8,128)(2,1)S(1)}, bf16[48,1920]{1,0:T(8,128)(2,1)}, u32[]{:S(2)}, u32[]{:S(2)}) collective-permute-start(bf16[48,1920]{1,0:T(8,128)(2,1)S(1)} %collective-permute-done.12.refs_1_), channel_id=1, source_target_pairs={{0,1},{1,0},{2,3},{3,2},{4,5},{5,4},{6,7},{7,6},{8,9},{9,8},{10,11... | collective-permute-start | bytes 552968 | tf_op jit(solution)/shard_map/ppermute | solution.py:398
  138.9 19.2 %collective-permute-start.21 = (bf16[48,1920]{1,0:T(8,128)(2,1)}, bf16[48,1920]{1,0:T(8,128)(2,1)}, u32[]{:S(2)}, u32[]{:S(2)}) collective-permute-start(bf16[48,1920]{1,0:T(8,128)(2,1)} %collective-permute-done.15.refs_4_), channel_id=1, source_target_pairs={{0,1},{1,0},{2,3},{3,2},{4,5},{5,4},{6,7},{7,6},{8,9},{9,8},{10,11... | collective-permute-start | bytes 552968 | tf_op jit(solution)/shard_map/ppermute | solution.py:398
  139.4 18.6 %collective-permute-start.22 = (bf16[32,1920]{1,0:T(8,128)(2,1)}, bf16[32,1920]{1,0:T(8,128)(2,1)S(1)}, u32[]{:S(2)}, u32[]{:S(2)}) collective-permute-start(bf16[32,1920]{1,0:T(8,128)(2,1)} %copy-done.3), channel_id=1, source_target_pairs={{0,1},{1,0},{2,3},{3,2},{4,5},{5,4},{6,7},{7,6},{8,9},{9,8},{10,11... | collective-permute-start | bytes 368648 | tf_op jit(solution)/shard_map/ppermute | solution.py:398
  165.6 10.2 %collective-permute-start.25 = (bf16[128,640]{1,0:T(8,128)(2,1)S(1)}, bf16[128,640]{1,0:T(8,128)(2,1)S(1)}, u32[]{:S(2)}, u32[]{:S(2)}) collective-permute-start(bf16[128,640]{1,0:T(8,128)(2,1)S(1)} %get-tuple-element.45), channel_id=1, source_target_pairs={{0,1},{1,5},{2,3},{3,7},{4,0},{5,4},{6,2},{7,6},{8,9},{9,13},{10,1... | collective-permute-start | bytes 491528 | tf_op jit(solution)/shard_map/ppermute | solution.py:398
  168.5 7.3 %collective-permute-start.26 = (bf16[128,640]{1,0:T(8,128)(2,1)S(1)}, bf16[128,640]{1,0:T(8,128)(2,1)S(1)}, u32[]{:S(2)}, u32[]{:S(2)}) collective-permute-start(bf16[128,640]{1,0:T(8,128)(2,1)S(1)} %get-tuple-element.46), channel_id=1, source_target_pairs={{0,3},{1,7},{2,1},{3,5},{4,2},{5,6},{6,0},{7,4},{8,11},{9,15},{10,... | collective-permute-start | bytes 491528 | tf_op jit(solution)/shard_map/ppermute | solution.py:398
  (31 other events, 324.4 us)

commit v9 on v7

--- a/solution.py
+++ b/solution.py
@@ -24,6 +24,8 @@
 PART_ATT = ATT_HEADS // PARTS
 SPAN = -(-HEAD_DIM // LANES) * LANES
 
+
+VMEM_BYTES = 67043328
 
 F32 = jnp.float32
 BF16 = jnp.bfloat16
@@ -56,7 +58,7 @@
         in_specs=specs,
         out_specs=out_specs or [pl.BlockSpec(memory_space=VMEM)] * len(outs),
         scratch_shapes=list(scratch),
-        compiler_params=pltpu.CompilerParams(vmem_limit_bytes=limit << 20),
+        compiler_params=pltpu.CompilerParams(vmem_limit_bytes=min(limit << 20, VMEM_BYTES)),
         cost_estimate=pl.CostEstimate(flops=flops, bytes_accessed=moved, transcendentals=0),
         **extra,
     )(*ins)
@@ -439,7 +441,7 @@
         smem=1, flops=2 * tok_dev * tok_dev * 3 * WIDTH,
     )
     heads_in = [heads_out[0]]
-    send_order = [2, 3, 6, 7, 4, 5, 1]
+    send_order = [2, 4, 3, 5, 6, 7, 1]
     for j in range(1, plane_size):
         heads_in.append(permute(heads_out[j], lambda z, y, x, c, j=j: (z, y ^ j >> 2, x ^ j >> 1 & 1, c ^ j & 1)))
 

time: 180 us -> 180 us (level)
  transfers between devices with their start and end apart: 28 -> 28, of which waited for: 11 -> 12; matrix products, arithmetic and copies ran while one was open for 4% -> 4% of each run, Pallas kernels for 16% -> 16%
where the time goes in v9:
time: 180 us; the launch traced here: 179 us
  waiting for transfers between devices  83.6 us (46%)
  Pallas kernels  43.9 us (24%)
  starting transfers between devices  34.9 us (19%)
  local copies, waits for them, and re-layouts  14 us (8%)
  other arithmetic  2.23 us (1%)
    ppermute x27, waiting for transfers between devices, permute(): return lax.ppermute(array, 'tok', route)  83.6 us
    pallas_call x9, Pallas kernels, call(): pl.pallas_call(kernel, out_shape=list(outs), in_specs=specs, out_specs=ou...  43.9 us
    ppermute x27, starting transfers between devices, permute(): return lax.ppermute(array, 'tok', route)  27.5 us
    unnamed x55, local copies, waits for them, and re-layouts  10.8 us
    all_to_all x1, starting transfers between devices, shards(): lax.all_to_all(packed.reshape(sections, slots, 3 * PART_WIDTH), 'tok', sp...  7.45 us
  transfers between devices with their start and end apart: 28, of which 12 were waited for; matrix products, arithmetic and copies ran while one was open for 4% of the time, Pallas kernels for 16%

profile of v9, /device:TPU:0, one launch (start us, length us, event | category | flops | bytes accessed | tf_op | source)
XLA Modules:
  0.0 179.2 jit_solution(5542532088737028245)
XLA Ops:
  0.7 4.3 %shard_map.83 = (bf16[4,4,2,16,1920]{4,3,2,1,0:T(8,128)(2,1)}, bf16[128,640]{1,0:T(8,128)(2,1)}, bf16[128,640]{1,0:T(8,128)(2,1)}, bf16[128,640]{1,0:T(8,128)(2,...) custom-call(s32[22]{0:T(128)} %stack.79.place_ref, ...), custom_call_target="tpu_custom_call" | custom-call | flops 251658240 | bytes 5263448 | tf_op jit(solution)/shard_map/pallas_call | solution.py:55
  5.0 7.5 %all-to-all-start = ((bf16[32,16,1920]{2,1,0:T(8,128)(2,1)}), bf16[32,16,1920]{2,1,0:T(8,128)(2,1)}, u32[]{:S(2)}, u32[]{:S(2)}) async-start(bf16[32,16,1920]{2,1,0:T(8,128)(2,1)} %bitcast.26), calls=%async_computation | async-start | bytes 3932160 | tf_op jit(solution)/shard_map/all_to_all | solution.py:448
  18.7 13.5 %collective-permute-done.6.refs_1_ = bf16[128,640]{1,0:T(8,128)(2,1)S(1)} collective-permute-done((bf16[128,640]{1,0:T(8,128)(2,1)S(1)}, bf16[128,640]{1,0:T(8,128)(2,1)S(1)}, u32[]{:S(2)}, u32[]{:S(2)}) %collective-permute-start.6) | collective-permute-done | bytes 163872 | tf_op jit(solution)/shard_map/ppermute | solution.py:399
  37.7 3.3 %copy.10 = bf16[640,3,640]{0,2,1:T(8,128)(2,1)} copy(bf16[640,3,640]{2,0,1:T(8,128)(2,1)S(1)} %constant_dynamic-slice_fusion) | data formatting | bytes 4915200
  41.0 6.4 %collective-permute-done.8.refs_3_ = bf16[128,640]{1,0:T(8,128)(2,1)} collective-permute-done((bf16[128,640]{1,0:T(8,128)(2,1)}, bf16[128,640]{1,0:T(8,128)(2,1)}, u32[]{:S(2)}, u32[]{:S(2)}) %collective-permute-start.8) | collective-permute-done | bytes 163872 | tf_op jit(solution)/shard_map/ppermute | solution.py:399
  47.4 5.4 %shard_map.87.refs_4_ = bf16[320,1920]{1,0:T(8,128)(2,1)} custom-call(s32[22]{0:T(128)} %stack.79.place_ref, bf16[3,640,640]{2,1,0:T(8,128)(2,1)} %bitcast.23, bf16[128,640]{1,0:T(8,128)(2,1)} %get-tuple-element.35.refs_0_, bf16[128,640]{1,0:T(8,128)(2,1)} %copy-done.23, bf16[128,640]{1,0:T(8,128)(2,1)} %copy-done.25, ...), custom_call_target="tpu_custom_call" | custom-call | flops 1258291200 | bytes 4341848 | tf_op jit(solution)/shard_map/pallas_call | solution.py:55
  53.6 5.8 %shard_map.88 = (bf16[80,1920]{1,0:T(8,128)(2,1)}, bf16[80,1920]{1,0:T(8,128)(2,1)}, bf16[80,1920]{1,0:T(8,128)(2,1)}, bf16[80,1920]{1,0:T(8,128)(2,1)}) custom-call(s32[22]{0:T(128)} %stack.79.place_ref, bf16[3,640,640]{2,1,0:T(8,128)(2,1)} %bitcast.24, bf16[128,640]{1,0:T(8,128)(2,1)} %copy-done.21, bf16[128,640]{1,0:T(8,128)(2,1)} %copy-done.22, ...), custom_call_target="tpu_custom_call" | custom-call | flops 1258291200 | bytes 5570648 | tf_op jit(solution)/shard_map/pallas_call | solution.py:55
  59.4 2.4 %collective-permute-start.10 = (bf16[80,1920]{1,0:T(8,128)(2,1)}, bf16[80,1920]{1,0:T(8,128)(2,1)S(1)}, u32[]{:S(2)}, u32[]{:S(2)}) collective-permute-start(bf16[80,1920]{1,0:T(8,128)(2,1)} %get-tuple-element.42), channel_id=1, source_target_pairs={{0,8},{1,9},{2,10},{3,11},{4,12},{5,13},{6,14},{7,15},{8,0},{9,1},... | collective-permute-start | bytes 921608 | tf_op jit(solution)/shard_map/ppermute | solution.py:399
  61.8 8.3 %collective-permute-done.10 = bf16[80,1920]{1,0:T(8,128)(2,1)S(1)} collective-permute-done((bf16[80,1920]{1,0:T(8,128)(2,1)}, bf16[80,1920]{1,0:T(8,128)(2,1)S(1)}, u32[]{:S(2)}, u32[]{:S(2)}) %collective-permute-start.10) | collective-permute-done | bytes 307232 | tf_op jit(solution)/shard_map/ppermute | solution.py:399
  71.2 3.9 %collective-permute-start.11 = (bf16[80,1920]{1,0:T(8,128)(2,1)S(1)}, bf16[80,1920]{1,0:T(8,128)(2,1)S(1)}, u32[]{:S(2)}, u32[]{:S(2)}) collective-permute-start(bf16[80,1920]{1,0:T(8,128)(2,1)S(1)} %add_convert_fusion.1), channel_id=1, source_target_pairs={{0,16},{1,17},{2,18},{3,19},{4,20},{5,21},{6,22},{7,23},{8,24},{9,... | collective-permute-start | bytes 921608 | tf_op jit(solution)/shard_map/ppermute | solution.py:399
  77.3 3.6 %collective-permute-done.9 = bf16[80,1920]{1,0:T(8,128)(2,1)S(1)} collective-permute-done((bf16[80,1920]{1,0:T(8,128)(2,1)}, bf16[80,1920]{1,0:T(8,128)(2,1)S(1)}, u32[]{:S(2)}, u32[]{:S(2)}) %collective-permute-start.9) | collective-permute-done | bytes 307232 | tf_op jit(solution)/shard_map/ppermute | solution.py:399
  80.8 8.1 %collective-permute-done.11 = bf16[80,1920]{1,0:T(8,128)(2,1)S(1)} collective-permute-done((bf16[80,1920]{1,0:T(8,128)(2,1)S(1)}, bf16[80,1920]{1,0:T(8,128)(2,1)S(1)}, u32[]{:S(2)}, u32[]{:S(2)}) %collective-permute-start.11) | collective-permute-done | bytes 307232 | tf_op jit(solution)/shard_map/ppermute | solution.py:399
  90.0 4.0 %shard_map.84 = (bf16[512,1280]{1,0:T(8,128)(2,1)}, bf16[512,640]{1,0:T(8,128)(2,1)}) custom-call(bf16[512,512]{1,0:T(8,128)(2,1)} %shard_map.82.choose_ref, bf16[512,1920]{1,0:T(8,128)(2,1)} %bitcast.22.in_ref), custom_call_target="tpu_custom_call" | custom-call | flops 1006632960 | bytes 4456448 | tf_op jit(solution)/shard_map/pallas_call | solution.py:55
  95.0 2.5 %collective-permute-start.12 = (bf16[48,1920]{1,0:T(8,128)(2,1)S(1)}, bf16[48,1920]{1,0:T(8,128)(2,1)S(1)}, u32[]{:S(2)}, u32[]{:S(2)}) collective-permute-start(bf16[48,1920]{1,0:T(8,128)(2,1)S(1)} %add_convert_fusion.3), channel_id=1, source_target_pairs={{0,16},{1,17},{2,18},{3,19},{4,20},{5,21},{6,22},{7,23},{8,24},{9,... | collective-permute-start | bytes 552968 | tf_op jit(solution)/shard_map/ppermute | solution.py:399
  98.1 3.3 %collective-permute-start.14 = (bf16[80,1920]{1,0:T(8,128)(2,1)S(1)}, bf16[80,1920]{1,0:T(8,128)(2,1)S(1)}, u32[]{:S(2)}, u32[]{:S(2)}) collective-permute-start(bf16[80,1920]{1,0:T(8,128)(2,1)S(1)} %get-tuple-element.47.refs_0_), channel_id=1, source_target_pairs={{0,8},{1,9},{2,10},{3,11},{4,12},{5,13},{6,14},{7,15},{8,0},{9,1},... | collective-permute-start | bytes 921608 | tf_op jit(solution)/shard_map/ppermute | solution.py:399
  101.4 24.8 %collective-permute-done.13.refs_2_ = bf16[32,1920]{1,0:T(8,128)(2,1)S(1)} collective-permute-done((bf16[32,1920]{1,0:T(8,128)(2,1)S(1)}, bf16[32,1920]{1,0:T(8,128)(2,1)S(1)}, u32[]{:S(2)}, u32[]{:S(2)}) %collective-permute-start.13) | collective-permute-done | bytes 122912 | tf_op jit(solution)/shard_map/ppermute | solution.py:399
  126.2 5.2 %collective-permute-done.16.refs_5_ = bf16[32,1920]{1,0:T(8,128)(2,1)S(1)} collective-permute-done((bf16[32,1920]{1,0:T(8,128)(2,1)S(1)}, bf16[32,1920]{1,0:T(8,128)(2,1)S(1)}, u32[]{:S(2)}, u32[]{:S(2)}) %collective-permute-start.16) | collective-permute-done | bytes 122912 | tf_op jit(solution)/shard_map/ppermute | solution.py:399
  132.7 4.4 %collective-permute-done.15.refs_4_ = bf16[48,1920]{1,0:T(8,128)(2,1)} collective-permute-done((bf16[48,1920]{1,0:T(8,128)(2,1)S(1)}, bf16[48,1920]{1,0:T(8,128)(2,1)}, u32[]{:S(2)}, u32[]{:S(2)}) %collective-permute-start.15) | collective-permute-done | bytes 184352 | tf_op jit(solution)/shard_map/ppermute | solution.py:399
  142.5 8.2 %shard_map.85 = (f32[512,640]{1,0:T(8,128)S(1)}, f32[512,128]{1,0:T(8,128)S(1)}) custom-call(s32[22]{0:T(128)S(1)} %copy-done.7, bf16[512,640]{1,0:T(8,128)(2,1)S(1)} %copy-done.1, s32[8,512]{1,0:T(8,128)S(1)} %reshape.18.ids_ref, bf16[512,1280]{1,0:T(8,128)(2,1)S(1)} %copy-done.8, bf16[512,1280]{1,0:T(8,128)(2,1)S(1)} %copy-done.10), custom_call_target="tpu_custom_call" | custom-call | flops 1006632960 | bytes 4866136 | tf_op jit(solution)/shard_map/pallas_call | solution.py:55
  150.8 6.5 %shard_map.86.attended_ref = f32[512,640]{1,0:T(8,128)S(1)} custom-call(s32[22]{0:T(128)S(1)} %copy-done.7, bf16[512,640]{1,0:T(8,128)(2,1)S(1)} %copy-done.2, s32[8,512]{1,0:T(8,128)S(1)} %reshape.18.ids_ref, f32[512,640]{1,0:T(8,128)S(1)} %get-tuple-element.29.near_ref, f32[512,128]{1,0:T(8,128)S(1)} %get-tuple-element.30.stat_ref, ...), custom_call_target="tpu_custom_call" | custom-call | flops 503316480 | bytes 4866136 | tf_op jit(solution)/shard_map/pallas_call | solution.py:55
  157.4 5.1 %shard_map.89 = (bf16[128,640]{1,0:T(8,128)(2,1)S(1)}, bf16[128,640]{1,0:T(8,128)(2,1)S(1)}, bf16[128,640]{1,0:T(8,128)(2,1)S(1)}, bf16[128,640]{1,0:T(8,128)(2,1)S(1)}) custom-call(s32[22]{0:T(128)S(1)} %copy-done.7, bf16[3,640,640]{2,1,0:T(8,128)(2,1)S(1)} %bitcast.25, bf16[512,640]{1,0:T(8,128)(2,1)S(1)} %copy-done.2, ...), custom_call_target="tpu_custom_call" | custom-call | flops 1258291200 | bytes 7536728 | tf_op jit(solution)/shard_map/pallas_call | solution.py:55
  164.0 3.6 %collective-permute-start.25 = (bf16[128,640]{1,0:T(8,128)(2,1)S(1)}, bf16[128,640]{1,0:T(8,128)(2,1)S(1)}, u32[]{:S(2)}, u32[]{:S(2)}) collective-permute-start(bf16[128,640]{1,0:T(8,128)(2,1)S(1)} %get-tuple-element.45), channel_id=1, source_target_pairs={{0,1},{1,5},{2,3},{3,7},{4,0},{5,4},{6,2},{7,6},{8,9},{9,13},{10,1... | collective-permute-start | bytes 491528 | tf_op jit(solution)/shard_map/ppermute | solution.py:399
  168.6 6.4 %collective-permute-done.25.refs_2_ = bf16[128,640]{1,0:T(8,128)(2,1)S(1)} collective-permute-done((bf16[128,640]{1,0:T(8,128)(2,1)S(1)}, bf16[128,640]{1,0:T(8,128)(2,1)S(1)}, u32[]{:S(2)}, u32[]{:S(2)}) %collective-permute-start.25) | collective-permute-done | bytes 163872 | tf_op jit(solution)/shard_map/ppermute | solution.py:399
  176.8 2.4 %shard_map.90 = bf16[128,2560]{1,0:T(8,128)(2,1)} custom-call(s32[22]{0:T(128)} %stack.79.place_ref, bf16[128,640]{1,0:T(8,128)(2,1)} %copy-done.11, bf16[128,640]{1,0:T(8,128)(2,1)} %copy-done.12, bf16[128,640]{1,0:T(8,128)(2,1)} %copy-done.13, bf16[128,640]{1,0:T(8,128)(2,1)} %copy-done.14, f32[1,2560]{1,0:T(1,128)} %reshape.19.refs_4_), custom_call_target="tpu_custom_call" | custom-call | flops 1966080 | bytes 1321048 | tf_op jit(solution)/shard_map/pallas_call | solution.py:55
  (104 shorter events, 30.0 us)
Async XLA Ops:
  5.0 85.0 %all-to-all-start = ((bf16[32,16,1920]{2,1,0:T(8,128)(2,1)}), bf16[32,16,1920]{2,1,0:T(8,128)(2,1)}, u32[]{:S(2)}, u32[]{:S(2)}) async-start(bf16[32,16,1920]{2,1,0:T(8,128)(2,1)} %bitcast.26), calls=%async_computation | async-start | bytes 3932160 | tf_op jit(solution)/shard_map/all_to_all | solution.py:448
  12.5 19.6 %collective-permute-start.6 = (bf16[128,640]{1,0:T(8,128)(2,1)S(1)}, bf16[128,640]{1,0:T(8,128)(2,1)S(1)}, u32[]{:S(2)}, u32[]{:S(2)}) collective-permute-start(bf16[128,640]{1,0:T(8,128)(2,1)S(1)} %copy-done.26), channel_id=1, source_target_pairs={{0,2},{1,3},{2,0},{3,1},{4,6},{5,7},{6,4},{7,5},{8,10},{9,11},{10,... | collective-permute-start | bytes 491528 | tf_op jit(solution)/shard_map/ppermute | solution.py:399
  14.3 19.6 %collective-permute-start.7 = (bf16[128,640]{1,0:T(8,128)(2,1)S(1)}, bf16[128,640]{1,0:T(8,128)(2,1)S(1)}, u32[]{:S(2)}, u32[]{:S(2)}) collective-permute-start(bf16[128,640]{1,0:T(8,128)(2,1)S(1)} %copy-done.24), channel_id=1, source_target_pairs={{0,4},{1,5},{2,6},{3,7},{4,0},{5,1},{6,2},{7,3},{8,12},{9,13},{10,... | collective-permute-start | bytes 491528 | tf_op jit(solution)/shard_map/ppermute | solution.py:399
  15.8 37.1 %collective-permute-start.2 = (bf16[128,640]{1,0:T(8,128)(2,1)S(1)}, bf16[128,640]{1,0:T(8,128)(2,1)S(1)}, u32[]{:S(2)}, u32[]{:S(2)}) collective-permute-start(bf16[128,640]{1,0:T(8,128)(2,1)S(1)} %copy-done.20), channel_id=1, source_target_pairs={{0,5},{1,4},{2,7},{3,6},{4,1},{5,0},{6,3},{7,2},{8,13},{9,12},{10,... | collective-permute-start | bytes 491528 | tf_op jit(solution)/shard_map/ppermute | solution.py:399
  15.8 37.1 %collective-permute-start.3 = (bf16[128,640]{1,0:T(8,128)(2,1)S(1)}, bf16[128,640]{1,0:T(8,128)(2,1)S(1)}, u32[]{:S(2)}, u32[]{:S(2)}) collective-permute-start(bf16[128,640]{1,0:T(8,128)(2,1)S(1)} %copy-done.19), channel_id=1, source_target_pairs={{0,6},{1,7},{2,4},{3,5},{4,2},{5,3},{6,0},{7,1},{8,14},{9,15},{10,... | collective-permute-start | bytes 491528 | tf_op jit(solution)/shard_map/ppermute | solution.py:399
  16.9 35.9 %collective-permute-start.4 = (bf16[128,640]{1,0:T(8,128)(2,1)S(1)}, bf16[128,640]{1,0:T(8,128)(2,1)}, u32[]{:S(2)}, u32[]{:S(2)}) collective-permute-start(bf16[128,640]{1,0:T(8,128)(2,1)S(1)} %copy-done.18), channel_id=1, source_target_pairs={{0,7},{1,6},{2,5},{3,4},{4,3},{5,2},{6,1},{7,0},{8,15},{9,14},{10,... | collective-permute-start | bytes 491528 | tf_op jit(solution)/shard_map/ppermute | solution.py:399
  32.2 20.7 %collective-permute-start.5 = (bf16[128,640]{1,0:T(8,128)(2,1)S(1)}, bf16[128,640]{1,0:T(8,128)(2,1)}, u32[]{:S(2)}, u32[]{:S(2)}) collective-permute-start(bf16[128,640]{1,0:T(8,128)(2,1)S(1)} %copy-done.17), channel_id=1, source_target_pairs={{0,1},{1,0},{2,3},{3,2},{4,5},{5,4},{6,7},{7,6},{8,9},{9,8},{10,11... | collective-permute-start | bytes 491528 | tf_op jit(solution)/shard_map/ppermute | solution.py:399
  34.5 12.9 %collective-permute-start.8 = (bf16[128,640]{1,0:T(8,128)(2,1)}, bf16[128,640]{1,0:T(8,128)(2,1)}, u32[]{:S(2)}, u32[]{:S(2)}) collective-permute-start(bf16[128,640]{1,0:T(8,128)(2,1)} %get-tuple-element.38), channel_id=1, source_target_pairs={{0,3},{1,2},{2,1},{3,0},{4,7},{5,6},{6,5},{7,4},{8,11},{9,10},{10,... | collective-permute-start | bytes 491528 | tf_op jit(solution)/shard_map/ppermute | solution.py:399
  59.4 10.7 %collective-permute-start.10 = (bf16[80,1920]{1,0:T(8,128)(2,1)}, bf16[80,1920]{1,0:T(8,128)(2,1)S(1)}, u32[]{:S(2)}, u32[]{:S(2)}) collective-permute-start(bf16[80,1920]{1,0:T(8,128)(2,1)} %get-tuple-element.42), channel_id=1, source_target_pairs={{0,8},{1,9},{2,10},{3,11},{4,12},{5,13},{6,14},{7,15},{8,0},{9,1},... | collective-permute-start | bytes 921608 | tf_op jit(solution)/shard_map/ppermute | solution.py:399
  61.8 19.1 %collective-permute-start.9 = (bf16[80,1920]{1,0:T(8,128)(2,1)}, bf16[80,1920]{1,0:T(8,128)(2,1)S(1)}, u32[]{:S(2)}, u32[]{:S(2)}) collective-permute-start(bf16[80,1920]{1,0:T(8,128)(2,1)} %get-tuple-element.40), channel_id=1, source_target_pairs={{0,8},{1,9},{2,10},{3,11},{4,12},{5,13},{6,14},{7,15},{8,0},{9,1},... | collective-permute-start | bytes 921608 | tf_op jit(solution)/shard_map/ppermute | solution.py:399
  71.2 17.8 %collective-permute-start.11 = (bf16[80,1920]{1,0:T(8,128)(2,1)S(1)}, bf16[80,1920]{1,0:T(8,128)(2,1)S(1)}, u32[]{:S(2)}, u32[]{:S(2)}) collective-permute-start(bf16[80,1920]{1,0:T(8,128)(2,1)S(1)} %add_convert_fusion.1), channel_id=1, source_target_pairs={{0,16},{1,17},{2,18},{3,19},{4,20},{5,21},{6,22},{7,23},{8,24},{9,... | collective-permute-start | bytes 921608 | tf_op jit(solution)/shard_map/ppermute | solution.py:399
  94.0 43.1 %collective-permute-start = (bf16[512,1280]{1,0:T(8,128)(2,1)}, bf16[512,1280]{1,0:T(8,128)(2,1)S(1)}, u32[]{:S(2)}, u32[]{:S(2)}) collective-permute-start(bf16[512,1280]{1,0:T(8,128)(2,1)} %get-tuple-element.28.kv_ref), channel_id=1, source_target_pairs={{0,1},{1,0},{2,3},{3,2},{4,5},{5,4},{6,7},{7,6},{8,9},{9,8},{10,11... | collective-permute-start | bytes 3932168 | tf_op jit(solution)/shard_map/ppermute | solution.py:399
  94.0 44.7 %collective-permute-start.1 = (bf16[512,1280]{1,0:T(8,128)(2,1)}, bf16[512,1280]{1,0:T(8,128)(2,1)S(1)}, u32[]{:S(2)}, u32[]{:S(2)}) collective-permute-start(bf16[512,1280]{1,0:T(8,128)(2,1)} %get-tuple-element.28.kv_ref), channel_id=1, source_target_pairs={{1,8},{3,10},{5,12},{7,14},{8,1},{9,16},{10,3},{11,18},{12,5},{13,... | collective-permute-start | bytes 3932168 | tf_op jit(solution)/shard_map/ppermute | solution.py:399
  95.0 31.2 %collective-permute-start.12 = (bf16[48,1920]{1,0:T(8,128)(2,1)S(1)}, bf16[48,1920]{1,0:T(8,128)(2,1)S(1)}, u32[]{:S(2)}, u32[]{:S(2)}) collective-permute-start(bf16[48,1920]{1,0:T(8,128)(2,1)S(1)} %add_convert_fusion.3), channel_id=1, source_target_pairs={{0,16},{1,17},{2,18},{3,19},{4,20},{5,21},{6,22},{7,23},{8,24},{9,... | collective-permute-start | bytes 552968 | tf_op jit(solution)/shard_map/ppermute | solution.py:399
  97.5 28.7 %collective-permute-start.13 = (bf16[32,1920]{1,0:T(8,128)(2,1)S(1)}, bf16[32,1920]{1,0:T(8,128)(2,1)S(1)}, u32[]{:S(2)}, u32[]{:S(2)}) collective-permute-start(bf16[32,1920]{1,0:T(8,128)(2,1)S(1)} %add_convert_fusion.4), channel_id=1, source_target_pairs={{0,16},{1,17},{2,18},{3,19},{4,20},{5,21},{6,22},{7,23},{8,24},{9,... | collective-permute-start | bytes 368648 | tf_op jit(solution)/shard_map/ppermute | solution.py:399
  98.1 34.1 %collective-permute-start.14 = (bf16[80,1920]{1,0:T(8,128)(2,1)S(1)}, bf16[80,1920]{1,0:T(8,128)(2,1)S(1)}, u32[]{:S(2)}, u32[]{:S(2)}) collective-permute-start(bf16[80,1920]{1,0:T(8,128)(2,1)S(1)} %get-tuple-element.47.refs_0_), channel_id=1, source_target_pairs={{0,8},{1,9},{2,10},{3,11},{4,12},{5,13},{6,14},{7,15},{8,0},{9,1},... | collective-permute-start | bytes 921608 | tf_op jit(solution)/shard_map/ppermute | solution.py:399
  132.2 25.2 %collective-permute-start.17 = (bf16[80,1920]{1,0:T(8,128)(2,1)S(1)}, bf16[80,1920]{1,0:T(8,128)(2,1)S(1)}, u32[]{:S(2)}, u32[]{:S(2)}) collective-permute-start(bf16[80,1920]{1,0:T(8,128)(2,1)S(1)} %get-tuple-element.47.refs_0_), channel_id=1, source_target_pairs={{0,1},{1,0},{2,3},{3,2},{4,5},{5,4},{6,7},{7,6},{8,9},{9,8},{10,11... | collective-permute-start | bytes 921608 | tf_op jit(solution)/shard_map/ppermute | solution.py:399
  132.2 25.2 %collective-permute-start.20 = (bf16[80,1920]{1,0:T(8,128)(2,1)S(1)}, bf16[80,1920]{1,0:T(8,128)(2,1)S(1)}, u32[]{:S(2)}, u32[]{:S(2)}) collective-permute-start(bf16[80,1920]{1,0:T(8,128)(2,1)S(1)} %collective-permute-done.14.refs_3_), channel_id=1, source_target_pairs={{0,1},{1,0},{2,3},{3,2},{4,5},{5,4},{6,7},{7,6},{8,9},{9,8},{10,11... | collective-permute-start | bytes 921608 | tf_op jit(solution)/shard_map/ppermute | solution.py:399
  137.1 20.2 %collective-permute-start.18 = (bf16[48,1920]{1,0:T(8,128)(2,1)S(1)}, bf16[48,1920]{1,0:T(8,128)(2,1)}, u32[]{:S(2)}, u32[]{:S(2)}) collective-permute-start(bf16[48,1920]{1,0:T(8,128)(2,1)S(1)} %collective-permute-done.12.refs_1_), channel_id=1, source_target_pairs={{0,1},{1,0},{2,3},{3,2},{4,5},{5,4},{6,7},{7,6},{8,9},{9,8},{10,11... | collective-permute-start | bytes 552968 | tf_op jit(solution)/shard_map/ppermute | solution.py:399
  138.2 19.2 %collective-permute-start.21 = (bf16[48,1920]{1,0:T(8,128)(2,1)}, bf16[48,1920]{1,0:T(8,128)(2,1)}, u32[]{:S(2)}, u32[]{:S(2)}) collective-permute-start(bf16[48,1920]{1,0:T(8,128)(2,1)} %collective-permute-done.15.refs_4_), channel_id=1, source_target_pairs={{0,1},{1,0},{2,3},{3,2},{4,5},{5,4},{6,7},{7,6},{8,9},{9,8},{10,11... | collective-permute-start | bytes 552968 | tf_op jit(solution)/shard_map/ppermute | solution.py:399
  138.7 18.6 %collective-permute-start.22 = (bf16[32,1920]{1,0:T(8,128)(2,1)}, bf16[32,1920]{1,0:T(8,128)(2,1)S(1)}, u32[]{:S(2)}, u32[]{:S(2)}) collective-permute-start(bf16[32,1920]{1,0:T(8,128)(2,1)} %copy-done.3), channel_id=1, source_target_pairs={{0,1},{1,0},{2,3},{3,2},{4,5},{5,4},{6,7},{7,6},{8,9},{9,8},{10,11... | collective-permute-start | bytes 368648 | tf_op jit(solution)/shard_map/ppermute | solution.py:399
  162.5 6.0 %collective-permute-start.23 = (bf16[128,640]{1,0:T(8,128)(2,1)S(1)}, bf16[128,640]{1,0:T(8,128)(2,1)S(1)}, u32[]{:S(2)}, u32[]{:S(2)}) collective-permute-start(bf16[128,640]{1,0:T(8,128)(2,1)S(1)} %get-tuple-element.43), channel_id=1, source_target_pairs={{0,0},{1,4},{2,2},{3,6},{4,1},{5,5},{6,3},{7,7},{8,8},{9,12},{10,1... | collective-permute-start | bytes 491528 | tf_op jit(solution)/shard_map/ppermute | solution.py:399
  164.0 11.0 %collective-permute-start.25 = (bf16[128,640]{1,0:T(8,128)(2,1)S(1)}, bf16[128,640]{1,0:T(8,128)(2,1)S(1)}, u32[]{:S(2)}, u32[]{:S(2)}) collective-permute-start(bf16[128,640]{1,0:T(8,128)(2,1)S(1)} %get-tuple-element.45), channel_id=1, source_target_pairs={{0,1},{1,5},{2,3},{3,7},{4,0},{5,4},{6,2},{7,6},{8,9},{9,13},{10,1... | collective-permute-start | bytes 491528 | tf_op jit(solution)/shard_map/ppermute | solution.py:399
  167.6 8.5 %collective-permute-start.26 = (bf16[128,640]{1,0:T(8,128)(2,1)S(1)}, bf16[128,640]{1,0:T(8,128)(2,1)S(1)}, u32[]{:S(2)}, u32[]{:S(2)}) collective-permute-start(bf16[128,640]{1,0:T(8,128)(2,1)S(1)} %get-tuple-element.46), channel_id=1, source_target_pairs={{0,3},{1,7},{2,1},{3,5},{4,2},{5,6},{6,0},{7,4},{8,11},{9,15},{10,... | collective-permute-start | bytes 491528 | tf_op jit(solution)/shard_map/ppermute | solution.py:399
  (31 other events, 314.4 us)

commit v10 on v9

--- a/solution.py
+++ b/solution.py
@@ -70,9 +70,9 @@
 
 
 def front_kernel(group_shift, slots, place_ref, order_ref, rate_ref, query_ref, key_ref, value_ref, *refs):
-    out_ref, head_refs, choose_buf = refs[0], refs[1:-1], refs[-1]
+    head_refs, out_refs, choose_buf = refs[: PARTS * PART_FAST], refs[PARTS * PART_FAST : -1], refs[-1]
     n, _ = key_ref.shape
-    planes, together, cores = out_ref.shape[:3]
+    planes, (together, cores) = len(out_refs), out_refs[0].shape[:2]
     step, part, core = pl.program_id(0), place_ref[1], place_ref[2]
 
     @pl.when(step == 0)
@@ -82,7 +82,8 @@
         group_col = column_of(group).astype(jnp.int32)
         earlier = (group_col == group) & (iota((n, n), 0) < iota((n, n), 1))
         rank = jnp.sum(jnp.where(earlier, 1.0, 0.0), axis=0, keepdims=True)
-        slot = group * slots + rank.astype(jnp.int32)
+        away = group ^ place_ref[3] // cores * cores
+        slot = away * slots + rank.astype(jnp.int32)
         choose_buf[...] = jnp.where(iota((n, n), 0) == slot, 1.0, 0.0).astype(BF16)
 
     choose = choose_buf[...]
@@ -93,7 +94,7 @@
             for plane in range(planes):
                 for at in range(cores):
                     first = (plane * cores + at) * slots
-                    out_ref[plane, local, at, :, lanes] = rows[first : first + slots]
+                    out_refs[plane][local, at, :, lanes] = rows[first : first + slots]
 
     lane = iota((n, SPAN), 1)
     tail = PART_WIDTH - SPAN
@@ -132,7 +133,12 @@
     rank = dot(jnp.where(mine, 1.0, 0.0).astype(BF16), before)
     within = orders & ((1 << group_shift) - 1)
     digits = (lax.shift_right_logical(within, low_shift).astype(F32), (within & ((1 << low_shift) - 1)).astype(F32))
-    spread = jnp.where(iota((sources, n), 1) // slots == iota((sources, n), 0), 1.0, 0.0).astype(BF16)
+    team = PARTS * PART_FAST
+    stages = sources // team // 2
+    row = iota((sources, n), 1)
+    distance = row // (n // stages) * 2 + row // slots % 2
+    source = (group // PART_FAST ^ distance) * team + row // (2 * slots) % team
+    spread = jnp.where(source == iota((sources, n), 0), 1.0, 0.0).astype(BF16)
     keep = iota((slots, n), 1) % slots == iota((slots, n), 0)
     column = iota((sources, slots), 1)
     pos = jnp.zeros((1, n), F32)
@@ -150,10 +156,12 @@
     choose_ref[...] = arrival_choice(group_shift, slots, order_ref[...], place_ref[3], choose_ref.shape[0])
 
 
-def place_kernel(choose_ref, in_ref, kv_ref, q_ref):
-    choose = choose_ref[...]
-    kv_ref[...] = dot(choose, in_ref[:, : 2 * PART_WIDTH]).astype(BF16)
-    q_ref[...] = dot(choose, in_ref[:, 2 * PART_WIDTH :]).astype(BF16)
+def place_kernel(choose_ref, *refs):
+    in_refs, (kv_ref, q_ref) = refs[:-2], refs[-2:]
+    size = in_refs[0].shape[0]
+    for ref, lanes in ((kv_ref, slice(0, 2 * PART_WIDTH)), (q_ref, slice(2 * PART_WIDTH, 3 * PART_WIDTH))):
+        parts = [dot(choose_ref[:, i * size : (i + 1) * size], part[:, lanes]) for i, part in enumerate(in_refs)]
+        ref[...] = functools.reduce(jnp.add, parts).astype(BF16)
 
 
 def grads_kernel(chunk, first_start, outs, place_ref, weight_ref, *refs):
@@ -429,25 +437,35 @@
     rates = learn_rates.T
     cut = pl.BlockSpec((tok_dev, WIDTH // steps), lambda h: (0, h))
     head_shape = jax.ShapeDtypeStruct((tok_dev, 2 * HEAD_DIM), BF16)
-    packed, *heads_out = call(
+    outs = call(
         functools.partial(front_kernel, group_shift, slots),
-        [jax.ShapeDtypeStruct((planes, PARTS, PART_FAST, slots, 3 * PART_WIDTH), BF16)] + [head_shape] * plane_size,
+        [head_shape] * plane_size + [jax.ShapeDtypeStruct((PARTS, PART_FAST, slots, 3 * PART_WIDTH), BF16)] * planes,
         [place, orders, rates, queries, key_rows, value_rows],
         in_specs=[full(orders), full(rates), cut, cut, cut],
-        out_specs=[pl.BlockSpec((planes, together, PART_FAST, slots, 3 * PART_WIDTH), lambda h: (0, h, 0, 0, 0))]
-        + [full(head_shape)] * plane_size,
+        out_specs=[full(head_shape)] * plane_size
+        + [pl.BlockSpec((together, PART_FAST, slots, 3 * PART_WIDTH), lambda h: (h, 0, 0, 0))] * planes,
         grid=(steps,),
         scratch=[VMEM((tok_dev, tok_dev), BF16)],
         smem=1, flops=2 * tok_dev * tok_dev * 3 * WIDTH,
     )
+    heads_out, packed = outs[:plane_size], [rows.reshape(plane_size, slots, 3 * PART_WIDTH) for rows in outs[plane_size:]]
     heads_in = [heads_out[0]]
     send_order = [2, 4, 3, 5, 6, 7, 1]
     for j in range(1, plane_size):
         heads_in.append(permute(heads_out[j], lambda z, y, x, c, j=j: (z, y ^ j >> 2, x ^ j >> 1 & 1, c ^ j & 1)))
 
-    arrived = lax.all_to_all(
-        packed.reshape(sections, slots, 3 * PART_WIDTH), "tok", split_axis=0, concat_axis=0, tiled=True
-    ).reshape(group_rows, 3 * PART_WIDTH)
+    teams = [[z * plane_size + i for i in range(plane_size)] for z in range(planes)]
+    arrived = []
+    for stage in range(planes // 2):
+        both = []
+        for distance in (2 * stage, 2 * stage + 1):
+            rows = packed[distance]
+            if distance:
+                rows = permute(rows, lambda z, y, x, c, m=distance: (z ^ m, y, x, c))
+            both.append(rows)
+        both = jnp.concatenate(both, axis=1)
+        both = lax.all_to_all(both, "tok", split_axis=0, concat_axis=0, axis_index_groups=teams, tiled=True)
+        arrived.append(both.reshape(plane_size * 2 * slots, 3 * PART_WIDTH))
 
     (choose,) = call(
         functools.partial(choose_kernel, group_shift, slots),
@@ -457,7 +475,7 @@
     kv_seq, query_seq = call(
         place_kernel,
         [jax.ShapeDtypeStruct((group_rows, width), BF16) for width in (2 * PART_WIDTH, PART_WIDTH)],
-        [choose, arrived], flops=2 * group_rows * group_rows * 3 * PART_WIDTH,
+        [choose] + arrived, flops=2 * group_rows * group_rows * 3 * PART_WIDTH,
     )
 
     swap = lambda z, y, x, c: (z, y, x, 1 - c)

time: 180 us -> 184 us (1.022)
  other arithmetic: 2.23 us -> 4.6 us
    concatenate x0 -> x2, other arithmetic: none -> 4.31 us  [shards(): both = jnp.concatenate(both, axis=1)]
    convert_element_type x4, other arithmetic: 2.23 us -> 0.29 us  [added(): return (first.astype(F32) + second.astype(F32)).astype(BF16)]
    ppermute x27 -> x30, starting transfers between devices: 27.5 us -> 28.8 us  [permute(): return lax.ppermute(array, 'tok', route)]
    all_to_all x1 -> x2, starting transfers between devices: 7.45 us -> 7.85 us  [shards(): lax.all_to_all(both, 'tok', split_axis=0, concat_axis=0, axis_index_group...]
    unnamed x55 -> x51, local copies, waits for them, and re-layouts: 10.8 us -> 11.2 us
    ppermute x27 -> x30, waiting for transfers between devices: 83.6 us -> 83.9 us  [permute(): return lax.ppermute(array, 'tok', route)]
  transfers between devices with their start and end apart: 28 -> 32, of which waited for: 12 -> 11; matrix products, arithmetic and copies ran while one was open for 4% -> 6% of each run, Pallas kernels for 16% -> 15%
where the time goes in v10:
time: 184 us
  waiting for transfers between devices  83.9 us (46%)
  Pallas kernels  43.9 us (24%)
  starting transfers between devices  36.6 us (20%)
  local copies, waits for them, and re-layouts  14.4 us (8%)
  other arithmetic  4.6 us (2%)
    ppermute x30, waiting for transfers between devices, permute(): return lax.ppermute(array, 'tok', route)  83.9 us
    pallas_call x9, Pallas kernels, call(): pl.pallas_call(kernel, out_shape=list(outs), in_specs=specs, out_specs=ou...  43.9 us
    ppermute x30, starting transfers between devices, permute(): return lax.ppermute(array, 'tok', route)  28.8 us
    unnamed x51, local copies, waits for them, and re-layouts  11.2 us
    all_to_all x2, starting transfers between devices, shards(): lax.all_to_all(both, 'tok', split_axis=0, concat_axis=0, axis_index_group...  7.85 us
    concatenate x2, other arithmetic, shards(): both = jnp.concatenate(both, axis=1)  4.31 us
  transfers between devices with their start and end apart: 32, of which 11 were waited for; matrix products, arithmetic and copies ran while one was open for 6% of the time, Pallas kernels for 15%

profile of v10, /device:TPU:0, one launch (start us, length us, event | category | flops | bytes accessed | tf_op | source)
XLA Modules:
  0.0 183.8 jit_solution(16801503003525551061)
XLA Ops:
  0.7 4.3 %shard_map.83 = (bf16[128,640]{1,0:T(8,128)(2,1)}, bf16[128,640]{1,0:T(8,128)(2,1)}, bf16[128,640]{1,0:T(8,128)(2,1)}, bf16[128,640]{1,0:T(8,128)(2,1)}, bf16[12...) custom-call(s32[22]{0:T(128)} %stack.79.place_ref, ...), custom_call_target="tpu_custom_call" | custom-call | flops 251658240 | bytes 5263448 | tf_op jit(solution)/shard_map/pallas_call | solution.py:55
  5.0 3.1 %collective-permute-start = (bf16[8,16,1920]{2,1,0:T(8,128)(2,1)}, bf16[8,16,1920]{2,1,0:T(8,128)(2,1)S(1)}, u32[]{:S(2)}, u32[]{:S(2)}) collective-permute-start(bf16[8,16,1920]{2,1,0:T(8,128)(2,1)} %bitcast.36), channel_id=1, source_target_pairs={{0,8},{1,9},{2,10},{3,11},{4,12},{5,13},{6,14},{7,15},{8,0},{9,1},... | collective-permute-start | bytes 1474568 | tf_op jit(solution)/shard_map/ppermute | solution.py:407
  11.4 8.2 %collective-permute-done = bf16[8,16,1920]{2,1,0:T(8,128)(2,1)S(1)} collective-permute-done((bf16[8,16,1920]{2,1,0:T(8,128)(2,1)}, bf16[8,16,1920]{2,1,0:T(8,128)(2,1)S(1)}, u32[]{:S(2)}, u32[]{:S(2)}) %collective-permute-start) | collective-permute-done | bytes 491552 | tf_op jit(solution)/shard_map/ppermute | solution.py:407
  21.7 3.9 %all-to-all-start = ((bf16[8,32,1920]{2,1,0:T(8,128)(2,1)}), bf16[8,32,1920]{2,1,0:T(8,128)(2,1)S(1)}, u32[]{:S(2)}, u32[]{:S(2)}) async-start(bf16[8,32,1920]{2,1,0:T(8,128)(2,1)} %pad_maximum_fusion), calls=%async_computation | async-start | bytes 1966080 | tf_op jit(solution)/shard_map/all_to_all | solution.py:467
  25.5 3.6 %collective-permute-start.2 = (bf16[8,16,1920]{2,1,0:T(8,128)(2,1)}, bf16[8,16,1920]{2,1,0:T(8,128)(2,1)}, u32[]{:S(2)}, u32[]{:S(2)}) collective-permute-start(bf16[8,16,1920]{2,1,0:T(8,128)(2,1)} %bitcast.25), channel_id=1, source_target_pairs={{0,24},{1,25},{2,26},{3,27},{4,28},{5,29},{6,30},{7,31},{8,16},{9,... | collective-permute-start | bytes 1474568 | tf_op jit(solution)/shard_map/ppermute | solution.py:407
  29.2 3.0 %collective-permute-start.6 = (bf16[128,640]{1,0:T(8,128)(2,1)}, bf16[128,640]{1,0:T(8,128)(2,1)}, u32[]{:S(2)}, u32[]{:S(2)}) collective-permute-start(bf16[128,640]{1,0:T(8,128)(2,1)} %get-tuple-element.38), channel_id=1, source_target_pairs={{0,6},{1,7},{2,4},{3,5},{4,2},{5,3},{6,0},{7,1},{8,14},{9,15},{10,... | collective-permute-start | bytes 491528 | tf_op jit(solution)/shard_map/ppermute | solution.py:407
  35.0 3.3 %copy.10 = bf16[640,3,640]{0,2,1:T(8,128)(2,1)} copy(bf16[640,3,640]{2,0,1:T(8,128)(2,1)S(1)} %constant_dynamic-slice_fusion) | data formatting | bytes 4915200
  38.3 5.3 %shard_map.87.refs_4_ = bf16[320,1920]{1,0:T(8,128)(2,1)} custom-call(s32[22]{0:T(128)} %stack.79.place_ref, bf16[3,640,640]{2,1,0:T(8,128)(2,1)} %bitcast.27, bf16[128,640]{1,0:T(8,128)(2,1)} %get-tuple-element.41.refs_0_, bf16[128,640]{1,0:T(8,128)(2,1)} %copy-done.22, bf16[128,640]{1,0:T(8,128)(2,1)} %copy-done.23, bf16[128,640]{1,0:T(8,128)(2,1)} %copy-done.24), custom_call_target="tpu_custom_call" | custom-call | flops 1258291200 | bytes 4341848 | tf_op jit(solution)/shard_map/pallas_call | solution.py:55
  44.4 2.4 %collective-permute-done.7.refs_2_ = bf16[128,640]{1,0:T(8,128)(2,1)} collective-permute-done((bf16[128,640]{1,0:T(8,128)(2,1)}, bf16[128,640]{1,0:T(8,128)(2,1)}, u32[]{:S(2)}, u32[]{:S(2)}) %collective-permute-start.7) | collective-permute-done | bytes 163872 | tf_op jit(solution)/shard_map/ppermute | solution.py:407
  46.8 5.8 %shard_map.88 = (bf16[80,1920]{1,0:T(8,128)(2,1)}, bf16[80,1920]{1,0:T(8,128)(2,1)}, bf16[80,1920]{1,0:T(8,128)(2,1)}, bf16[80,1920]{1,0:T(8,128)(2,1)}) custom-call(s32[22]{0:T(128)} %stack.79.place_ref, bf16[3,640,640]{2,1,0:T(8,128)(2,1)} %bitcast.28, bf16[128,640]{1,0:T(8,128)(2,1)} %copy-done.21, bf16[128,640]{1,0:T(8,128)(2,1)} %collective-permute-done.6.refs_1_, ...), custom_call_target="tpu_custom_call" | custom-call | flops 1258291200 | bytes 5570648 | tf_op jit(solution)/shard_map/pallas_call | solution.py:55
  54.6 17.6 %collective-permute-done.1 = bf16[8,16,1920]{2,1,0:T(8,128)(2,1)} collective-permute-done((bf16[8,16,1920]{2,1,0:T(8,128)(2,1)}, bf16[8,16,1920]{2,1,0:T(8,128)(2,1)}, u32[]{:S(2)}, u32[]{:S(2)}) %collective-permute-start.1) | collective-permute-done | bytes 491552 | tf_op jit(solution)/shard_map/ppermute | solution.py:407
  74.4 4.0 %all-to-all-start.1 = ((bf16[8,32,1920]{2,1,0:T(8,128)(2,1)}), bf16[8,32,1920]{2,1,0:T(8,128)(2,1)S(1)}, u32[]{:S(2)}, u32[]{:S(2)}) async-start(bf16[8,32,1920]{2,1,0:T(8,128)(2,1)} %pad_maximum_fusion.1), calls=%async_computation.1 | async-start | bytes 1966080 | tf_op jit(solution)/shard_map/all_to_all | solution.py:467
  80.9 14.7 %collective-permute-done.14 = bf16[80,1920]{1,0:T(8,128)(2,1)S(1)} collective-permute-done((bf16[80,1920]{1,0:T(8,128)(2,1)S(1)}, bf16[80,1920]{1,0:T(8,128)(2,1)S(1)}, u32[]{:S(2)}, u32[]{:S(2)}) %collective-permute-start.14) | collective-permute-done | bytes 307232 | tf_op jit(solution)/shard_map/ppermute | solution.py:407
  96.7 3.9 %shard_map.84 = (bf16[512,1280]{1,0:T(8,128)(2,1)}, bf16[512,640]{1,0:T(8,128)(2,1)}) custom-call(bf16[512,512]{1,0:T(8,128)(2,1)} %shard_map.82.choose_ref, bf16[256,1920]{1,0:T(8,128)(2,1)} %bitcast.30, bf16[256,1920]{1,0:T(8,128)(2,1)} %bitcast.31), custom_call_target="tpu_custom_call" | custom-call | flops 1006632960 | bytes 4456448 | tf_op jit(solution)/shard_map/pallas_call | solution.py:55
  104.7 3.2 %collective-permute-start.17 = (bf16[80,1920]{1,0:T(8,128)(2,1)S(1)}, bf16[80,1920]{1,0:T(8,128)(2,1)S(1)}, u32[]{:S(2)}, u32[]{:S(2)}) collective-permute-start(bf16[80,1920]{1,0:T(8,128)(2,1)S(1)} %get-tuple-element.53.refs_0_), channel_id=1, source_target_pairs={{0,8},{1,9},{2,10},{3,11},{4,12},{5,13},{6,14},{7,15},{8,0},{9,1},... | collective-permute-start | bytes 921608 | tf_op jit(solution)/shard_map/ppermute | solution.py:407
  108.0 23.8 %collective-permute-done.16.refs_2_ = bf16[32,1920]{1,0:T(8,128)(2,1)S(1)} collective-permute-done((bf16[32,1920]{1,0:T(8,128)(2,1)S(1)}, bf16[32,1920]{1,0:T(8,128)(2,1)S(1)}, u32[]{:S(2)}, u32[]{:S(2)}) %collective-permute-start.16) | collective-permute-done | bytes 122912 | tf_op jit(solution)/shard_map/ppermute | solution.py:407
  131.7 4.9 %collective-permute-done.19.refs_5_ = bf16[32,1920]{1,0:T(8,128)(2,1)S(1)} collective-permute-done((bf16[32,1920]{1,0:T(8,128)(2,1)S(1)}, bf16[32,1920]{1,0:T(8,128)(2,1)S(1)}, u32[]{:S(2)}, u32[]{:S(2)}) %collective-permute-start.19) | collective-permute-done | bytes 122912 | tf_op jit(solution)/shard_map/ppermute | solution.py:407
  137.8 4.4 %collective-permute-done.18.refs_4_ = bf16[48,1920]{1,0:T(8,128)(2,1)} collective-permute-done((bf16[48,1920]{1,0:T(8,128)(2,1)S(1)}, bf16[48,1920]{1,0:T(8,128)(2,1)}, u32[]{:S(2)}, u32[]{:S(2)}) %collective-permute-start.18) | collective-permute-done | bytes 184352 | tf_op jit(solution)/shard_map/ppermute | solution.py:407
  147.7 8.2 %shard_map.85 = (f32[512,640]{1,0:T(8,128)S(1)}, f32[512,128]{1,0:T(8,128)S(1)}) custom-call(s32[22]{0:T(128)S(1)} %copy-done.7, bf16[512,640]{1,0:T(8,128)(2,1)S(1)} %copy-done.1, s32[8,512]{1,0:T(8,128)S(1)} %reshape.34.ids_ref, bf16[512,1280]{1,0:T(8,128)(2,1)S(1)} %copy-done.8, bf16[512,1280]{1,0:T(8,128)(2,1)S(1)} %copy-done.10), custom_call_target="tpu_custom_call" | custom-call | flops 1006632960 | bytes 4866136 | tf_op jit(solution)/shard_map/pallas_call | solution.py:55
  156.0 6.5 %shard_map.86.attended_ref = f32[512,640]{1,0:T(8,128)S(1)} custom-call(s32[22]{0:T(128)S(1)} %copy-done.7, bf16[512,640]{1,0:T(8,128)(2,1)S(1)} %copy-done.2, s32[8,512]{1,0:T(8,128)S(1)} %reshape.34.ids_ref, f32[512,640]{1,0:T(8,128)S(1)} %get-tuple-element.35.near_ref, f32[512,128]{1,0:T(8,128)S(1)} %get-tuple-element.36.stat_ref, ...), custom_call_target="tpu_custom_call" | custom-call | flops 503316480 | bytes 4866136 | tf_op jit(solution)/shard_map/pallas_call | solution.py:55
  162.6 5.1 %shard_map.89 = (bf16[128,640]{1,0:T(8,128)(2,1)S(1)}, bf16[128,640]{1,0:T(8,128)(2,1)S(1)}, bf16[128,640]{1,0:T(8,128)(2,1)S(1)}, bf16[128,640]{1,0:T(8,128)(2,1)S(1)}) custom-call(s32[22]{0:T(128)S(1)} %copy-done.7, bf16[3,640,640]{2,1,0:T(8,128)(2,1)S(1)} %bitcast.29, bf16[512,640]{1,0:T(8,128)(2,1)S(1)} %copy-done.2, ...), custom_call_target="tpu_custom_call" | custom-call | flops 1258291200 | bytes 7536728 | tf_op jit(solution)/shard_map/pallas_call | solution.py:55
  170.1 2.9 %collective-permute-start.28 = (bf16[128,640]{1,0:T(8,128)(2,1)S(1)}, bf16[128,640]{1,0:T(8,128)(2,1)S(1)}, u32[]{:S(2)}, u32[]{:S(2)}) collective-permute-start(bf16[128,640]{1,0:T(8,128)(2,1)S(1)} %get-tuple-element.51), channel_id=1, source_target_pairs={{0,1},{1,5},{2,3},{3,7},{4,0},{5,4},{6,2},{7,6},{8,9},{9,13},{10,1... | collective-permute-start | bytes 491528 | tf_op jit(solution)/shard_map/ppermute | solution.py:407
  173.8 6.1 %collective-permute-done.28.refs_2_ = bf16[128,640]{1,0:T(8,128)(2,1)S(1)} collective-permute-done((bf16[128,640]{1,0:T(8,128)(2,1)S(1)}, bf16[128,640]{1,0:T(8,128)(2,1)S(1)}, u32[]{:S(2)}, u32[]{:S(2)}) %collective-permute-start.28) | collective-permute-done | bytes 163872 | tf_op jit(solution)/shard_map/ppermute | solution.py:407
  181.4 2.4 %shard_map.90 = bf16[128,2560]{1,0:T(8,128)(2,1)} custom-call(s32[22]{0:T(128)} %stack.79.place_ref, bf16[128,640]{1,0:T(8,128)(2,1)} %copy-done.15, bf16[128,640]{1,0:T(8,128)(2,1)} %copy-done.16, bf16[128,640]{1,0:T(8,128)(2,1)} %copy-done.17, bf16[128,640]{1,0:T(8,128)(2,1)} %copy-done.18, f32[1,2560]{1,0:T(1,128)} %reshape.35.refs_4_), custom_call_target="tpu_custom_call" | custom-call | flops 1966080 | bytes 1321048 | tf_op jit(solution)/shard_map/pallas_call | solution.py:55
  (110 shorter events, 32.8 us)
Async XLA Ops:
  5.0 14.5 %collective-permute-start = (bf16[8,16,1920]{2,1,0:T(8,128)(2,1)}, bf16[8,16,1920]{2,1,0:T(8,128)(2,1)S(1)}, u32[]{:S(2)}, u32[]{:S(2)}) collective-permute-start(bf16[8,16,1920]{2,1,0:T(8,128)(2,1)} %bitcast.36), channel_id=1, source_target_pairs={{0,8},{1,9},{2,10},{3,11},{4,12},{5,13},{6,14},{7,15},{8,0},{9,1},... | collective-permute-start | bytes 1474568 | tf_op jit(solution)/shard_map/ppermute | solution.py:407
  8.1 21.0 %collective-permute-start.5 = (bf16[128,640]{1,0:T(8,128)(2,1)}, bf16[128,640]{1,0:T(8,128)(2,1)S(1)}, u32[]{:S(2)}, u32[]{:S(2)}) collective-permute-start(bf16[128,640]{1,0:T(8,128)(2,1)} %get-tuple-element.37), channel_id=1, source_target_pairs={{0,5},{1,4},{2,7},{3,6},{4,1},{5,0},{6,3},{7,2},{8,13},{9,12},{10,... | collective-permute-start | bytes 491528 | tf_op jit(solution)/shard_map/ppermute | solution.py:407
  8.8 20.4 %collective-permute-start.9 = (bf16[128,640]{1,0:T(8,128)(2,1)}, bf16[128,640]{1,0:T(8,128)(2,1)S(1)}, u32[]{:S(2)}, u32[]{:S(2)}) collective-permute-start(bf16[128,640]{1,0:T(8,128)(2,1)} %get-tuple-element.42), channel_id=1, source_target_pairs={{0,2},{1,3},{2,0},{3,1},{4,6},{5,7},{6,4},{7,5},{8,10},{9,11},{10,... | collective-permute-start | bytes 491528 | tf_op jit(solution)/shard_map/ppermute | solution.py:407
  10.3 21.9 %collective-permute-start.10 = (bf16[128,640]{1,0:T(8,128)(2,1)}, bf16[128,640]{1,0:T(8,128)(2,1)S(1)}, u32[]{:S(2)}, u32[]{:S(2)}) collective-permute-start(bf16[128,640]{1,0:T(8,128)(2,1)} %get-tuple-element.43), channel_id=1, source_target_pairs={{0,4},{1,5},{2,6},{3,7},{4,0},{5,1},{6,2},{7,3},{8,12},{9,13},{10,... | collective-permute-start | bytes 491528 | tf_op jit(solution)/shard_map/ppermute | solution.py:407
  11.2 21.0 %collective-permute-start.11 = (bf16[128,640]{1,0:T(8,128)(2,1)}, bf16[128,640]{1,0:T(8,128)(2,1)S(1)}, u32[]{:S(2)}, u32[]{:S(2)}) collective-permute-start(bf16[128,640]{1,0:T(8,128)(2,1)} %get-tuple-element.44), channel_id=1, source_target_pairs={{0,3},{1,2},{2,1},{3,0},{4,7},{5,6},{6,5},{7,4},{8,11},{9,10},{10,... | collective-permute-start | bytes 491528 | tf_op jit(solution)/shard_map/ppermute | solution.py:407
  21.7 52.8 %all-to-all-start = ((bf16[8,32,1920]{2,1,0:T(8,128)(2,1)}), bf16[8,32,1920]{2,1,0:T(8,128)(2,1)S(1)}, u32[]{:S(2)}, u32[]{:S(2)}) async-start(bf16[8,32,1920]{2,1,0:T(8,128)(2,1)} %pad_maximum_fusion), calls=%async_computation | async-start | bytes 1966080 | tf_op jit(solution)/shard_map/all_to_all | solution.py:467
  25.5 29.1 %collective-permute-start.2 = (bf16[8,16,1920]{2,1,0:T(8,128)(2,1)}, bf16[8,16,1920]{2,1,0:T(8,128)(2,1)}, u32[]{:S(2)}, u32[]{:S(2)}) collective-permute-start(bf16[8,16,1920]{2,1,0:T(8,128)(2,1)} %bitcast.25), channel_id=1, source_target_pairs={{0,24},{1,25},{2,26},{3,27},{4,28},{5,29},{6,30},{7,31},{8,16},{9,... | collective-permute-start | bytes 1474568 | tf_op jit(solution)/shard_map/ppermute | solution.py:407
  29.1 43.1 %collective-permute-start.1 = (bf16[8,16,1920]{2,1,0:T(8,128)(2,1)}, bf16[8,16,1920]{2,1,0:T(8,128)(2,1)}, u32[]{:S(2)}, u32[]{:S(2)}) collective-permute-start(bf16[8,16,1920]{2,1,0:T(8,128)(2,1)} %bitcast.24), channel_id=1, source_target_pairs={{0,16},{1,17},{2,18},{3,19},{4,20},{5,21},{6,22},{7,23},{8,24},{9,... | collective-permute-start | bytes 1474568 | tf_op jit(solution)/shard_map/ppermute | solution.py:407
  29.2 15.2 %collective-permute-start.6 = (bf16[128,640]{1,0:T(8,128)(2,1)}, bf16[128,640]{1,0:T(8,128)(2,1)}, u32[]{:S(2)}, u32[]{:S(2)}) collective-permute-start(bf16[128,640]{1,0:T(8,128)(2,1)} %get-tuple-element.38), channel_id=1, source_target_pairs={{0,6},{1,7},{2,4},{3,5},{4,2},{5,3},{6,0},{7,1},{8,14},{9,15},{10,... | collective-permute-start | bytes 491528 | tf_op jit(solution)/shard_map/ppermute | solution.py:407
  32.2 14.6 %collective-permute-start.7 = (bf16[128,640]{1,0:T(8,128)(2,1)}, bf16[128,640]{1,0:T(8,128)(2,1)}, u32[]{:S(2)}, u32[]{:S(2)}) collective-permute-start(bf16[128,640]{1,0:T(8,128)(2,1)} %get-tuple-element.39), channel_id=1, source_target_pairs={{0,7},{1,6},{2,5},{3,4},{4,3},{5,2},{6,1},{7,0},{8,15},{9,14},{10,... | collective-permute-start | bytes 491528 | tf_op jit(solution)/shard_map/ppermute | solution.py:407
  52.6 25.8 %collective-permute-start.13 = (bf16[80,1920]{1,0:T(8,128)(2,1)}, bf16[80,1920]{1,0:T(8,128)(2,1)S(1)}, u32[]{:S(2)}, u32[]{:S(2)}) collective-permute-start(bf16[80,1920]{1,0:T(8,128)(2,1)} %get-tuple-element.48), channel_id=1, source_target_pairs={{0,8},{1,9},{2,10},{3,11},{4,12},{5,13},{6,14},{7,15},{8,0},{9,1},... | collective-permute-start | bytes 921608 | tf_op jit(solution)/shard_map/ppermute | solution.py:407
  54.2 26.7 %collective-permute-start.12 = (bf16[80,1920]{1,0:T(8,128)(2,1)}, bf16[80,1920]{1,0:T(8,128)(2,1)S(1)}, u32[]{:S(2)}, u32[]{:S(2)}) collective-permute-start(bf16[80,1920]{1,0:T(8,128)(2,1)} %get-tuple-element.46), channel_id=1, source_target_pairs={{0,8},{1,9},{2,10},{3,11},{4,12},{5,13},{6,14},{7,15},{8,0},{9,1},... | collective-permute-start | bytes 921608 | tf_op jit(solution)/shard_map/ppermute | solution.py:407
  74.4 21.2 %all-to-all-start.1 = ((bf16[8,32,1920]{2,1,0:T(8,128)(2,1)}), bf16[8,32,1920]{2,1,0:T(8,128)(2,1)S(1)}, u32[]{:S(2)}, u32[]{:S(2)}) async-start(bf16[8,32,1920]{2,1,0:T(8,128)(2,1)} %pad_maximum_fusion.1), calls=%async_computation.1 | async-start | bytes 1966080 | tf_op jit(solution)/shard_map/all_to_all | solution.py:467
  78.5 17.0 %collective-permute-start.14 = (bf16[80,1920]{1,0:T(8,128)(2,1)S(1)}, bf16[80,1920]{1,0:T(8,128)(2,1)S(1)}, u32[]{:S(2)}, u32[]{:S(2)}) collective-permute-start(bf16[80,1920]{1,0:T(8,128)(2,1)S(1)} %add_convert_fusion.1), channel_id=1, source_target_pairs={{0,16},{1,17},{2,18},{3,19},{4,20},{5,21},{6,22},{7,23},{8,24},{9,... | collective-permute-start | bytes 921608 | tf_op jit(solution)/shard_map/ppermute | solution.py:407
  100.6 41.7 %collective-permute-start.3 = (bf16[512,1280]{1,0:T(8,128)(2,1)}, bf16[512,1280]{1,0:T(8,128)(2,1)S(1)}, u32[]{:S(2)}, u32[]{:S(2)}) collective-permute-start(bf16[512,1280]{1,0:T(8,128)(2,1)} %get-tuple-element.34.kv_ref), channel_id=1, source_target_pairs={{0,1},{1,0},{2,3},{3,2},{4,5},{5,4},{6,7},{7,6},{8,9},{9,8},{10,11... | collective-permute-start | bytes 3932168 | tf_op jit(solution)/shard_map/ppermute | solution.py:407
  100.7 43.2 %collective-permute-start.4 = (bf16[512,1280]{1,0:T(8,128)(2,1)}, bf16[512,1280]{1,0:T(8,128)(2,1)S(1)}, u32[]{:S(2)}, u32[]{:S(2)}) collective-permute-start(bf16[512,1280]{1,0:T(8,128)(2,1)} %get-tuple-element.34.kv_ref), channel_id=1, source_target_pairs={{1,8},{3,10},{5,12},{7,14},{8,1},{9,16},{10,3},{11,18},{12,5},{13,... | collective-permute-start | bytes 3932168 | tf_op jit(solution)/shard_map/ppermute | solution.py:407
  101.6 30.1 %collective-permute-start.15 = (bf16[48,1920]{1,0:T(8,128)(2,1)S(1)}, bf16[48,1920]{1,0:T(8,128)(2,1)S(1)}, u32[]{:S(2)}, u32[]{:S(2)}) collective-permute-start(bf16[48,1920]{1,0:T(8,128)(2,1)S(1)} %add_convert_fusion.3), channel_id=1, source_target_pairs={{0,16},{1,17},{2,18},{3,19},{4,20},{5,21},{6,22},{7,23},{8,24},{9,... | collective-permute-start | bytes 552968 | tf_op jit(solution)/shard_map/ppermute | solution.py:407
  103.0 28.7 %collective-permute-start.16 = (bf16[32,1920]{1,0:T(8,128)(2,1)S(1)}, bf16[32,1920]{1,0:T(8,128)(2,1)S(1)}, u32[]{:S(2)}, u32[]{:S(2)}) collective-permute-start(bf16[32,1920]{1,0:T(8,128)(2,1)S(1)} %add_convert_fusion.4), channel_id=1, source_target_pairs={{0,16},{1,17},{2,18},{3,19},{4,20},{5,21},{6,22},{7,23},{8,24},{9,... | collective-permute-start | bytes 368648 | tf_op jit(solution)/shard_map/ppermute | solution.py:407
  104.7 32.6 %collective-permute-start.17 = (bf16[80,1920]{1,0:T(8,128)(2,1)S(1)}, bf16[80,1920]{1,0:T(8,128)(2,1)S(1)}, u32[]{:S(2)}, u32[]{:S(2)}) collective-permute-start(bf16[80,1920]{1,0:T(8,128)(2,1)S(1)} %get-tuple-element.53.refs_0_), channel_id=1, source_target_pairs={{0,8},{1,9},{2,10},{3,11},{4,12},{5,13},{6,14},{7,15},{8,0},{9,1},... | collective-permute-start | bytes 921608 | tf_op jit(solution)/shard_map/ppermute | solution.py:407
  137.3 25.2 %collective-permute-start.20 = (bf16[80,1920]{1,0:T(8,128)(2,1)S(1)}, bf16[80,1920]{1,0:T(8,128)(2,1)S(1)}, u32[]{:S(2)}, u32[]{:S(2)}) collective-permute-start(bf16[80,1920]{1,0:T(8,128)(2,1)S(1)} %get-tuple-element.53.refs_0_), channel_id=1, source_target_pairs={{0,1},{1,0},{2,3},{3,2},{4,5},{5,4},{6,7},{7,6},{8,9},{9,8},{10,11... | collective-permute-start | bytes 921608 | tf_op jit(solution)/shard_map/ppermute | solution.py:407
  137.3 25.3 %collective-permute-start.23 = (bf16[80,1920]{1,0:T(8,128)(2,1)S(1)}, bf16[80,1920]{1,0:T(8,128)(2,1)S(1)}, u32[]{:S(2)}, u32[]{:S(2)}) collective-permute-start(bf16[80,1920]{1,0:T(8,128)(2,1)S(1)} %collective-permute-done.17.refs_3_), channel_id=1, source_target_pairs={{0,1},{1,0},{2,3},{3,2},{4,5},{5,4},{6,7},{7,6},{8,9},{9,8},{10,11... | collective-permute-start | bytes 921608 | tf_op jit(solution)/shard_map/ppermute | solution.py:407
  142.2 20.3 %collective-permute-start.21 = (bf16[48,1920]{1,0:T(8,128)(2,1)S(1)}, bf16[48,1920]{1,0:T(8,128)(2,1)}, u32[]{:S(2)}, u32[]{:S(2)}) collective-permute-start(bf16[48,1920]{1,0:T(8,128)(2,1)S(1)} %collective-permute-done.15.refs_1_), channel_id=1, source_target_pairs={{0,1},{1,0},{2,3},{3,2},{4,5},{5,4},{6,7},{7,6},{8,9},{9,8},{10,11... | collective-permute-start | bytes 552968 | tf_op jit(solution)/shard_map/ppermute | solution.py:407
  143.4 19.2 %collective-permute-start.24 = (bf16[48,1920]{1,0:T(8,128)(2,1)}, bf16[48,1920]{1,0:T(8,128)(2,1)}, u32[]{:S(2)}, u32[]{:S(2)}) collective-permute-start(bf16[48,1920]{1,0:T(8,128)(2,1)} %collective-permute-done.18.refs_4_), channel_id=1, source_target_pairs={{0,1},{1,0},{2,3},{3,2},{4,5},{5,4},{6,7},{7,6},{8,9},{9,8},{10,11... | collective-permute-start | bytes 552968 | tf_op jit(solution)/shard_map/ppermute | solution.py:407
  143.9 18.6 %collective-permute-start.25 = (bf16[32,1920]{1,0:T(8,128)(2,1)}, bf16[32,1920]{1,0:T(8,128)(2,1)S(1)}, u32[]{:S(2)}, u32[]{:S(2)}) collective-permute-start(bf16[32,1920]{1,0:T(8,128)(2,1)} %copy-done.3), channel_id=1, source_target_pairs={{0,1},{1,0},{2,3},{3,2},{4,5},{5,4},{6,7},{7,6},{8,9},{9,8},{10,11... | collective-permute-start | bytes 368648 | tf_op jit(solution)/shard_map/ppermute | solution.py:407
  (33 other events, 322.0 us)

commit v11 on v10

--- a/solution.py
+++ b/solution.py
@@ -267,7 +267,8 @@
             stat_ref[here, :] = jnp.where(lane == 2 * head + 1, total, stat)
 
 
-def far_kernel(block, place_ref, query_ref, ids_ref, near_ref, stat_ref, kv_ref, out_ref, bias):
+def far_kernel(block, first_goal, place_ref, query_ref, ids_ref, near_ref, stat_ref, fast_ref, kv_ref, *refs):
+    out_refs, (bias, rows_buf) = refs[:-2], refs[-2:]
     n = query_ref.shape[0]
     count = n // block
     core, group = place_ref[2], place_ref[3]
@@ -301,13 +302,18 @@
             score = jnp.exp2((score - peak) * FACTOR)
             total = old_total * keep + jnp.sum(score, axis=1, keepdims=True)
             mixed = near_ref[here, keys] * keep + dot(score.astype(BF16), kv_ref[there, values])
-            out_ref[here, keys] = mixed / total
-
-
-def apply_kernel(first_goal, first_rows, place_ref, weight_ref, query_ref, attended_ref, *refs):
+            rows_buf[here, keys] = (mixed / total + fast_ref[here, keys]).astype(BF16)
+
+    rows = out_refs[0].shape[0]
+    for index, ref in enumerate(out_refs):
+        begin = pl.multiple_of(place_ref[first_goal + index] * rows, rows)
+        ref[...] = rows_buf[pl.ds(begin, rows), :]
+
+
+def apply_kernel(first_rows, place_ref, weight_ref, query_ref, *refs):
     hidden = weight_ref.shape[2]
-    out_refs, (fresh, scales, rows_buf) = refs[-3 - PARTS : -3], refs[-3:]
-    count = (len(refs) - 3 - PARTS) // 2
+    out_ref, fresh, scales = refs[-3:]
+    count = (len(refs) - 3) // 2
     mine_refs, other_refs = refs[:count], refs[count : 2 * count]
     core = place_ref[2]
     for head in range(PART_FAST):
@@ -341,11 +347,7 @@
         parts.append((begin, dot(product, fresh[head, 2], ((1,), (1,)))))
     for lane in range(0, PART_WIDTH, LANES):
         inside = [value[:, lane - begin : lane - begin + LANES] for begin, value in parts if begin <= lane < begin + SPAN]
-        rows_buf[:, lane : lane + LANES] = functools.reduce(jnp.add, inside, attended_ref[:, lane : lane + LANES]).astype(BF16)
-    block = out_refs[0].shape[0]
-    for index, ref in enumerate(out_refs):
-        begin = pl.multiple_of(place_ref[first_goal + index] * block, block)
-        ref[...] = rows_buf[pl.ds(begin, block), :]
+        out_ref[:, lane : lane + LANES] = functools.reduce(jnp.add, inside)
 
 
 def norm_kernel(place_ref, *refs):
@@ -545,24 +547,19 @@
         scratch=[VMEM((group_rows, group_rows), F32), VMEM((count, block, group_rows), F32)],
         smem=1, flops=6 * group_rows * group_rows * PART_WIDTH, limit=24,
     )
-    (attended,) = call(
-        functools.partial(far_kernel, block),
+    (fast_out,) = call(
+        functools.partial(apply_kernel, first_rows),
         [wide],
-        [place, query_seq, ids, near_mixed, stats, kv_far],
-        scratch=[VMEM((count, block, group_rows), F32)],
+        [place, weights, query_seq] + pieces + pieces_other,
+        scratch=[VMEM((PART_FAST, 3, SPAN, hidden), BF16), VMEM((PART_FAST * 3, hidden), F32)],
+        smem=1, flops=6 * group_rows * PART_WIDTH * hidden, limit=40,
+    )
+    blocks = call(
+        functools.partial(far_kernel, block, first_goal),
+        [jax.ShapeDtypeStruct((tok_dev, PART_WIDTH), BF16)] * PARTS,
+        [place, query_seq, ids, near_mixed, stats, fast_out, kv_far],
+        scratch=[VMEM((count, block, group_rows), F32), VMEM((group_rows, PART_WIDTH), BF16)],
         smem=1, flops=3 * group_rows * group_rows * PART_WIDTH, limit=24,
-    )
-
-    blocks = call(
-        functools.partial(apply_kernel, first_goal, first_rows),
-        [jax.ShapeDtypeStruct((tok_dev, PART_WIDTH), BF16)] * PARTS,
-        [place, weights, query_seq, attended] + pieces + pieces_other,
-        scratch=[
-            VMEM((PART_FAST, 3, SPAN, hidden), BF16),
-            VMEM((PART_FAST * 3, hidden), F32),
-            VMEM((group_rows, PART_WIDTH), BF16),
-        ],
-        smem=1, flops=6 * group_rows * PART_WIDTH * hidden, limit=40,
     )
 
     parts = []

time: 184 us -> 207 us (1.12)
  starting transfers between devices: 36.6 us -> 50.3 us
  waiting for transfers between devices: 83.9 us -> 90.2 us
    ppermute x30, starting transfers between devices: 28.8 us -> 41.7 us  [permute(): return lax.ppermute(array, 'tok', route)]
    ppermute x30, waiting for transfers between devices: 83.9 us -> 90.1 us  [permute(): return lax.ppermute(array, 'tok', route)]
    concatenate x2, other arithmetic: 4.31 us -> 2.08 us  [shards(): both = jnp.concatenate(both, axis=1)]
    unnamed x51 -> x53, local copies, waits for them, and re-layouts: 11.2 us -> 12.7 us
  transfers between devices with their start and end apart: 32 -> 32, of which waited for: 11 -> 11; matrix products, arithmetic and copies ran while one was open for 6% -> 5% of each run, Pallas kernels for 15% -> 15%
where the time goes in v11:
time: 207 us
  waiting for transfers between devices  90.2 us (44%)
  starting transfers between devices  50.3 us (24%)
  Pallas kernels  45.9 us (22%)
  local copies, waits for them, and re-layouts  15.9 us (8%)
  other arithmetic  4.01 us (2%)
    ppermute x30, waiting for transfers between devices, permute(): return lax.ppermute(array, 'tok', route)  90.1 us
    pallas_call x9, Pallas kernels, call(): pl.pallas_call(kernel, out_shape=list(outs), in_specs=specs, out_specs=ou...  45.9 us
    ppermute x30, starting transfers between devices, permute(): return lax.ppermute(array, 'tok', route)  41.7 us
    unnamed x53, local copies, waits for them, and re-layouts  12.7 us
    all_to_all x2, starting transfers between devices, shards(): lax.all_to_all(both, 'tok', split_axis=0, concat_axis=0, axis_index_group...  8.64 us
  transfers between devices with their start and end apart: 32, of which 11 were waited for; matrix products, arithmetic and copies ran while one was open for 5% of the time, Pallas kernels for 15%

profile of v11, /device:TPU:0, one launch (start us, length us, event | category | flops | bytes accessed | tf_op | source)
XLA Modules:
  0.0 206.5 jit_solution(13957477847980874314)
XLA Ops:
  0.6 4.4 %shard_map.83 = (bf16[128,640]{1,0:T(8,128)(2,1)}, bf16[128,640]{1,0:T(8,128)(2,1)}, bf16[128,640]{1,0:T(8,128)(2,1)}, bf16[128,640]{1,0:T(8,128)(2,1)}, bf16[12...) custom-call(s32[22]{0:T(128)} %stack.79.place_ref, ...), custom_call_target="tpu_custom_call" | custom-call | flops 251658240 | bytes 5263448 | tf_op jit(solution)/shard_map/pallas_call | solution.py:55
  5.0 3.0 %collective-permute-start.8 = (bf16[128,640]{1,0:T(8,128)(2,1)}, bf16[128,640]{1,0:T(8,128)(2,1)S(1)}, u32[]{:S(2)}, u32[]{:S(2)}) collective-permute-start(bf16[128,640]{1,0:T(8,128)(2,1)} %get-tuple-element.42), channel_id=1, source_target_pairs={{0,2},{1,3},{2,0},{3,1},{4,6},{5,7},{6,4},{7,5},{8,10},{9,11},{10,... | collective-permute-start | bytes 491528 | tf_op jit(solution)/shard_map/ppermute | solution.py:409
  12.7 3.6 %collective-permute-start.5 = (bf16[128,640]{1,0:T(8,128)(2,1)}, bf16[128,640]{1,0:T(8,128)(2,1)}, u32[]{:S(2)}, u32[]{:S(2)}) collective-permute-start(bf16[128,640]{1,0:T(8,128)(2,1)} %get-tuple-element.38), channel_id=1, source_target_pairs={{0,6},{1,7},{2,4},{3,5},{4,2},{5,3},{6,0},{7,1},{8,14},{9,15},{10,... | collective-permute-start | bytes 491528 | tf_op jit(solution)/shard_map/ppermute | solution.py:409
  19.1 3.3 %copy.10 = bf16[640,3,640]{0,2,1:T(8,128)(2,1)} copy(bf16[640,3,640]{2,0,1:T(8,128)(2,1)S(1)} %constant_dynamic-slice_fusion) | data formatting | bytes 4915200
  22.3 5.4 %shard_map.86.refs_4_ = bf16[320,1920]{1,0:T(8,128)(2,1)} custom-call(s32[22]{0:T(128)} %stack.79.place_ref, bf16[3,640,640]{2,1,0:T(8,128)(2,1)} %bitcast.27, bf16[128,640]{1,0:T(8,128)(2,1)} %get-tuple-element.41.refs_0_, bf16[128,640]{1,0:T(8,128)(2,1)} %copy-done.23, bf16[128,640]{1,0:T(8,128)(2,1)} %copy-done.24, bf16[128,640]{1,0:T(8,128)(2,1)} %copy-done.25), custom_call_target="tpu_custom_call" | custom-call | flops 1258291200 | bytes 4341848 | tf_op jit(solution)/shard_map/pallas_call | solution.py:55
  28.4 5.8 %shard_map.87 = (bf16[80,1920]{1,0:T(8,128)(2,1)}, bf16[80,1920]{1,0:T(8,128)(2,1)}, bf16[80,1920]{1,0:T(8,128)(2,1)}, bf16[80,1920]{1,0:T(8,128)(2,1)}) custom-call(s32[22]{0:T(128)} %stack.79.place_ref, bf16[3,640,640]{2,1,0:T(8,128)(2,1)} %bitcast.28, bf16[128,640]{1,0:T(8,128)(2,1)} %copy-done.22, bf16[128,640]{1,0:T(8,128)(2,1)} %collective-permute-done.5.refs_1_, ...), custom_call_target="tpu_custom_call" | custom-call | flops 1258291200 | bytes 5570648 | tf_op jit(solution)/shard_map/pallas_call | solution.py:55
  36.9 4.6 %all-to-all-start = ((bf16[8,32,1920]{2,1,0:T(8,128)(2,1)}), bf16[8,32,1920]{2,1,0:T(8,128)(2,1)S(1)}, u32[]{:S(2)}, u32[]{:S(2)}) async-start(bf16[8,32,1920]{2,1,0:T(8,128)(2,1)} %pad_maximum_fusion), calls=%async_computation | async-start | bytes 1966080 | tf_op jit(solution)/shard_map/all_to_all | solution.py:469
  41.5 2.6 %collective-permute-start.1 = (bf16[8,16,1920]{2,1,0:T(8,128)(2,1)}, bf16[8,16,1920]{2,1,0:T(8,128)(2,1)S(1)}, u32[]{:S(2)}, u32[]{:S(2)}) collective-permute-start(bf16[8,16,1920]{2,1,0:T(8,128)(2,1)} %bitcast.23), channel_id=1, source_target_pairs={{0,16},{1,17},{2,18},{3,19},{4,20},{5,21},{6,22},{7,23},{8,24},{9,... | collective-permute-start | bytes 1474568 | tf_op jit(solution)/shard_map/ppermute | solution.py:409
  45.1 3.6 %collective-permute-start.13 = (bf16[80,1920]{1,0:T(8,128)(2,1)S(1)}, bf16[80,1920]{1,0:T(8,128)(2,1)S(1)}, u32[]{:S(2)}, u32[]{:S(2)}) collective-permute-start(bf16[80,1920]{1,0:T(8,128)(2,1)S(1)} %add_convert_fusion.1), channel_id=1, source_target_pairs={{0,16},{1,17},{2,18},{3,19},{4,20},{5,21},{6,22},{7,23},{8,24},{9,... | collective-permute-start | bytes 921608 | tf_op jit(solution)/shard_map/ppermute | solution.py:409
  48.7 2.3 %shard_map.82.choose_ref = bf16[512,512]{1,0:T(8,128)(2,1)} custom-call(s32[22]{0:T(128)} %stack.79.place_ref, s32[32,128]{1,0:T(8,128)} %bitcast.34), custom_call_target="tpu_custom_call" | custom-call | flops 524288 | bytes 540760 | tf_op jit(solution)/shard_map/pallas_call | solution.py:55
  50.9 33.2 %collective-permute-done.1 = bf16[8,16,1920]{2,1,0:T(8,128)(2,1)S(1)} collective-permute-done((bf16[8,16,1920]{2,1,0:T(8,128)(2,1)}, bf16[8,16,1920]{2,1,0:T(8,128)(2,1)S(1)}, u32[]{:S(2)}, u32[]{:S(2)}) %collective-permute-start.1) | collective-permute-done | bytes 491552 | tf_op jit(solution)/shard_map/ppermute | solution.py:409
  85.1 4.0 %all-to-all-start.1 = ((bf16[8,32,1920]{2,1,0:T(8,128)(2,1)}), bf16[8,32,1920]{2,1,0:T(8,128)(2,1)S(1)}, u32[]{:S(2)}, u32[]{:S(2)}) async-start(bf16[8,32,1920]{2,1,0:T(8,128)(2,1)} %pad_maximum_fusion.1), calls=%async_computation.1 | async-start | bytes 1966080 | tf_op jit(solution)/shard_map/all_to_all | solution.py:469
  89.2 11.8 %collective-permute-done.13 = bf16[80,1920]{1,0:T(8,128)(2,1)S(1)} collective-permute-done((bf16[80,1920]{1,0:T(8,128)(2,1)S(1)}, bf16[80,1920]{1,0:T(8,128)(2,1)S(1)}, u32[]{:S(2)}, u32[]{:S(2)}) %collective-permute-start.13) | collective-permute-done | bytes 307232 | tf_op jit(solution)/shard_map/ppermute | solution.py:409
  105.3 4.1 %shard_map.84 = (bf16[512,1280]{1,0:T(8,128)(2,1)}, bf16[512,640]{1,0:T(8,128)(2,1)}) custom-call(bf16[512,512]{1,0:T(8,128)(2,1)} %shard_map.82.choose_ref, bf16[256,1920]{1,0:T(8,128)(2,1)} %bitcast.30, bf16[256,1920]{1,0:T(8,128)(2,1)} %bitcast.31), custom_call_target="tpu_custom_call" | custom-call | flops 1006632960 | bytes 4456448 | tf_op jit(solution)/shard_map/pallas_call | solution.py:55
  111.1 11.1 %collective-permute-start.3 = (bf16[512,1280]{1,0:T(8,128)(2,1)}, bf16[512,1280]{1,0:T(8,128)(2,1)}, u32[]{:S(2)}, u32[]{:S(2)}) collective-permute-start(bf16[512,1280]{1,0:T(8,128)(2,1)} %get-tuple-element.34.kv_ref), channel_id=1, source_target_pairs={{0,1},{1,0},{2,3},{3,2},{4,5},{5,4},{6,7},{7,6},{8,9},{9,8},{10,11... | collective-permute-start | bytes 3932168 | tf_op jit(solution)/shard_map/ppermute | solution.py:409
  124.0 20.5 %collective-permute-done.15.refs_2_ = bf16[32,1920]{1,0:T(8,128)(2,1)S(1)} collective-permute-done((bf16[32,1920]{1,0:T(8,128)(2,1)S(1)}, bf16[32,1920]{1,0:T(8,128)(2,1)S(1)}, u32[]{:S(2)}, u32[]{:S(2)}) %collective-permute-start.15) | collective-permute-done | bytes 122912 | tf_op jit(solution)/shard_map/ppermute | solution.py:409
  147.1 9.6 %collective-permute-done.18.refs_5_ = bf16[32,1920]{1,0:T(8,128)(2,1)S(1)} collective-permute-done((bf16[32,1920]{1,0:T(8,128)(2,1)S(1)}, bf16[32,1920]{1,0:T(8,128)(2,1)S(1)}, u32[]{:S(2)}, u32[]{:S(2)}) %collective-permute-start.18) | collective-permute-done | bytes 122912 | tf_op jit(solution)/shard_map/ppermute | solution.py:409
  159.2 4.1 %collective-permute-done.17.refs_4_ = bf16[48,1920]{1,0:T(8,128)(2,1)} collective-permute-done((bf16[48,1920]{1,0:T(8,128)(2,1)}, bf16[48,1920]{1,0:T(8,128)(2,1)}, u32[]{:S(2)}, u32[]{:S(2)}) %collective-permute-start.17) | collective-permute-done | bytes 184352 | tf_op jit(solution)/shard_map/ppermute | solution.py:409
  168.8 5.3 %shard_map.88.fast_ref = f32[512,640]{1,0:T(8,128)S(1)} custom-call(s32[22]{0:T(128)S(1)} %copy-done.8, bf16[3,640,640]{2,1,0:T(8,128)(2,1)S(1)} %bitcast.29, bf16[512,640]{1,0:T(8,128)(2,1)S(1)} %copy-done.1, bf16[80,1920]{1,0:T(8,128)(2,1)S(1)} %get-tuple-element.53.refs_0_, bf16[48,1920]{1,0:T(8,128)(2,1)} %collective-permute-done.14.refs_1_, ...), custom_call_target="tpu_custom_call" | custom-call | flops 1258291200 | bytes 6881368 | tf_op jit(solution)/shard_map/pallas_call | solution.py:55
  174.1 9.0 %shard_map.85 = (f32[512,640]{1,0:T(8,128)S(1)}, f32[512,128]{1,0:T(8,128)S(1)}) custom-call(s32[22]{0:T(128)S(1)} %copy-done.8, bf16[512,640]{1,0:T(8,128)(2,1)S(1)} %copy-done.1, s32[8,512]{1,0:T(8,128)S(1)} %reshape.34.ids_ref, bf16[512,1280]{1,0:T(8,128)(2,1)S(1)} %copy-done.9, bf16[512,1280]{1,0:T(8,128)(2,1)} %collective-permute-done.3.chip_ref), custom_call_target="tpu_custom_call" | custom-call | flops 1006632960 | bytes 4866136 | tf_op jit(solution)/shard_map/pallas_call | solution.py:55
  183.2 7.4 %shard_map.89 = (bf16[128,640]{1,0:T(8,128)(2,1)S(1)}, bf16[128,640]{1,0:T(8,128)(2,1)S(1)}, bf16[128,640]{1,0:T(8,128)(2,1)S(1)}, bf16[128,640]{1,0:T(8,128)(2,1)S(1)}) custom-call(s32[22]{0:T(128)S(1)} %copy-done.8, bf16[512,640]{1,0:T(8,128)(2,1)S(1)} %copy-done.1, s32[8,512]{1,0:T(8,128)S(1)} %reshape.34.ids_ref, ...), custom_call_target="tpu_custom_call" | custom-call | flops 503316480 | bytes 5521496 | tf_op jit(solution)/shard_map/pallas_call | solution.py:55
  191.9 2.6 %collective-permute-start.28 = (bf16[128,640]{1,0:T(8,128)(2,1)S(1)}, bf16[128,640]{1,0:T(8,128)(2,1)S(1)}, u32[]{:S(2)}, u32[]{:S(2)}) collective-permute-start(bf16[128,640]{1,0:T(8,128)(2,1)S(1)} %get-tuple-element.51), channel_id=1, source_target_pairs={{0,1},{1,5},{2,3},{3,7},{4,0},{5,4},{6,2},{7,6},{8,9},{9,13},{10,1... | collective-permute-start | bytes 491528 | tf_op jit(solution)/shard_map/ppermute | solution.py:409
  196.7 6.2 %collective-permute-done.28.refs_2_ = bf16[128,640]{1,0:T(8,128)(2,1)S(1)} collective-permute-done((bf16[128,640]{1,0:T(8,128)(2,1)S(1)}, bf16[128,640]{1,0:T(8,128)(2,1)S(1)}, u32[]{:S(2)}, u32[]{:S(2)}) %collective-permute-start.28) | collective-permute-done | bytes 163872 | tf_op jit(solution)/shard_map/ppermute | solution.py:409
  204.2 2.4 %shard_map.90 = bf16[128,2560]{1,0:T(8,128)(2,1)} custom-call(s32[22]{0:T(128)} %stack.79.place_ref, bf16[128,640]{1,0:T(8,128)(2,1)} %copy-done.16, bf16[128,640]{1,0:T(8,128)(2,1)} %copy-done.17, bf16[128,640]{1,0:T(8,128)(2,1)} %copy-done.18, bf16[128,640]{1,0:T(8,128)(2,1)} %copy-done.19, f32[1,2560]{1,0:T(1,128)} %reshape.35.refs_4_), custom_call_target="tpu_custom_call" | custom-call | flops 1966080 | bytes 1321048 | tf_op jit(solution)/shard_map/pallas_call | solution.py:55
  (112 shorter events, 36.7 us)
Async XLA Ops:
  5.0 7.7 %collective-permute-start.8 = (bf16[128,640]{1,0:T(8,128)(2,1)}, bf16[128,640]{1,0:T(8,128)(2,1)S(1)}, u32[]{:S(2)}, u32[]{:S(2)}) collective-permute-start(bf16[128,640]{1,0:T(8,128)(2,1)} %get-tuple-element.42), channel_id=1, source_target_pairs={{0,2},{1,3},{2,0},{3,1},{4,6},{5,7},{6,4},{7,5},{8,10},{9,11},{10,... | collective-permute-start | bytes 491528 | tf_op jit(solution)/shard_map/ppermute | solution.py:409
  8.0 8.2 %collective-permute-start.9 = (bf16[128,640]{1,0:T(8,128)(2,1)}, bf16[128,640]{1,0:T(8,128)(2,1)S(1)}, u32[]{:S(2)}, u32[]{:S(2)}) collective-permute-start(bf16[128,640]{1,0:T(8,128)(2,1)} %get-tuple-element.43), channel_id=1, source_target_pairs={{0,4},{1,5},{2,6},{3,7},{4,0},{5,1},{6,2},{7,3},{8,12},{9,13},{10,... | collective-permute-start | bytes 491528 | tf_op jit(solution)/shard_map/ppermute | solution.py:409
  9.5 26.3 %collective-permute-start = (bf16[8,16,1920]{2,1,0:T(8,128)(2,1)}, bf16[8,16,1920]{2,1,0:T(8,128)(2,1)S(1)}, u32[]{:S(2)}, u32[]{:S(2)}) collective-permute-start(bf16[8,16,1920]{2,1,0:T(8,128)(2,1)} %bitcast.36), channel_id=1, source_target_pairs={{0,8},{1,9},{2,10},{3,11},{4,12},{5,13},{6,14},{7,15},{8,0},{9,1},... | collective-permute-start | bytes 1474568 | tf_op jit(solution)/shard_map/ppermute | solution.py:409
  11.1 16.6 %collective-permute-start.4 = (bf16[128,640]{1,0:T(8,128)(2,1)}, bf16[128,640]{1,0:T(8,128)(2,1)S(1)}, u32[]{:S(2)}, u32[]{:S(2)}) collective-permute-start(bf16[128,640]{1,0:T(8,128)(2,1)} %get-tuple-element.37), channel_id=1, source_target_pairs={{0,5},{1,4},{2,7},{3,6},{4,1},{5,0},{6,3},{7,2},{8,13},{9,12},{10,... | collective-permute-start | bytes 491528 | tf_op jit(solution)/shard_map/ppermute | solution.py:409
  12.7 15.0 %collective-permute-start.5 = (bf16[128,640]{1,0:T(8,128)(2,1)}, bf16[128,640]{1,0:T(8,128)(2,1)}, u32[]{:S(2)}, u32[]{:S(2)}) collective-permute-start(bf16[128,640]{1,0:T(8,128)(2,1)} %get-tuple-element.38), channel_id=1, source_target_pairs={{0,6},{1,7},{2,4},{3,5},{4,2},{5,3},{6,0},{7,1},{8,14},{9,15},{10,... | collective-permute-start | bytes 491528 | tf_op jit(solution)/shard_map/ppermute | solution.py:409
  16.3 11.5 %collective-permute-start.6 = (bf16[128,640]{1,0:T(8,128)(2,1)}, bf16[128,640]{1,0:T(8,128)(2,1)}, u32[]{:S(2)}, u32[]{:S(2)}) collective-permute-start(bf16[128,640]{1,0:T(8,128)(2,1)} %get-tuple-element.39), channel_id=1, source_target_pairs={{0,7},{1,6},{2,5},{3,4},{4,3},{5,2},{6,1},{7,0},{8,15},{9,14},{10,... | collective-permute-start | bytes 491528 | tf_op jit(solution)/shard_map/ppermute | solution.py:409
  17.0 10.7 %collective-permute-start.7 = (bf16[128,640]{1,0:T(8,128)(2,1)}, bf16[128,640]{1,0:T(8,128)(2,1)}, u32[]{:S(2)}, u32[]{:S(2)}) collective-permute-start(bf16[128,640]{1,0:T(8,128)(2,1)} %get-tuple-element.40), channel_id=1, source_target_pairs={{0,1},{1,0},{2,3},{3,2},{4,5},{5,4},{6,7},{7,6},{8,9},{9,8},{10,11... | collective-permute-start | bytes 491528 | tf_op jit(solution)/shard_map/ppermute | solution.py:409
  34.2 10.8 %collective-permute-start.12 = (bf16[80,1920]{1,0:T(8,128)(2,1)}, bf16[80,1920]{1,0:T(8,128)(2,1)S(1)}, u32[]{:S(2)}, u32[]{:S(2)}) collective-permute-start(bf16[80,1920]{1,0:T(8,128)(2,1)} %get-tuple-element.48), channel_id=1, source_target_pairs={{0,8},{1,9},{2,10},{3,11},{4,12},{5,13},{6,14},{7,15},{8,0},{9,1},... | collective-permute-start | bytes 921608 | tf_op jit(solution)/shard_map/ppermute | solution.py:409
  36.9 48.2 %all-to-all-start = ((bf16[8,32,1920]{2,1,0:T(8,128)(2,1)}), bf16[8,32,1920]{2,1,0:T(8,128)(2,1)S(1)}, u32[]{:S(2)}, u32[]{:S(2)}) async-start(bf16[8,32,1920]{2,1,0:T(8,128)(2,1)} %pad_maximum_fusion), calls=%async_computation | async-start | bytes 1966080 | tf_op jit(solution)/shard_map/all_to_all | solution.py:469
  41.5 42.6 %collective-permute-start.1 = (bf16[8,16,1920]{2,1,0:T(8,128)(2,1)}, bf16[8,16,1920]{2,1,0:T(8,128)(2,1)S(1)}, u32[]{:S(2)}, u32[]{:S(2)}) collective-permute-start(bf16[8,16,1920]{2,1,0:T(8,128)(2,1)} %bitcast.23), channel_id=1, source_target_pairs={{0,16},{1,17},{2,18},{3,19},{4,20},{5,21},{6,22},{7,23},{8,24},{9,... | collective-permute-start | bytes 1474568 | tf_op jit(solution)/shard_map/ppermute | solution.py:409
  44.1 40.0 %collective-permute-start.2 = (bf16[8,16,1920]{2,1,0:T(8,128)(2,1)}, bf16[8,16,1920]{2,1,0:T(8,128)(2,1)S(1)}, u32[]{:S(2)}, u32[]{:S(2)}) collective-permute-start(bf16[8,16,1920]{2,1,0:T(8,128)(2,1)} %bitcast.24), channel_id=1, source_target_pairs={{0,24},{1,25},{2,26},{3,27},{4,28},{5,29},{6,30},{7,31},{8,16},{9,... | collective-permute-start | bytes 1474568 | tf_op jit(solution)/shard_map/ppermute | solution.py:409
  44.3 44.8 %collective-permute-start.11 = (bf16[80,1920]{1,0:T(8,128)(2,1)}, bf16[80,1920]{1,0:T(8,128)(2,1)S(1)}, u32[]{:S(2)}, u32[]{:S(2)}) collective-permute-start(bf16[80,1920]{1,0:T(8,128)(2,1)} %get-tuple-element.46), channel_id=1, source_target_pairs={{0,8},{1,9},{2,10},{3,11},{4,12},{5,13},{6,14},{7,15},{8,0},{9,1},... | collective-permute-start | bytes 921608 | tf_op jit(solution)/shard_map/ppermute | solution.py:409
  45.1 55.9 %collective-permute-start.13 = (bf16[80,1920]{1,0:T(8,128)(2,1)S(1)}, bf16[80,1920]{1,0:T(8,128)(2,1)S(1)}, u32[]{:S(2)}, u32[]{:S(2)}) collective-permute-start(bf16[80,1920]{1,0:T(8,128)(2,1)S(1)} %add_convert_fusion.1), channel_id=1, source_target_pairs={{0,16},{1,17},{2,18},{3,19},{4,20},{5,21},{6,22},{7,23},{8,24},{9,... | collective-permute-start | bytes 921608 | tf_op jit(solution)/shard_map/ppermute | solution.py:409
  85.1 19.2 %all-to-all-start.1 = ((bf16[8,32,1920]{2,1,0:T(8,128)(2,1)}), bf16[8,32,1920]{2,1,0:T(8,128)(2,1)S(1)}, u32[]{:S(2)}, u32[]{:S(2)}) async-start(bf16[8,32,1920]{2,1,0:T(8,128)(2,1)} %pad_maximum_fusion.1), calls=%async_computation.1 | async-start | bytes 1966080 | tf_op jit(solution)/shard_map/all_to_all | solution.py:469
  102.8 41.6 %collective-permute-start.14 = (bf16[48,1920]{1,0:T(8,128)(2,1)}, bf16[48,1920]{1,0:T(8,128)(2,1)}, u32[]{:S(2)}, u32[]{:S(2)}) collective-permute-start(bf16[48,1920]{1,0:T(8,128)(2,1)} %add_convert_fusion.3), channel_id=1, source_target_pairs={{0,16},{1,17},{2,18},{3,19},{4,20},{5,21},{6,22},{7,23},{8,24},{9,... | collective-permute-start | bytes 552968 | tf_op jit(solution)/shard_map/ppermute | solution.py:409
  109.3 73.8 %collective-permute-start.25 = (bf16[512,1280]{1,0:T(8,128)(2,1)}, bf16[512,1280]{1,0:T(8,128)(2,1)}, u32[]{:S(2)}, u32[]{:S(2)}) collective-permute-start(bf16[512,1280]{1,0:T(8,128)(2,1)} %get-tuple-element.34.kv_ref), channel_id=1, source_target_pairs={{1,8},{3,10},{5,12},{7,14},{8,1},{9,16},{10,3},{11,18},{12,5},{13,... | collective-permute-start | bytes 3932168 | tf_op jit(solution)/shard_map/ppermute | solution.py:409
  111.1 63.0 %collective-permute-start.3 = (bf16[512,1280]{1,0:T(8,128)(2,1)}, bf16[512,1280]{1,0:T(8,128)(2,1)}, u32[]{:S(2)}, u32[]{:S(2)}) collective-permute-start(bf16[512,1280]{1,0:T(8,128)(2,1)} %get-tuple-element.34.kv_ref), channel_id=1, source_target_pairs={{0,1},{1,0},{2,3},{3,2},{4,5},{5,4},{6,7},{7,6},{8,9},{9,8},{10,11... | collective-permute-start | bytes 3932168 | tf_op jit(solution)/shard_map/ppermute | solution.py:409
  122.3 22.2 %collective-permute-start.15 = (bf16[32,1920]{1,0:T(8,128)(2,1)S(1)}, bf16[32,1920]{1,0:T(8,128)(2,1)S(1)}, u32[]{:S(2)}, u32[]{:S(2)}) collective-permute-start(bf16[32,1920]{1,0:T(8,128)(2,1)S(1)} %add_convert_fusion.4), channel_id=1, source_target_pairs={{0,16},{1,17},{2,18},{3,19},{4,20},{5,21},{6,22},{7,23},{8,24},{9,... | collective-permute-start | bytes 368648 | tf_op jit(solution)/shard_map/ppermute | solution.py:409
  123.7 33.3 %collective-permute-start.19 = (bf16[80,1920]{1,0:T(8,128)(2,1)S(1)}, bf16[80,1920]{1,0:T(8,128)(2,1)S(1)}, u32[]{:S(2)}, u32[]{:S(2)}) collective-permute-start(bf16[80,1920]{1,0:T(8,128)(2,1)S(1)} %get-tuple-element.53.refs_0_), channel_id=1, source_target_pairs={{0,1},{1,0},{2,3},{3,2},{4,5},{5,4},{6,7},{7,6},{8,9},{9,8},{10,11... | collective-permute-start | bytes 921608 | tf_op jit(solution)/shard_map/ppermute | solution.py:409
  144.4 13.3 %collective-permute-start.16 = (bf16[80,1920]{1,0:T(8,128)(2,1)S(1)}, bf16[80,1920]{1,0:T(8,128)(2,1)S(1)}, u32[]{:S(2)}, u32[]{:S(2)}) collective-permute-start(bf16[80,1920]{1,0:T(8,128)(2,1)S(1)} %get-tuple-element.53.refs_0_), channel_id=1, source_target_pairs={{0,8},{1,9},{2,10},{3,11},{4,12},{5,13},{6,14},{7,15},{8,0},{9,1},... | collective-permute-start | bytes 921608 | tf_op jit(solution)/shard_map/ppermute | solution.py:409
  146.4 10.3 %collective-permute-start.18 = (bf16[32,1920]{1,0:T(8,128)(2,1)S(1)}, bf16[32,1920]{1,0:T(8,128)(2,1)S(1)}, u32[]{:S(2)}, u32[]{:S(2)}) collective-permute-start(bf16[32,1920]{1,0:T(8,128)(2,1)S(1)} %collective-permute-done.15.refs_2_), channel_id=1, source_target_pairs={{0,8},{1,9},{2,10},{3,11},{4,12},{5,13},{6,14},{7,15},{8,0},{9,1},... | collective-permute-start | bytes 368648 | tf_op jit(solution)/shard_map/ppermute | solution.py:409
  157.7 7.3 %collective-permute-start.22 = (bf16[80,1920]{1,0:T(8,128)(2,1)S(1)}, bf16[80,1920]{1,0:T(8,128)(2,1)}, u32[]{:S(2)}, u32[]{:S(2)}) collective-permute-start(bf16[80,1920]{1,0:T(8,128)(2,1)S(1)} %collective-permute-done.16.refs_3_), channel_id=1, source_target_pairs={{0,1},{1,0},{2,3},{3,2},{4,5},{5,4},{6,7},{7,6},{8,9},{9,8},{10,11... | collective-permute-start | bytes 921608 | tf_op jit(solution)/shard_map/ppermute | solution.py:409
  191.9 11.0 %collective-permute-start.28 = (bf16[128,640]{1,0:T(8,128)(2,1)S(1)}, bf16[128,640]{1,0:T(8,128)(2,1)S(1)}, u32[]{:S(2)}, u32[]{:S(2)}) collective-permute-start(bf16[128,640]{1,0:T(8,128)(2,1)S(1)} %get-tuple-element.51), channel_id=1, source_target_pairs={{0,1},{1,5},{2,3},{3,7},{4,0},{5,4},{6,2},{7,6},{8,9},{9,13},{10,1... | collective-permute-start | bytes 491528 | tf_op jit(solution)/shard_map/ppermute | solution.py:409
  194.4 8.4 %collective-permute-start.29 = (bf16[128,640]{1,0:T(8,128)(2,1)S(1)}, bf16[128,640]{1,0:T(8,128)(2,1)S(1)}, u32[]{:S(2)}, u32[]{:S(2)}) collective-permute-start(bf16[128,640]{1,0:T(8,128)(2,1)S(1)} %get-tuple-element.52), channel_id=1, source_target_pairs={{0,3},{1,7},{2,1},{3,5},{4,2},{5,6},{6,0},{7,4},{8,11},{9,15},{10,... | collective-permute-start | bytes 491528 | tf_op jit(solution)/shard_map/ppermute | solution.py:409
  (34 other events, 356.3 us)

commit v12 on v9

--- a/solution.py
+++ b/solution.py
@@ -259,7 +259,8 @@
             stat_ref[here, :] = jnp.where(lane == 2 * head + 1, total, stat)
 
 
-def far_kernel(block, place_ref, query_ref, ids_ref, near_ref, stat_ref, kv_ref, out_ref, bias):
+def far_kernel(block, first_goal, place_ref, query_ref, ids_ref, near_ref, stat_ref, fast_ref, kv_ref, *refs):
+    out_refs, (bias, rows_buf) = refs[:-2], refs[-2:]
     n = query_ref.shape[0]
     count = n // block
     core, group = place_ref[2], place_ref[3]
@@ -293,13 +294,18 @@
             score = jnp.exp2((score - peak) * FACTOR)
             total = old_total * keep + jnp.sum(score, axis=1, keepdims=True)
             mixed = near_ref[here, keys] * keep + dot(score.astype(BF16), kv_ref[there, values])
-            out_ref[here, keys] = mixed / total
-
-
-def apply_kernel(first_goal, first_rows, place_ref, weight_ref, query_ref, attended_ref, *refs):
+            rows_buf[here, keys] = (mixed / total + fast_ref[here, keys]).astype(BF16)
+
+    rows = out_refs[0].shape[0]
+    for index, ref in enumerate(out_refs):
+        begin = pl.multiple_of(place_ref[first_goal + index] * rows, rows)
+        ref[...] = rows_buf[pl.ds(begin, rows), :]
+
+
+def apply_kernel(first_rows, place_ref, weight_ref, query_ref, *refs):
     hidden = weight_ref.shape[2]
-    out_refs, (fresh, scales, rows_buf) = refs[-3 - PARTS : -3], refs[-3:]
-    count = (len(refs) - 3 - PARTS) // 2
+    out_ref, fresh, scales = refs[-3:]
+    count = (len(refs) - 3) // 2
     mine_refs, other_refs = refs[:count], refs[count : 2 * count]
     core = place_ref[2]
     for head in range(PART_FAST):
@@ -333,11 +339,7 @@
         parts.append((begin, dot(product, fresh[head, 2], ((1,), (1,)))))
     for lane in range(0, PART_WIDTH, LANES):
         inside = [value[:, lane - begin : lane - begin + LANES] for begin, value in parts if begin <= lane < begin + SPAN]
-        rows_buf[:, lane : lane + LANES] = functools.reduce(jnp.add, inside, attended_ref[:, lane : lane + LANES]).astype(BF16)
-    block = out_refs[0].shape[0]
-    for index, ref in enumerate(out_refs):
-        begin = pl.multiple_of(place_ref[first_goal + index] * block, block)
-        ref[...] = rows_buf[pl.ds(begin, block), :]
+        out_ref[:, lane : lane + LANES] = functools.reduce(jnp.add, inside)
 
 
 def norm_kernel(place_ref, *refs):
@@ -527,24 +529,19 @@
         scratch=[VMEM((group_rows, group_rows), F32), VMEM((count, block, group_rows), F32)],
         smem=1, flops=6 * group_rows * group_rows * PART_WIDTH, limit=24,
     )
-    (attended,) = call(
-        functools.partial(far_kernel, block),
+    (fast_out,) = call(
+        functools.partial(apply_kernel, first_rows),
         [wide],
-        [place, query_seq, ids, near_mixed, stats, kv_far],
-        scratch=[VMEM((count, block, group_rows), F32)],
+        [place, weights, query_seq] + pieces + pieces_other,
+        scratch=[VMEM((PART_FAST, 3, SPAN, hidden), BF16), VMEM((PART_FAST * 3, hidden), F32)],
+        smem=1, flops=6 * group_rows * PART_WIDTH * hidden, limit=40,
+    )
+    blocks = call(
+        functools.partial(far_kernel, block, first_goal),
+        [jax.ShapeDtypeStruct((tok_dev, PART_WIDTH), BF16)] * PARTS,
+        [place, query_seq, ids, near_mixed, stats, fast_out, kv_far],
+        scratch=[VMEM((count, block, group_rows), F32), VMEM((group_rows, PART_WIDTH), BF16)],
         smem=1, flops=3 * group_rows * group_rows * PART_WIDTH, limit=24,
-    )
-
-    blocks = call(
-        functools.partial(apply_kernel, first_goal, first_rows),
-        [jax.ShapeDtypeStruct((tok_dev, PART_WIDTH), BF16)] * PARTS,
-        [place, weights, query_seq, attended] + pieces + pieces_other,
-        scratch=[
-            VMEM((PART_FAST, 3, SPAN, hidden), BF16),
-            VMEM((PART_FAST * 3, hidden), F32),
-            VMEM((group_rows, PART_WIDTH), BF16),
-        ],
-        smem=1, flops=6 * group_rows * PART_WIDTH * hidden, limit=40,
     )
 
     parts = []

time: 180 us -> 184 us (1.022)
  waiting for transfers between devices: 83.6 us -> 86.5 us
  Pallas kernels: 43.9 us -> 45.9 us
    ppermute x27, waiting for transfers between devices: 83.6 us -> 86.5 us  [permute(): return lax.ppermute(array, 'tok', route)]
    pallas_call x9, Pallas kernels: 43.9 us -> 45.9 us  [call(): pl.pallas_call(kernel, out_shape=list(outs), in_specs=specs, out_specs=ou...]
    unnamed x55 -> x53, local copies, waits for them, and re-layouts: 10.8 us -> 11.1 us
  transfers between devices with their start and end apart: 28 -> 28, of which waited for: 12 -> 15; matrix products, arithmetic and copies ran while one was open for 4% -> 5% of each run, Pallas kernels for 16% -> 17%
where the time goes in v12:
time: 184 us
  waiting for transfers between devices  86.5 us (47%)
  Pallas kernels  45.9 us (25%)
  starting transfers between devices  33.7 us (18%)
  local copies, waits for them, and re-layouts  14.3 us (8%)
  other arithmetic  2.93 us (2%)
    ppermute x27, waiting for transfers between devices, permute(): return lax.ppermute(array, 'tok', route)  86.5 us
    pallas_call x9, Pallas kernels, call(): pl.pallas_call(kernel, out_shape=list(outs), in_specs=specs, out_specs=ou...  45.9 us
    ppermute x27, starting transfers between devices, permute(): return lax.ppermute(array, 'tok', route)  26.2 us
    unnamed x53, local copies, waits for them, and re-layouts  11.1 us
    all_to_all x1, starting transfers between devices, shards(): lax.all_to_all(packed.reshape(sections, slots, 3 * PART_WIDTH), 'tok', sp...  7.45 us
  transfers between devices with their start and end apart: 28, of which 15 were waited for; matrix products, arithmetic and copies ran while one was open for 5% of the time, Pallas kernels for 17%

profile of v12, /device:TPU:0, one launch (start us, length us, event | category | flops | bytes accessed | tf_op | source)
XLA Modules:
  0.0 183.6 jit_solution(18347267017346957754)
XLA Ops:
  0.7 4.3 %shard_map.83 = (bf16[4,4,2,16,1920]{4,3,2,1,0:T(8,128)(2,1)}, bf16[128,640]{1,0:T(8,128)(2,1)}, bf16[128,640]{1,0:T(8,128)(2,1)}, bf16[128,640]{1,0:T(8,128)(2,...) custom-call(s32[22]{0:T(128)} %stack.79.place_ref, ...), custom_call_target="tpu_custom_call" | custom-call | flops 251658240 | bytes 5263448 | tf_op jit(solution)/shard_map/pallas_call | solution.py:55
  5.1 7.4 %all-to-all-start = ((bf16[32,16,1920]{2,1,0:T(8,128)(2,1)}), bf16[32,16,1920]{2,1,0:T(8,128)(2,1)}, u32[]{:S(2)}, u32[]{:S(2)}) async-start(bf16[32,16,1920]{2,1,0:T(8,128)(2,1)} %bitcast.26), calls=%async_computation | async-start | bytes 3932160 | tf_op jit(solution)/shard_map/all_to_all | solution.py:450
  18.7 13.5 %collective-permute-done.5.refs_1_ = bf16[128,640]{1,0:T(8,128)(2,1)S(1)} collective-permute-done((bf16[128,640]{1,0:T(8,128)(2,1)S(1)}, bf16[128,640]{1,0:T(8,128)(2,1)S(1)}, u32[]{:S(2)}, u32[]{:S(2)}) %collective-permute-start.5) | collective-permute-done | bytes 163872 | tf_op jit(solution)/shard_map/ppermute | solution.py:401
  37.7 3.3 %copy.10 = bf16[640,3,640]{0,2,1:T(8,128)(2,1)} copy(bf16[640,3,640]{2,0,1:T(8,128)(2,1)S(1)} %constant_dynamic-slice_fusion) | data formatting | bytes 4915200
  41.0 6.4 %collective-permute-done.7.refs_3_ = bf16[128,640]{1,0:T(8,128)(2,1)} collective-permute-done((bf16[128,640]{1,0:T(8,128)(2,1)}, bf16[128,640]{1,0:T(8,128)(2,1)}, u32[]{:S(2)}, u32[]{:S(2)}) %collective-permute-start.7) | collective-permute-done | bytes 163872 | tf_op jit(solution)/shard_map/ppermute | solution.py:401
  47.5 5.4 %shard_map.86.refs_4_ = bf16[320,1920]{1,0:T(8,128)(2,1)} custom-call(s32[22]{0:T(128)} %stack.79.place_ref, bf16[3,640,640]{2,1,0:T(8,128)(2,1)} %bitcast.23, bf16[128,640]{1,0:T(8,128)(2,1)} %get-tuple-element.35.refs_0_, bf16[128,640]{1,0:T(8,128)(2,1)} %copy-done.22, bf16[128,640]{1,0:T(8,128)(2,1)} %copy-done.24, ...), custom_call_target="tpu_custom_call" | custom-call | flops 1258291200 | bytes 4341848 | tf_op jit(solution)/shard_map/pallas_call | solution.py:55
  53.6 5.8 %shard_map.87 = (bf16[80,1920]{1,0:T(8,128)(2,1)}, bf16[80,1920]{1,0:T(8,128)(2,1)}, bf16[80,1920]{1,0:T(8,128)(2,1)}, bf16[80,1920]{1,0:T(8,128)(2,1)}) custom-call(s32[22]{0:T(128)} %stack.79.place_ref, bf16[3,640,640]{2,1,0:T(8,128)(2,1)} %bitcast.24, bf16[128,640]{1,0:T(8,128)(2,1)} %copy-done.20, bf16[128,640]{1,0:T(8,128)(2,1)} %copy-done.21, ...), custom_call_target="tpu_custom_call" | custom-call | flops 1258291200 | bytes 5570648 | tf_op jit(solution)/shard_map/pallas_call | solution.py:55
  59.4 2.4 %collective-permute-start.9 = (bf16[80,1920]{1,0:T(8,128)(2,1)}, bf16[80,1920]{1,0:T(8,128)(2,1)S(1)}, u32[]{:S(2)}, u32[]{:S(2)}) collective-permute-start(bf16[80,1920]{1,0:T(8,128)(2,1)} %get-tuple-element.42), channel_id=1, source_target_pairs={{0,8},{1,9},{2,10},{3,11},{4,12},{5,13},{6,14},{7,15},{8,0},{9,1},... | collective-permute-start | bytes 921608 | tf_op jit(solution)/shard_map/ppermute | solution.py:401
  61.8 8.3 %collective-permute-done.9 = bf16[80,1920]{1,0:T(8,128)(2,1)S(1)} collective-permute-done((bf16[80,1920]{1,0:T(8,128)(2,1)}, bf16[80,1920]{1,0:T(8,128)(2,1)S(1)}, u32[]{:S(2)}, u32[]{:S(2)}) %collective-permute-start.9) | collective-permute-done | bytes 307232 | tf_op jit(solution)/shard_map/ppermute | solution.py:401
  71.2 3.9 %collective-permute-start.10 = (bf16[80,1920]{1,0:T(8,128)(2,1)S(1)}, bf16[80,1920]{1,0:T(8,128)(2,1)S(1)}, u32[]{:S(2)}, u32[]{:S(2)}) collective-permute-start(bf16[80,1920]{1,0:T(8,128)(2,1)S(1)} %add_convert_fusion.1), channel_id=1, source_target_pairs={{0,16},{1,17},{2,18},{3,19},{4,20},{5,21},{6,22},{7,23},{8,24},{9,... | collective-permute-start | bytes 921608 | tf_op jit(solution)/shard_map/ppermute | solution.py:401
  75.1 2.2 %shard_map.82.choose_ref = bf16[512,512]{1,0:T(8,128)(2,1)} custom-call(s32[22]{0:T(128)} %stack.79.place_ref, s32[32,128]{1,0:T(8,128)} %bitcast.28), custom_call_target="tpu_custom_call" | custom-call | flops 524288 | bytes 540760 | tf_op jit(solution)/shard_map/pallas_call | solution.py:55
  77.3 3.6 %collective-permute-done.8 = bf16[80,1920]{1,0:T(8,128)(2,1)S(1)} collective-permute-done((bf16[80,1920]{1,0:T(8,128)(2,1)}, bf16[80,1920]{1,0:T(8,128)(2,1)S(1)}, u32[]{:S(2)}, u32[]{:S(2)}) %collective-permute-start.8) | collective-permute-done | bytes 307232 | tf_op jit(solution)/shard_map/ppermute | solution.py:401
  80.9 8.1 %collective-permute-done.10 = bf16[80,1920]{1,0:T(8,128)(2,1)S(1)} collective-permute-done((bf16[80,1920]{1,0:T(8,128)(2,1)S(1)}, bf16[80,1920]{1,0:T(8,128)(2,1)S(1)}, u32[]{:S(2)}, u32[]{:S(2)}) %collective-permute-start.10) | collective-permute-done | bytes 307232 | tf_op jit(solution)/shard_map/ppermute | solution.py:401
  90.8 4.1 %shard_map.84 = (bf16[512,1280]{1,0:T(8,128)(2,1)}, bf16[512,640]{1,0:T(8,128)(2,1)}) custom-call(bf16[512,512]{1,0:T(8,128)(2,1)} %shard_map.82.choose_ref, bf16[512,1920]{1,0:T(8,128)(2,1)} %bitcast.21.in_ref), custom_call_target="tpu_custom_call" | custom-call | flops 1006632960 | bytes 4456448 | tf_op jit(solution)/shard_map/pallas_call | solution.py:55
  96.6 3.6 %collective-permute-start = (bf16[512,1280]{1,0:T(8,128)(2,1)}, bf16[512,1280]{1,0:T(8,128)(2,1)}, u32[]{:S(2)}, u32[]{:S(2)}) collective-permute-start(bf16[512,1280]{1,0:T(8,128)(2,1)} %get-tuple-element.28.kv_ref), channel_id=1, source_target_pairs={{0,1},{1,0},{2,3},{3,2},{4,5},{5,4},{6,7},{7,6},{8,9},{9,8},{10,11... | collective-permute-start | bytes 3932168 | tf_op jit(solution)/shard_map/ppermute | solution.py:401
  100.4 20.5 %collective-permute-done.12.refs_2_ = bf16[32,1920]{1,0:T(8,128)(2,1)S(1)} collective-permute-done((bf16[32,1920]{1,0:T(8,128)(2,1)S(1)}, bf16[32,1920]{1,0:T(8,128)(2,1)S(1)}, u32[]{:S(2)}, u32[]{:S(2)}) %collective-permute-start.12) | collective-permute-done | bytes 122912 | tf_op jit(solution)/shard_map/ppermute | solution.py:401
  123.6 9.6 %collective-permute-done.15.refs_5_ = bf16[32,1920]{1,0:T(8,128)(2,1)S(1)} collective-permute-done((bf16[32,1920]{1,0:T(8,128)(2,1)S(1)}, bf16[32,1920]{1,0:T(8,128)(2,1)S(1)}, u32[]{:S(2)}, u32[]{:S(2)}) %collective-permute-start.15) | collective-permute-done | bytes 122912 | tf_op jit(solution)/shard_map/ppermute | solution.py:401
  135.6 4.1 %collective-permute-done.14.refs_4_ = bf16[48,1920]{1,0:T(8,128)(2,1)} collective-permute-done((bf16[48,1920]{1,0:T(8,128)(2,1)}, bf16[48,1920]{1,0:T(8,128)(2,1)}, u32[]{:S(2)}, u32[]{:S(2)}) %collective-permute-start.14) | collective-permute-done | bytes 184352 | tf_op jit(solution)/shard_map/ppermute | solution.py:401
  145.3 5.3 %shard_map.88.fast_ref = f32[512,640]{1,0:T(8,128)S(1)} custom-call(s32[22]{0:T(128)S(1)} %copy-done.8, bf16[3,640,640]{2,1,0:T(8,128)(2,1)S(1)} %bitcast.25, bf16[512,640]{1,0:T(8,128)(2,1)S(1)} %copy-done.1, bf16[80,1920]{1,0:T(8,128)(2,1)S(1)} %get-tuple-element.47.refs_0_, bf16[48,1920]{1,0:T(8,128)(2,1)} %collective-permute-done.11.refs_1_, ...), custom_call_target="tpu_custom_call" | custom-call | flops 1258291200 | bytes 6881368 | tf_op jit(solution)/shard_map/pallas_call | solution.py:55
  150.6 9.0 %shard_map.85 = (f32[512,640]{1,0:T(8,128)S(1)}, f32[512,128]{1,0:T(8,128)S(1)}) custom-call(s32[22]{0:T(128)S(1)} %copy-done.8, bf16[512,640]{1,0:T(8,128)(2,1)S(1)} %copy-done.1, s32[8,512]{1,0:T(8,128)S(1)} %reshape.18.ids_ref, bf16[512,1280]{1,0:T(8,128)(2,1)S(1)} %copy-done.9, bf16[512,1280]{1,0:T(8,128)(2,1)} %collective-permute-done.chip_ref), custom_call_target="tpu_custom_call" | custom-call | flops 1006632960 | bytes 4866136 | tf_op jit(solution)/shard_map/pallas_call | solution.py:55
  159.7 7.4 %shard_map.89 = (bf16[128,640]{1,0:T(8,128)(2,1)S(1)}, bf16[128,640]{1,0:T(8,128)(2,1)S(1)}, bf16[128,640]{1,0:T(8,128)(2,1)S(1)}, bf16[128,640]{1,0:T(8,128)(2,1)S(1)}) custom-call(s32[22]{0:T(128)S(1)} %copy-done.8, bf16[512,640]{1,0:T(8,128)(2,1)S(1)} %copy-done.1, s32[8,512]{1,0:T(8,128)S(1)} %reshape.18.ids_ref, ...), custom_call_target="tpu_custom_call" | custom-call | flops 503316480 | bytes 5521496 | tf_op jit(solution)/shard_map/pallas_call | solution.py:55
  169.9 2.6 %collective-permute-start.25 = (bf16[128,640]{1,0:T(8,128)(2,1)S(1)}, bf16[128,640]{1,0:T(8,128)(2,1)S(1)}, u32[]{:S(2)}, u32[]{:S(2)}) collective-permute-start(bf16[128,640]{1,0:T(8,128)(2,1)S(1)} %get-tuple-element.45), channel_id=1, source_target_pairs={{0,1},{1,5},{2,3},{3,7},{4,0},{5,4},{6,2},{7,6},{8,9},{9,13},{10,1... | collective-permute-start | bytes 491528 | tf_op jit(solution)/shard_map/ppermute | solution.py:401
  173.2 5.9 %collective-permute-done.25.refs_2_ = bf16[128,640]{1,0:T(8,128)(2,1)S(1)} collective-permute-done((bf16[128,640]{1,0:T(8,128)(2,1)S(1)}, bf16[128,640]{1,0:T(8,128)(2,1)S(1)}, u32[]{:S(2)}, u32[]{:S(2)}) %collective-permute-start.25) | collective-permute-done | bytes 163872 | tf_op jit(solution)/shard_map/ppermute | solution.py:401
  181.3 2.4 %shard_map.90 = bf16[128,2560]{1,0:T(8,128)(2,1)} custom-call(s32[22]{0:T(128)} %stack.79.place_ref, bf16[128,640]{1,0:T(8,128)(2,1)} %copy-done.10, bf16[128,640]{1,0:T(8,128)(2,1)} %copy-done.11, bf16[128,640]{1,0:T(8,128)(2,1)} %copy-done.12, bf16[128,640]{1,0:T(8,128)(2,1)} %copy-done.13, f32[1,2560]{1,0:T(1,128)} %reshape.19.refs_4_), custom_call_target="tpu_custom_call" | custom-call | flops 1966080 | bytes 1321048 | tf_op jit(solution)/shard_map/pallas_call | solution.py:55
  (102 shorter events, 34.3 us)
Async XLA Ops:
  5.1 85.7 %all-to-all-start = ((bf16[32,16,1920]{2,1,0:T(8,128)(2,1)}), bf16[32,16,1920]{2,1,0:T(8,128)(2,1)}, u32[]{:S(2)}, u32[]{:S(2)}) async-start(bf16[32,16,1920]{2,1,0:T(8,128)(2,1)} %bitcast.26), calls=%async_computation | async-start | bytes 3932160 | tf_op jit(solution)/shard_map/all_to_all | solution.py:450
  12.5 19.6 %collective-permute-start.5 = (bf16[128,640]{1,0:T(8,128)(2,1)S(1)}, bf16[128,640]{1,0:T(8,128)(2,1)S(1)}, u32[]{:S(2)}, u32[]{:S(2)}) collective-permute-start(bf16[128,640]{1,0:T(8,128)(2,1)S(1)} %copy-done.25), channel_id=1, source_target_pairs={{0,2},{1,3},{2,0},{3,1},{4,6},{5,7},{6,4},{7,5},{8,10},{9,11},{10,... | collective-permute-start | bytes 491528 | tf_op jit(solution)/shard_map/ppermute | solution.py:401
  14.3 19.6 %collective-permute-start.6 = (bf16[128,640]{1,0:T(8,128)(2,1)S(1)}, bf16[128,640]{1,0:T(8,128)(2,1)S(1)}, u32[]{:S(2)}, u32[]{:S(2)}) collective-permute-start(bf16[128,640]{1,0:T(8,128)(2,1)S(1)} %copy-done.23), channel_id=1, source_target_pairs={{0,4},{1,5},{2,6},{3,7},{4,0},{5,1},{6,2},{7,3},{8,12},{9,13},{10,... | collective-permute-start | bytes 491528 | tf_op jit(solution)/shard_map/ppermute | solution.py:401
  15.8 37.1 %collective-permute-start.1 = (bf16[128,640]{1,0:T(8,128)(2,1)S(1)}, bf16[128,640]{1,0:T(8,128)(2,1)S(1)}, u32[]{:S(2)}, u32[]{:S(2)}) collective-permute-start(bf16[128,640]{1,0:T(8,128)(2,1)S(1)} %copy-done.19), channel_id=1, source_target_pairs={{0,5},{1,4},{2,7},{3,6},{4,1},{5,0},{6,3},{7,2},{8,13},{9,12},{10,... | collective-permute-start | bytes 491528 | tf_op jit(solution)/shard_map/ppermute | solution.py:401
  15.8 37.1 %collective-permute-start.2 = (bf16[128,640]{1,0:T(8,128)(2,1)S(1)}, bf16[128,640]{1,0:T(8,128)(2,1)S(1)}, u32[]{:S(2)}, u32[]{:S(2)}) collective-permute-start(bf16[128,640]{1,0:T(8,128)(2,1)S(1)} %copy-done.18), channel_id=1, source_target_pairs={{0,6},{1,7},{2,4},{3,5},{4,2},{5,3},{6,0},{7,1},{8,14},{9,15},{10,... | collective-permute-start | bytes 491528 | tf_op jit(solution)/shard_map/ppermute | solution.py:401
  17.0 35.9 %collective-permute-start.3 = (bf16[128,640]{1,0:T(8,128)(2,1)S(1)}, bf16[128,640]{1,0:T(8,128)(2,1)}, u32[]{:S(2)}, u32[]{:S(2)}) collective-permute-start(bf16[128,640]{1,0:T(8,128)(2,1)S(1)} %copy-done.17), channel_id=1, source_target_pairs={{0,7},{1,6},{2,5},{3,4},{4,3},{5,2},{6,1},{7,0},{8,15},{9,14},{10,... | collective-permute-start | bytes 491528 | tf_op jit(solution)/shard_map/ppermute | solution.py:401
  32.2 20.7 %collective-permute-start.4 = (bf16[128,640]{1,0:T(8,128)(2,1)S(1)}, bf16[128,640]{1,0:T(8,128)(2,1)}, u32[]{:S(2)}, u32[]{:S(2)}) collective-permute-start(bf16[128,640]{1,0:T(8,128)(2,1)S(1)} %copy-done.16), channel_id=1, source_target_pairs={{0,1},{1,0},{2,3},{3,2},{4,5},{5,4},{6,7},{7,6},{8,9},{9,8},{10,11... | collective-permute-start | bytes 491528 | tf_op jit(solution)/shard_map/ppermute | solution.py:401
  34.5 12.9 %collective-permute-start.7 = (bf16[128,640]{1,0:T(8,128)(2,1)}, bf16[128,640]{1,0:T(8,128)(2,1)}, u32[]{:S(2)}, u32[]{:S(2)}) collective-permute-start(bf16[128,640]{1,0:T(8,128)(2,1)} %get-tuple-element.38), channel_id=1, source_target_pairs={{0,3},{1,2},{2,1},{3,0},{4,7},{5,6},{6,5},{7,4},{8,11},{9,10},{10,... | collective-permute-start | bytes 491528 | tf_op jit(solution)/shard_map/ppermute | solution.py:401
  59.4 10.7 %collective-permute-start.9 = (bf16[80,1920]{1,0:T(8,128)(2,1)}, bf16[80,1920]{1,0:T(8,128)(2,1)S(1)}, u32[]{:S(2)}, u32[]{:S(2)}) collective-permute-start(bf16[80,1920]{1,0:T(8,128)(2,1)} %get-tuple-element.42), channel_id=1, source_target_pairs={{0,8},{1,9},{2,10},{3,11},{4,12},{5,13},{6,14},{7,15},{8,0},{9,1},... | collective-permute-start | bytes 921608 | tf_op jit(solution)/shard_map/ppermute | solution.py:401
  61.8 19.1 %collective-permute-start.8 = (bf16[80,1920]{1,0:T(8,128)(2,1)}, bf16[80,1920]{1,0:T(8,128)(2,1)S(1)}, u32[]{:S(2)}, u32[]{:S(2)}) collective-permute-start(bf16[80,1920]{1,0:T(8,128)(2,1)} %get-tuple-element.40), channel_id=1, source_target_pairs={{0,8},{1,9},{2,10},{3,11},{4,12},{5,13},{6,14},{7,15},{8,0},{9,1},... | collective-permute-start | bytes 921608 | tf_op jit(solution)/shard_map/ppermute | solution.py:401
  71.2 17.7 %collective-permute-start.10 = (bf16[80,1920]{1,0:T(8,128)(2,1)S(1)}, bf16[80,1920]{1,0:T(8,128)(2,1)S(1)}, u32[]{:S(2)}, u32[]{:S(2)}) collective-permute-start(bf16[80,1920]{1,0:T(8,128)(2,1)S(1)} %add_convert_fusion.1), channel_id=1, source_target_pairs={{0,16},{1,17},{2,18},{3,19},{4,20},{5,21},{6,22},{7,23},{8,24},{9,... | collective-permute-start | bytes 921608 | tf_op jit(solution)/shard_map/ppermute | solution.py:401
  90.8 30.1 %collective-permute-start.11 = (bf16[48,1920]{1,0:T(8,128)(2,1)}, bf16[48,1920]{1,0:T(8,128)(2,1)}, u32[]{:S(2)}, u32[]{:S(2)}) collective-permute-start(bf16[48,1920]{1,0:T(8,128)(2,1)} %add_convert_fusion.3), channel_id=1, source_target_pairs={{0,16},{1,17},{2,18},{3,19},{4,20},{5,21},{6,22},{7,23},{8,24},{9,... | collective-permute-start | bytes 552968 | tf_op jit(solution)/shard_map/ppermute | solution.py:401
  94.9 64.7 %collective-permute-start.22 = (bf16[512,1280]{1,0:T(8,128)(2,1)}, bf16[512,1280]{1,0:T(8,128)(2,1)}, u32[]{:S(2)}, u32[]{:S(2)}) collective-permute-start(bf16[512,1280]{1,0:T(8,128)(2,1)} %get-tuple-element.28.kv_ref), channel_id=1, source_target_pairs={{1,8},{3,10},{5,12},{7,14},{8,1},{9,16},{10,3},{11,18},{12,5},{13,... | collective-permute-start | bytes 3932168 | tf_op jit(solution)/shard_map/ppermute | solution.py:401
  96.6 54.0 %collective-permute-start = (bf16[512,1280]{1,0:T(8,128)(2,1)}, bf16[512,1280]{1,0:T(8,128)(2,1)}, u32[]{:S(2)}, u32[]{:S(2)}) collective-permute-start(bf16[512,1280]{1,0:T(8,128)(2,1)} %get-tuple-element.28.kv_ref), channel_id=1, source_target_pairs={{0,1},{1,0},{2,3},{3,2},{4,5},{5,4},{6,7},{7,6},{8,9},{9,8},{10,11... | collective-permute-start | bytes 3932168 | tf_op jit(solution)/shard_map/ppermute | solution.py:401
  100.3 20.6 %collective-permute-start.12 = (bf16[32,1920]{1,0:T(8,128)(2,1)S(1)}, bf16[32,1920]{1,0:T(8,128)(2,1)S(1)}, u32[]{:S(2)}, u32[]{:S(2)}) collective-permute-start(bf16[32,1920]{1,0:T(8,128)(2,1)S(1)} %add_convert_fusion.4), channel_id=1, source_target_pairs={{0,16},{1,17},{2,18},{3,19},{4,20},{5,21},{6,22},{7,23},{8,24},{9,... | collective-permute-start | bytes 368648 | tf_op jit(solution)/shard_map/ppermute | solution.py:401
  100.3 33.2 %collective-permute-start.16 = (bf16[80,1920]{1,0:T(8,128)(2,1)S(1)}, bf16[80,1920]{1,0:T(8,128)(2,1)S(1)}, u32[]{:S(2)}, u32[]{:S(2)}) collective-permute-start(bf16[80,1920]{1,0:T(8,128)(2,1)S(1)} %get-tuple-element.47.refs_0_), channel_id=1, source_target_pairs={{0,1},{1,0},{2,3},{3,2},{4,5},{5,4},{6,7},{7,6},{8,9},{9,8},{10,11... | collective-permute-start | bytes 921608 | tf_op jit(solution)/shard_map/ppermute | solution.py:401
  120.9 13.3 %collective-permute-start.13 = (bf16[80,1920]{1,0:T(8,128)(2,1)S(1)}, bf16[80,1920]{1,0:T(8,128)(2,1)S(1)}, u32[]{:S(2)}, u32[]{:S(2)}) collective-permute-start(bf16[80,1920]{1,0:T(8,128)(2,1)S(1)} %get-tuple-element.47.refs_0_), channel_id=1, source_target_pairs={{0,8},{1,9},{2,10},{3,11},{4,12},{5,13},{6,14},{7,15},{8,0},{9,1},... | collective-permute-start | bytes 921608 | tf_op jit(solution)/shard_map/ppermute | solution.py:401
  122.9 10.3 %collective-permute-start.15 = (bf16[32,1920]{1,0:T(8,128)(2,1)S(1)}, bf16[32,1920]{1,0:T(8,128)(2,1)S(1)}, u32[]{:S(2)}, u32[]{:S(2)}) collective-permute-start(bf16[32,1920]{1,0:T(8,128)(2,1)S(1)} %collective-permute-done.12.refs_2_), channel_id=1, source_target_pairs={{0,8},{1,9},{2,10},{3,11},{4,12},{5,13},{6,14},{7,15},{8,0},{9,1},... | collective-permute-start | bytes 368648 | tf_op jit(solution)/shard_map/ppermute | solution.py:401
  133.2 6.5 %collective-permute-start.14 = (bf16[48,1920]{1,0:T(8,128)(2,1)}, bf16[48,1920]{1,0:T(8,128)(2,1)}, u32[]{:S(2)}, u32[]{:S(2)}) collective-permute-start(bf16[48,1920]{1,0:T(8,128)(2,1)} %collective-permute-done.11.refs_1_), channel_id=1, source_target_pairs={{0,8},{1,9},{2,10},{3,11},{4,12},{5,13},{6,14},{7,15},{8,0},{9,1},... | collective-permute-start | bytes 552968 | tf_op jit(solution)/shard_map/ppermute | solution.py:401
  134.2 7.3 %collective-permute-start.19 = (bf16[80,1920]{1,0:T(8,128)(2,1)S(1)}, bf16[80,1920]{1,0:T(8,128)(2,1)}, u32[]{:S(2)}, u32[]{:S(2)}) collective-permute-start(bf16[80,1920]{1,0:T(8,128)(2,1)S(1)} %collective-permute-done.13.refs_3_), channel_id=1, source_target_pairs={{0,1},{1,0},{2,3},{3,2},{4,5},{5,4},{6,7},{7,6},{8,9},{9,8},{10,11... | collective-permute-start | bytes 921608 | tf_op jit(solution)/shard_map/ppermute | solution.py:401
  167.1 6.0 %collective-permute-start.23 = (bf16[128,640]{1,0:T(8,128)(2,1)S(1)}, bf16[128,640]{1,0:T(8,128)(2,1)S(1)}, u32[]{:S(2)}, u32[]{:S(2)}) collective-permute-start(bf16[128,640]{1,0:T(8,128)(2,1)S(1)} %get-tuple-element.43), channel_id=1, source_target_pairs={{0,0},{1,4},{2,2},{3,6},{4,1},{5,5},{6,3},{7,7},{8,8},{9,12},{10,1... | collective-permute-start | bytes 491528 | tf_op jit(solution)/shard_map/ppermute | solution.py:401
  167.8 5.4 %collective-permute-start.24 = (bf16[128,640]{1,0:T(8,128)(2,1)S(1)}, bf16[128,640]{1,0:T(8,128)(2,1)S(1)}, u32[]{:S(2)}, u32[]{:S(2)}) collective-permute-start(bf16[128,640]{1,0:T(8,128)(2,1)S(1)} %get-tuple-element.44), channel_id=1, source_target_pairs={{0,2},{1,6},{2,0},{3,4},{4,3},{5,7},{6,1},{7,5},{8,10},{9,14},{10,... | collective-permute-start | bytes 491528 | tf_op jit(solution)/shard_map/ppermute | solution.py:401
  169.9 9.2 %collective-permute-start.25 = (bf16[128,640]{1,0:T(8,128)(2,1)S(1)}, bf16[128,640]{1,0:T(8,128)(2,1)S(1)}, u32[]{:S(2)}, u32[]{:S(2)}) collective-permute-start(bf16[128,640]{1,0:T(8,128)(2,1)S(1)} %get-tuple-element.45), channel_id=1, source_target_pairs={{0,1},{1,5},{2,3},{3,7},{4,0},{5,4},{6,2},{7,6},{8,9},{9,13},{10,1... | collective-permute-start | bytes 491528 | tf_op jit(solution)/shard_map/ppermute | solution.py:401
  172.4 8.2 %collective-permute-start.26 = (bf16[128,640]{1,0:T(8,128)(2,1)S(1)}, bf16[128,640]{1,0:T(8,128)(2,1)S(1)}, u32[]{:S(2)}, u32[]{:S(2)}) collective-permute-start(bf16[128,640]{1,0:T(8,128)(2,1)S(1)} %get-tuple-element.46), channel_id=1, source_target_pairs={{0,3},{1,7},{2,1},{3,5},{4,2},{5,6},{6,0},{7,4},{8,11},{9,15},{10,... | collective-permute-start | bytes 491528 | tf_op jit(solution)/shard_map/ppermute | solution.py:401
  (30 other events, 281.1 us)
